TPU v7x, 32 devices: a whole 2x2x4 slice. The times are simulated.
32 devices in a mesh: spot: 8 (over z, y), gene: 4 (over x, core).
Axes of the slice: x: 2, y: 2, z: 4, core: 2. Of those that a mesh axis runs over, the one named last changes fastest.
Arguments:
- logits: float32 [2048, 16384], P(None, 'spot'), may hold values from -9 to 9
- centroid_expr: float32 [2048, 2048], P('spot', 'gene'), may hold values from -6 to 6
- spatial: float32 [16384, 2048], P('spot', 'gene'), may hold values from -6 to 6
- cluster_cells: int32 [2048], replicated, may hold values from 1 to 176, 45056 in all
- density: float32 [16384], P('spot'), may hold values from 0.2 to 5
- gene_order: int32 [2048], P('gene'), may hold values from 0 to 2047, as said below
Outputs:
- loss_terms: float32 [3], replicated
- gene_pred: float32 [16384, 2048], P('spot', 'gene')
- grad_logits: float32 [2048, 16384], P('gene', 'spot')
Inputs may be any that keep to these rules, and one draw needn't show every extreme that they name: cluster_cells sum to 45056. gene_order is a permutation of the genes that maps each aligned block of 512 positions onto the same block of genes.
All inputs are finite; a program needn't handle non-finite values.
Results may differ from a plain program's by a relative error of at most 0.00021.
Values sent between devices are 32-bit elements; how exact they have to be, the bound alone decides.
No kernel may reach another device: no remote copies, remote signals or barrier semaphores. Data moves between devices by JAX's collectives and lax.ppermute only.
A program may use at most 192 MiB of HBM per device.

v0:
```python
import jax
import jax.numpy as jnp
from jax import lax
from jax.sharding import PartitionSpec as P

G = 2048
GB = 512


EPS = 1e-06
HI = lax.Precision.HIGHEST
FIRST = (((0,), (0,)), ((), ()))
SECOND = (((1,), (1,)), ((), ()))


def local(logits, centroid_expr, spatial, cluster_cells, density, gene_order):
    n_spot = lax.axis_size("spot")
    n_gene = lax.axis_size("gene")
    cents, spot_dev = logits.shape
    gene_dev = spatial.shape[1]
    batches = G // GB
    width = gene_dev // batches
    spots_all = spot_dev * n_spot
    scale = float(spots_all * cents)
    probs = jax.nn.softmax(logits, axis=0)
    weights = cluster_cells.astype(jnp.float32)
    weights = weights / jnp.sum(weights)
    raw = jnp.dot(weights, probs, precision=HI, preferred_element_type=jnp.float32)
    local_order = (gene_order - lax.axis_index("gene") * gene_dev).reshape(batches, width)
    kept = []
    targets = []
    preds = []
    gene_parts = []
    spot_parts = []
    predicted = jnp.zeros((spot_dev, gene_dev), jnp.float32)
    for batch in range(batches):
        columns = local_order[batch]
        block = jnp.take(centroid_expr, columns, axis=1)
        target = jnp.take(spatial, columns, axis=1)
        kept.append(block)
        pred = lax.dot_general(
            probs,
            lax.all_gather(block, "spot", axis=0, tiled=True),
            FIRST,
            precision=HI,
            preferred_element_type=jnp.float32,
        )
        predicted = predicted.at[:, columns].set(pred)
        gene_three = jnp.stack(
            [
                jnp.sum(pred * target, axis=0),
                jnp.sum(pred * pred, axis=0),
                jnp.sum(target * target, axis=0),
            ]
        )
        spot_three = jnp.stack(
            [
                jnp.sum(pred * target, axis=1),
                jnp.sum(pred * pred, axis=1),
                jnp.sum(target * target, axis=1),
            ]
        )
        gene_three = lax.psum(gene_three, "spot")
        spot_three = lax.psum(spot_three, "gene")
        gene_parts.append(gene_three)
        spot_parts.append(spot_three)
        targets.append(target)
        preds.append(pred)
    raw_total, dens_total = lax.psum((jnp.sum(raw), jnp.sum(density)), "spot")
    gene_all = jnp.stack(gene_parts, 0)
    spot_all = jnp.stack(spot_parts, 0)
    partial_value = jnp.zeros((cents, spot_dev), jnp.float32)
    gene_cos_sum = jnp.float32(0.0)
    spot_cos_sum = jnp.float32(0.0)
    for batch in range(batches):
        upper = gene_all[batch, 1] + EPS
        inv_gene = lax.rsqrt(upper) * lax.rsqrt(gene_all[batch, 2] + EPS)
        gene_cos = gene_all[batch, 0] * inv_gene
        supper = spot_all[batch, 1] + EPS
        inv_spot = lax.rsqrt(supper) * lax.rsqrt(spot_all[batch, 2] + EPS)
        spot_cos = spot_all[batch, 0] * inv_spot
        gene_cos_sum = gene_cos_sum + jnp.sum(gene_cos)
        spot_cos_sum = spot_cos_sum + jnp.sum(spot_cos)
        pred = preds[batch]
        target = targets[batch]
        grad_pred = -(scale / G) * (target * inv_gene[None, :] - (gene_cos / upper)[None, :] * pred)
        grad_pred = grad_pred - scale / (batches * spots_all) * (
            target * inv_spot[:, None] - (spot_cos / supper)[:, None] * pred
        )

        def back_rows(piece, start, grad_pred=grad_pred):
            return lax.dot_general(
                piece, grad_pred, SECOND, precision=HI, preferred_element_type=jnp.float32
            )

        partial_value = partial_value + back_rows(
            lax.all_gather(kept[batch], "spot", axis=0, tiled=True), jnp.int32(0)
        )
    dens_norm = density / dens_total
    grad_raw = scale * (-dens_norm / raw + 1.0 / raw_total)
    share_rows = cents // n_gene
    first_row = lax.axis_index("gene") * share_rows
    summed = lax.psum(partial_value, "gene")
    grad_probs = summed + weights[:, None] * grad_raw[None, :]
    column = jnp.sum(probs * grad_probs, axis=0)
    grad_every = probs * (grad_probs - column[None, :])
    grad_logits = lax.dynamic_slice_in_dim(grad_every, first_row, share_rows, 0)
    diverge = jnp.sum(dens_norm * (jnp.log(dens_norm) - jnp.log(raw / raw_total)))
    local_terms = jnp.stack(
        [
            -gene_cos_sum / G / n_spot,
            -spot_cos_sum / (batches * spots_all) / n_gene,
            diverge / n_gene,
        ]
    )
    loss_terms = lax.psum(local_terms, ("spot", "gene"))
    return (loss_terms, predicted, grad_logits)


def solution(mesh):
    return jax.shard_map(
        local,
        mesh=mesh,
        in_specs=(P(None, "spot"), P("spot", "gene"), P("spot", "gene"), P(), P("spot"), P("gene")),
        out_specs=(P(), P("spot", "gene"), P("gene", "spot")),
        check_vma=False,
    )
```

profile of v0, /device:TPU:1, one launch (start us, length us, event | category | flops | bytes accessed | tf_op | source)
XLA Modules:
  0.0 661.2 jit_solution(2332930670432425123)
XLA Ops:
  15.5 5.3 copy.10
  20.8 4.7 gather_fusion.7
  25.5 3.6 gather_fusion.5
  29.2 4.6 gather_fusion.3
  33.7 4.6 gather_fusion.1
  39.9 6.6 %reduce_max.9 = f32[2048]{0:T(1024)S(1)} reduce(f32[2048,2048]{1,0:T(8,128)} %param.10, f32[]{:T(128)} %constant.12.clone.1), dimensions={0}, to_apply=%region_0.0 | reduce | flops 4192256 | bytes 16785412 | tf_op jit(solution)/shard_map/reduce_max | solution.py:25
  46.5 8.1 %fusion.1 = f32[2048]{0:T(1024)S(1)} fusion(f32[2048,2048]{1,0:T(8,128)} %param.10, f32[2048]{0:T(1024)S(1)} %reduce_max.9), kind=kLoop, calls=%fused_computation.17 | loop fusion | flops 8386560 | bytes 16793600 | tf_op jit(solution)/shard_map/reduce_sum | solution.py:25
  54.6 11.8 %fusion = f32[2048,2048]{1,0:T(8,128)} fusion(f32[2048,2048]{1,0:T(8,128)} %param.10, f32[2048]{0:T(1024)S(1)} %fusion.1, f32[2048]{0:T(1024)S(1)} %reduce_max.9), kind=kLoop, calls=%fused_computation.16 | loop fusion | flops 8388608 | bytes 33570816 | tf_op jit(solution)/shard_map/div | solution.py:25
  67.8 2.5 copy.14
  70.3 2.5 copy.11
  74.1 11.7 %fusion.115 = f32[1,2048]{1,0:T(1,128)S(1)} fusion(f32[2048,1]{0,1:T(1,128)S(1)} %bitcast.255, f32[2048,2048]{1,0:T(8,128)} %fusion), kind=kOutput, calls=%fused_computation.220 | convolution fusion | flops 50331648 | bytes 16793600 | tf_op jit(solution)/shard_map/dot_general | solution.py:28
  87.0 30.2 %fusion.94 = (f32[128]{0:T(128)S(1)}, f32[2048]{0:T(1024)S(1)}, f32[128]{0:T(128)S(1)}, f32[2048]{0:T(1024)S(1)}, f32[2048]{0:T(1024)S(1)}, /*index=5*/f32[128]{0:T(128)S(1)}, f32[2048,128]{1,0:T(8,128)S(1)}) fusion(f32[128,2048]{0,1:T(8,128)S(1)} %copy.20, pred[128]{0:T(512)(128)(4,1)S(1)} %get-tuple-element.60, f32[2048,2048]{1,0:T(8,128)} %fusion, ...), kind=kOutput, calls=%fused_computation.128 | convolution fusion | flops 6445065728 | bytes 19949184 | tf_op jit(solution)/shard_map/dot_general | solution.py:41
  117.2 31.2 %fusion.92 = (f32[128]{0:T(128)S(1)}, f32[2048]{0:T(1024)S(1)}, f32[128]{0:T(128)S(1)}, f32[2048]{0:T(1024)S(1)}, f32[2048]{0:T(1024)S(1)}, /*index=5*/f32[128]{0:T(128)S(1)}, f32[2048,128]{1,0:T(8,128)}) fusion(f32[128,2048]{0,1:T(8,128)} %copy.17, pred[128]{0:T(512)(128)(4,1)S(1)} %get-tuple-element.82, f32[2048,2048]{1,0:T(8,128)} %fusion, ...), kind=kOutput, calls=%fused_computation.126 | convolution fusion | flops 6445065728 | bytes 19949184 | tf_op jit(solution)/shard_map/dot_general | solution.py:41
  148.5 31.3 %fusion.90 = (f32[128]{0:T(128)S(1)}, f32[2048]{0:T(1024)S(1)}, f32[128]{0:T(128)S(1)}, f32[2048]{0:T(1024)S(1)}, f32[2048]{0:T(1024)S(1)}, /*index=5*/f32[128]{0:T(128)S(1)}, f32[2048,128]{1,0:T(8,128)}) fusion(f32[128,2048]{0,1:T(8,128)} %copy.14, pred[128]{0:T(512)(128)(4,1)S(1)} %get-tuple-element.84, f32[2048,2048]{1,0:T(8,128)} %fusion, ...), kind=kOutput, calls=%fused_computation.124 | convolution fusion | flops 6445065728 | bytes 19949184 | tf_op jit(solution)/shard_map/dot_general | solution.py:41
  179.8 31.0 %fusion.88 = (f32[128]{0:T(128)S(1)}, f32[2048]{0:T(1024)S(1)}, f32[128]{0:T(128)S(1)}, f32[2048]{0:T(1024)S(1)}, f32[2048]{0:T(1024)S(1)}, /*index=5*/f32[128]{0:T(128)S(1)}, f32[2048,128]{1,0:T(8,128)}) fusion(f32[128,2048]{0,1:T(8,128)} %copy.11, pred[128]{0:T(512)(128)(4,1)S(1)} %get-tuple-element.86, f32[2048,2048]{1,0:T(8,128)} %fusion, ...), kind=kOutput, calls=%fused_computation.122 | convolution fusion | flops 6445065728 | bytes 19949184 | tf_op jit(solution)/shard_map/dot_general | solution.py:41
  210.8 19.8 %all-reduce = (f32[]{:T(128)}, f32[]{:T(128)}, f32[1,3,128]{2,1,0:T(4,128)S(1)}, f32[1,3,128]{2,1,0:T(4,128)S(1)}, f32[1,3,128]{2,1,0:T(4,128)S(1)}, /*index=5*/f32[1,3,128]{2,1,0:T(4,128)S(1)}) all-reduce(f32[]{:T(128)} %reduce_sum.377, f32[]{:T(128)} %reduce_sum.375, ...), channel_id=1, replica_groups=mesh['spot'=8,'gene'=4] {'spot'}, use_global_device_ids=true, to_apply=%region_46.49 | all-reduce | flops 1538 | bytes 12304 | tf_op jit(solution)/shard_map/psum | solution.py:69
  233.3 31.3 %all-reduce.7.cloned.1.call-done = (f32[1,3,2048]{2,1,0:T(4,128)}, f32[1,3,2048]{2,1,0:T(4,128)}, f32[1,3,2048]{2,1,0:T(4,128)}, f32[1,3,2048]{2,1,0:T(4,128)}) async-done(((f32[1,3,2048]{2,1,0:T(4,128)}, f32[1,3,2048]{2,1,0:T(4,128)}, f32[1,3,2048]{2,1,0:T(4,128)}, f32[1,3,2048]{2,1,0:T(4,128)}), (f32[1,3,2048]{2,1,0:T(4,128)}, f32[1,3,2048]{2,1,0:T(4,128)}, f32[1,3,2048]{2,1,0:T(4,128)}, ...) | async-done | bytes 98320 | tf_op jit(solution)/shard_map/psum | solution.py:64
  266.6 16.4 %fusion.22 = f32[2048,2048]{1,0:T(8,128)S(1)} fusion(f32[2048,128]{0,1:T(8,128)} %all-gather.7.cloned.1.call-done, f32[2048,128]{1,0:T(8,128)} %get-tuple-element.89, f32[128,2048]{0,1:T(8,128)} %copy.14, f32[2048]{0:T(1024)S(1)} %get-tuple-element.50, f32[2048]{0:T(1024)S(1)} %get-tuple-element.51, f32[128]{0:T(128)S(1)} %get-tuple-element.48, ...), kind=kOutput, calls=%fused_computation.48 | convolution fusion | flops 6445072384 | bytes 19940480 | tf_op jit(solution)/shard_map/dot_general | solution.py:92
  283.1 20.3 %fusion.30 = f32[2048,2048]{1,0:T(8,128)} fusion(f32[2048,128]{0,1:T(8,128)} %all-gather.5.cloned.1.call-done, f32[2048,128]{1,0:T(8,128)S(1)} %copy-done.3, f32[128,2048]{0,1:T(8,128)} %copy.11, f32[2048]{0:T(1024)S(1)} %get-tuple-element.54, f32[2048]{0:T(1024)S(1)} %get-tuple-element.55, f32[128]{0:T(128)S(1)} %get-tuple-element.52, ...), kind=kOutput, calls=%fused_computation.58 | convolution fusion | flops 6445072384 | bytes 19940480 | tf_op jit(solution)/shard_map/dot_general | solution.py:92
  303.4 18.0 %fusion.14 = f32[2048,2048]{1,0:T(8,128)} fusion(f32[2048,128]{0,1:T(8,128)S(1)} %copy-done.4, f32[2048,128]{1,0:T(8,128)S(1)} %copy-done, f32[128,2048]{0,1:T(8,128)S(1)} %copy-done.2, f32[2048]{0:T(1024)S(1)} %get-tuple-element.58, f32[2048]{0:T(1024)S(1)} %get-tuple-element.59, f32[128]{0:T(128)S(1)} %get-tuple-element.56, ...), kind=kOutput, calls=%fused_computation.38 | convolution fusion | flops 6445072384 | bytes 19940480 | tf_op jit(solution)/shard_map/dot_general | solution.py:92
  321.4 23.8 %add_add_fusion = f32[2048,2048]{1,0:T(8,128)} fusion(f32[2048,2048]{1,0:T(8,128)} %fusion.14, f32[2048,2048]{1,0:T(8,128)} %fusion.30, f32[2048,2048]{1,0:T(8,128)S(1)} %fusion.22, f32[2048,128]{0,1:T(8,128)} %all-gather.11.cloned.1.call-done, f32[2048,128]{1,0:T(8,128)S(1)} %get-tuple-element.91, f32[128,2048]{0,1:T(8,128)S(1)} %copy.20, ...), kind=kOutput, calls=%fused_computation.14 | convolution fusion | flops 6457655296 | bytes 70272128 | tf_op jit(solution)/shard_map/dot_general | solution.py:92
  345.2 2.6 copy.21
  347.9 4.1 scatter_custom_fusion
  352.0 2.8 copy.22
  360.7 6.1 scatter_fusion
  366.8 5.7 scatter_fusion.1
  372.5 5.4 scatter_fusion.2
  385.6 5.3 copy.25
  390.9 42.3 %psum.94 = f32[3]{0:T(128)} all-reduce(f32[3]{0:T(128)S(1)} %pad_maximum_fusion), channel_id=1, replica_groups=mesh['spot'=8,'gene'=4] {'spot','gene'}, use_global_device_ids=true, to_apply=%region_48.51 | all-reduce | flops 3 | bytes 24 | tf_op jit(solution)/shard_map/psum | solution.py:116
  433.2 203.3 %all-reduce.5.cloned.1.call-done = f32[2048,2048]{1,0:T(8,128)} async-done(((f32[2048,2048]{1,0:T(8,128)}), f32[2048,2048]{1,0:T(8,128)}) %all-reduce.5.cloned.1.call-update) | async-done | bytes 16777232 | tf_op jit(solution)/shard_map/psum | solution.py:103
  636.5 12.2 %multiply_reduce_fusion = (f32[2048]{0:T(1024)S(1)}, f32[2048,2048]{1,0:T(8,128)S(1)}) fusion(f32[2048,2048]{1,0:T(8,128)} %all-reduce.5.cloned.1.call-done, f32[2048]{0:T(1024)S(1)} %get-tuple-element.80, f32[2048]{0:T(1024)S(1)} %convert_divide_fusion, f32[2048]{0:T(1024)S(1)} %fusion.1, f32[2048,2048]{1,0:T(8,128)} %param.10, f32[2048]{0:T(1024)S(1)} %reduce_max.9), kind=kLoop, calls=%fused_computation.12 | loop fusion | flops 25163776 | bytes 50372608 | tf_op jit(solution)/shard_map/reduce_sum | solution.py:105
  648.7 5.2 dynamic-slice_multiply_fusion
  (81 shorter events, 25.6 us)
Async XLA Ops:
  7.2 79.8 %all-gather.11.cloned.1.call-start = ((), (), s32[]{:S(2)}) async-start(), calls=%async_computation.3 | async-start | bytes 1179648 | tf_op jit(solution)/shard_map/all_gather | solution.py:43
  10.7 106.5 %all-gather.9.cloned.1.call-start = ((), (), s32[]{:S(2)}) async-start(), calls=%async_computation.2 | async-start | bytes 1179648 | tf_op jit(solution)/shard_map/all_gather | solution.py:43
  12.3 136.2 %all-gather.7.cloned.1.call-start = ((), (), s32[]{:S(2)}) async-start(), calls=%async_computation.1 | async-start | bytes 1179648 | tf_op jit(solution)/shard_map/all_gather | solution.py:43
  13.9 165.9 %all-gather.5.cloned.1.call-start = ((), (), s32[]{:S(2)}) async-start(), calls=%async_computation | async-start | bytes 1179648 | tf_op jit(solution)/shard_map/all_gather | solution.py:43
  15.4 249.2 %all-reduce.7.cloned.1.call-start = ((), (), s32[]{:S(2)}) async-start(), calls=%async_computation.5 | async-start | bytes 262144 | tf_op jit(solution)/shard_map/psum | solution.py:64
  54.6 18.2 %copy-start.6 = (s32[2048]{0:T(1024)S(1)}, s32[2048]{0:T(1024)}, u32[]{:S(2)}) copy-start(s32[2048]{0:T(1024)} %param.13) | copy-start | bytes 24580
  66.4 20.0 %copy-start.7 = (f32[2048]{0:T(1024)S(1)}, f32[2048]{0:T(1024)}, u32[]{:S(2)}) copy-start(f32[2048]{0:T(1024)} %param.14) | copy-start | bytes 24580
  233.2 403.3 %all-reduce.5.cloned.1.call-start = ((), (), s32[]{:S(2)}) async-start(), calls=%async_computation.4 | async-start | bytes 33554432 | tf_op jit(solution)/shard_map/psum | solution.py:103
  264.6 18.5 %copy-start.3 = (f32[2048,128]{1,0:T(8,128)S(1)}, f32[2048,128]{1,0:T(8,128)}, u32[]{:S(2)}) copy-start(f32[2048,128]{1,0:T(8,128)} %get-tuple-element.88) | copy-start | bytes 3145732
  283.1 20.4 %copy-start = (f32[2048,128]{1,0:T(8,128)S(1)}, f32[2048,128]{1,0:T(8,128)}, u32[]{:S(2)}) copy-start(f32[2048,128]{1,0:T(8,128)} %get-tuple-element.90) | copy-start | bytes 3145732
  283.1 20.4 %copy-start.2 = (f32[128,2048]{0,1:T(8,128)S(1)}, f32[128,2048]{0,1:T(8,128)}, u32[]{:S(2)}) copy-start(f32[128,2048]{0,1:T(8,128)} %copy.17) | copy-start | bytes 3145732
  283.1 20.4 %copy-start.4 = (f32[2048,128]{0,1:T(8,128)S(1)}, f32[2048,128]{0,1:T(8,128)}, u32[]{:S(2)}) copy-start(f32[2048,128]{0,1:T(8,128)} %all-gather.9.cloned.1.call-done) | copy-start | bytes 3145732
  345.2 9.6 %copy-start.1 = (f32[2048,128]{1,0:T(8,128)S(1)}, f32[2048,128]{1,0:T(8,128)}, u32[]{:S(2)}) copy-start(f32[2048,128]{1,0:T(8,128)} %get-tuple-element.90) | copy-start | bytes 3145732
  356.5 10.3 %copy-start.5 = (f32[128,2048]{1,0:T(8,128)S(1)}, f32[128,2048]{1,0:T(8,128)}, u32[]{:S(2)}) copy-start(f32[128,2048]{1,0:T(8,128)} %copy.23) | copy-start | bytes 3145732
Sparse Core Ops, SparseCore 0:
  10.8 39.1 all-gather.10
  52.1 38.4 all-gather.8
  92.6 38.4 all-gather.6
  132.9 38.8 all-gather.4
  233.3 31.2 all-reduce.6
  345.4 291.0 all-reduce.4
where the time goes:
time: 671 us; the launch traced here: 661 us
  waiting for transfers between devices  235 us (35%)
  matrix products  214 us (32%)
  local copies, waits for them, and re-layouts  68.8 us (10%)
  blocking collectives  62.1 us (9%)
  other arithmetic  60.2 us (9%)
  between operations  21.1 us (3%)
    psum x1, waiting for transfers between devices, local(): summed = lax.psum(partial_value, 'gene')  203 us
    dot_general x4, matrix products, local(): lax.dot_general(probs, lax.all_gather(block, 'spot', axis=0, tiled=True),...  124 us
    dot_general x4, matrix products, back_rows(): lax.dot_general(piece, grad_pred, SECOND, precision=HI, preferred_element...  78.6 us
    psum x1, blocking collectives, local(): loss_terms = lax.psum(local_terms, ('spot', 'gene'))  42.3 us
    psum x1, waiting for transfers between devices, local(): spot_three = lax.psum(spot_three, 'gene')  31.3 us
    gather x8, local copies, waits for them, and re-layouts, local(): target = jnp.take(spatial, columns, axis=1)  25.4 us
    scatter x4, local copies, waits for them, and re-layouts, local(): predicted = predicted.at[:, columns].set(pred)  21.3 us
    psum x1, blocking collectives, local(): raw_total, dens_total = lax.psum((jnp.sum(raw), jnp.sum(density)), 'spot')  19.8 us
  transfers between devices with their start and end apart: 6, of which 2 were waited for; matrix products, arithmetic and copies ran while one was open for 31% of the time, Pallas kernels for 0%

commit v1 on v0

v1 whole, which is shorter than its diff:
```python
import functools
import jax
import jax.numpy as jnp
from jax import lax
from jax.experimental import pallas as pl
from jax.experimental.pallas import tpu as pltpu
from jax.sharding import PartitionSpec as P

NB = 4
EPS = 1e-06
BF = jnp.bfloat16
F32 = jnp.float32
KC = 256
NT = (((1,), (1,)), ((), ()))
TN = (((0,), (0,)), ((), ()))
VMEM_LIMIT = 60 << 20


def split(value):
    high = value.astype(BF)
    return high, (value - high.astype(F32)).astype(BF)


def store_left(ref, rows, start, value):
    high, low = split(value)
    width = value.shape[1]
    ref[rows, start : start + width] = high
    ref[rows, start + width : start + 2 * width] = high
    ref[rows, start + 2 * width : start + 3 * width] = low


def store_right(ref, start, value):
    high, low = split(value)
    depth = value.shape[0]
    ref[start : start + depth] = high
    ref[start + depth : start + 2 * depth] = low
    ref[start + 2 * depth : start + 3 * depth] = high


def params():
    return pltpu.CompilerParams(dimension_semantics=("arbitrary",), vmem_limit_bytes=VMEM_LIMIT)


def turn_kernel(order_ref, x_ref, out_ref):
    high, low = split(x_ref[...])
    pick = order_ref[...]
    out_ref[...] = lax.dot_general(pick, high, NT, preferred_element_type=F32) + lax.dot_general(
        pick, low, NT, preferred_element_type=F32
    )


def turn(pick, x, tile=256):
    spots, genes = x.shape
    return pl.pallas_call(
        turn_kernel,
        out_shape=jax.ShapeDtypeStruct((genes, spots), F32),
        grid=(spots // tile,),
        in_specs=[
            pl.BlockSpec((genes, genes), lambda i: (0, 0)),
            pl.BlockSpec((tile, genes), lambda i: (i, 0)),
        ],
        out_specs=pl.BlockSpec((genes, tile), lambda i: (0, i)),
        compiler_params=params(),
        cost_estimate=pl.CostEstimate(
            flops=4 * genes * genes * spots, bytes_accessed=8 * genes * spots, transcendentals=0
        ),
        name="turn",
    )(pick, x)


def products(ah, bh, l_refs, first_sum=None, w_refs=None):
    total = weighted = None
    at = 0
    for number, l_ref in enumerate(l_refs):
        for part in range(l_ref.shape[0] // KC):
            rows = slice(part * KC, part * KC + KC)
            value = jnp.exp(l_ref[rows, :])
            store_right(bh, at, value)
            at += 3 * KC
            if w_refs is not None:
                one = jnp.sum(value, axis=0, keepdims=True)
                two = jnp.sum(value * w_refs[number][rows, :], axis=0, keepdims=True)
                total = one if total is None else total + one
                weighted = two if weighted is None else weighted + two
    return jnp.dot(ah[...], bh[...], preferred_element_type=F32), total, weighted


def load_left(ah, s_refs):
    at = 0
    for s_ref in s_refs:
        for part in range(s_ref.shape[1] // KC):
            store_left(ah, slice(None), at, s_ref[:, part * KC : part * KC + KC])
            at += 3 * KC


def own_kernel(count, cents, *refs):
    refs = refs[1:]
    s_refs, l_refs, w_refs = refs[:count], refs[count : 2 * count], refs[2 * count : 3 * count]
    x_ref, d_ref, pick_ref, pred_ref, out_ref, info_ref, ah, bh, sums, scal = refs[3 * count :]
    step = pl.program_id(0)
    tile = x_ref.shape[1]
    genes = x_ref.shape[0]
    width = genes // NB

    @pl.when(step == 0)
    def _():
        load_left(ah, s_refs)
        sums[...] = jnp.zeros_like(sums)
        scal[...] = jnp.zeros_like(scal)
        info_ref[...] = jnp.zeros_like(info_ref)

    value, total, weighted = products(ah, bh, l_refs, w_refs=w_refs)
    inv = 1.0 / total
    pred = value * inv
    pred_ref[...] = pred
    high, low = split(pred)
    pick = pick_ref[...]
    out_ref[...] = lax.dot_general(high, pick, TN, preferred_element_type=F32) + lax.dot_general(
        low, pick, TN, preferred_element_type=F32
    )
    x = x_ref[...]
    rows = []
    for number, product in enumerate((pred * x, pred * pred, x * x)):
        for batch in range(NB):
            rows.append(
                jnp.sum(product[batch * width : (batch + 1) * width], axis=0, keepdims=True)
            )
        lanes = product[:, :128]
        for group in range(1, tile // 128):
            lanes = lanes + product[:, group * 128 : group * 128 + 128]
        sums[number] += lanes
    raw = weighted * inv
    dens = d_ref[...]
    at = pl.ds(pl.multiple_of(step * tile, 128), tile)
    info_ref[0 : 3 * NB, at] = jnp.concatenate(rows, axis=0)
    info_ref[13:14, at] = inv
    info_ref[14:15, at] = raw
    scal[0:1] += dens
    scal[1:2] += raw
    scal[2:3] += dens * (jnp.log(dens) - jnp.log(raw * cents))

    @pl.when(step == pl.num_programs(0) - 1)
    def _():
        for number in range(3):
            info_ref[12:13, number * genes : (number + 1) * genes] = jnp.sum(
                sums[number].T, axis=0, keepdims=True
            )
        for number in range(3):
            info_ref[15:16, number * 128 : number * 128 + 128] = jnp.broadcast_to(
                jnp.sum(scal[number : number + 1], axis=1, keepdims=True), (1, 128)
            )


def own_part(blocks, index, logits, weights, x_own, density, pick, tile=256):
    cents, spots = logits.shape
    genes, deep = blocks[0].shape
    count = len(blocks)
    whole = lambda i, ix: (0, 0)
    specs = [pl.BlockSpec((genes, deep), whole, pipeline_mode=pl.Buffered(1)) for _ in blocks]
    specs += [
        pl.BlockSpec((deep, tile), functools.partial(lambda b, i, ix: (ix[b], i), b))
        for b in range(count)
    ]
    specs += [
        pl.BlockSpec((deep, 1), functools.partial(lambda b, i, ix: (ix[b], 0), b))
        for b in range(count)
    ]
    specs += [
        pl.BlockSpec((genes, tile), lambda i, ix: (0, i)),
        pl.BlockSpec((1, tile), lambda i, ix: (0, i)),
        pl.BlockSpec((genes, genes), whole),
    ]
    return pl.pallas_call(
        functools.partial(own_kernel, count, float(cents)),
        out_shape=(
            jax.ShapeDtypeStruct((genes, spots), F32),
            jax.ShapeDtypeStruct((spots, genes), F32),
            jax.ShapeDtypeStruct((16, spots), F32),
        ),
        grid_spec=pltpu.PrefetchScalarGridSpec(
            num_scalar_prefetch=1,
            grid=(spots // tile,),
            in_specs=specs,
            out_specs=(
                pl.BlockSpec((genes, tile), lambda i, ix: (0, i)),
                pl.BlockSpec((tile, genes), lambda i, ix: (i, 0)),
                pl.BlockSpec((16, spots), whole),
            ),
            scratch_shapes=[
                pltpu.VMEM((genes, 3 * cents), BF),
                pltpu.VMEM((3 * cents, tile), BF),
                pltpu.VMEM((3, genes, 128), F32),
                pltpu.VMEM((8, tile), F32),
            ],
        ),
        compiler_params=params(),
        cost_estimate=pl.CostEstimate(
            flops=6 * genes * cents * spots, bytes_accessed=4 * cents * spots, transcendentals=0
        ),
        name="own_part",
    )(index, *blocks, *([logits] * count), *([weights] * count), x_own, density, pick)


def other_kernel(count, first, last, *refs):
    refs = refs[1:]
    s_refs, l_refs = refs[:count], refs[count : 2 * count]
    refs = refs[2 * count :]
    if not first:
        acc_ref, refs = refs[0], refs[1:]
    if last:
        info_ref, refs = refs[0], refs[1:]
    out_ref, ah, bh = refs

    @pl.when(pl.program_id(0) == 0)
    def _():
        load_left(ah, s_refs)

    value, _, _ = products(ah, bh, l_refs)
    if not first:
        value = value + acc_ref[...]
    if last:
        value = value * info_ref[5:6, :]
    out_ref[...] = value


def other_part(blocks, index, logits, acc, info, tile=256):
    cents, spots = logits.shape
    genes, deep = blocks[0].shape
    count = len(blocks)
    first, last = acc is None, info is not None
    whole = lambda i, ix: (0, 0)
    specs = [pl.BlockSpec((genes, deep), whole, pipeline_mode=pl.Buffered(1)) for _ in blocks]
    specs += [
        pl.BlockSpec((deep, tile), functools.partial(lambda b, i, ix: (ix[b], i), b))
        for b in range(count)
    ]
    args = [index, *blocks, *([logits] * count)]
    alias = {}
    if not first:
        alias = {len(args): 0}
        specs.append(pl.BlockSpec((genes, tile), lambda i, ix: (0, i)))
        args.append(acc)
    if last:
        specs.append(pl.BlockSpec((8, tile), lambda i, ix: (1, i)))
        args.append(info)
    return pl.pallas_call(
        functools.partial(other_kernel, count, first, last),
        out_shape=jax.ShapeDtypeStruct((genes, spots), F32),
        grid_spec=pltpu.PrefetchScalarGridSpec(
            num_scalar_prefetch=1,
            grid=(spots // tile,),
            in_specs=specs,
            out_specs=pl.BlockSpec((genes, tile), lambda i, ix: (0, i)),
            scratch_shapes=[
                pltpu.VMEM((genes, 3 * deep * count), BF),
                pltpu.VMEM((3 * deep * count, tile), BF),
            ],
        ),
        input_output_aliases=alias,
        compiler_params=params(),
        cost_estimate=pl.CostEstimate(
            flops=6 * genes * deep * count * spots,
            bytes_accessed=4 * deep * count * spots + 8 * genes * spots,
            transcendentals=0,
        ),
        name="other_part",
    )(*args)


def cosine(inner, left, right):
    left = left + EPS
    inv = lax.rsqrt(left) * lax.rsqrt(right + EPS)
    cos = inner * inv
    return cos, inv, cos / left


def pack_kernel(spots_ref, mine_ref, theirs_ref, out_ref):
    genes = out_ref.shape[1] // 2
    totals = spots_ref[...]
    cos, _, _ = cosine(totals[0:NB], totals[NB : 2 * NB], totals[2 * NB : 3 * NB])
    out_ref[...] = jnp.zeros_like(out_ref)
    for number in range(3):
        at = slice(number * genes, (number + 1) * genes)
        out_ref[number : number + 1, 0:genes] = mine_ref[12:13, at]
        out_ref[number : number + 1, genes : 2 * genes] = theirs_ref[12:13, at]
        out_ref[3 + number : 4 + number, 0:128] = mine_ref[15:16, number * 128 : number * 128 + 128]
    out_ref[6:7, 0:128] = jnp.broadcast_to(
        jnp.sum(jnp.sum(cos, axis=0, keepdims=True), axis=1, keepdims=True), (1, 128)
    )


def pack(spot_totals, mine, theirs, genes):
    return pl.pallas_call(
        pack_kernel,
        out_shape=jax.ShapeDtypeStruct((8, 2 * genes), F32),
        compiler_params=pltpu.CompilerParams(vmem_limit_bytes=VMEM_LIMIT),
        name="pack",
    )(spot_totals, mine, theirs)


def rows_left(ah, buffer, sem, which, refs, of_part, rows):
    genes, deep = refs[0][0].shape
    for part in range(2):
        for piece in range(rows // KC):
            at = slice(piece * KC, piece * KC + KC)
            block, offset = of_part(which, piece)
            if len(refs[part]) == 1:
                src = refs[part][0].at[:, pl.ds(pl.multiple_of(offset, KC), KC)]
                pltpu.make_async_copy(src, buffer, sem).start()
            else:
                for number, ref in enumerate(refs[part]):

                    @pl.when(block == number)
                    def _(ref=ref):
                        pltpu.make_async_copy(ref, buffer, sem).start()

            pltpu.make_async_copy(refs[part][0].at[:, 0:KC], buffer, sem).wait()
            high, low = split(buffer[...].T)
            width = 2 * genes
            start = part * genes
            ah[at, start : start + genes] = high
            ah[at, width + start : width + start + genes] = high
            ah[at, 2 * width + start : 2 * width + start + genes] = low


def back_kernel(count, final, sizes, *refs):
    batches_scale, gene_scale, scale, loss_scale, of_part = sizes
    where = refs[0]
    refs = refs[1:]
    parts = (refs[:count], refs[count : 2 * count])
    refs = refs[2 * count :]
    pred_refs, x_refs = refs[0:2], refs[2:4]
    totals_ref, spot_ref, info_ref, dens_ref = refs[4:8]
    refs = refs[8:]
    if final:
        sent_ref, got_ref, logit_ref, w_ref, out_ref, loss_ref, ah, bh, coef, buffer, sem = refs
    else:
        out_ref, ah, bh, coef, buffer, sem = refs
    genes, tile = pred_refs[0].shape
    rows = ah.shape[0]
    width = genes // NB

    gene_cos, inv_gene, over_gene = cosine(
        totals_ref[0:1, :], totals_ref[1:2, :], totals_ref[2:3, :]
    )

    @pl.when(pl.program_id(0) == 0)
    def _():
        coef[0] = jnp.broadcast_to(-gene_scale * inv_gene, (128, 2 * genes)).T
        coef[1] = jnp.broadcast_to(gene_scale * over_gene, (128, 2 * genes)).T
        rows_left(ah, buffer, sem, where, parts, of_part, rows)

    spot = spot_ref[...]
    _, inv_spot, over_spot = cosine(spot[0:NB], spot[NB : 2 * NB], spot[2 * NB : 3 * NB])
    column = jnp.zeros((1, tile), F32)
    for part in range(2):
        for batch in range(NB):
            at = slice(batch * width, (batch + 1) * width)
            here = slice(part * genes + batch * width, part * genes + (batch + 1) * width)
            x_by = jnp.concatenate([coef[0, here]] * (tile // 128), axis=1) - (
                batches_scale * inv_spot[batch : batch + 1]
            )
            p_by = jnp.concatenate([coef[1, here]] * (tile // 128), axis=1) + (
                batches_scale * over_spot[batch : batch + 1]
            )
            pred = pred_refs[part][at, :]
            grad = x_refs[part][at, :] * x_by + pred * p_by
            high, low = split(grad)
            bh[here] = high
            bh[2 * genes + here.start : 2 * genes + here.stop] = low
            bh[4 * genes + here.start : 4 * genes + here.stop] = high
            if not final:
                column = column + jnp.sum(pred * grad, axis=0, keepdims=True)
    value = jnp.dot(ah[...], bh[...], preferred_element_type=F32)
    if not final:
        out_ref[0:rows] = value
        out_ref[rows : rows + 1] = column
        out_ref[rows + 1 : rows + 2] = jnp.broadcast_to(
            jnp.sum(gene_cos, axis=1, keepdims=True), (1, tile)
        )
        out_ref[rows + 2 : rows + 8] = jnp.zeros((6, tile), F32)
        return
    raw = info_ref[6:7, :]
    dens = totals_ref[3:4, 0:1]
    mass = totals_ref[4:5, 0:1]
    grad_raw = scale * (1.0 / mass - dens_ref[...] / (dens * raw))
    column = sent_ref[0:1, :] + got_ref[rows : rows + 1, :] + raw * grad_raw
    value = value + got_ref[0:rows, :] + w_ref[...] * grad_raw
    out_ref[...] = jnp.exp(logit_ref[...]) * info_ref[5:6, :] * (value - column)

    @pl.when(pl.program_id(0) == 0)
    def _():
        gene_scale_loss, spot_scale_loss, per_cent, spots_all = loss_scale
        gene = (sent_ref[1:2, 0:128] + got_ref[rows + 1 : rows + 2, 0:128]) * gene_scale_loss
        cos = totals_ref[6:7, 0:128] * spot_scale_loss
        kl = (
            totals_ref[5:6, 0:128] / totals_ref[3:4, 0:128]
            + jnp.log(totals_ref[4:5, 0:128] * (per_cent / spots_all))
            - jnp.log(totals_ref[3:4, 0:128] * (1.0 / spots_all))
        )
        loss_ref[...] = jnp.concatenate([gene, cos, kl, jnp.zeros((5, 128), F32)], axis=0)


def back(
    which, own, other, preds, xs, totals, spot, info, density, consts, of_part, rows, final, tile=256
):
    genes, spots = preds[0].shape
    count = len(own)
    by_tile = lambda height: pl.BlockSpec((height, tile), lambda i, ix: (0, i))
    specs = [pl.BlockSpec(memory_space=pl.ANY)] * (2 * count)
    specs += [by_tile(genes)] * 4
    specs += [
        pl.BlockSpec((8, 2 * genes), lambda i, ix: (0, 0)),
        by_tile(16),
        pl.BlockSpec((8, tile), lambda i, ix: (1, i)),
        by_tile(1),
    ]
    args = [which, *own, *other, *preds, *xs, totals, spot, info, density]
    if final is None:
        shapes = jax.ShapeDtypeStruct((rows + 8, spots), F32)
        outs = by_tile(rows + 8)
    else:
        sent, got, logits, weights = final
        args += [sent, got, logits, weights]
        specs += [
            pl.BlockSpec((8, tile), lambda i, ix: (rows // 8, i)),
            by_tile(rows + 8),
            pl.BlockSpec((rows, tile), lambda i, ix: (ix[0], i)),
            pl.BlockSpec((rows, 1), lambda i, ix: (ix[0], 0)),
        ]
        shapes = (
            jax.ShapeDtypeStruct((rows, spots), F32),
            jax.ShapeDtypeStruct((8, 128), F32),
        )
        outs = (by_tile(rows), pl.BlockSpec((8, 128), lambda i, ix: (0, 0)))
    return pl.pallas_call(
        functools.partial(back_kernel, count, final is not None, (*consts, of_part)),
        out_shape=shapes,
        grid_spec=pltpu.PrefetchScalarGridSpec(
            num_scalar_prefetch=1,
            grid=(spots // tile,),
            in_specs=specs,
            out_specs=outs,
            scratch_shapes=[
                pltpu.VMEM((rows, 6 * genes), BF),
                pltpu.VMEM((6 * genes, tile), BF),
                pltpu.VMEM((2, 2 * genes, 128), F32),
                pltpu.VMEM((genes, KC), F32),
                pltpu.SemaphoreType.DMA,
            ],
        ),
        compiler_params=params(),
        cost_estimate=pl.CostEstimate(
            flops=12 * genes * rows * spots, bytes_accessed=24 * genes * spots, transcendentals=0
        ),
        name="back_sum" if final is None else "back_end",
    )(*args)


def swap(value, axis, bit):
    return lax.ppermute(value, axis, [(i, i ^ bit) for i in range(lax.axis_size(axis))])


def local(logits, centroid_expr, spatial, cluster_cells, density, gene_order):
    n_spot = lax.axis_size("spot")
    n_gene = lax.axis_size("gene")
    me = lax.axis_index("spot")
    col = lax.axis_index("gene")
    cents, spots = logits.shape
    genes = spatial.shape[1]
    genes_all = genes * n_gene
    spots_all = spots * n_spot
    rows = cents // n_gene
    scale = float(spots_all * cents)
    consts = (
        scale / (NB * spots_all),
        scale / genes_all,
        scale,
        (-1.0 / genes_all, -1.0 / (NB * spots_all), float(cents), float(spots_all)),
    )
    ring = n_spot == 8 and cents // n_spot == KC

    order = (gene_order - col * genes).reshape(genes, 1)
    lanes = lax.broadcasted_iota(jnp.int32, (genes, genes), 1)
    pick = order == lanes
    mine = lax.dot_general(
        pick.astype(F32), centroid_expr, NT, precision=lax.Precision.HIGHEST, preferred_element_type=F32
    )
    pick = pick.astype(BF)
    theirs = swap(mine, "gene", 2)
    order_other = swap(gene_order, "gene", 2) - (col ^ 2) * genes
    pick_other = (order_other.reshape(genes, 1) == lanes).astype(BF)
    cut = spots * 3 // 4
    x_other = [swap(spatial[:cut], "gene", 2), swap(spatial[cut:], "gene", 2)]

    if ring:
        def gather(block):
            got = [block] + [swap(block, "spot", bit) for bit in (2, 4, 6)]
            out = []
            for one in got:
                out += [one, swap(one, "spot", 1)]
            return out

        own = gather(mine)
        other = gather(theirs)
        index = me ^ jnp.arange(n_spot, dtype=jnp.int32)
        of_part = lambda where, piece: ((where[0] * (rows // KC) + piece) ^ where[1], 0)
        early = 6
    else:
        own = [lax.all_gather(mine, "spot", axis=1, tiled=True)]
        other = [lax.all_gather(theirs, "spot", axis=1, tiled=True)]
        index = jnp.zeros((1,), jnp.int32)
        of_part = lambda where, piece: (0, where[0] * rows + piece * KC)
        early = 0

    weights = cluster_cells.astype(F32)
    weights = (weights / jnp.sum(weights)).reshape(cents, 1)
    dens_row = density.reshape(1, spots)
    x_own = turn(pick, spatial)
    pred_own, predicted, info = own_part(own, index, logits, weights, x_own, dens_row, pick)

    info_x = swap(info, "gene", 2)
    half = info + info_x
    spot = half + swap(half, "gene", 1)
    totals = pack(spot, info, info_x, genes)
    if ring:
        for bit in (1, 2, 4):
            totals = totals + swap(totals, "spot", bit)
    else:
        totals = lax.psum(totals, "spot")

    acc = None
    if early:
        acc = other_part(other[:early], index[:early], logits, None, None)
    pred_other = other_part(other[early:], index[early:], logits, acc, info)
    x_turned = jnp.concatenate([turn(pick_other, one) for one in x_other], axis=1)

    partner = jnp.stack([col ^ 1, me]).astype(jnp.int32)
    self_at = jnp.stack([col, me]).astype(jnp.int32)
    common = (own, other, (pred_own, pred_other), (x_own, x_turned), totals, spot, info, dens_row, consts, of_part, rows)
    sent = back(partner, *common, None)
    got = swap(sent, "gene", 1)
    grad_logits, loss = back(self_at, *common, (sent, got, logits, weights))
    return loss[0:3, 0], predicted, grad_logits


def solution(mesh):
    return jax.shard_map(
        local,
        mesh=mesh,
        in_specs=(P(None, "spot"), P("spot", "gene"), P("spot", "gene"), P(), P("spot"), P("gene")),
        out_specs=(P(), P("spot", "gene"), P("gene", "spot")),
        check_vma=False,
    )
```

time: 671 us -> 313 us (0.47); the launches traced: 661 us -> 311 us
  matrix products: 214 us -> 0.68 us
  Pallas kernels: 0 us -> 120 us
  waiting for transfers between devices: 235 us -> 117 us
  blocking collectives: 62.1 us -> 0 us
  local copies, waits for them, and re-layouts: 68.8 us -> 10.6 us
  starting transfers between devices: 0.25 us -> 47.5 us
  other arithmetic: 60.2 us -> 14.2 us
  between operations: 21.1 us -> 0.82 us
    psum x2 -> x0, waiting for transfers between devices: 235 us -> none  [the longest x1 203 us: local(): summed = lax.psum(partial_value, 'gene')]
    dot_general x9 -> x1, matrix products: 214 us -> 0.68 us  [local(): lax.dot_general(pick.astype(F32), centroid_expr, NT, precision=lax.Precis...]
    pallas_call x0 -> x9, Pallas kernels: none -> 120 us  [the longest x2 41.1 us: back(): pl.pallas_call(functools.partial(back_kernel, count, final is not None, (...]
    ppermute x0 -> x24, waiting for transfers between devices: none -> 117 us  [swap(): lax.ppermute(value, axis, [(i, i ^ bit) for i in range(lax.axis_size(axis...]
    psum x2 -> x0, blocking collectives: 62.1 us -> none  [the longest x1 42.3 us: local(): loss_terms = lax.psum(local_terms, ('spot', 'gene'))]
    ppermute x0 -> x24, starting transfers between devices: none -> 47.5 us  [swap(): lax.ppermute(value, axis, [(i, i ^ bit) for i in range(lax.axis_size(axis...]
    gather x12 -> x0, local copies, waits for them, and re-layouts: 28.4 us -> none  [the longest x8 25.4 us: local(): target = jnp.take(spatial, columns, axis=1)]
    reduce_sum x11 -> x1, other arithmetic: 25.8 us -> 1.3 us  [local(): weights = (weights / jnp.sum(weights)).reshape(cents, 1)]
  transfers between devices with their start and end apart: 6 -> 24, of which waited for: 2 -> 11; matrix products, arithmetic and copies ran while one was open for 31% -> 6% of each run, Pallas kernels for 0% -> 23%
where the time goes in v1:
time: 313 us; the launch traced here: 311 us
  Pallas kernels  120 us (38%)
  waiting for transfers between devices  117 us (37%)
  starting transfers between devices  47.5 us (15%)
  other arithmetic  14.2 us (5%)
  local copies, waits for them, and re-layouts  10.6 us (3%)
    ppermute x24, waiting for transfers between devices, swap(): lax.ppermute(value, axis, [(i, i ^ bit) for i in range(lax.axis_size(axis...  117 us
    ppermute x24, starting transfers between devices, swap(): lax.ppermute(value, axis, [(i, i ^ bit) for i in range(lax.axis_size(axis...  47.5 us
    pallas_call x2, Pallas kernels, back(): pl.pallas_call(functools.partial(back_kernel, count, final is not None, (...  41.1 us
    pallas_call x1, Pallas kernels, own_part(): pl.pallas_call(functools.partial(own_kernel, count, float(cents)), out_sh...  31.2 us
    pallas_call x2, Pallas kernels, other_part(): pl.pallas_call(functools.partial(other_kernel, count, first, last), out_s...  28 us
    pallas_call x3, Pallas kernels, turn(): pl.pallas_call(turn_kernel, out_shape=jax.ShapeDtypeStruct((genes, spots)...  18.1 us
  transfers between devices with their start and end apart: 24, of which 11 were waited for; matrix products, arithmetic and copies ran while one was open for 6% of the time, Pallas kernels for 23%

profile of v1, /device:TPU:1, one launch (start us, length us, event | category | flops | bytes accessed | tf_op | source)
XLA Modules:
  0.0 311.0 jit_solution(1838252098716987698)
XLA Ops:
  2.4 4.2 %collective-permute-start.5 = (f32[512,256]{1,0:T(8,128)S(1)}, f32[512,256]{1,0:T(8,128)S(1)}, u32[]{:S(2)}, u32[]{:S(2)}) collective-permute-start(f32[512,256]{1,0:T(8,128)S(1)} %fusion.1.refs_1_), channel_id=1, source_target_pairs={{0,24},{4,28},{8,16},{12,20},{16,8},{20,12},{24,0},{28,4},{1,25},{... | collective-permute-start | bytes 1572872 | tf_op jit(solution)/shard_map/ppermute | solution.py:461
  9.4 1.3 convert_reduce_fusion
  10.7 1.3 convert_divide_fusion
  12.1 1.3 copy.10.refs_17_.refs_18_.refs_19_.refs_20_.refs_21_.refs_22_.refs_23_.refs_24_.refs_28_
  13.4 3.9 %slice.17 = f32[1536,512]{1,0:T(8,128)} slice(f32[2048,512]{1,0:T(8,128)} %x_ref.1), slice={[0:1536], [0:512]} | slice | bytes 6291456 | tf_op jit(solution)/shard_map/slice | solution.py:494
  19.4 31.6 %collective-permute-done.3.refs_5_ = f32[512,256]{1,0:T(8,128)S(1)} collective-permute-done((f32[512,256]{1,0:T(8,128)S(1)}, f32[512,256]{1,0:T(8,128)S(1)}, u32[]{:S(2)}, u32[]{:S(2)}) %collective-permute-start.3) | collective-permute-done | bytes 524320 | tf_op jit(solution)/shard_map/ppermute | solution.py:461
  53.9 8.4 %turn.3.refs_25_.refs_19_ = f32[512,2048]{1,0:T(8,128)} custom-call(bf16[512,512]{1,0:T(8,128)(2,1)} %fusion.order_ref.refs_27_, f32[2048,512]{1,0:T(8,128)} %x_ref.1), custom_call_target="tpu_custom_call" | custom-call | flops 2147483648 | bytes 8388608 | tf_op jit(solution)/shard_map/turn/pallas_call | solution.py:54
  63.6 10.7 %collective-permute-done.2.refs_4_ = f32[512,256]{1,0:T(8,128)} collective-permute-done((f32[512,256]{1,0:T(8,128)S(1)}, f32[512,256]{1,0:T(8,128)}, u32[]{:S(2)}, u32[]{:S(2)}) %collective-permute-start.2) | collective-permute-done | bytes 524320 | tf_op jit(solution)/shard_map/ppermute | solution.py:461
  74.4 31.2 %own_part.1 = (f32[512,2048]{1,0:T(8,128)}, f32[2048,512]{1,0:T(8,128)}, f32[16,2048]{1,0:T(8,128)}) custom-call(s32[8]{0:T(128)} %iota_xor_fusion.refs_0_, f32[512,256]{1,0:T(8,128)} %copy-done.2, f32[512,256]{1,0:T(8,128)} %copy-done.7, f32[512,256]{1,0:T(8,128)} %copy-done.5, f32[512,256]{1,0:T(8,128)} %collective-permute-done.2.refs_4_, ...), custom_call_target="tpu_custom_call" | custom-call | flops 12884901888 | bytes 16777216 | tf_op jit(solution)/shard_map/own_part/pallas_call | solution.py:173
  105.6 1.3 collective-permute-start.18
  106.9 26.3 %collective-permute-done.18.theirs_ref = f32[16,2048]{1,0:T(8,128)S(1)} collective-permute-done((f32[16,2048]{1,0:T(8,128)}, f32[16,2048]{1,0:T(8,128)S(1)}, u32[]{:S(2)}, u32[]{:S(2)}) %collective-permute-start.18) | collective-permute-done | bytes 131104 | tf_op jit(solution)/shard_map/ppermute | solution.py:461
  134.2 2.8 collective-permute-start.19
  137.0 2.0 collective-permute-start.13
  139.0 1.5 collective-permute-start.9
  142.5 1.8 pack.1
  145.5 2.3 slice.18
  148.8 3.5 %collective-permute-done.13.refs_1_.refs_15_ = f32[512,256]{1,0:T(8,128)S(1)} collective-permute-done((f32[512,256]{1,0:T(8,128)S(1)}, f32[512,256]{1,0:T(8,128)S(1)}, u32[]{:S(2)}, u32[]{:S(2)}) %collective-permute-start.13) | collective-permute-done | bytes 524320 | tf_op jit(solution)/shard_map/ppermute | solution.py:461
  152.4 19.9 %collective-permute-start.21 = (f32[8,1024]{1,0:T(8,128)S(1)}, f32[8,1024]{1,0:T(8,128)S(1)}, u32[]{:S(2)}, u32[]{:S(2)}) collective-permute-start(f32[8,1024]{1,0:T(8,128)S(1)} %add.17), channel_id=1, source_target_pairs={{0,8},{4,12},{8,0},{12,4},{16,24},{20,28},{24,16},{28,20},{1,9},{5... | collective-permute-start | bytes 98312 | tf_op jit(solution)/shard_map/ppermute | solution.py:461
  172.3 10.9 %collective-permute-done.11.refs_5_.refs_13_ = f32[512,256]{1,0:T(8,128)S(1)} collective-permute-done((f32[512,256]{1,0:T(8,128)S(1)}, f32[512,256]{1,0:T(8,128)S(1)}, u32[]{:S(2)}, u32[]{:S(2)}) %collective-permute-start.11) | collective-permute-done | bytes 524320 | tf_op jit(solution)/shard_map/ppermute | solution.py:461
  188.1 3.0 turn.5
  192.6 3.0 collective-permute-done.8.refs_2_.refs_10_
  195.6 11.2 %collective-permute-done.12.refs_6_.refs_14_ = f32[512,256]{1,0:T(8,128)S(1)} collective-permute-done((f32[512,256]{1,0:T(8,128)S(1)}, f32[512,256]{1,0:T(8,128)S(1)}, u32[]{:S(2)}, u32[]{:S(2)}) %collective-permute-start.12) | collective-permute-done | bytes 524320 | tf_op jit(solution)/shard_map/ppermute | solution.py:461
  206.9 11.3 %collective-permute-done.10.refs_4_.refs_12_ = f32[512,256]{1,0:T(8,128)} collective-permute-done((f32[512,256]{1,0:T(8,128)S(1)}, f32[512,256]{1,0:T(8,128)}, u32[]{:S(2)}, u32[]{:S(2)}) %collective-permute-start.10) | collective-permute-done | bytes 524320 | tf_op jit(solution)/shard_map/ppermute | solution.py:461
  218.2 17.0 %other_part.2.refs_5_ = f32[512,2048]{1,0:T(8,128)} custom-call(s32[6]{0:T(128)} %bitcast.11, f32[512,256]{1,0:T(8,128)} %copy-done.6, f32[512,256]{1,0:T(8,128)} %copy-done.12, f32[512,256]{1,0:T(8,128)} %copy-done.11, f32[512,256]{1,0:T(8,128)} %collective-permute-done.10.refs_4_.refs_12_, f32[512,256]{1,0:T(8,128)} %copy-done.10, f32[512,256]{1,0:T(8,128)} %copy-done.13, ...), custom_call_target="tpu_custom_call" | custom-call | flops 9663676416 | bytes 20971520 | tf_op jit(solution)/shard_map/other_part/pallas_call | solution.py:246
  236.0 11.0 %other_part.3.refs_18_ = f32[512,2048]{1,0:T(8,128)} custom-call(s32[2]{0:T(128)} %slice.15.refs_0_, f32[512,256]{1,0:T(8,128)} %copy-done.9, f32[512,256]{1,0:T(8,128)} %copy-done.14, f32[2048,2048]{1,0:T(8,128)} %refs_27_.1, f32[2048,2048]{1,0:T(8,128)} %refs_27_.1, f32[512,2048]{1,0:T(8,128)} %other_part.2.refs_5_, ...), custom_call_target="tpu_custom_call", output_to_operand_aliasing={{}: (5, {})} | custom-call | flops 3221225472 | bytes 12582912 | tf_op jit(solution)/shard_map/other_part/pallas_call | solution.py:246
  247.1 6.7 %turn.4 = f32[512,1536]{1,0:T(8,128)} custom-call(bf16[512,512]{1,0:T(8,128)(2,1)} %fusion.2.order_ref, f32[1536,512]{1,0:T(8,128)} %collective-permute-done.16.x_ref), custom_call_target="tpu_custom_call" | custom-call | flops 1610612736 | bytes 6291456 | tf_op jit(solution)/shard_map/turn/pallas_call | solution.py:54
  253.8 4.2 %pad_maximum_fusion.refs_20_ = f32[512,2048]{1,0:T(8,128)} fusion(f32[512,512]{1,0:T(8,128)S(1)} %copy-done.15, f32[512,1536]{1,0:T(8,128)} %turn.4), kind=kLoop, calls=%fused_computation | loop fusion | flops 1048576 | bytes 8388608 | tf_op jit(solution)/shard_map/concatenate | solution.py:536
  258.0 19.7 %back_sum.1.refs_25_ = f32[520,2048]{1,0:T(8,128)} custom-call(s32[2]{0:T(128)} %pad_add_fusion.1.refs_0_, f32[512,256]{1,0:T(8,128)} %copy-done.2, f32[512,256]{1,0:T(8,128)} %copy-done.7, f32[512,256]{1,0:T(8,128)} %copy-done.5, f32[512,256]{1,0:T(8,128)} %collective-permute-done.2.refs_4_, f32[512,256]{1,0:T(8,128)} %copy-done.4, ...), custom_call_target="tpu_custom_call" | custom-call | flops 6442450944 | bytes 25165824 | tf_op jit(solution)/shard_map/back_sum/pallas_call | solution.py:436
  277.7 3.3 %collective-permute-start.23 = (f32[520,2048]{1,0:T(8,128)}, f32[520,2048]{1,0:T(8,128)}, u32[]{:S(2)}, u32[]{:S(2)}) collective-permute-start(f32[520,2048]{1,0:T(8,128)} %back_sum.1.refs_25_), channel_id=1, source_target_pairs={{0,1},{1,0},{2,3},{3,2},{4,5},{5,4},{6,7},{7,6},{8,9},{9,8},{10,11... | collective-permute-start | bytes 12779528 | tf_op jit(solution)/shard_map/ppermute | solution.py:461
  281.6 6.6 %collective-permute-done.23.refs_26_ = f32[520,2048]{1,0:T(8,128)} collective-permute-done((f32[520,2048]{1,0:T(8,128)}, f32[520,2048]{1,0:T(8,128)}, u32[]{:S(2)}, u32[]{:S(2)}) %collective-permute-start.23) | collective-permute-done | bytes 4259872 | tf_op jit(solution)/shard_map/ppermute | solution.py:461
  288.2 21.5 %back_end.1 = (f32[512,2048]{1,0:T(8,128)}, f32[8,128]{1,0:T(8,128)}) custom-call(s32[2]{0:T(128)} %pad_add_fusion.refs_0_, f32[512,256]{1,0:T(8,128)} %copy-done.2, f32[512,256]{1,0:T(8,128)} %copy-done.7, f32[512,256]{1,0:T(8,128)} %copy-done.5, f32[512,256]{1,0:T(8,128)} %collective-permute-done.2.refs_4_, f32[512,256]{1,0:T(8,128)} %copy-done.4, ...), custom_call_target="tpu_custom_call" | custom-call | flops 6442450944 | bytes 25165824 | tf_op jit(solution)/shard_map/back_end/pallas_call | solution.py:436
  309.7 1.3 slice_reduce_fusion
  (84 shorter events, 23.9 us)
Async XLA Ops:
  2.4 59.9 %copy-start.2 = (f32[512,256]{1,0:T(8,128)}, f32[512,256]{1,0:T(8,128)S(1)}, u32[]{:S(2)}) copy-start(f32[512,256]{1,0:T(8,128)S(1)} %fusion.1.refs_1_) | copy-start | bytes 1572868
  2.4 16.0 %collective-permute-start.5 = (f32[512,256]{1,0:T(8,128)S(1)}, f32[512,256]{1,0:T(8,128)S(1)}, u32[]{:S(2)}, u32[]{:S(2)}) collective-permute-start(f32[512,256]{1,0:T(8,128)S(1)} %fusion.1.refs_1_), channel_id=1, source_target_pairs={{0,24},{4,28},{8,16},{12,20},{16,8},{20,12},{24,0},{28,4},{1,25},{... | collective-permute-start | bytes 1572872 | tf_op jit(solution)/shard_map/ppermute | solution.py:461
  6.6 44.4 %collective-permute-start.3 = (f32[512,256]{1,0:T(8,128)S(1)}, f32[512,256]{1,0:T(8,128)S(1)}, u32[]{:S(2)}, u32[]{:S(2)}) collective-permute-start(f32[512,256]{1,0:T(8,128)S(1)} %fusion.1.refs_1_), channel_id=1, source_target_pairs={{0,16},{4,20},{8,24},{12,28},{16,0},{20,4},{24,8},{28,12},{1,17},{... | collective-permute-start | bytes 1572872 | tf_op jit(solution)/shard_map/ppermute | solution.py:461
  6.6 45.6 %collective-permute-start.1 = (f32[512,256]{1,0:T(8,128)S(1)}, f32[512,256]{1,0:T(8,128)S(1)}, u32[]{:S(2)}, u32[]{:S(2)}) collective-permute-start(f32[512,256]{1,0:T(8,128)S(1)} %fusion.1.refs_1_), channel_id=1, source_target_pairs={{0,8},{4,12},{8,0},{12,4},{16,24},{20,28},{24,16},{28,20},{1,9},{5... | collective-permute-start | bytes 1572872 | tf_op jit(solution)/shard_map/ppermute | solution.py:461
  7.0 130.0 %collective-permute-start.7 = (f32[512,256]{1,0:T(8,128)S(1)}, f32[512,256]{1,0:T(8,128)S(1)}, u32[]{:S(2)}, u32[]{:S(2)}) collective-permute-start(f32[512,256]{1,0:T(8,128)S(1)} %fusion.1.refs_1_), channel_id=1, source_target_pairs={{0,2},{1,3},{2,0},{3,1},{4,6},{5,7},{6,4},{7,5},{8,10},{9,11},{10,... | collective-permute-start | bytes 1572872 | tf_op jit(solution)/shard_map/ppermute | solution.py:461
  8.2 54.2 %collective-permute-start = (f32[512,256]{1,0:T(8,128)S(1)}, f32[512,256]{1,0:T(8,128)S(1)}, u32[]{:S(2)}, u32[]{:S(2)}) collective-permute-start(f32[512,256]{1,0:T(8,128)S(1)} %fusion.1.refs_1_), channel_id=1, source_target_pairs={{0,4},{4,0},{8,12},{12,8},{16,20},{20,16},{24,28},{28,24},{1,5},{5... | collective-permute-start | bytes 1572872 | tf_op jit(solution)/shard_map/ppermute | solution.py:461
  18.4 44.0 %copy-start.3 = (f32[512,256]{1,0:T(8,128)}, f32[512,256]{1,0:T(8,128)S(1)}, u32[]{:S(2)}) copy-start(f32[512,256]{1,0:T(8,128)S(1)} %collective-permute-done.5.refs_7_) | copy-start | bytes 1572868
  18.4 45.3 %collective-permute-start.6 = (f32[512,256]{1,0:T(8,128)S(1)}, f32[512,256]{1,0:T(8,128)S(1)}, u32[]{:S(2)}, u32[]{:S(2)}) collective-permute-start(f32[512,256]{1,0:T(8,128)S(1)} %collective-permute-done.5.refs_7_), channel_id=1, source_target_pairs={{0,4},{4,0},{8,12},{12,8},{16,20},{20,16},{24,28},{28,24},{1,5},{5... | collective-permute-start | bytes 1572872 | tf_op jit(solution)/shard_map/ppermute | solution.py:461
  51.0 12.7 %collective-permute-start.4 = (f32[512,256]{1,0:T(8,128)S(1)}, f32[512,256]{1,0:T(8,128)}, u32[]{:S(2)}, u32[]{:S(2)}) collective-permute-start(f32[512,256]{1,0:T(8,128)S(1)} %collective-permute-done.3.refs_5_), channel_id=1, source_target_pairs={{0,4},{4,0},{8,12},{12,8},{16,20},{20,16},{24,28},{28,24},{1,5},{5... | collective-permute-start | bytes 1572872 | tf_op jit(solution)/shard_map/ppermute | solution.py:461
  52.2 22.1 %collective-permute-start.2 = (f32[512,256]{1,0:T(8,128)S(1)}, f32[512,256]{1,0:T(8,128)}, u32[]{:S(2)}, u32[]{:S(2)}) collective-permute-start(f32[512,256]{1,0:T(8,128)S(1)} %collective-permute-done.1.refs_3_), channel_id=1, source_target_pairs={{0,4},{4,0},{8,12},{12,8},{16,20},{20,16},{24,28},{28,24},{1,5},{5... | collective-permute-start | bytes 1572872 | tf_op jit(solution)/shard_map/ppermute | solution.py:461
  62.4 184.7 %collective-permute-start.16 = (f32[1536,512]{1,0:T(8,128)}, f32[1536,512]{1,0:T(8,128)}, u32[]{:S(2)}, u32[]{:S(2)}) collective-permute-start(f32[1536,512]{1,0:T(8,128)} %slice.17), channel_id=1, source_target_pairs={{0,2},{1,3},{2,0},{3,1},{4,6},{5,7},{6,4},{7,5},{8,10},{9,11},{10,... | collective-permute-start | bytes 9437192 | tf_op jit(solution)/shard_map/ppermute | solution.py:461
  74.4 66.2 %copy-start.17 = (s32[512]{0:T(512)S(1)}, s32[512]{0:T(512)}, u32[]{:S(2)}) copy-start(s32[512]{0:T(512)} %param.11) | copy-start | bytes 6148
  74.4 112.1 %copy-start.18 = (s32[8]{0:T(128)S(1)}, s32[8]{0:T(128)}, u32[]{:S(2)}) copy-start(s32[8]{0:T(128)} %iota_xor_fusion.refs_0_) | copy-start | bytes 100
  105.6 27.6 %collective-permute-start.18 = (f32[16,2048]{1,0:T(8,128)}, f32[16,2048]{1,0:T(8,128)S(1)}, u32[]{:S(2)}, u32[]{:S(2)}) collective-permute-start(f32[16,2048]{1,0:T(8,128)} %get-tuple-element.9.refs_6_.mine_ref.refs_23_), channel_id=1, source_target_pairs={{0,2},{1,3},{2,0},{3,1},{4,6},{5,7},{6,4},{7,5},{8,10},{9,11},{10,... | collective-permute-start | bytes 393224 | tf_op jit(solution)/shard_map/ppermute | solution.py:461
  134.2 6.4 %collective-permute-start.19 = (f32[16,2048]{1,0:T(8,128)S(1)}, f32[16,2048]{1,0:T(8,128)S(1)}, u32[]{:S(2)}, u32[]{:S(2)}) collective-permute-start(f32[16,2048]{1,0:T(8,128)S(1)} %add.15), channel_id=1, source_target_pairs={{0,1},{1,0},{2,3},{3,2},{4,5},{5,4},{6,7},{7,6},{8,9},{9,8},{10,11... | collective-permute-start | bytes 393224 | tf_op jit(solution)/shard_map/ppermute | solution.py:461
  137.0 81.2 %copy-start.6 = (f32[512,256]{1,0:T(8,128)}, f32[512,256]{1,0:T(8,128)S(1)}, u32[]{:S(2)}) copy-start(f32[512,256]{1,0:T(8,128)S(1)} %collective-permute-done.7.refs_1_.refs_9_) | copy-start | bytes 1572868
  137.0 15.4 %collective-permute-start.13 = (f32[512,256]{1,0:T(8,128)S(1)}, f32[512,256]{1,0:T(8,128)S(1)}, u32[]{:S(2)}, u32[]{:S(2)}) collective-permute-start(f32[512,256]{1,0:T(8,128)S(1)} %collective-permute-done.7.refs_1_.refs_9_), channel_id=1, source_target_pairs={{0,24},{4,28},{8,16},{12,20},{16,8},{20,12},{24,0},{28,4},{1,25},{... | collective-permute-start | bytes 1572872 | tf_op jit(solution)/shard_map/ppermute | solution.py:461
  139.0 44.1 %collective-permute-start.11 = (f32[512,256]{1,0:T(8,128)S(1)}, f32[512,256]{1,0:T(8,128)S(1)}, u32[]{:S(2)}, u32[]{:S(2)}) collective-permute-start(f32[512,256]{1,0:T(8,128)S(1)} %collective-permute-done.7.refs_1_.refs_9_), channel_id=1, source_target_pairs={{0,16},{4,20},{8,24},{12,28},{16,0},{20,4},{24,8},{28,12},{1,17},{... | collective-permute-start | bytes 1572872 | tf_op jit(solution)/shard_map/ppermute | solution.py:461
  139.0 45.4 %collective-permute-start.9 = (f32[512,256]{1,0:T(8,128)S(1)}, f32[512,256]{1,0:T(8,128)S(1)}, u32[]{:S(2)}, u32[]{:S(2)}) collective-permute-start(f32[512,256]{1,0:T(8,128)S(1)} %collective-permute-done.7.refs_1_.refs_9_), channel_id=1, source_target_pairs={{0,8},{4,12},{8,0},{12,4},{16,24},{20,28},{24,16},{28,20},{1,9},{5... | collective-permute-start | bytes 1572872 | tf_op jit(solution)/shard_map/ppermute | solution.py:461
  140.6 3.6 %collective-permute-start.15 = (s32[512]{0:T(512)S(1)}, s32[512]{0:T(512)S(1)}, u32[]{:S(2)}, u32[]{:S(2)}) collective-permute-start(s32[512]{0:T(512)S(1)} %copy-done.17), channel_id=1, source_target_pairs={{0,2},{1,3},{2,0},{3,1},{4,6},{5,7},{6,4},{7,5},{8,10},{9,11},{10,... | collective-permute-start | bytes 6152 | tf_op jit(solution)/shard_map/ppermute | solution.py:461
  144.2 3.6 %collective-permute-start.20 = (f32[8,1024]{1,0:T(8,128)}, f32[8,1024]{1,0:T(8,128)S(1)}, u32[]{:S(2)}, u32[]{:S(2)}) collective-permute-start(f32[8,1024]{1,0:T(8,128)} %pack.1), channel_id=1, source_target_pairs={{0,4},{4,0},{8,12},{12,8},{16,20},{20,16},{24,28},{28,24},{1,5},{5... | collective-permute-start | bytes 98312 | tf_op jit(solution)/shard_map/ppermute | solution.py:461
  147.8 40.3 %collective-permute-start.17 = (f32[512,512]{1,0:T(8,128)}, f32[512,512]{1,0:T(8,128)}, u32[]{:S(2)}, u32[]{:S(2)}) collective-permute-start(f32[512,512]{1,0:T(8,128)} %slice.18), channel_id=1, source_target_pairs={{0,2},{1,3},{2,0},{3,1},{4,6},{5,7},{6,4},{7,5},{8,10},{9,11},{10,... | collective-permute-start | bytes 3145736 | tf_op jit(solution)/shard_map/ppermute | solution.py:461
  152.4 82.8 %copy-start.9 = (f32[512,256]{1,0:T(8,128)}, f32[512,256]{1,0:T(8,128)S(1)}, u32[]{:S(2)}) copy-start(f32[512,256]{1,0:T(8,128)S(1)} %collective-permute-done.13.refs_1_.refs_15_) | copy-start | bytes 1572868
  152.4 32.2 %collective-permute-start.21 = (f32[8,1024]{1,0:T(8,128)S(1)}, f32[8,1024]{1,0:T(8,128)S(1)}, u32[]{:S(2)}, u32[]{:S(2)}) collective-permute-start(f32[8,1024]{1,0:T(8,128)S(1)} %add.17), channel_id=1, source_target_pairs={{0,8},{4,12},{8,0},{12,4},{16,24},{20,28},{24,16},{28,20},{1,9},{5... | collective-permute-start | bytes 98312 | tf_op jit(solution)/shard_map/ppermute | solution.py:461
  183.1 35.1 %copy-start.10 = (f32[512,256]{1,0:T(8,128)}, f32[512,256]{1,0:T(8,128)S(1)}, u32[]{:S(2)}) copy-start(f32[512,256]{1,0:T(8,128)S(1)} %collective-permute-done.11.refs_5_.refs_13_) | copy-start | bytes 1572868
  183.1 12.5 %collective-permute-start.8 = (f32[512,256]{1,0:T(8,128)S(1)}, f32[512,256]{1,0:T(8,128)S(1)}, u32[]{:S(2)}, u32[]{:S(2)}) collective-permute-start(f32[512,256]{1,0:T(8,128)S(1)} %collective-permute-done.7.refs_1_.refs_9_), channel_id=1, source_target_pairs={{0,4},{4,0},{8,12},{12,8},{16,20},{20,16},{24,28},{28,24},{1,5},{5... | collective-permute-start | bytes 1572872 | tf_op jit(solution)/shard_map/ppermute | solution.py:461
  184.4 33.8 %copy-start.11 = (f32[512,256]{1,0:T(8,128)}, f32[512,256]{1,0:T(8,128)S(1)}, u32[]{:S(2)}) copy-start(f32[512,256]{1,0:T(8,128)S(1)} %collective-permute-done.9.refs_3_.refs_11_) | copy-start | bytes 1572868
  184.4 22.5 %collective-permute-start.12 = (f32[512,256]{1,0:T(8,128)S(1)}, f32[512,256]{1,0:T(8,128)S(1)}, u32[]{:S(2)}, u32[]{:S(2)}) collective-permute-start(f32[512,256]{1,0:T(8,128)S(1)} %collective-permute-done.11.refs_5_.refs_13_), channel_id=1, source_target_pairs={{0,4},{4,0},{8,12},{12,8},{16,20},{20,16},{24,28},{28,24},{1,5},{5... | collective-permute-start | bytes 1572872 | tf_op jit(solution)/shard_map/ppermute | solution.py:461
  184.6 33.6 %collective-permute-start.10 = (f32[512,256]{1,0:T(8,128)S(1)}, f32[512,256]{1,0:T(8,128)}, u32[]{:S(2)}, u32[]{:S(2)}) collective-permute-start(f32[512,256]{1,0:T(8,128)S(1)} %collective-permute-done.9.refs_3_.refs_11_), channel_id=1, source_target_pairs={{0,4},{4,0},{8,12},{12,8},{16,20},{20,16},{24,28},{28,24},{1,5},{5... | collective-permute-start | bytes 1572872 | tf_op jit(solution)/shard_map/ppermute | solution.py:461
  188.0 3.7 %collective-permute-start.22 = (f32[8,1024]{1,0:T(8,128)S(1)}, f32[8,1024]{1,0:T(8,128)S(1)}, u32[]{:S(2)}, u32[]{:S(2)}) collective-permute-start(f32[8,1024]{1,0:T(8,128)S(1)} %add.18), channel_id=1, source_target_pairs={{0,16},{4,20},{8,24},{12,28},{16,0},{20,4},{24,8},{28,12},{1,17},{... | collective-permute-start | bytes 98312 | tf_op jit(solution)/shard_map/ppermute | solution.py:461
  191.8 43.4 %collective-permute-start.14 = (f32[512,256]{1,0:T(8,128)S(1)}, f32[512,256]{1,0:T(8,128)S(1)}, u32[]{:S(2)}, u32[]{:S(2)}) collective-permute-start(f32[512,256]{1,0:T(8,128)S(1)} %collective-permute-done.13.refs_1_.refs_15_), channel_id=1, source_target_pairs={{0,4},{4,0},{8,12},{12,8},{16,20},{20,16},{24,28},{28,24},{1,5},{5... | collective-permute-start | bytes 1572872 | tf_op jit(solution)/shard_map/ppermute | solution.py:461
  277.7 10.6 %collective-permute-start.23 = (f32[520,2048]{1,0:T(8,128)}, f32[520,2048]{1,0:T(8,128)}, u32[]{:S(2)}, u32[]{:S(2)}) collective-permute-start(f32[520,2048]{1,0:T(8,128)} %back_sum.1.refs_25_), channel_id=1, source_target_pairs={{0,1},{1,0},{2,3},{3,2},{4,5},{5,4},{6,7},{7,6},{8,9},{9,8},{10,11... | collective-permute-start | bytes 12779528 | tf_op jit(solution)/shard_map/ppermute | solution.py:461
  (11 other events, 118.7 us)

commit v2 on v0

v2 whole, which is shorter than its diff:
```python
import functools
import jax
import jax.numpy as jnp
from jax import lax
from jax.experimental import pallas as pl
from jax.experimental.pallas import tpu as pltpu
from jax.sharding import PartitionSpec as P

NB = 4
XS = 2
EPS = 1e-06
BF = jnp.bfloat16
F32 = jnp.float32
KC = 256
NT = (((1,), (1,)), ((), ()))
TN = (((0,), (0,)), ((), ()))
VMEM_LIMIT = 67043328
CHEAP = pl.CostEstimate(flops=1000, bytes_accessed=1000, transcendentals=0)


def split(value):
    high = value.astype(BF)
    return high, (value - high.astype(F32)).astype(BF)


def dot(left, right, dims=(((1,), (0,)), ((), ()))):
    return lax.dot_general(left, right, dims, preferred_element_type=F32)


def call(kernel, name, where, args, specs, out_shape, out_specs, grid, scratch=(), alias=None):
    return pl.pallas_call(
        kernel,
        out_shape=out_shape,
        grid_spec=pltpu.PrefetchScalarGridSpec(
            num_scalar_prefetch=1,
            grid=grid,
            in_specs=specs,
            out_specs=out_specs,
            scratch_shapes=list(scratch),
        ),
        input_output_aliases=alias or {},
        compiler_params=pltpu.CompilerParams(
            dimension_semantics=("arbitrary",), vmem_limit_bytes=VMEM_LIMIT
        ),
        cost_estimate=CHEAP,
        name=name,
    )(where, *args)


def fixed(shape):
    return pl.BlockSpec(shape, lambda i, ix: (0,) * len(shape), pipeline_mode=pl.Buffered(1))


def by_tile(height, tile, row=0, start=0):
    return pl.BlockSpec((height, tile), lambda i, ix: (row, i + start))


def exp_kernel(cents, where, l_ref, w_ref, d_ref, high_ref, low_ref, info_ref, scal):
    step = pl.program_id(0)
    tile = l_ref.shape[1]

    @pl.when(step == 0)
    def _():
        scal[...] = jnp.zeros_like(scal)

    total = weighted = jnp.zeros((1, tile), F32)
    for part in range(l_ref.shape[0] // KC):
        rows = slice(part * KC, part * KC + KC)
        value = jnp.exp(l_ref[rows, :])
        high, low = split(value)
        high_ref[rows, :] = high
        low_ref[rows, :] = low
        total = total + jnp.sum(value, axis=0, keepdims=True)
        weighted = weighted + jnp.sum(value * w_ref[rows, :], axis=0, keepdims=True)
    inv = 1.0 / total
    raw = weighted * inv
    dens = d_ref[...]
    scal[0:1] += dens
    scal[1:2] += raw
    scal[2:3] += dens * (jnp.log(dens) - jnp.log(raw * cents))
    sums = jnp.broadcast_to(jnp.sum(scal[...], axis=1, keepdims=True), (8, tile))
    info_ref[0:1, :] = inv
    info_ref[1:2, :] = raw
    info_ref[2:8, :] = sums[0:6]


def exp_parts(where, logits, weights, density, tile):
    cents, spots = logits.shape
    return call(
        functools.partial(exp_kernel, float(cents)),
        "exp_parts",
        where,
        [logits, weights, density],
        [by_tile(cents, tile), fixed((cents, 1)), by_tile(1, tile)],
        (
            jax.ShapeDtypeStruct((cents, spots), BF),
            jax.ShapeDtypeStruct((cents, spots), BF),
            jax.ShapeDtypeStruct((8, spots), F32),
        ),
        (by_tile(cents, tile), by_tile(cents, tile), by_tile(8, tile)),
        (spots // tile,),
        [pltpu.VMEM((8, tile), F32)],
    )


def turn_kernel(where, pick_ref, x_ref, *out_refs):
    high, low = split(x_ref[...])
    pick = pick_ref[...]
    value = dot(pick, high, NT) + dot(pick, low, NT)
    width = out_refs[0].shape[0]
    for batch, out_ref in enumerate(out_refs):
        out_ref[...] = value[batch * width : (batch + 1) * width]


def turn(where, pick, x, tile):
    spots, genes = x.shape
    width = genes // XS
    return call(
        turn_kernel,
        "turn",
        where,
        [pick, x],
        [fixed((genes, genes)), pl.BlockSpec((tile, genes), lambda i, ix: (i, 0))],
        (jax.ShapeDtypeStruct((width, spots), F32),) * XS,
        (by_tile(width, tile),) * XS,
        (spots // tile,),
    )


def of_batch(refs, batch, width):
    each = NB // XS
    start = batch % each * width
    return refs[batch // each][start : start + width, :]


def load_left(groups, high, low):
    at = 0
    for group in groups:
        value = group[0][...]
        for ref in group[1:]:
            value = value + ref[...]
        wide = value.shape[1]
        high[:, at : at + wide], low[:, at : at + wide] = split(value)
        at += wide


def flat(blocks):
    sizes = [len(block) if isinstance(block, tuple) else 1 for block in blocks]
    arrays = [one for block in blocks for one in (block if isinstance(block, tuple) else (block,))]
    return sizes, arrays


def grouped(sizes, refs):
    out, at = [], 0
    for size in sizes:
        out.append(refs[at : at + size])
        at += size
    return out


def product(high, low, e_high, e_low):
    right = jnp.concatenate([ref[...] for ref in e_high], axis=0)
    value = dot(high[...], right) + dot(low[...], right)
    return value + dot(high[...], jnp.concatenate([ref[...] for ref in e_low], axis=0))


def pred_kernel(sizes, first, last, stats, where, *refs):
    count = len(sizes)
    s_refs, refs = grouped(sizes, refs), refs[sum(sizes) :]
    h_refs, l_refs = refs[:count], refs[count : 2 * count]
    refs = refs[2 * count :]
    if not first:
        acc_ref, refs = refs[0], refs[1:]
    if last:
        zinfo_ref, refs = refs[0], refs[1:]
    if stats:
        x_refs, (out_ref, info_ref, high, low, sums) = refs[:XS], refs[XS:]
    else:
        out_ref, high, low = refs
    step = pl.program_id(0)
    genes, tile = out_ref.shape
    width = genes // NB

    @pl.when(step == 0)
    def _():
        load_left(s_refs, high, low)
        if stats:
            sums[...] = jnp.zeros_like(sums)
            info_ref[...] = jnp.zeros_like(info_ref)

    value = product(high, low, h_refs, l_refs)
    if not first:
        value = value + acc_ref[...]
    if last:
        value = value * zinfo_ref[0:1, :]
    out_ref[...] = value
    if not stats:
        return
    rows = [[], [], []]
    for batch in range(NB):
        at = slice(batch * width, (batch + 1) * width)
        pred, x = value[at], of_batch(x_refs, batch, width)
        for number, term in enumerate((pred * x, pred * pred, x * x)):
            rows[number].append(jnp.sum(term, axis=0, keepdims=True))
            lanes = term[:, :128]
            for group in range(1, tile // 128):
                lanes = lanes + term[:, group * 128 : group * 128 + 128]
            sums[number, at] += lanes
    info_ref[0 : 3 * NB, pl.ds(pl.multiple_of(step * tile, 128), tile)] = jnp.concatenate(
        rows[0] + rows[1] + rows[2], axis=0
    )

    @pl.when(step == pl.num_programs(0) - 1)
    def _():
        for number in range(3):
            info_ref[12:13, number * genes : (number + 1) * genes] = jnp.sum(
                sums[number].T, axis=0, keepdims=True
            )


def pred_part(where, keys, blocks, e_high, e_low, acc, zinfo, x, tile, name):
    cents, spots = e_high.shape
    sizes, blocks = flat(blocks)
    genes, deep = blocks[0].shape
    count = len(sizes)
    first, last, stats = acc is None, zinfo is not None, x is not None
    rows = [
        pl.BlockSpec((deep, tile), functools.partial(lambda key, i, ix: (key(ix), i), key))
        for key in keys
    ]
    specs = [fixed((genes, deep)) for _ in blocks] + rows + rows
    args = [*blocks, *([e_high] * count), *([e_low] * count)]
    alias = {}
    if not first:
        alias = {len(args) + 1: 0}
        specs.append(by_tile(genes, tile))
        args.append(acc)
    if last:
        specs.append(by_tile(8, tile))
        args.append(zinfo)
    shapes = jax.ShapeDtypeStruct((genes, spots), F32)
    outs = by_tile(genes, tile)
    scratch = [pltpu.VMEM((genes, deep * count), BF)] * 2
    if stats:
        specs += [by_tile(genes // XS, tile)] * XS
        args += x
        shapes = (shapes, jax.ShapeDtypeStruct((16, spots), F32))
        outs = (outs, fixed_out((16, spots)))
        scratch.append(pltpu.VMEM((3, genes, 128), F32))
    return call(
        functools.partial(pred_kernel, sizes, first, last, stats),
        name,
        where,
        args,
        specs,
        shapes,
        outs,
        (spots // tile,),
        scratch,
        alias,
    )


def fixed_out(shape):
    return pl.BlockSpec(shape, lambda i, ix: (0,) * len(shape))


def emit_kernel(where, pred_ref, pick_ref, out_ref):
    high, low = split(pred_ref[...].T)
    pick = pick_ref[...]
    out_ref[...] = dot(high, pick) + dot(low, pick)


def emit(where, pred, pick, tile):
    genes, spots = pred.shape
    return call(
        emit_kernel,
        "emit",
        where,
        [pred, pick],
        [by_tile(genes, tile), fixed((genes, genes))],
        jax.ShapeDtypeStruct((spots, genes), F32),
        pl.BlockSpec((tile, genes), lambda i, ix: (i, 0)),
        (spots // tile,),
    )


def cosine(inner, left, right):
    left = left + EPS
    inv = lax.rsqrt(left) * lax.rsqrt(right + EPS)
    cos = inner * inv
    return cos, inv, cos / left


def pack_kernel(half_ref, core_ref, mine_ref, theirs_ref, z_ref, out_ref, spot_ref):
    genes = out_ref.shape[1] // 2
    totals = half_ref[...] + core_ref[...]
    spot_ref[...] = totals
    cos, _, _ = cosine(totals[0:NB], totals[NB : 2 * NB], totals[2 * NB : 3 * NB])
    out_ref[...] = jnp.zeros_like(out_ref)
    spots = z_ref.shape[1]
    for number in range(3):
        at = slice(number * genes, (number + 1) * genes)
        out_ref[number : number + 1, 0:genes] = mine_ref[12:13, at]
        out_ref[number : number + 1, genes : 2 * genes] = theirs_ref[12:13, at]
        out_ref[3 + number : 4 + number, 0:128] = z_ref[2 + number : 3 + number, spots - 128 :]
    out_ref[6:7, 0:128] = jnp.broadcast_to(
        jnp.sum(jnp.sum(cos, axis=0, keepdims=True), axis=1, keepdims=True), (1, 128)
    )


def pack(half, core, mine, theirs, zinfo, genes):
    return pl.pallas_call(
        pack_kernel,
        out_shape=(
            jax.ShapeDtypeStruct((8, 2 * genes), F32),
            jax.ShapeDtypeStruct(half.shape, F32),
        ),
        compiler_params=pltpu.CompilerParams(vmem_limit_bytes=VMEM_LIMIT),
        cost_estimate=CHEAP,
        name="pack",
    )(half, core, mine, theirs, zinfo)


def rows_kernel(sizes, chosen, where, *refs):
    s_refs = grouped(sizes, refs)
    high_ref, low_ref, buffer, sem = refs[sum(sizes) :]
    rows = high_ref.shape[0] // 2
    pieces = rows // KC
    deepest = max(sizes)
    for slot in range(2 * pieces):
        which = where[1 - slot // pieces]
        piece = slot % pieces
        if chosen is not None:
            hits = chosen(where, which * pieces + piece)
            for hit, group in zip(hits, s_refs):

                @pl.when(hit)
                def _(group=group):
                    for number in range(deepest):
                        ref = group[min(number, len(group) - 1)]
                        pltpu.make_async_copy(ref, buffer.at[slot, number], sem.at[slot, number]).start()

        else:
            at = pl.ds(pl.multiple_of(which * rows + piece * KC, KC), KC)
            pltpu.make_async_copy(s_refs[0][0].at[:, at], buffer.at[slot, 0], sem.at[slot, 0]).start()
    for slot in range(2 * pieces):
        for number in range(deepest):
            pltpu.make_async_copy(s_refs[0][0].at[:, 0:KC], buffer.at[slot, number], sem.at[slot, number]).wait()
        at = slice(slot * KC, slot * KC + KC)
        value = buffer[slot, 0]
        if deepest > 1:
            value = jnp.where(value == 0.0, buffer[slot, 1], value)
        high_ref[at, :], low_ref[at, :] = split(value.T)


def rows_left(where, blocks, rows, chosen):
    sizes, blocks = flat(blocks)
    genes = blocks[0].shape[0]
    shape = jax.ShapeDtypeStruct((2 * rows, genes), BF)
    slots = (2 * rows // KC, max(sizes))
    return call(
        functools.partial(rows_kernel, sizes, chosen),
        "rows_left",
        where,
        list(blocks),
        [pl.BlockSpec(memory_space=pl.ANY)] * len(blocks),
        (shape, shape),
        (fixed_out((2 * rows, genes)), fixed_out((2 * rows, genes))),
        (1,),
        [pltpu.VMEM((*slots, genes, KC), F32), pltpu.SemaphoreType.DMA(slots)],
    )


def back_kernel(final, sizes, where, *refs):
    batch_scale, gene_scale, scale, loss_scale = sizes
    pred_refs, x_refs, refs = refs[0:2], refs[2 : 2 + 2 * XS], refs[2 + 2 * XS :]
    high_refs, low_refs = refs[0:2], refs[2:4]
    totals_ref, spot_ref, z_ref, dens_ref = refs[4:8]
    refs = refs[8:]
    if final:
        sent_ref, got_ref, logit_ref, w_ref, out_ref, loss_ref, bhigh, blow, coef = refs
    else:
        out_ref, bhigh, blow, coef = refs
    genes, tile = pred_refs[0].shape
    rows = high_refs[0].shape[0]
    width = genes // NB
    gene_cos, inv_gene, over_gene = cosine(
        totals_ref[0:1, :], totals_ref[1:2, :], totals_ref[2:3, :]
    )

    @pl.when(pl.program_id(0) == 0)
    def _():
        coef[0] = jnp.broadcast_to(-gene_scale * inv_gene, (128, 2 * genes)).T
        coef[1] = jnp.broadcast_to(gene_scale * over_gene, (128, 2 * genes)).T

    spot = spot_ref[...]
    _, inv_spot, over_spot = cosine(spot[0:NB], spot[NB : 2 * NB], spot[2 * NB : 3 * NB])
    column = jnp.zeros((1, tile), F32)
    value = None
    for part in range(2):
        for batch in range(NB):
            at = slice(batch * width, (batch + 1) * width)
            here = slice(part * genes + batch * width, part * genes + (batch + 1) * width)
            x_by = jnp.concatenate([coef[0, here]] * (tile // 128), axis=1) - (
                batch_scale * inv_spot[batch : batch + 1]
            )
            p_by = jnp.concatenate([coef[1, here]] * (tile // 128), axis=1) + (
                batch_scale * over_spot[batch : batch + 1]
            )
            pred = pred_refs[part][at, :]
            grad = of_batch(x_refs[part * XS :], batch, width) * x_by + pred * p_by
            bhigh[here], blow[here] = split(grad)
            if not final:
                column = column + jnp.sum(pred * grad, axis=0, keepdims=True)
        at = slice(part * genes, (part + 1) * genes)
        one = dot(high_refs[part][...], bhigh[at]) + dot(low_refs[part][...], bhigh[at])
        one = one + dot(high_refs[part][...], blow[at])
        value = one if value is None else value + one
    if not final:
        out_ref[0:rows] = value
        out_ref[rows : rows + 1] = column
        out_ref[rows + 1 : rows + 2] = jnp.broadcast_to(
            jnp.sum(gene_cos, axis=1, keepdims=True), (1, tile)
        )
        out_ref[rows + 2 : rows + 8] = jnp.zeros((6, tile), F32)
        return
    inv, raw = z_ref[0:1, :], z_ref[1:2, :]
    dens = totals_ref[3:4, 0:1]
    mass = totals_ref[4:5, 0:1]
    grad_raw = scale * (1.0 / mass - dens_ref[...] / (dens * raw))
    column = sent_ref[0:1, :] + got_ref[rows : rows + 1, :] + raw * grad_raw
    value = value + got_ref[0:rows, :] + w_ref[...] * grad_raw
    out_ref[...] = jnp.exp(logit_ref[...]) * inv * (value - column)

    @pl.when(pl.program_id(0) == 0)
    def _():
        gene_loss, spot_loss, cents, spots_all = loss_scale
        gene = (sent_ref[1:2, 0:128] + got_ref[rows + 1 : rows + 2, 0:128]) * gene_loss
        cos = totals_ref[6:7, 0:128] * spot_loss
        kl = (
            totals_ref[5:6, 0:128] / totals_ref[3:4, 0:128]
            + jnp.log(totals_ref[4:5, 0:128] * (cents / spots_all))
            - jnp.log(totals_ref[3:4, 0:128] * (1.0 / spots_all))
        )
        lane = lax.broadcasted_iota(jnp.int32, (1, 128), 1)
        loss_ref[...] = jnp.where(lane == 0, gene, jnp.where(lane == 1, cos, kl))


def back(where, preds, xs, lefts, totals, spot, zinfo, density, consts, rows, final, tile):
    genes, spots = preds[0].shape
    left = pl.BlockSpec(
        (rows, genes), lambda i, ix: (0 if final is None else 1, 0), pipeline_mode=pl.Buffered(1)
    )
    specs = [by_tile(genes, tile)] * 2 + [by_tile(genes // XS, tile)] * (2 * XS) + [left] * 4
    specs += [fixed((8, 2 * genes)), by_tile(16, tile), by_tile(8, tile), by_tile(1, tile)]
    args = [*preds, *xs, lefts[0][0], lefts[1][0], lefts[0][1], lefts[1][1]]
    args += [totals, spot, zinfo, density]
    if final is None:
        shapes = jax.ShapeDtypeStruct((rows + 8, spots), F32)
        outs = by_tile(rows + 8, tile)
    else:
        args += final
        specs += [
            by_tile(8, tile, rows // 8),
            by_tile(rows + 8, tile),
            pl.BlockSpec((rows, tile), lambda i, ix: (ix[0], i)),
            pl.BlockSpec((rows, 1), lambda i, ix: (ix[0], 0)),
        ]
        shapes = (
            jax.ShapeDtypeStruct((rows, spots), F32),
            jax.ShapeDtypeStruct((1, 128), F32),
        )
        outs = (by_tile(rows, tile), fixed_out((1, 128)))
    return call(
        functools.partial(back_kernel, final is not None, consts),
        "back_sum" if final is None else "back_end",
        where,
        args,
        specs,
        shapes,
        outs,
        (spots // tile,),
        [
            pltpu.VMEM((2 * genes, tile), BF),
            pltpu.VMEM((2 * genes, tile), BF),
            pltpu.VMEM((2, 2 * genes, 128), F32),
        ],
    )


def swap(value, axis, bit):
    return lax.ppermute(value, axis, [(i, i ^ bit) for i in range(lax.axis_size(axis))])


def after(value, *others):
    return lax.optimization_barrier((value, *others))[0]


def tie(*values):
    return lax.optimization_barrier(values)


def local(logits, centroid_expr, spatial, cluster_cells, density, gene_order):
    n_spot = lax.axis_size("spot")
    n_gene = lax.axis_size("gene")
    me = lax.axis_index("spot")
    col = lax.axis_index("gene")
    cents, spots = logits.shape
    genes = spatial.shape[1]
    genes_all = genes * n_gene
    spots_all = spots * n_spot
    rows = cents // n_gene
    scale = float(spots_all * cents)
    consts = (
        scale / (NB * spots_all),
        scale / genes_all,
        scale,
        (-1.0 / genes_all, -1.0 / (NB * spots_all), float(cents), float(spots_all)),
    )
    ring = n_spot == 8 and cents // n_spot == KC
    where = jnp.stack([col, col ^ 1, me]).astype(jnp.int32)
    tile = 512

    order = (gene_order - col * genes).reshape(genes, 1)
    pick = order == lax.broadcasted_iota(jnp.int32, (genes, genes), 1)
    mine = lax.dot_general(
        pick.astype(F32), centroid_expr, NT, precision=lax.Precision.HIGHEST, preferred_element_type=F32
    )
    pick = pick.astype(BF)
    theirs = swap(mine, "gene", 2)
    weights = cluster_cells.astype(F32)
    weights = (weights / jnp.sum(weights)).reshape(cents, 1)
    dens_row = density.reshape(1, spots)
    fwd = lambda name, keys, blocks, acc, scale_by, x: pred_part(
        where, keys, blocks, e_high, e_low, acc, scale_by, x, tile, name
    )
    if ring:
        hop = lambda block, bit: swap(block, "spot", bit)
        keys = [functools.partial(lambda k, ix: ix[2] ^ k, k) for k in range(n_spot)]
        o1, o2, o3, oy = hop(mine, 2), hop(mine, 4), hop(mine, 6), hop(mine, 1)
        x_own = turn(where, pick, spatial, tile)
        o1, oy, theirs, logits, *x_own = tie(o1, oy, theirs, logits, *x_own)
        o1y, ty = hop(o1, 1), hop(theirs, 1)
        x_got = [swap(x_own[0], "gene", 2)]
        e_high, e_low, zinfo = exp_parts(where, logits, weights, dens_row, tile)
        mine, o1y, e_high = tie(mine, o1y, e_high)
        acc = fwd("own_early", keys[:4], [mine, oy, o1, o1y], None, None, None)
        acc, o2, ty, theirs = tie(acc, o2, ty, theirs)
        o2y, t1, t2 = hop(o2, 1), hop(theirs, 2), hop(theirs, 4)
        theirs, ty, acc, o3 = tie(theirs, ty, acc, o3)
        o3y = hop(o3, 1)
        acc_other = fwd("other_early", keys[:2], [theirs, ty], None, None, None)
        acc, acc_other, o2y, o3y, x_got[0], t1, theirs = tie(acc, acc_other, o2y, o3y, x_got[0], t1, theirs)
        t1y, t3 = hop(t1, 1), hop(theirs, 6)
        pred_own, info = fwd("own_late", keys[4:], [o2, o2y, o3, o3y], acc, zinfo, x_own)
        own = [mine, oy, o1, o1y, o2, o2y, o3, o3y]
        own_pick = lambda ix, block: [(block ^ ix[2]) == key for key in range(n_spot)]
    else:
        x_own = turn(where, pick, spatial, tile)
        x_got = [swap(x_own[0], "gene", 2)]
        e_high, e_low, zinfo = exp_parts(where, logits, weights, dens_row, tile)
        own = [lax.all_gather(mine, "spot", axis=1, tiled=True)]
        other = [lax.all_gather(theirs, "spot", axis=1, tiled=True)]
        first = [lambda ix: 0]
        pred_own, info = fwd("own_late", first, own, None, zinfo, x_own)
        own_pick = None

    info_x = swap(info, "gene", 2)
    left_own = rows_left(where, own, rows, own_pick)
    if ring:
        t2, t3, info_x, left_own = tie(t2, t3, info_x, left_own)
    else:
        info_x, left_own = tie(info_x, left_own)
    half = info + info_x
    totals, spot = pack(half, swap(half, "gene", 1), info, info_x, zinfo, genes)
    x_got += [swap(after(one, info_x), "gene", 2) for one in x_own[1:]]
    if ring:
        t2, t1y, totals, acc_other = tie(t2, t1y, totals, acc_other)
        t2y = hop(t2, 1)
        got = swap(totals, "spot", 1)
        acc_other = fwd("other_mid", [keys[2], keys[3], keys[4]], [t1, t1y, t2], acc_other, None, None)
        t3, acc_other, got = tie(t3, acc_other, got)
        totals = totals + got
        t3y = hop(t3, 1)
        for bit in (2, 4):
            totals = totals + swap(totals, "spot", bit)
        acc_other, totals, t2y = tie(acc_other, totals, t2y)
        pred_other = fwd("other_late", keys[5:], [t2y, t3, t3y], acc_other, zinfo, None)
        other = [theirs, ty, t1, t1y, t2, t2y, t3, t3y]
    else:
        totals = lax.psum(totals, "spot")
        pred_other = fwd("other_late", first, other, None, zinfo, None)
    left_other = rows_left(where, other, rows, own_pick)

    common = (
        (pred_own, pred_other), (*x_own, *x_got), (left_own, left_other), totals, spot, zinfo, dens_row, consts, rows,
    )
    sent = back(where, *common, None, tile)
    got = swap(sent, "gene", 1)
    predicted = emit(where, after(pred_own, sent), pick, tile)
    predicted, got = tie(predicted, got)
    grad, loss = back(where, *common, [sent, got, logits, weights], tile)
    return loss[0, 0:3], predicted, grad


def solution(mesh):
    return jax.shard_map(
        local,
        mesh=mesh,
        in_specs=(P(None, "spot"), P("spot", "gene"), P("spot", "gene"), P(), P("spot"), P("gene")),
        out_specs=(P(), P("spot", "gene"), P("gene", "spot")),
        check_vma=False,
    )
```

time: 671 us -> 210 us (0.31); the launches traced: 661 us -> 208 us
  waiting for transfers between devices: 235 us -> 16.8 us
  matrix products: 214 us -> 2.52 us
  Pallas kernels: 0 us -> 125 us
  local copies, waits for them, and re-layouts: 68.8 us -> 3.15 us
  blocking collectives: 62.1 us -> 0 us
  other arithmetic: 60.2 us -> 7.33 us
  starting transfers between devices: 0.25 us -> 53.1 us
  between operations: 21.1 us -> 0.72 us
    psum x2 -> x0, waiting for transfers between devices: 235 us -> none  [the longest x1 203 us: local(): summed = lax.psum(partial_value, 'gene')]
    dot_general x9 -> x1, matrix products: 214 us -> 2.52 us  [local(): lax.dot_general(pick.astype(F32), centroid_expr, NT, precision=lax.Precis...]
    pallas_call x0 -> x13, Pallas kernels: none -> 125 us  [the longest x12 123 us: call(): pl.pallas_call(kernel, out_shape=out_shape, grid_spec=pltpu.PrefetchScala...]
    psum x2 -> x0, blocking collectives: 62.1 us -> none  [the longest x1 42.3 us: local(): loss_terms = lax.psum(local_terms, ('spot', 'gene'))]
    ppermute x0 -> x23, starting transfers between devices: none -> 53.1 us  [swap(): lax.ppermute(value, axis, [(i, i ^ bit) for i in range(lax.axis_size(axis...]
    gather x12 -> x0, local copies, waits for them, and re-layouts: 28.4 us -> none  [the longest x8 25.4 us: local(): target = jnp.take(spatial, columns, axis=1)]
    reduce_sum x11 -> x1, other arithmetic: 25.8 us -> 1.3 us  [local(): weights = (weights / jnp.sum(weights)).reshape(cents, 1)]
    scatter x4 -> x0, local copies, waits for them, and re-layouts: 21.3 us -> none  [local(): predicted = predicted.at[:, columns].set(pred)]
  transfers between devices with their start and end apart: 6 -> 23, of which waited for: 2 -> 10; matrix products, arithmetic and copies ran while one was open for 31% -> 4% of each run, Pallas kernels for 0% -> 45%
where the time goes in v2:
time: 210 us; the launch traced here: 208 us
  Pallas kernels  125 us (60%)
  starting transfers between devices  53.1 us (25%)
  waiting for transfers between devices  16.8 us (8%)
  other arithmetic  7.33 us (3%)
  local copies, waits for them, and re-layouts  3.15 us (2%)
  matrix products  2.52 us (1%)
    pallas_call x12, Pallas kernels, call(): pl.pallas_call(kernel, out_shape=out_shape, grid_spec=pltpu.PrefetchScala...  123 us
    ppermute x23, starting transfers between devices, swap(): lax.ppermute(value, axis, [(i, i ^ bit) for i in range(lax.axis_size(axis...  53.1 us
    ppermute x23, waiting for transfers between devices, swap(): lax.ppermute(value, axis, [(i, i ^ bit) for i in range(lax.axis_size(axis...  16.8 us
  transfers between devices with their start and end apart: 23, of which 10 were waited for; matrix products, arithmetic and copies ran while one was open for 4% of the time, Pallas kernels for 45%

profile of v2, /device:TPU:1, one launch (start us, length us, event | category | flops | bytes accessed | tf_op | source)
XLA Modules:
  0.0 208.3 jit_solution(415190358682090106)
XLA Ops:
  1.3 2.5 %fusion.1.refs_0_ = f32[512,256]{1,0:T(8,128)} fusion(f32[256,512]{1,0:T(8,128)} %param.7, s32[512]{0:T(512)S(1)} %broadcast_subtract_fusion), kind=kOutput, calls=%fused_computation.2 | convolution fusion | flops 805568512 | bytes 1050624 | tf_op jit(solution)/shard_map/dot_general | solution.py:527
  3.8 2.1 %collective-permute-start = (f32[512,256]{1,0:T(8,128)}, f32[512,256]{1,0:T(8,128)}, u32[]{:S(2)}, u32[]{:S(2)}) collective-permute-start(f32[512,256]{1,0:T(8,128)} %fusion.1.refs_0_), channel_id=1, source_target_pairs={{0,8},{4,12},{8,0},{12,4},{16,24},{20,28},{24,16},{28,20},{1,9},{5... | collective-permute-start | bytes 1572872 | tf_op jit(solution)/shard_map/ppermute | solution.py:493
  6.0 1.2 collective-permute-start.1
  7.2 1.2 collective-permute-start.2
  10.0 6.9 %turn.1 = (f32[256,2048]{1,0:T(8,128)}, f32[256,2048]{1,0:T(8,128)}) custom-call(s32[3]{0:T(128)} %pad_add_fusion.where, bf16[512,512]{1,0:T(8,128)(2,1)} %fusion.pick_ref, f32[2048,512]{1,0:T(8,128)} %x_ref.1), custom_call_target="tpu_custom_call" | custom-call | flops 1000 | bytes 1000 | tf_op jit(solution)/shard_map/turn/pallas_call | solution.py:31
  19.7 1.2 collective-permute-start.9
  21.2 2.3 %collective-permute-start.4 = (f32[512,256]{1,0:T(8,128)}, f32[512,256]{1,0:T(8,128)}, u32[]{:S(2)}, u32[]{:S(2)}) collective-permute-start(f32[512,256]{1,0:T(8,128)} %fusion.1.refs_0_), channel_id=1, source_target_pairs={{0,16},{4,20},{8,24},{12,28},{16,0},{20,4},{24,8},{28,12},{1,17},{... | collective-permute-start | bytes 1572872 | tf_op jit(solution)/shard_map/ppermute | solution.py:493
  24.7 1.3 convert_reduce_fusion
  26.0 1.3 convert_divide_fusion
  27.4 1.4 copy.12.w_ref.refs_17_
  28.7 14.3 %exp_parts.1 = (bf16[2048,2048]{1,0:T(8,128)(2,1)}, bf16[2048,2048]{1,0:T(8,128)(2,1)}, f32[8,2048]{1,0:T(8,128)}) custom-call(s32[3]{0:T(128)} %pad_add_fusion.where, f32[2048,2048]{1,0:T(8,128)} %refs_16_, f32[2048,1]{1,0:T(8,128)} %copy.12.w_ref.refs_17_, f32[1,2048]{1,0:T(1,128)} %bitcast.8), custom_call_target="tpu_custom_call" | custom-call | flops 1000 | bytes 1000 | tf_op jit(solution)/shard_map/exp_parts/pallas_call | solution.py:31
  43.0 12.2 %own_early.1.refs_12_ = f32[512,2048]{1,0:T(8,128)} custom-call(s32[3]{0:T(128)} %pad_add_fusion.where, f32[512,256]{1,0:T(8,128)} %fusion.1.refs_0_, f32[512,256]{1,0:T(8,128)} %collective-permute-done.1.refs_1_, f32[512,256]{1,0:T(8,128)} %collective-permute-done.refs_2_, f32[512,256]{1,0:T(8,128)} %collective-permute-done.3.refs_3_, ...), custom_call_target="tpu_custom_call" | custom-call | flops 1000 | bytes 1000 | tf_op jit(solution)/shard_map/own_early/pallas_call | solution.py:31
  55.3 3.4 %collective-permute-done.4.refs_0_.refs_4_ = f32[512,256]{1,0:T(8,128)} collective-permute-done((f32[512,256]{1,0:T(8,128)}, f32[512,256]{1,0:T(8,128)}, u32[]{:S(2)}, u32[]{:S(2)}) %collective-permute-start.4) | collective-permute-done | bytes 524320 | tf_op jit(solution)/shard_map/ppermute | solution.py:493
  60.2 11.7 %collective-permute-start.11 = (f32[512,256]{1,0:T(8,128)}, f32[512,256]{1,0:T(8,128)}, u32[]{:S(2)}, u32[]{:S(2)}) collective-permute-start(f32[512,256]{1,0:T(8,128)} %collective-permute-done.2.refs_0_), channel_id=1, source_target_pairs={{0,16},{4,20},{8,24},{12,28},{16,0},{20,4},{24,8},{28,12},{1,17},{... | collective-permute-start | bytes 1572872 | tf_op jit(solution)/shard_map/ppermute | solution.py:493
  72.0 8.2 %other_early.1.refs_9_ = f32[512,2048]{1,0:T(8,128)} custom-call(s32[3]{0:T(128)} %pad_add_fusion.where, f32[512,256]{1,0:T(8,128)} %collective-permute-done.2.refs_0_, f32[512,256]{1,0:T(8,128)} %collective-permute-done.5.refs_1_, bf16[2048,2048]{1,0:T(8,128)(2,1)} %get-tuple-element.69.refs_4_.refs_5_.refs_6_.refs_7_.refs_2_.refs_3_, ...), custom_call_target="tpu_custom_call" | custom-call | flops 1000 | bytes 1000 | tf_op jit(solution)/shard_map/other_early/pallas_call | solution.py:31
  80.2 2.3 %collective-permute-done.7.refs_1_.refs_5_ = f32[512,256]{1,0:T(8,128)} collective-permute-done((f32[512,256]{1,0:T(8,128)}, f32[512,256]{1,0:T(8,128)}, u32[]{:S(2)}, u32[]{:S(2)}) %collective-permute-start.7) | collective-permute-done | bytes 524320 | tf_op jit(solution)/shard_map/ppermute | solution.py:493
  82.8 14.5 %own_late.1 = (f32[512,2048]{1,0:T(8,128)}, f32[16,2048]{1,0:T(8,128)}) custom-call(s32[3]{0:T(128)} %pad_add_fusion.where, f32[512,256]{1,0:T(8,128)} %collective-permute-done.4.refs_0_.refs_4_, f32[512,256]{1,0:T(8,128)} %collective-permute-done.7.refs_1_.refs_5_, ...), custom_call_target="tpu_custom_call", output_to_operand_aliasing={{0}: (13, {})} | custom-call | flops 1000 | bytes 1000 | tf_op jit(solution)/shard_map/own_late/pallas_call | solution.py:31
  97.6 3.9 %rows_left.2 = (bf16[1024,512]{1,0:T(8,128)(2,1)}, bf16[1024,512]{1,0:T(8,128)(2,1)}) custom-call(s32[3]{0:T(128)} %pad_add_fusion.where, f32[512,256]{1,0:T(8,128)} %fusion.1.refs_0_, f32[512,256]{1,0:T(8,128)} %collective-permute-done.1.refs_1_, f32[512,256]{1,0:T(8,128)} %collective-permute-done.refs_2_, f32[512,256]{1,0:T(8,128)} %collective-permute-done.3.refs_3_, ...), custom_call_target="tpu_custom_call" | custom-call | flops 1000 | bytes 1000 | tf_op jit(solution)/shard_map/rows_left/pallas_call | solution.py:31
  101.4 3.8 %collective-permute-done.11.refs_2_.refs_4_ = f32[512,256]{1,0:T(8,128)} collective-permute-done((f32[512,256]{1,0:T(8,128)}, f32[512,256]{1,0:T(8,128)}, u32[]{:S(2)}, u32[]{:S(2)}) %collective-permute-start.11) | collective-permute-done | bytes 524320 | tf_op jit(solution)/shard_map/ppermute | solution.py:493
  107.8 5.4 %collective-permute-start.15 = (f32[16,2048]{1,0:T(8,128)S(1)}, f32[16,2048]{1,0:T(8,128)}, u32[]{:S(2)}, u32[]{:S(2)}) collective-permute-start(f32[16,2048]{1,0:T(8,128)S(1)} %add.12.half_ref), channel_id=1, source_target_pairs={{0,1},{1,0},{2,3},{3,2},{4,5},{5,4},{6,7},{7,6},{8,9},{9,8},{10,11... | collective-permute-start | bytes 393224 | tf_op jit(solution)/shard_map/ppermute | solution.py:493
  114.3 1.8 pack.1
  117.6 10.9 %other_mid.1.refs_9_ = f32[512,2048]{1,0:T(8,128)} custom-call(s32[3]{0:T(128)} %pad_add_fusion.where, f32[512,256]{1,0:T(8,128)} %collective-permute-done.10.refs_0_.refs_2_, f32[512,256]{1,0:T(8,128)} %collective-permute-done.14.refs_1_.refs_3_, f32[512,256]{1,0:T(8,128)} %collective-permute-done.11.refs_2_.refs_4_, ...), custom_call_target="tpu_custom_call", output_to_operand_aliasing={{}: (10, {})} | custom-call | flops 1000 | bytes 1000 | tf_op jit(solution)/shard_map/other_mid/pallas_call | solution.py:31
  129.7 12.0 %collective-permute-start.17 = (f32[8,1024]{1,0:T(8,128)S(1)}, f32[8,1024]{1,0:T(8,128)S(1)}, u32[]{:S(2)}, u32[]{:S(2)}) collective-permute-start(f32[8,1024]{1,0:T(8,128)S(1)} %add.13), channel_id=1, source_target_pairs={{0,8},{4,12},{8,0},{12,4},{16,24},{20,28},{24,16},{28,20},{1,9},{5... | collective-permute-start | bytes 98312 | tf_op jit(solution)/shard_map/ppermute | solution.py:493
  141.8 1.7 collective-permute-done.17
  143.5 4.2 %collective-permute-start.18 = (f32[8,1024]{1,0:T(8,128)S(1)}, f32[8,1024]{1,0:T(8,128)S(1)}, u32[]{:S(2)}, u32[]{:S(2)}) collective-permute-start(f32[8,1024]{1,0:T(8,128)S(1)} %add.14), channel_id=1, source_target_pairs={{0,16},{4,20},{8,24},{12,28},{16,0},{20,4},{24,8},{28,12},{1,17},{... | collective-permute-start | bytes 98312 | tf_op jit(solution)/shard_map/ppermute | solution.py:493
  147.7 1.4 collective-permute-done.18
  149.7 3.9 %rows_left.3 = (bf16[1024,512]{1,0:T(8,128)(2,1)}, bf16[1024,512]{1,0:T(8,128)(2,1)}) custom-call(s32[3]{0:T(128)} %pad_add_fusion.where, f32[512,256]{1,0:T(8,128)} %collective-permute-done.2.refs_0_, f32[512,256]{1,0:T(8,128)} %collective-permute-done.5.refs_1_, f32[512,256]{1,0:T(8,128)} %collective-permute-done.10.refs_0_.refs_2_, ...), custom_call_target="tpu_custom_call" | custom-call | flops 1000 | bytes 1000 | tf_op jit(solution)/shard_map/rows_left/pallas_call | solution.py:31
  153.5 11.0 %other_late.1.refs_1_ = f32[512,2048]{1,0:T(8,128)} custom-call(s32[3]{0:T(128)} %pad_add_fusion.where, f32[512,256]{1,0:T(8,128)} %collective-permute-done.19.refs_0_.refs_5_, f32[512,256]{1,0:T(8,128)} %collective-permute-done.12.refs_1_.refs_6_, f32[512,256]{1,0:T(8,128)} %collective-permute-done.20.refs_2_.refs_7_, ...), custom_call_target="tpu_custom_call", output_to_operand_aliasing={{}: (10, {})} | custom-call | flops 1000 | bytes 1000 | tf_op jit(solution)/shard_map/other_late/pallas_call | solution.py:31
  164.5 14.3 %back_sum.1.refs_14_ = f32[520,2048]{1,0:T(8,128)} custom-call(s32[3]{0:T(128)} %pad_add_fusion.where, f32[512,2048]{1,0:T(8,128)} %get-tuple-element.114.refs_0_.pred_ref, f32[512,2048]{1,0:T(8,128)} %other_late.1.refs_1_, f32[256,2048]{1,0:T(8,128)} %get-tuple-element.80.refs_14_.refs_2_, f32[256,2048]{1,0:T(8,128)} %get-tuple-element.107.refs_15_.refs_3_, ...), custom_call_target="tpu_custom_call" | custom-call | flops 1000 | bytes 1000 | tf_op jit(solution)/shard_map/back_sum/pallas_call | solution.py:31
  178.9 5.3 %collective-permute-start.22 = (f32[520,2048]{1,0:T(8,128)}, f32[520,2048]{1,0:T(8,128)}, u32[]{:S(2)}, u32[]{:S(2)}) collective-permute-start(f32[520,2048]{1,0:T(8,128)} %back_sum.1.refs_14_), channel_id=1, source_target_pairs={{0,1},{1,0},{2,3},{3,2},{4,5},{5,4},{6,7},{7,6},{8,9},{9,8},{10,11... | collective-permute-start | bytes 12779528 | tf_op jit(solution)/shard_map/ppermute | solution.py:493
  184.1 7.0 %emit.1 = f32[2048,512]{1,0:T(8,128)} custom-call(s32[3]{0:T(128)} %pad_add_fusion.where, f32[512,2048]{1,0:T(8,128)} %get-tuple-element.114.refs_0_.pred_ref, bf16[512,512]{1,0:T(8,128)(2,1)} %fusion.pick_ref), custom_call_target="tpu_custom_call" | custom-call | flops 1000 | bytes 1000 | tf_op jit(solution)/shard_map/emit/pallas_call | solution.py:31
  191.3 15.8 %back_end.1 = (f32[512,2048]{1,0:T(8,128)}, f32[1,128]{1,0:T(1,128)}) custom-call(s32[3]{0:T(128)} %pad_add_fusion.where, f32[512,2048]{1,0:T(8,128)} %get-tuple-element.114.refs_0_.pred_ref, f32[512,2048]{1,0:T(8,128)} %other_late.1.refs_1_, f32[256,2048]{1,0:T(8,128)} %get-tuple-element.80.refs_14_.refs_2_, ...), custom_call_target="tpu_custom_call" | custom-call | flops 1000 | bytes 1000 | tf_op jit(solution)/shard_map/back_end/pallas_call | solution.py:31
  (41 shorter events, 17.0 us)
Async XLA Ops:
  3.8 14.1 %collective-permute-start = (f32[512,256]{1,0:T(8,128)}, f32[512,256]{1,0:T(8,128)}, u32[]{:S(2)}, u32[]{:S(2)}) collective-permute-start(f32[512,256]{1,0:T(8,128)} %fusion.1.refs_0_), channel_id=1, source_target_pairs={{0,8},{4,12},{8,0},{12,4},{16,24},{20,28},{24,16},{28,20},{1,9},{5... | collective-permute-start | bytes 1572872 | tf_op jit(solution)/shard_map/ppermute | solution.py:493
  6.0 12.8 %collective-permute-start.1 = (f32[512,256]{1,0:T(8,128)}, f32[512,256]{1,0:T(8,128)}, u32[]{:S(2)}, u32[]{:S(2)}) collective-permute-start(f32[512,256]{1,0:T(8,128)} %fusion.1.refs_0_), channel_id=1, source_target_pairs={{0,4},{4,0},{8,12},{12,8},{16,20},{20,16},{24,28},{28,24},{1,5},{5... | collective-permute-start | bytes 1572872 | tf_op jit(solution)/shard_map/ppermute | solution.py:493
  7.2 12.5 %collective-permute-start.2 = (f32[512,256]{1,0:T(8,128)}, f32[512,256]{1,0:T(8,128)}, u32[]{:S(2)}, u32[]{:S(2)}) collective-permute-start(f32[512,256]{1,0:T(8,128)} %fusion.1.refs_0_), channel_id=1, source_target_pairs={{0,2},{1,3},{2,0},{3,1},{4,6},{5,7},{6,4},{7,5},{8,10},{9,11},{10,... | collective-permute-start | bytes 1572872 | tf_op jit(solution)/shard_map/ppermute | solution.py:493
  19.7 62.7 %collective-permute-start.9 = (f32[256,2048]{1,0:T(8,128)}, f32[256,2048]{1,0:T(8,128)}, u32[]{:S(2)}, u32[]{:S(2)}) collective-permute-start(f32[256,2048]{1,0:T(8,128)} %get-tuple-element.80.refs_14_.refs_2_), channel_id=1, source_target_pairs={{0,2},{1,3},{2,0},{3,1},{4,6},{5,7},{6,4},{7,5},{8,10},{9,11},{10,... | collective-permute-start | bytes 6291464 | tf_op jit(solution)/shard_map/ppermute | solution.py:493
  20.9 22.1 %collective-permute-start.3 = (f32[512,256]{1,0:T(8,128)}, f32[512,256]{1,0:T(8,128)}, u32[]{:S(2)}, u32[]{:S(2)}) collective-permute-start(f32[512,256]{1,0:T(8,128)} %collective-permute-done.refs_2_), channel_id=1, source_target_pairs={{0,4},{4,0},{8,12},{12,8},{16,20},{20,16},{24,28},{28,24},{1,5},{5... | collective-permute-start | bytes 1572872 | tf_op jit(solution)/shard_map/ppermute | solution.py:493
  21.2 37.5 %collective-permute-start.4 = (f32[512,256]{1,0:T(8,128)}, f32[512,256]{1,0:T(8,128)}, u32[]{:S(2)}, u32[]{:S(2)}) collective-permute-start(f32[512,256]{1,0:T(8,128)} %fusion.1.refs_0_), channel_id=1, source_target_pairs={{0,16},{4,20},{8,24},{12,28},{16,0},{20,4},{24,8},{28,12},{1,17},{... | collective-permute-start | bytes 1572872 | tf_op jit(solution)/shard_map/ppermute | solution.py:493
  23.5 35.2 %collective-permute-start.5 = (f32[512,256]{1,0:T(8,128)}, f32[512,256]{1,0:T(8,128)}, u32[]{:S(2)}, u32[]{:S(2)}) collective-permute-start(f32[512,256]{1,0:T(8,128)} %collective-permute-done.2.refs_0_), channel_id=1, source_target_pairs={{0,4},{4,0},{8,12},{12,8},{16,20},{20,16},{24,28},{28,24},{1,5},{5... | collective-permute-start | bytes 1572872 | tf_op jit(solution)/shard_map/ppermute | solution.py:493
  24.7 34.0 %collective-permute-start.6 = (f32[512,256]{1,0:T(8,128)}, f32[512,256]{1,0:T(8,128)}, u32[]{:S(2)}, u32[]{:S(2)}) collective-permute-start(f32[512,256]{1,0:T(8,128)} %fusion.1.refs_0_), channel_id=1, source_target_pairs={{0,24},{4,28},{8,16},{12,20},{16,8},{20,12},{24,0},{28,4},{1,25},{... | collective-permute-start | bytes 1572872 | tf_op jit(solution)/shard_map/ppermute | solution.py:493
  58.7 21.5 %collective-permute-start.10 = (f32[512,256]{1,0:T(8,128)}, f32[512,256]{1,0:T(8,128)}, u32[]{:S(2)}, u32[]{:S(2)}) collective-permute-start(f32[512,256]{1,0:T(8,128)} %collective-permute-done.2.refs_0_), channel_id=1, source_target_pairs={{0,8},{4,12},{8,0},{12,4},{16,24},{20,28},{24,16},{28,20},{1,9},{5... | collective-permute-start | bytes 1572872 | tf_op jit(solution)/shard_map/ppermute | solution.py:493
  58.7 21.4 %collective-permute-start.8 = (f32[512,256]{1,0:T(8,128)}, f32[512,256]{1,0:T(8,128)}, u32[]{:S(2)}, u32[]{:S(2)}) collective-permute-start(f32[512,256]{1,0:T(8,128)} %collective-permute-done.6.refs_2_.refs_6_), channel_id=1, source_target_pairs={{0,4},{4,0},{8,12},{12,8},{16,20},{20,16},{24,28},{28,24},{1,5},{5... | collective-permute-start | bytes 1572872 | tf_op jit(solution)/shard_map/ppermute | solution.py:493
  59.9 22.6 %collective-permute-start.7 = (f32[512,256]{1,0:T(8,128)}, f32[512,256]{1,0:T(8,128)}, u32[]{:S(2)}, u32[]{:S(2)}) collective-permute-start(f32[512,256]{1,0:T(8,128)} %collective-permute-done.4.refs_0_.refs_4_), channel_id=1, source_target_pairs={{0,4},{4,0},{8,12},{12,8},{16,20},{20,16},{24,28},{28,24},{1,5},{5... | collective-permute-start | bytes 1572872 | tf_op jit(solution)/shard_map/ppermute | solution.py:493
  60.2 45.0 %collective-permute-start.11 = (f32[512,256]{1,0:T(8,128)}, f32[512,256]{1,0:T(8,128)}, u32[]{:S(2)}, u32[]{:S(2)}) collective-permute-start(f32[512,256]{1,0:T(8,128)} %collective-permute-done.2.refs_0_), channel_id=1, source_target_pairs={{0,16},{4,20},{8,24},{12,28},{16,0},{20,4},{24,8},{28,12},{1,17},{... | collective-permute-start | bytes 1572872 | tf_op jit(solution)/shard_map/ppermute | solution.py:493
  82.5 22.8 %collective-permute-start.12 = (f32[512,256]{1,0:T(8,128)}, f32[512,256]{1,0:T(8,128)}, u32[]{:S(2)}, u32[]{:S(2)}) collective-permute-start(f32[512,256]{1,0:T(8,128)} %collective-permute-done.2.refs_0_), channel_id=1, source_target_pairs={{0,24},{4,28},{8,16},{12,20},{16,8},{20,12},{24,0},{28,4},{1,25},{... | collective-permute-start | bytes 1572872 | tf_op jit(solution)/shard_map/ppermute | solution.py:493
  97.2 8.0 %collective-permute-start.13 = (f32[16,2048]{1,0:T(8,128)}, f32[16,2048]{1,0:T(8,128)}, u32[]{:S(2)}, u32[]{:S(2)}) collective-permute-start(f32[16,2048]{1,0:T(8,128)} %get-tuple-element.88.mine_ref), channel_id=1, source_target_pairs={{0,2},{1,3},{2,0},{3,1},{4,6},{5,7},{6,4},{7,5},{8,10},{9,11},{10,... | collective-permute-start | bytes 393224 | tf_op jit(solution)/shard_map/ppermute | solution.py:493
  105.3 59.2 %collective-permute-start.21 = (f32[256,2048]{1,0:T(8,128)}, f32[256,2048]{1,0:T(8,128)}, u32[]{:S(2)}, u32[]{:S(2)}) collective-permute-start(f32[256,2048]{1,0:T(8,128)} %get-tuple-element.107.refs_15_.refs_3_), channel_id=1, source_target_pairs={{0,2},{1,3},{2,0},{3,1},{4,6},{5,7},{6,4},{7,5},{8,10},{9,11},{10,... | collective-permute-start | bytes 6291464 | tf_op jit(solution)/shard_map/ppermute | solution.py:493
  105.5 10.6 %collective-permute-start.14 = (f32[512,256]{1,0:T(8,128)}, f32[512,256]{1,0:T(8,128)}, u32[]{:S(2)}, u32[]{:S(2)}) collective-permute-start(f32[512,256]{1,0:T(8,128)} %collective-permute-done.10.refs_0_.refs_2_), channel_id=1, source_target_pairs={{0,4},{4,0},{8,12},{12,8},{16,20},{20,16},{24,28},{28,24},{1,5},{5... | collective-permute-start | bytes 1572872 | tf_op jit(solution)/shard_map/ppermute | solution.py:493
  107.1 0.7 copy-start
  107.8 6.5 %collective-permute-start.15 = (f32[16,2048]{1,0:T(8,128)S(1)}, f32[16,2048]{1,0:T(8,128)}, u32[]{:S(2)}, u32[]{:S(2)}) collective-permute-start(f32[16,2048]{1,0:T(8,128)S(1)} %add.12.half_ref), channel_id=1, source_target_pairs={{0,1},{1,0},{2,3},{3,2},{4,5},{5,4},{6,7},{7,6},{8,9},{9,8},{10,11... | collective-permute-start | bytes 393224 | tf_op jit(solution)/shard_map/ppermute | solution.py:493
  116.1 12.4 %collective-permute-start.16 = (f32[8,1024]{1,0:T(8,128)}, f32[8,1024]{1,0:T(8,128)}, u32[]{:S(2)}, u32[]{:S(2)}) collective-permute-start(f32[8,1024]{1,0:T(8,128)} %get-tuple-element.100), channel_id=1, source_target_pairs={{0,4},{4,0},{8,12},{12,8},{16,20},{20,16},{24,28},{28,24},{1,5},{5... | collective-permute-start | bytes 98312 | tf_op jit(solution)/shard_map/ppermute | solution.py:493
  116.5 33.2 %collective-permute-start.19 = (f32[512,256]{1,0:T(8,128)}, f32[512,256]{1,0:T(8,128)}, u32[]{:S(2)}, u32[]{:S(2)}) collective-permute-start(f32[512,256]{1,0:T(8,128)} %collective-permute-done.11.refs_2_.refs_4_), channel_id=1, source_target_pairs={{0,4},{4,0},{8,12},{12,8},{16,20},{20,16},{24,28},{28,24},{1,5},{5... | collective-permute-start | bytes 1572872 | tf_op jit(solution)/shard_map/ppermute | solution.py:493
  128.5 21.1 %collective-permute-start.20 = (f32[512,256]{1,0:T(8,128)}, f32[512,256]{1,0:T(8,128)}, u32[]{:S(2)}, u32[]{:S(2)}) collective-permute-start(f32[512,256]{1,0:T(8,128)} %collective-permute-done.12.refs_1_.refs_6_), channel_id=1, source_target_pairs={{0,4},{4,0},{8,12},{12,8},{16,20},{20,16},{24,28},{28,24},{1,5},{5... | collective-permute-start | bytes 1572872 | tf_op jit(solution)/shard_map/ppermute | solution.py:493
  129.7 13.7 %collective-permute-start.17 = (f32[8,1024]{1,0:T(8,128)S(1)}, f32[8,1024]{1,0:T(8,128)S(1)}, u32[]{:S(2)}, u32[]{:S(2)}) collective-permute-start(f32[8,1024]{1,0:T(8,128)S(1)} %add.13), channel_id=1, source_target_pairs={{0,8},{4,12},{8,0},{12,4},{16,24},{20,28},{24,16},{28,20},{1,9},{5... | collective-permute-start | bytes 98312 | tf_op jit(solution)/shard_map/ppermute | solution.py:493
  143.5 5.6 %collective-permute-start.18 = (f32[8,1024]{1,0:T(8,128)S(1)}, f32[8,1024]{1,0:T(8,128)S(1)}, u32[]{:S(2)}, u32[]{:S(2)}) collective-permute-start(f32[8,1024]{1,0:T(8,128)S(1)} %add.14), channel_id=1, source_target_pairs={{0,16},{4,20},{8,24},{12,28},{16,0},{20,4},{24,8},{28,12},{1,17},{... | collective-permute-start | bytes 98312 | tf_op jit(solution)/shard_map/ppermute | solution.py:493
  178.9 12.5 %collective-permute-start.22 = (f32[520,2048]{1,0:T(8,128)}, f32[520,2048]{1,0:T(8,128)}, u32[]{:S(2)}, u32[]{:S(2)}) collective-permute-start(f32[520,2048]{1,0:T(8,128)} %back_sum.1.refs_14_), channel_id=1, source_target_pairs={{0,1},{1,0},{2,3},{3,2},{4,5},{5,4},{6,7},{7,6},{8,9},{9,8},{10,11... | collective-permute-start | bytes 12779528 | tf_op jit(solution)/shard_map/ppermute | solution.py:493

commit v3 on v2

--- a/solution.py
+++ b/solution.py
@@ -372,32 +372,37 @@
     )
 
 
-def back_kernel(final, sizes, where, *refs):
-    batch_scale, gene_scale, scale, loss_scale = sizes
+def back_dots(high_refs, low_refs, bhigh, blow, genes):
+    value = None
+    for part in range(2):
+        at = slice(part * genes, (part + 1) * genes)
+        one = dot(high_refs[part][...], bhigh[at]) + dot(low_refs[part][...], bhigh[at])
+        one = one + dot(high_refs[part][...], blow[at])
+        value = one if value is None else value + one
+    return value
+
+
+def back_sum_kernel(sizes, where, *refs):
+    batch_scale, gene_scale = sizes
     pred_refs, x_refs, refs = refs[0:2], refs[2 : 2 + 2 * XS], refs[2 + 2 * XS :]
     high_refs, low_refs = refs[0:2], refs[2:4]
-    totals_ref, spot_ref, z_ref, dens_ref = refs[4:8]
-    refs = refs[8:]
-    if final:
-        sent_ref, got_ref, logit_ref, w_ref, out_ref, loss_ref, bhigh, blow, coef = refs
-    else:
-        out_ref, bhigh, blow, coef = refs
+    totals_ref, more_ref, spot_ref, out_ref, bhigh, blow, sum_ref, coef = refs[4:]
     genes, tile = pred_refs[0].shape
     rows = high_refs[0].shape[0]
     width = genes // NB
-    gene_cos, inv_gene, over_gene = cosine(
-        totals_ref[0:1, :], totals_ref[1:2, :], totals_ref[2:3, :]
-    )
 
     @pl.when(pl.program_id(0) == 0)
     def _():
+        totals = totals_ref[...] + more_ref[...]
+        gene_cos, inv_gene, over_gene = cosine(totals[0:1], totals[1:2], totals[2:3])
         coef[0] = jnp.broadcast_to(-gene_scale * inv_gene, (128, 2 * genes)).T
         coef[1] = jnp.broadcast_to(gene_scale * over_gene, (128, 2 * genes)).T
+        cos = jnp.broadcast_to(jnp.sum(gene_cos, axis=1, keepdims=True), (1, 128))
+        sum_ref[...] = jnp.concatenate([totals[3:7, 0:128], cos, jnp.zeros((3, 128), F32)], axis=0)
 
     spot = spot_ref[...]
     _, inv_spot, over_spot = cosine(spot[0:NB], spot[NB : 2 * NB], spot[2 * NB : 3 * NB])
     column = jnp.zeros((1, tile), F32)
-    value = None
     for part in range(2):
         for batch in range(NB):
             at = slice(batch * width, (batch + 1) * width)
@@ -411,23 +416,45 @@
             pred = pred_refs[part][at, :]
             grad = of_batch(x_refs[part * XS :], batch, width) * x_by + pred * p_by
             bhigh[here], blow[here] = split(grad)
-            if not final:
-                column = column + jnp.sum(pred * grad, axis=0, keepdims=True)
-        at = slice(part * genes, (part + 1) * genes)
-        one = dot(high_refs[part][...], bhigh[at]) + dot(low_refs[part][...], bhigh[at])
-        one = one + dot(high_refs[part][...], blow[at])
-        value = one if value is None else value + one
-    if not final:
-        out_ref[0:rows] = value
-        out_ref[rows : rows + 1] = column
-        out_ref[rows + 1 : rows + 2] = jnp.broadcast_to(
-            jnp.sum(gene_cos, axis=1, keepdims=True), (1, tile)
-        )
-        out_ref[rows + 2 : rows + 8] = jnp.zeros((6, tile), F32)
-        return
+            column = column + jnp.sum(pred * grad, axis=0, keepdims=True)
+    out_ref[0:rows] = back_dots(high_refs, low_refs, bhigh, blow, genes)
+    out_ref[rows : rows + 1] = column
+    out_ref[rows + 1 : rows + 2] = jnp.concatenate([sum_ref[4:5]] * (tile // 128), axis=1)
+    out_ref[rows + 2 : rows + 8] = jnp.zeros((6, tile), F32)
+
+
+def back_sum(where, preds, xs, lefts, totals, more, spot, consts, rows, tile):
+    genes, spots = preds[0].shape
+    left = pl.BlockSpec((rows, genes), lambda i, ix: (0, 0), pipeline_mode=pl.Buffered(1))
+    specs = [by_tile(genes, tile)] * 2 + [by_tile(genes // XS, tile)] * (2 * XS) + [left] * 4
+    specs += [fixed((8, 2 * genes))] * 2 + [by_tile(16, tile)]
+    args = [*preds, *xs, lefts[0][0], lefts[1][0], lefts[0][1], lefts[1][1], totals, more, spot]
+    return call(
+        functools.partial(back_sum_kernel, consts[:2]),
+        "back_sum",
+        where,
+        args,
+        specs,
+        (
+            jax.ShapeDtypeStruct((rows + 8, spots), F32),
+            jax.ShapeDtypeStruct((2 * genes, spots), BF),
+            jax.ShapeDtypeStruct((2 * genes, spots), BF),
+            jax.ShapeDtypeStruct((8, 128), F32),
+        ),
+        (by_tile(rows + 8, tile), by_tile(2 * genes, tile), by_tile(2 * genes, tile), fixed_out((8, 128))),
+        (spots // tile,),
+        [pltpu.VMEM((2, 2 * genes, 128), F32)],
+    )
+
+
+def back_end_kernel(sizes, where, *refs):
+    scale, (gene_loss, spot_loss, cents, spots_all) = sizes
+    high_refs, low_refs = refs[0:2], refs[2:4]
+    bhigh, blow, sum_ref, z_ref, dens_ref, sent_ref, got_ref, logit_ref, w_ref, out_ref, loss_ref = refs[4:]
+    rows, genes = high_refs[0].shape
+    value = back_dots(high_refs, low_refs, bhigh, blow, genes)
     inv, raw = z_ref[0:1, :], z_ref[1:2, :]
-    dens = totals_ref[3:4, 0:1]
-    mass = totals_ref[4:5, 0:1]
+    dens, mass = sum_ref[0:1, 0:1], sum_ref[1:2, 0:1]
     grad_raw = scale * (1.0 / mass - dens_ref[...] / (dens * raw))
     column = sent_ref[0:1, :] + got_ref[rows : rows + 1, :] + raw * grad_raw
     value = value + got_ref[0:rows, :] + w_ref[...] * grad_raw
@@ -435,57 +462,33 @@
 
     @pl.when(pl.program_id(0) == 0)
     def _():
-        gene_loss, spot_loss, cents, spots_all = loss_scale
-        gene = (sent_ref[1:2, 0:128] + got_ref[rows + 1 : rows + 2, 0:128]) * gene_loss
-        cos = totals_ref[6:7, 0:128] * spot_loss
-        kl = (
-            totals_ref[5:6, 0:128] / totals_ref[3:4, 0:128]
-            + jnp.log(totals_ref[4:5, 0:128] * (cents / spots_all))
-            - jnp.log(totals_ref[3:4, 0:128] * (1.0 / spots_all))
-        )
-        lane = lax.broadcasted_iota(jnp.int32, (1, 128), 1)
-        loss_ref[...] = jnp.where(lane == 0, gene, jnp.where(lane == 1, cos, kl))
-
-
-def back(where, preds, xs, lefts, totals, spot, zinfo, density, consts, rows, final, tile):
-    genes, spots = preds[0].shape
-    left = pl.BlockSpec(
-        (rows, genes), lambda i, ix: (0 if final is None else 1, 0), pipeline_mode=pl.Buffered(1)
-    )
-    specs = [by_tile(genes, tile)] * 2 + [by_tile(genes // XS, tile)] * (2 * XS) + [left] * 4
-    specs += [fixed((8, 2 * genes)), by_tile(16, tile), by_tile(8, tile), by_tile(1, tile)]
-    args = [*preds, *xs, lefts[0][0], lefts[1][0], lefts[0][1], lefts[1][1]]
-    args += [totals, spot, zinfo, density]
-    if final is None:
-        shapes = jax.ShapeDtypeStruct((rows + 8, spots), F32)
-        outs = by_tile(rows + 8, tile)
-    else:
-        args += final
-        specs += [
-            by_tile(8, tile, rows // 8),
-            by_tile(rows + 8, tile),
-            pl.BlockSpec((rows, tile), lambda i, ix: (ix[0], i)),
-            pl.BlockSpec((rows, 1), lambda i, ix: (ix[0], 0)),
-        ]
-        shapes = (
-            jax.ShapeDtypeStruct((rows, spots), F32),
-            jax.ShapeDtypeStruct((1, 128), F32),
-        )
-        outs = (by_tile(rows, tile), fixed_out((1, 128)))
+        dens, mass, log_sum, cos = (sum_ref[k : k + 1] for k in range(4))
+        gene = (sum_ref[4:5] + got_ref[rows + 1 : rows + 2, 0:128]) * gene_loss
+        kl = log_sum / dens + jnp.log(mass * (cents / spots_all)) - jnp.log(dens * (1.0 / spots_all))
+        for number, term in enumerate((gene, cos * spot_loss, kl)):
+            loss_ref[number] = term[0, 0]
+
+
+def back_end(where, highs, lefts, sums, zinfo, density, sent, got, logits, weights, consts, rows, tile):
+    twice, spots = highs[0].shape
+    left = pl.BlockSpec((rows, twice // 2), lambda i, ix: (1, 0), pipeline_mode=pl.Buffered(1))
+    specs = [left] * 4 + [by_tile(twice, tile)] * 2
+    specs += [fixed((8, 128)), by_tile(8, tile), by_tile(1, tile), by_tile(8, tile, rows // 8), by_tile(rows + 8, tile)]
+    specs += [
+        pl.BlockSpec((rows, tile), lambda i, ix: (ix[0], i)),
+        pl.BlockSpec((rows, 1), lambda i, ix: (ix[0], 0)),
+    ]
+    args = [lefts[0][0], lefts[1][0], lefts[0][1], lefts[1][1], *highs]
+    args += [sums, zinfo, density, sent, got, logits, weights]
     return call(
-        functools.partial(back_kernel, final is not None, consts),
-        "back_sum" if final is None else "back_end",
+        functools.partial(back_end_kernel, consts[2:]),
+        "back_end",
         where,
         args,
         specs,
-        shapes,
-        outs,
+        (jax.ShapeDtypeStruct((rows, spots), F32), jax.ShapeDtypeStruct((3,), F32)),
+        (by_tile(rows, tile), pl.BlockSpec(memory_space=pltpu.SMEM)),
         (spots // tile,),
-        [
-            pltpu.VMEM((2 * genes, tile), BF),
-            pltpu.VMEM((2 * genes, tile), BF),
-            pltpu.VMEM((2, 2 * genes, 128), F32),
-        ],
     )
 
 
@@ -537,28 +540,26 @@
     )
     if ring:
         hop = lambda block, bit: swap(block, "spot", bit)
+        send = lambda one, *others: swap(after(one, *others), "gene", 2)
         keys = [functools.partial(lambda k, ix: ix[2] ^ k, k) for k in range(n_spot)]
-        o1, o2, o3, oy = hop(mine, 2), hop(mine, 4), hop(mine, 6), hop(mine, 1)
+        o1, o2, oy = [hop(mine, bit) for bit in (2, 4, 1)]
         x_own = turn(where, pick, spatial, tile)
-        o1, oy, theirs, logits, *x_own = tie(o1, oy, theirs, logits, *x_own)
-        o1y, ty = hop(o1, 1), hop(theirs, 1)
-        x_got = [swap(x_own[0], "gene", 2)]
+        logits, *x_own = tie(logits, *x_own)
         e_high, e_low, zinfo = exp_parts(where, logits, weights, dens_row, tile)
-        mine, o1y, e_high = tie(mine, o1y, e_high)
-        acc = fwd("own_early", keys[:4], [mine, oy, o1, o1y], None, None, None)
-        acc, o2, ty, theirs = tie(acc, o2, ty, theirs)
-        o2y, t1, t2 = hop(o2, 1), hop(theirs, 2), hop(theirs, 4)
-        theirs, ty, acc, o3 = tie(theirs, ty, acc, o3)
-        o3y = hop(o3, 1)
-        acc_other = fwd("other_early", keys[:2], [theirs, ty], None, None, None)
-        acc, acc_other, o2y, o3y, x_got[0], t1, theirs = tie(acc, acc_other, o2y, o3y, x_got[0], t1, theirs)
-        t1y, t3 = hop(t1, 1), hop(theirs, 6)
-        pred_own, info = fwd("own_late", keys[4:], [o2, o2y, o3, o3y], acc, zinfo, x_own)
+        o1, oy, o2, theirs, e_high, *x_own = tie(o1, oy, o2, theirs, e_high, *x_own)
+        o2y, o3, o1y = hop(o2, 1), hop(o2, 2), hop(oy, 2)
+        x0, t2 = send(x_own[0]), hop(theirs, 4)
+        acc = fwd("own_early", keys[:3] + keys[4:5], [mine, oy, o1, o2], None, None, None)
+        acc, o2y, o3, theirs = tie(acc, o2y, o3, theirs)
+        o3y, ty = hop(o3, 1), hop(theirs, 1)
+        acc, o3y, o1y, theirs = tie(acc, o3y, o1y, theirs)
+        t1 = hop(theirs, 2)
+        pred_own, info = fwd("own_late", keys[3:4] + keys[5:], [o1y, o2y, o3, o3y], acc, zinfo, x_own)
         own = [mine, oy, o1, o1y, o2, o2y, o3, o3y]
         own_pick = lambda ix, block: [(block ^ ix[2]) == key for key in range(n_spot)]
     else:
         x_own = turn(where, pick, spatial, tile)
-        x_got = [swap(x_own[0], "gene", 2)]
+        x_got = [swap(one, "gene", 2) for one in x_own]
         e_high, e_low, zinfo = exp_parts(where, logits, weights, dens_row, tile)
         own = [lax.all_gather(mine, "spot", axis=1, tiled=True)]
         other = [lax.all_gather(theirs, "spot", axis=1, tiled=True)]
@@ -567,41 +568,53 @@
         own_pick = None
 
     info_x = swap(info, "gene", 2)
+    if ring:
+        pred_own, t2, x0, ty, mine = tie(pred_own, t2, x0, ty, mine)
+        own[0] = mine
+        t3, t2y = hop(t2, 2), hop(t2, 1)
     left_own = rows_left(where, own, rows, own_pick)
     if ring:
-        t2, t3, info_x, left_own = tie(t2, t3, info_x, left_own)
-    else:
-        info_x, left_own = tie(info_x, left_own)
+        info_x, left_own, t1, held = tie(info_x, left_own, t1, x_own[1])
+        x1 = send(held)
     half = info + info_x
     totals, spot = pack(half, swap(half, "gene", 1), info, info_x, zinfo, genes)
-    x_got += [swap(after(one, info_x), "gene", 2) for one in x_own[1:]]
     if ring:
-        t2, t1y, totals, acc_other = tie(t2, t1y, totals, acc_other)
-        t2y = hop(t2, 1)
+        totals, t1, t2y = tie(totals, t1, t2y)
+        t1y, t3y = hop(t1, 1), hop(t2y, 2)
         got = swap(totals, "spot", 1)
-        acc_other = fwd("other_mid", [keys[2], keys[3], keys[4]], [t1, t1y, t2], acc_other, None, None)
-        t3, acc_other, got = tie(t3, acc_other, got)
+        acc_other = fwd(
+            "other_mid", [keys[k] for k in (0, 1, 2, 4, 5)], [theirs, ty, t1, t2, t2y], None, None, None
+        )
+        acc_other, got, t1y, t3, t3y = tie(acc_other, got, t1y, t3, t3y)
         totals = totals + got
-        t3y = hop(t3, 1)
-        for bit in (2, 4):
-            totals = totals + swap(totals, "spot", bit)
-        acc_other, totals, t2y = tie(acc_other, totals, t2y)
-        pred_other = fwd("other_late", keys[5:], [t2y, t3, t3y], acc_other, zinfo, None)
+        got = swap(totals, "spot", 2)
         other = [theirs, ty, t1, t1y, t2, t2y, t3, t3y]
+        left_other = rows_left(where, other, rows, own_pick)
+        left_other, got = tie(left_other, got)
+        totals = totals + got
+        got = swap(totals, "spot", 4)
+        acc_other, _ = tie(acc_other, left_other)
+        pred_other = fwd("other_late", [keys[k] for k in (3, 6, 7)], [t1y, t3, t3y], acc_other, zinfo, None)
+        pred_other, got = tie(pred_other, got)
+        more = got
+        x_got = [x0, x1]
     else:
         totals = lax.psum(totals, "spot")
+        more = jnp.zeros_like(totals)
         pred_other = fwd("other_late", first, other, None, zinfo, None)
-    left_other = rows_left(where, other, rows, own_pick)
-
-    common = (
-        (pred_own, pred_other), (*x_own, *x_got), (left_own, left_other), totals, spot, zinfo, dens_row, consts, rows,
-    )
-    sent = back(where, *common, None, tile)
+        left_other = rows_left(where, other, rows, own_pick)
+
+    lefts = (left_own, left_other)
+    sent, *highs, sums = back_sum(
+        where, (pred_own, pred_other), (*x_own, *x_got), lefts, totals, more, spot, consts, rows, tile
+    )
     got = swap(sent, "gene", 1)
     predicted = emit(where, after(pred_own, sent), pick, tile)
     predicted, got = tie(predicted, got)
-    grad, loss = back(where, *common, [sent, got, logits, weights], tile)
-    return loss[0, 0:3], predicted, grad
+    grad, loss = back_end(
+        where, highs, lefts, sums, zinfo, dens_row, sent, got, logits, weights, consts, rows, tile
+    )
+    return loss, predicted, grad
 
 
 def solution(mesh):

time: 210 us -> 182 us (0.87)
  starting transfers between devices: 53.1 us -> 27.9 us
  Pallas kernels: 125 us -> 118 us
  waiting for transfers between devices: 16.8 us -> 20 us
    ppermute x23, starting transfers between devices: 53.1 us -> 27.9 us  [swap(): lax.ppermute(value, axis, [(i, i ^ bit) for i in range(lax.axis_size(axis...]
    pallas_call x12 -> x11, Pallas kernels: 123 us -> 117 us  [call(): pl.pallas_call(kernel, out_shape=out_shape, grid_spec=pltpu.PrefetchScala...]
    ppermute x23, waiting for transfers between devices: 16.8 us -> 20 us  [swap(): lax.ppermute(value, axis, [(i, i ^ bit) for i in range(lax.axis_size(axis...]
  transfers between devices with their start and end apart: 23 -> 23, of which waited for: 10 -> 4; matrix products, arithmetic and copies ran while one was open for 4% -> 5% of each run, Pallas kernels for 45% -> 49%
where the time goes in v3:
time: 182 us; the launch traced here: 180 us
  Pallas kernels  118 us (65%)
  starting transfers between devices  27.9 us (15%)
  waiting for transfers between devices  20 us (11%)
  other arithmetic  8.69 us (5%)
  matrix products  2.52 us (1%)
  local copies, waits for them, and re-layouts  2.07 us (1%)
    pallas_call x11, Pallas kernels, call(): pl.pallas_call(kernel, out_shape=out_shape, grid_spec=pltpu.PrefetchScala...  117 us
    ppermute x23, starting transfers between devices, swap(): lax.ppermute(value, axis, [(i, i ^ bit) for i in range(lax.axis_size(axis...  27.9 us
    ppermute x23, waiting for transfers between devices, swap(): lax.ppermute(value, axis, [(i, i ^ bit) for i in range(lax.axis_size(axis...  20 us
  transfers between devices with their start and end apart: 23, of which 4 were waited for; matrix products, arithmetic and copies ran while one was open for 5% of the time, Pallas kernels for 49%

profile of v3, /device:TPU:1, one launch (start us, length us, event | category | flops | bytes accessed | tf_op | source)
XLA Modules:
  0.0 180.4 jit_solution(6392642911894183112)
XLA Ops:
  1.3 2.5 %fusion.1.refs_0_ = f32[512,256]{1,0:T(8,128)} fusion(f32[256,512]{1,0:T(8,128)} %param.7, s32[512]{0:T(512)S(1)} %broadcast_subtract_fusion), kind=kOutput, calls=%fused_computation.2 | convolution fusion | flops 805568512 | bytes 1050624 | tf_op jit(solution)/shard_map/dot_general | solution.py:530
  3.8 2.1 %collective-permute-start = (f32[512,256]{1,0:T(8,128)}, f32[512,256]{1,0:T(8,128)}, u32[]{:S(2)}, u32[]{:S(2)}) collective-permute-start(f32[512,256]{1,0:T(8,128)} %fusion.1.refs_0_), channel_id=1, source_target_pairs={{0,8},{4,12},{8,0},{12,4},{16,24},{20,28},{24,16},{28,20},{1,9},{5... | collective-permute-start | bytes 1572872 | tf_op jit(solution)/shard_map/ppermute | solution.py:496
  6.0 1.2 collective-permute-start.1
  7.2 2.3 %collective-permute-start.2 = (f32[512,256]{1,0:T(8,128)}, f32[512,256]{1,0:T(8,128)}, u32[]{:S(2)}, u32[]{:S(2)}) collective-permute-start(f32[512,256]{1,0:T(8,128)} %fusion.1.refs_0_), channel_id=1, source_target_pairs={{0,16},{4,20},{8,24},{12,28},{16,0},{20,4},{24,8},{28,12},{1,17},{... | collective-permute-start | bytes 1572872 | tf_op jit(solution)/shard_map/ppermute | solution.py:496
  12.3 6.8 %turn.1 = (f32[256,2048]{1,0:T(8,128)}, f32[256,2048]{1,0:T(8,128)}) custom-call(s32[3]{0:T(128)} %pad_add_fusion.where, bf16[512,512]{1,0:T(8,128)(2,1)} %fusion.pick_ref, f32[2048,512]{1,0:T(8,128)} %x_ref.1), custom_call_target="tpu_custom_call" | custom-call | flops 1000 | bytes 1000 | tf_op jit(solution)/shard_map/turn/pallas_call | solution.py:31
  19.2 1.3 convert_reduce_fusion
  20.5 1.3 convert_divide_fusion
  21.8 1.4 copy.11.w_ref.refs_12_
  23.2 14.4 %exp_parts.1 = (bf16[2048,2048]{1,0:T(8,128)(2,1)}, bf16[2048,2048]{1,0:T(8,128)(2,1)}, f32[8,2048]{1,0:T(8,128)}) custom-call(s32[3]{0:T(128)} %pad_add_fusion.where, f32[2048,2048]{1,0:T(8,128)} %refs_11_, f32[2048,1]{1,0:T(8,128)} %copy.11.w_ref.refs_12_, f32[1,2048]{1,0:T(1,128)} %bitcast.6), custom_call_target="tpu_custom_call" | custom-call | flops 1000 | bytes 1000 | tf_op jit(solution)/shard_map/exp_parts/pallas_call | solution.py:31
  38.4 1.3 collective-permute-start.7
  39.7 12.1 %own_early.1.refs_12_ = f32[512,2048]{1,0:T(8,128)} custom-call(s32[3]{0:T(128)} %pad_add_fusion.where, f32[512,256]{1,0:T(8,128)} %fusion.1.refs_0_, f32[512,256]{1,0:T(8,128)} %collective-permute-done.1.refs_1_, f32[512,256]{1,0:T(8,128)} %collective-permute-done.refs_2_, f32[512,256]{1,0:T(8,128)} %collective-permute-done.2.refs_3_.refs_4_, ...), custom_call_target="tpu_custom_call" | custom-call | flops 1000 | bytes 1000 | tf_op jit(solution)/shard_map/own_early/pallas_call | solution.py:31
  51.8 1.3 collective-permute-start.6
  53.4 14.0 %collective-permute-done.7.refs_0_.refs_3_ = f32[512,256]{1,0:T(8,128)} collective-permute-done((f32[512,256]{1,0:T(8,128)}, f32[512,256]{1,0:T(8,128)}, u32[]{:S(2)}, u32[]{:S(2)}) %collective-permute-start.7) | collective-permute-done | bytes 524320 | tf_op jit(solution)/shard_map/ppermute | solution.py:496
  67.4 14.3 %own_late.1 = (f32[512,2048]{1,0:T(8,128)}, f32[16,2048]{1,0:T(8,128)}) custom-call(s32[3]{0:T(128)} %pad_add_fusion.where, f32[512,256]{1,0:T(8,128)} %collective-permute-done.7.refs_0_.refs_3_, f32[512,256]{1,0:T(8,128)} %collective-permute-done.4.refs_1_.refs_5_, ...), custom_call_target="tpu_custom_call", output_to_operand_aliasing={{0}: (13, {})} | custom-call | flops 1000 | bytes 1000 | tf_op jit(solution)/shard_map/own_late/pallas_call | solution.py:31
  81.7 1.3 collective-permute-start.8
  83.4 3.9 %rows_left.2 = (bf16[1024,512]{1,0:T(8,128)(2,1)}, bf16[1024,512]{1,0:T(8,128)(2,1)}) custom-call(s32[3]{0:T(128)} %pad_add_fusion.where, f32[512,256]{1,0:T(8,128)} %fusion.1.refs_0_, f32[512,256]{1,0:T(8,128)} %collective-permute-done.1.refs_1_, f32[512,256]{1,0:T(8,128)} %collective-permute-done.refs_2_, ...), custom_call_target="tpu_custom_call" | custom-call | flops 1000 | bytes 1000 | tf_op jit(solution)/shard_map/rows_left/pallas_call | solution.py:31
  87.7 1.9 %collective-permute-start.14 = (f32[512,256]{1,0:T(8,128)}, f32[512,256]{1,0:T(8,128)}, u32[]{:S(2)}, u32[]{:S(2)}) collective-permute-start(f32[512,256]{1,0:T(8,128)} %collective-permute-done.9.refs_3_.refs_4_), channel_id=1, source_target_pairs={{0,4},{4,0},{8,12},{12,8},{16,20},{20,16},{24,28},{28,24},{1,5},{5... | collective-permute-start | bytes 1572872 | tf_op jit(solution)/shard_map/ppermute | solution.py:496
  91.2 5.7 %collective-permute-start.13 = (f32[16,2048]{1,0:T(8,128)S(1)}, f32[16,2048]{1,0:T(8,128)}, u32[]{:S(2)}, u32[]{:S(2)}) collective-permute-start(f32[16,2048]{1,0:T(8,128)S(1)} %add.9.half_ref), channel_id=1, source_target_pairs={{0,1},{1,0},{2,3},{3,2},{4,5},{5,4},{6,7},{7,6},{8,9},{9,8},{10,11... | collective-permute-start | bytes 393224 | tf_op jit(solution)/shard_map/ppermute | solution.py:496
  96.9 2.0 %collective-permute-start.17 = (f32[512,256]{1,0:T(8,128)}, f32[512,256]{1,0:T(8,128)}, u32[]{:S(2)}, u32[]{:S(2)}) collective-permute-start(f32[512,256]{1,0:T(8,128)} %collective-permute-done.9.refs_3_.refs_4_), channel_id=1, source_target_pairs={{0,8},{4,12},{8,0},{12,4},{16,24},{20,28},{24,16},{28,20},{1,9},{5... | collective-permute-start | bytes 1572872 | tf_op jit(solution)/shard_map/ppermute | solution.py:496
  98.8 1.8 %pack.1 = (f32[8,1024]{1,0:T(8,128)}, f32[16,2048]{1,0:T(8,128)}) custom-call(f32[16,2048]{1,0:T(8,128)} %copy-done, f32[16,2048]{1,0:T(8,128)} %collective-permute-done.13.core_ref, f32[16,2048]{1,0:T(8,128)} %get-tuple-element.89.mine_ref, f32[16,2048]{1,0:T(8,128)} %collective-permute-done.8.theirs_ref, ...), custom_call_target="tpu_custom_call" | custom-call | flops 1000 | bytes 1000 | tf_op jit(solution)/shard_map/pack/pallas_call | solution.py:313
  101.9 1.4 collective-permute-start.15
  103.3 14.0 %other_mid.1.refs_9_ = f32[512,2048]{1,0:T(8,128)} custom-call(s32[3]{0:T(128)} %pad_add_fusion.where, f32[512,256]{1,0:T(8,128)} %collective-permute-done.3.refs_0_, f32[512,256]{1,0:T(8,128)} %collective-permute-done.11.refs_1_, f32[512,256]{1,0:T(8,128)} %collective-permute-done.12.refs_2_, f32[512,256]{1,0:T(8,128)} %collective-permute-done.9.refs_3_.refs_4_, ...), custom_call_target="tpu_custom_call" | custom-call | flops 1000 | bytes 1000 | tf_op jit(solution)/shard_map/other_mid/pallas_call | solution.py:31
  117.3 5.4 %collective-permute-done.18.refs_7_.refs_2_ = f32[512,256]{1,0:T(8,128)} collective-permute-done((f32[512,256]{1,0:T(8,128)}, f32[512,256]{1,0:T(8,128)}, u32[]{:S(2)}, u32[]{:S(2)}) %collective-permute-start.18) | collective-permute-done | bytes 524320 | tf_op jit(solution)/shard_map/ppermute | solution.py:496
  122.7 1.4 add.10
  124.1 1.3 collective-permute-start.19
  125.3 3.9 %rows_left.3 = (bf16[1024,512]{1,0:T(8,128)(2,1)}, bf16[1024,512]{1,0:T(8,128)(2,1)}) custom-call(s32[3]{0:T(128)} %pad_add_fusion.where, f32[512,256]{1,0:T(8,128)} %collective-permute-done.3.refs_0_, f32[512,256]{1,0:T(8,128)} %collective-permute-done.11.refs_1_, f32[512,256]{1,0:T(8,128)} %collective-permute-done.12.refs_2_, ...), custom_call_target="tpu_custom_call" | custom-call | flops 1000 | bytes 1000 | tf_op jit(solution)/shard_map/rows_left/pallas_call | solution.py:31
  129.2 1.4 add.11.refs_10_
  131.8 10.9 %other_late.1.refs_1_ = f32[512,2048]{1,0:T(8,128)} custom-call(s32[3]{0:T(128)} %pad_add_fusion.where, f32[512,256]{1,0:T(8,128)} %collective-permute-done.16.refs_3_.refs_0_, f32[512,256]{1,0:T(8,128)} %collective-permute-done.17.refs_6_.refs_1_, f32[512,256]{1,0:T(8,128)} %collective-permute-done.18.refs_7_.refs_2_, ...), custom_call_target="tpu_custom_call", output_to_operand_aliasing={{}: (10, {})} | custom-call | flops 1000 | bytes 1000 | tf_op jit(solution)/shard_map/other_late/pallas_call | solution.py:31
  142.7 15.5 %back_sum.1 = (f32[520,2048]{1,0:T(8,128)}, bf16[1024,2048]{1,0:T(8,128)(2,1)}, bf16[1024,2048]{1,0:T(8,128)(2,1)}, f32[8,128]{1,0:T(8,128)}) custom-call(s32[3]{0:T(128)} %pad_add_fusion.where, f32[512,2048]{1,0:T(8,128)} %get-tuple-element.126.refs_0_.pred_ref, f32[512,2048]{1,0:T(8,128)} %other_late.1.refs_1_, ...), custom_call_target="tpu_custom_call" | custom-call | flops 1000 | bytes 1000 | tf_op jit(solution)/shard_map/back_sum/pallas_call | solution.py:31
  158.2 1.3 collective-permute-start.22
  159.5 7.0 %emit.1 = f32[2048,512]{1,0:T(8,128)} custom-call(s32[3]{0:T(128)} %pad_add_fusion.where, f32[512,2048]{1,0:T(8,128)} %get-tuple-element.126.refs_0_.pred_ref, bf16[512,512]{1,0:T(8,128)(2,1)} %fusion.pick_ref), custom_call_target="tpu_custom_call" | custom-call | flops 1000 | bytes 1000 | tf_op jit(solution)/shard_map/emit/pallas_call | solution.py:31
  166.7 13.7 %back_end.1 = (f32[512,2048]{1,0:T(8,128)}, f32[3]{0:T(128)}) custom-call(s32[3]{0:T(128)} %pad_add_fusion.where, bf16[1024,512]{1,0:T(8,128)(2,1)} %get-tuple-element.95.refs_6_.refs_0_, bf16[1024,512]{1,0:T(8,128)(2,1)} %get-tuple-element.110.refs_7_.refs_1_, bf16[1024,512]{1,0:T(8,128)(2,1)} %get-tuple-element.111.refs_8_.refs_2_, ...), custom_call_target="tpu_custom_call" | custom-call | flops 1000 | bytes 1000 | tf_op jit(solution)/shard_map/back_end/pallas_call | solution.py:31
  (38 shorter events, 9.5 us)
Async XLA Ops:
  3.8 33.8 %collective-permute-start = (f32[512,256]{1,0:T(8,128)}, f32[512,256]{1,0:T(8,128)}, u32[]{:S(2)}, u32[]{:S(2)}) collective-permute-start(f32[512,256]{1,0:T(8,128)} %fusion.1.refs_0_), channel_id=1, source_target_pairs={{0,8},{4,12},{8,0},{12,4},{16,24},{20,28},{24,16},{28,20},{1,9},{5... | collective-permute-start | bytes 1572872 | tf_op jit(solution)/shard_map/ppermute | solution.py:496
  6.0 31.7 %collective-permute-start.1 = (f32[512,256]{1,0:T(8,128)}, f32[512,256]{1,0:T(8,128)}, u32[]{:S(2)}, u32[]{:S(2)}) collective-permute-start(f32[512,256]{1,0:T(8,128)} %fusion.1.refs_0_), channel_id=1, source_target_pairs={{0,4},{4,0},{8,12},{12,8},{16,20},{20,16},{24,28},{28,24},{1,5},{5... | collective-permute-start | bytes 1572872 | tf_op jit(solution)/shard_map/ppermute | solution.py:496
  7.2 30.4 %collective-permute-start.2 = (f32[512,256]{1,0:T(8,128)}, f32[512,256]{1,0:T(8,128)}, u32[]{:S(2)}, u32[]{:S(2)}) collective-permute-start(f32[512,256]{1,0:T(8,128)} %fusion.1.refs_0_), channel_id=1, source_target_pairs={{0,16},{4,20},{8,24},{12,28},{16,0},{20,4},{24,8},{28,12},{1,17},{... | collective-permute-start | bytes 1572872 | tf_op jit(solution)/shard_map/ppermute | solution.py:496
  9.5 28.1 %collective-permute-start.3 = (f32[512,256]{1,0:T(8,128)}, f32[512,256]{1,0:T(8,128)}, u32[]{:S(2)}, u32[]{:S(2)}) collective-permute-start(f32[512,256]{1,0:T(8,128)} %fusion.1.refs_0_), channel_id=1, source_target_pairs={{0,2},{1,3},{2,0},{3,1},{4,6},{5,7},{6,4},{7,5},{8,10},{9,11},{10,... | collective-permute-start | bytes 1572872 | tf_op jit(solution)/shard_map/ppermute | solution.py:496
  37.7 45.7 %collective-permute-start.10 = (f32[256,2048]{1,0:T(8,128)}, f32[256,2048]{1,0:T(8,128)}, u32[]{:S(2)}, u32[]{:S(2)}) collective-permute-start(f32[256,2048]{1,0:T(8,128)} %get-tuple-element.87.refs_14_.refs_2_), channel_id=1, source_target_pairs={{0,2},{1,3},{2,0},{3,1},{4,6},{5,7},{6,4},{7,5},{8,10},{9,11},{10,... | collective-permute-start | bytes 6291464 | tf_op jit(solution)/shard_map/ppermute | solution.py:496
  38.0 13.8 %collective-permute-start.4 = (f32[512,256]{1,0:T(8,128)}, f32[512,256]{1,0:T(8,128)}, u32[]{:S(2)}, u32[]{:S(2)}) collective-permute-start(f32[512,256]{1,0:T(8,128)} %collective-permute-done.2.refs_3_.refs_4_), channel_id=1, source_target_pairs={{0,4},{4,0},{8,12},{12,8},{16,20},{20,16},{24,28},{28,24},{1,5},{5... | collective-permute-start | bytes 1572872 | tf_op jit(solution)/shard_map/ppermute | solution.py:496
  38.2 13.5 %collective-permute-start.5 = (f32[512,256]{1,0:T(8,128)}, f32[512,256]{1,0:T(8,128)}, u32[]{:S(2)}, u32[]{:S(2)}) collective-permute-start(f32[512,256]{1,0:T(8,128)} %collective-permute-done.2.refs_3_.refs_4_), channel_id=1, source_target_pairs={{0,8},{4,12},{8,0},{12,4},{16,24},{20,28},{24,16},{28,20},{1,9},{5... | collective-permute-start | bytes 1572872 | tf_op jit(solution)/shard_map/ppermute | solution.py:496
  38.4 29.0 %collective-permute-start.7 = (f32[512,256]{1,0:T(8,128)}, f32[512,256]{1,0:T(8,128)}, u32[]{:S(2)}, u32[]{:S(2)}) collective-permute-start(f32[512,256]{1,0:T(8,128)} %collective-permute-done.1.refs_1_), channel_id=1, source_target_pairs={{0,8},{4,12},{8,0},{12,4},{16,24},{20,28},{24,16},{28,20},{1,9},{5... | collective-permute-start | bytes 1572872 | tf_op jit(solution)/shard_map/ppermute | solution.py:496
  51.8 15.6 %collective-permute-start.6 = (f32[512,256]{1,0:T(8,128)}, f32[512,256]{1,0:T(8,128)}, u32[]{:S(2)}, u32[]{:S(2)}) collective-permute-start(f32[512,256]{1,0:T(8,128)} %collective-permute-done.5.refs_2_.refs_6_), channel_id=1, source_target_pairs={{0,4},{4,0},{8,12},{12,8},{16,20},{20,16},{24,28},{28,24},{1,5},{5... | collective-permute-start | bytes 1572872 | tf_op jit(solution)/shard_map/ppermute | solution.py:496
  53.1 29.9 %collective-permute-start.9 = (f32[512,256]{1,0:T(8,128)}, f32[512,256]{1,0:T(8,128)}, u32[]{:S(2)}, u32[]{:S(2)}) collective-permute-start(f32[512,256]{1,0:T(8,128)} %collective-permute-done.3.refs_0_), channel_id=1, source_target_pairs={{0,16},{4,20},{8,24},{12,28},{16,0},{20,4},{24,8},{28,12},{1,17},{... | collective-permute-start | bytes 1572872 | tf_op jit(solution)/shard_map/ppermute | solution.py:496
  53.2 29.9 %collective-permute-start.11 = (f32[512,256]{1,0:T(8,128)}, f32[512,256]{1,0:T(8,128)}, u32[]{:S(2)}, u32[]{:S(2)}) collective-permute-start(f32[512,256]{1,0:T(8,128)} %collective-permute-done.3.refs_0_), channel_id=1, source_target_pairs={{0,4},{4,0},{8,12},{12,8},{16,20},{20,16},{24,28},{28,24},{1,5},{5... | collective-permute-start | bytes 1572872 | tf_op jit(solution)/shard_map/ppermute | solution.py:496
  67.4 20.0 %collective-permute-start.12 = (f32[512,256]{1,0:T(8,128)}, f32[512,256]{1,0:T(8,128)}, u32[]{:S(2)}, u32[]{:S(2)}) collective-permute-start(f32[512,256]{1,0:T(8,128)} %collective-permute-done.3.refs_0_), channel_id=1, source_target_pairs={{0,8},{4,12},{8,0},{12,4},{16,24},{20,28},{24,16},{28,20},{1,9},{5... | collective-permute-start | bytes 1572872 | tf_op jit(solution)/shard_map/ppermute | solution.py:496
  81.7 5.6 %collective-permute-start.8 = (f32[16,2048]{1,0:T(8,128)}, f32[16,2048]{1,0:T(8,128)}, u32[]{:S(2)}, u32[]{:S(2)}) collective-permute-start(f32[16,2048]{1,0:T(8,128)} %get-tuple-element.89.mine_ref), channel_id=1, source_target_pairs={{0,2},{1,3},{2,0},{3,1},{4,6},{5,7},{6,4},{7,5},{8,10},{9,11},{10,... | collective-permute-start | bytes 393224 | tf_op jit(solution)/shard_map/ppermute | solution.py:496
  87.3 55.4 %collective-permute-start.21 = (f32[256,2048]{1,0:T(8,128)}, f32[256,2048]{1,0:T(8,128)}, u32[]{:S(2)}, u32[]{:S(2)}) collective-permute-start(f32[256,2048]{1,0:T(8,128)} %get-tuple-element.119.refs_15_.refs_3_), channel_id=1, source_target_pairs={{0,2},{1,3},{2,0},{3,1},{4,6},{5,7},{6,4},{7,5},{8,10},{9,11},{10,... | collective-permute-start | bytes 6291464 | tf_op jit(solution)/shard_map/ppermute | solution.py:496
  87.7 13.0 %collective-permute-start.14 = (f32[512,256]{1,0:T(8,128)}, f32[512,256]{1,0:T(8,128)}, u32[]{:S(2)}, u32[]{:S(2)}) collective-permute-start(f32[512,256]{1,0:T(8,128)} %collective-permute-done.9.refs_3_.refs_4_), channel_id=1, source_target_pairs={{0,4},{4,0},{8,12},{12,8},{16,20},{20,16},{24,28},{28,24},{1,5},{5... | collective-permute-start | bytes 1572872 | tf_op jit(solution)/shard_map/ppermute | solution.py:496
  90.6 0.7 copy-start
  91.2 7.6 %collective-permute-start.13 = (f32[16,2048]{1,0:T(8,128)S(1)}, f32[16,2048]{1,0:T(8,128)}, u32[]{:S(2)}, u32[]{:S(2)}) collective-permute-start(f32[16,2048]{1,0:T(8,128)S(1)} %add.9.half_ref), channel_id=1, source_target_pairs={{0,1},{1,0},{2,3},{3,2},{4,5},{5,4},{6,7},{7,6},{8,9},{9,8},{10,11... | collective-permute-start | bytes 393224 | tf_op jit(solution)/shard_map/ppermute | solution.py:496
  96.9 20.4 %collective-permute-start.17 = (f32[512,256]{1,0:T(8,128)}, f32[512,256]{1,0:T(8,128)}, u32[]{:S(2)}, u32[]{:S(2)}) collective-permute-start(f32[512,256]{1,0:T(8,128)} %collective-permute-done.9.refs_3_.refs_4_), channel_id=1, source_target_pairs={{0,8},{4,12},{8,0},{12,4},{16,24},{20,28},{24,16},{28,20},{1,9},{5... | collective-permute-start | bytes 1572872 | tf_op jit(solution)/shard_map/ppermute | solution.py:496
  100.7 16.6 %collective-permute-start.16 = (f32[512,256]{1,0:T(8,128)}, f32[512,256]{1,0:T(8,128)}, u32[]{:S(2)}, u32[]{:S(2)}) collective-permute-start(f32[512,256]{1,0:T(8,128)} %collective-permute-done.12.refs_2_), channel_id=1, source_target_pairs={{0,4},{4,0},{8,12},{12,8},{16,20},{20,16},{24,28},{28,24},{1,5},{5... | collective-permute-start | bytes 1572872 | tf_op jit(solution)/shard_map/ppermute | solution.py:496
  100.7 22.0 %collective-permute-start.18 = (f32[512,256]{1,0:T(8,128)}, f32[512,256]{1,0:T(8,128)}, u32[]{:S(2)}, u32[]{:S(2)}) collective-permute-start(f32[512,256]{1,0:T(8,128)} %collective-permute-done.14.refs_4_.refs_5_), channel_id=1, source_target_pairs={{0,8},{4,12},{8,0},{12,4},{16,24},{20,28},{24,16},{28,20},{1,9},{5... | collective-permute-start | bytes 1572872 | tf_op jit(solution)/shard_map/ppermute | solution.py:496
  101.9 15.4 %collective-permute-start.15 = (f32[8,1024]{1,0:T(8,128)}, f32[8,1024]{1,0:T(8,128)}, u32[]{:S(2)}, u32[]{:S(2)}) collective-permute-start(f32[8,1024]{1,0:T(8,128)} %get-tuple-element.103), channel_id=1, source_target_pairs={{0,4},{4,0},{8,12},{12,8},{16,20},{20,16},{24,28},{28,24},{1,5},{5... | collective-permute-start | bytes 98312 | tf_op jit(solution)/shard_map/ppermute | solution.py:496
  124.1 5.1 %collective-permute-start.19 = (f32[8,1024]{1,0:T(8,128)}, f32[8,1024]{1,0:T(8,128)}, u32[]{:S(2)}, u32[]{:S(2)}) collective-permute-start(f32[8,1024]{1,0:T(8,128)} %add.10), channel_id=1, source_target_pairs={{0,8},{4,12},{8,0},{12,4},{16,24},{20,28},{24,16},{28,20},{1,9},{5... | collective-permute-start | bytes 98312 | tf_op jit(solution)/shard_map/ppermute | solution.py:496
  130.6 12.1 %collective-permute-start.20 = (f32[8,1024]{1,0:T(8,128)}, f32[8,1024]{1,0:T(8,128)}, u32[]{:S(2)}, u32[]{:S(2)}) collective-permute-start(f32[8,1024]{1,0:T(8,128)} %add.11.refs_10_), channel_id=1, source_target_pairs={{0,16},{4,20},{8,24},{12,28},{16,0},{20,4},{24,8},{28,12},{1,17},{... | collective-permute-start | bytes 98312 | tf_op jit(solution)/shard_map/ppermute | solution.py:496
  158.2 8.5 %collective-permute-start.22 = (f32[520,2048]{1,0:T(8,128)}, f32[520,2048]{1,0:T(8,128)}, u32[]{:S(2)}, u32[]{:S(2)}) collective-permute-start(f32[520,2048]{1,0:T(8,128)} %get-tuple-element.125.refs_9_), channel_id=1, source_target_pairs={{0,1},{1,0},{2,3},{3,2},{4,5},{5,4},{6,7},{7,6},{8,9},{9,8},{10,11... | collective-permute-start | bytes 12779528 | tf_op jit(solution)/shard_map/ppermute | solution.py:496

commit v4 on v3

--- a/solution.py
+++ b/solution.py
@@ -55,23 +55,36 @@
     return pl.BlockSpec((height, tile), lambda i, ix: (row, i + start))
 
 
-def exp_kernel(cents, where, l_ref, w_ref, d_ref, high_ref, low_ref, info_ref, scal):
+def exp_kernel(cents, count, first, last, where, *refs):
+    l_refs, w_refs, d_ref, refs = refs[:count], refs[count : 2 * count], refs[2 * count], refs[2 * count + 1 :]
+    if not first:
+        before_ref, refs = refs[0], refs[1:]
+    high_ref, low_ref, info_ref, scal = refs
     step = pl.program_id(0)
-    tile = l_ref.shape[1]
+    tile = d_ref.shape[1]
 
     @pl.when(step == 0)
     def _():
         scal[...] = jnp.zeros_like(scal)
 
-    total = weighted = jnp.zeros((1, tile), F32)
-    for part in range(l_ref.shape[0] // KC):
-        rows = slice(part * KC, part * KC + KC)
-        value = jnp.exp(l_ref[rows, :])
-        high, low = split(value)
-        high_ref[rows, :] = high
-        low_ref[rows, :] = low
-        total = total + jnp.sum(value, axis=0, keepdims=True)
-        weighted = weighted + jnp.sum(value * w_ref[rows, :], axis=0, keepdims=True)
+    if first:
+        total = weighted = jnp.zeros((1, tile), F32)
+    else:
+        total, weighted = before_ref[0:1, :], before_ref[1:2, :]
+    start = 0
+    for l_ref, w_ref in zip(l_refs, w_refs):
+        for part in range(l_ref.shape[0] // KC):
+            rows = slice(part * KC, part * KC + KC)
+            value = jnp.exp(l_ref[rows, :])
+            high, low = split(value)
+            high_ref[start : start + KC, :] = high
+            low_ref[start : start + KC, :] = low
+            start += KC
+            total = total + jnp.sum(value, axis=0, keepdims=True)
+            weighted = weighted + jnp.sum(value * w_ref[rows, :], axis=0, keepdims=True)
+    if not last:
+        info_ref[...] = jnp.concatenate([total, weighted, jnp.zeros((6, tile), F32)], axis=0)
+        return
     inv = 1.0 / total
     raw = weighted * inv
     dens = d_ref[...]
@@ -84,20 +97,31 @@
     info_ref[2:8, :] = sums[0:6]
 
 
-def exp_parts(where, logits, weights, density, tile):
+def exp_parts(where, keys, deep, logits, weights, density, before, last, tile):
     cents, spots = logits.shape
+    count = len(keys)
+    specs = [
+        pl.BlockSpec((deep, tile), functools.partial(lambda key, i, ix: (key(ix), i), key)) for key in keys
+    ]
+    specs += [pl.BlockSpec((deep, 1), functools.partial(lambda key, i, ix: (key(ix), 0), key)) for key in keys]
+    specs.append(by_tile(1, tile))
+    args = [*([logits] * count), *([weights] * count), density]
+    if before is not None:
+        specs.append(by_tile(8, tile))
+        args.append(before)
+    rows = deep * count
     return call(
-        functools.partial(exp_kernel, float(cents)),
+        functools.partial(exp_kernel, float(cents), count, before is None, last),
         "exp_parts",
         where,
-        [logits, weights, density],
-        [by_tile(cents, tile), fixed((cents, 1)), by_tile(1, tile)],
+        args,
+        specs,
         (
-            jax.ShapeDtypeStruct((cents, spots), BF),
-            jax.ShapeDtypeStruct((cents, spots), BF),
+            jax.ShapeDtypeStruct((rows, spots), BF),
+            jax.ShapeDtypeStruct((rows, spots), BF),
             jax.ShapeDtypeStruct((8, spots), F32),
         ),
-        (by_tile(cents, tile), by_tile(cents, tile), by_tile(8, tile)),
+        (by_tile(rows, tile), by_tile(rows, tile), by_tile(8, tile)),
         (spots // tile,),
         [pltpu.VMEM((8, tile), F32)],
     )
@@ -133,29 +157,12 @@
     return refs[batch // each][start : start + width, :]
 
 
-def load_left(groups, high, low):
+def load_left(refs, high, low):
     at = 0
-    for group in groups:
-        value = group[0][...]
-        for ref in group[1:]:
-            value = value + ref[...]
-        wide = value.shape[1]
-        high[:, at : at + wide], low[:, at : at + wide] = split(value)
+    for ref in refs:
+        wide = ref.shape[1]
+        high[:, at : at + wide], low[:, at : at + wide] = split(ref[...])
         at += wide
-
-
-def flat(blocks):
-    sizes = [len(block) if isinstance(block, tuple) else 1 for block in blocks]
-    arrays = [one for block in blocks for one in (block if isinstance(block, tuple) else (block,))]
-    return sizes, arrays
-
-
-def grouped(sizes, refs):
-    out, at = [], 0
-    for size in sizes:
-        out.append(refs[at : at + size])
-        at += size
-    return out
 
 
 def product(high, low, e_high, e_low):
@@ -164,9 +171,8 @@
     return value + dot(high[...], jnp.concatenate([ref[...] for ref in e_low], axis=0))
 
 
-def pred_kernel(sizes, first, last, stats, where, *refs):
-    count = len(sizes)
-    s_refs, refs = grouped(sizes, refs), refs[sum(sizes) :]
+def pred_kernel(blocks, count, first, last, stats, where, *refs):
+    s_refs, refs = refs[:blocks], refs[blocks:]
     h_refs, l_refs = refs[:count], refs[count : 2 * count]
     refs = refs[2 * count :]
     if not first:
@@ -218,18 +224,13 @@
             )
 
 
-def pred_part(where, keys, blocks, e_high, e_low, acc, zinfo, x, tile, name):
-    cents, spots = e_high.shape
-    sizes, blocks = flat(blocks)
+def pred_part(where, blocks, terms, acc, zinfo, x, tile, name):
+    spots = terms[0][0].shape[1]
     genes, deep = blocks[0].shape
-    count = len(sizes)
     first, last, stats = acc is None, zinfo is not None, x is not None
-    rows = [
-        pl.BlockSpec((deep, tile), functools.partial(lambda key, i, ix: (key(ix), i), key))
-        for key in keys
-    ]
-    specs = [fixed((genes, deep)) for _ in blocks] + rows + rows
-    args = [*blocks, *([e_high] * count), *([e_low] * count)]
+    specs = [fixed((genes, deep)) for _ in blocks]
+    specs += [by_tile(rows, tile, place) for _, _, rows, place in terms] * 2
+    args = [*blocks, *(term[0] for term in terms), *(term[1] for term in terms)]
     alias = {}
     if not first:
         alias = {len(args) + 1: 0}
@@ -240,7 +241,7 @@
         args.append(zinfo)
     shapes = jax.ShapeDtypeStruct((genes, spots), F32)
     outs = by_tile(genes, tile)
-    scratch = [pltpu.VMEM((genes, deep * count), BF)] * 2
+    scratch = [pltpu.VMEM((genes, deep * len(blocks)), BF)] * 2
     if stats:
         specs += [by_tile(genes // XS, tile)] * XS
         args += x
@@ -248,7 +249,7 @@
         outs = (outs, fixed_out((16, spots)))
         scratch.append(pltpu.VMEM((3, genes, 128), F32))
     return call(
-        functools.partial(pred_kernel, sizes, first, last, stats),
+        functools.partial(pred_kernel, len(blocks), len(terms), first, last, stats),
         name,
         where,
         args,
@@ -292,9 +293,9 @@
     return cos, inv, cos / left
 
 
-def pack_kernel(half_ref, core_ref, mine_ref, theirs_ref, z_ref, out_ref, spot_ref):
+def pack_kernel(mine_ref, theirs_ref, core_ref, far_ref, z_ref, out_ref, spot_ref):
     genes = out_ref.shape[1] // 2
-    totals = half_ref[...] + core_ref[...]
+    totals = (mine_ref[...] + theirs_ref[...]) + (core_ref[...] + far_ref[...])
     spot_ref[...] = totals
     cos, _, _ = cosine(totals[0:NB], totals[NB : 2 * NB], totals[2 * NB : 3 * NB])
     out_ref[...] = jnp.zeros_like(out_ref)
@@ -309,58 +310,48 @@
     )
 
 
-def pack(half, core, mine, theirs, zinfo, genes):
+def pack(mine, theirs, core, far, zinfo, genes):
     return pl.pallas_call(
         pack_kernel,
         out_shape=(
             jax.ShapeDtypeStruct((8, 2 * genes), F32),
-            jax.ShapeDtypeStruct(half.shape, F32),
+            jax.ShapeDtypeStruct(mine.shape, F32),
         ),
         compiler_params=pltpu.CompilerParams(vmem_limit_bytes=VMEM_LIMIT),
         cost_estimate=CHEAP,
         name="pack",
-    )(half, core, mine, theirs, zinfo)
-
-
-def rows_kernel(sizes, chosen, where, *refs):
-    s_refs = grouped(sizes, refs)
-    high_ref, low_ref, buffer, sem = refs[sum(sizes) :]
+    )(mine, theirs, core, far, zinfo)
+
+
+def rows_kernel(count, chosen, where, *refs):
+    s_refs, (high_ref, low_ref, buffer, sem) = refs[:count], refs[count:]
     rows = high_ref.shape[0] // 2
     pieces = rows // KC
-    deepest = max(sizes)
     for slot in range(2 * pieces):
         which = where[1 - slot // pieces]
         piece = slot % pieces
         if chosen is not None:
-            hits = chosen(where, which * pieces + piece)
-            for hit, group in zip(hits, s_refs):
+            for hit, ref in zip(chosen(where, which * pieces + piece), s_refs):
 
                 @pl.when(hit)
-                def _(group=group):
-                    for number in range(deepest):
-                        ref = group[min(number, len(group) - 1)]
-                        pltpu.make_async_copy(ref, buffer.at[slot, number], sem.at[slot, number]).start()
+                def _(ref=ref):
+                    pltpu.make_async_copy(ref, buffer.at[slot], sem.at[slot]).start()
 
         else:
             at = pl.ds(pl.multiple_of(which * rows + piece * KC, KC), KC)
-            pltpu.make_async_copy(s_refs[0][0].at[:, at], buffer.at[slot, 0], sem.at[slot, 0]).start()
+            pltpu.make_async_copy(s_refs[0].at[:, at], buffer.at[slot], sem.at[slot]).start()
     for slot in range(2 * pieces):
-        for number in range(deepest):
-            pltpu.make_async_copy(s_refs[0][0].at[:, 0:KC], buffer.at[slot, number], sem.at[slot, number]).wait()
+        pltpu.make_async_copy(s_refs[0].at[:, 0:KC], buffer.at[slot], sem.at[slot]).wait()
         at = slice(slot * KC, slot * KC + KC)
-        value = buffer[slot, 0]
-        if deepest > 1:
-            value = jnp.where(value == 0.0, buffer[slot, 1], value)
-        high_ref[at, :], low_ref[at, :] = split(value.T)
+        high_ref[at, :], low_ref[at, :] = split(buffer[slot].T)
 
 
 def rows_left(where, blocks, rows, chosen):
-    sizes, blocks = flat(blocks)
     genes = blocks[0].shape[0]
     shape = jax.ShapeDtypeStruct((2 * rows, genes), BF)
-    slots = (2 * rows // KC, max(sizes))
+    slots = 2 * rows // KC
     return call(
-        functools.partial(rows_kernel, sizes, chosen),
+        functools.partial(rows_kernel, len(blocks), chosen),
         "rows_left",
         where,
         list(blocks),
@@ -368,7 +359,7 @@
         (shape, shape),
         (fixed_out((2 * rows, genes)), fixed_out((2 * rows, genes))),
         (1,),
-        [pltpu.VMEM((*slots, genes, KC), F32), pltpu.SemaphoreType.DMA(slots)],
+        [pltpu.VMEM((slots, genes, KC), F32), pltpu.SemaphoreType.DMA((slots,))],
     )
 
 
@@ -535,73 +526,75 @@
     weights = cluster_cells.astype(F32)
     weights = (weights / jnp.sum(weights)).reshape(cents, 1)
     dens_row = density.reshape(1, spots)
-    fwd = lambda name, keys, blocks, acc, scale_by, x: pred_part(
-        where, keys, blocks, e_high, e_low, acc, scale_by, x, tile, name
+    fwd = lambda name, blocks, terms, acc, scale_by, x: pred_part(
+        where, blocks, terms, acc, scale_by, x, tile, name
     )
     if ring:
         hop = lambda block, bit: swap(block, "spot", bit)
         send = lambda one, *others: swap(after(one, *others), "gene", 2)
-        keys = [functools.partial(lambda k, ix: ix[2] ^ k, k) for k in range(n_spot)]
+        keys = lambda *order: [functools.partial(lambda k, ix: ix[2] ^ k, k) for k in order]
         o1, o2, oy = [hop(mine, bit) for bit in (2, 4, 1)]
-        x_own = turn(where, pick, spatial, tile)
+        x_own = turn(where, pick, spatial, 2 * tile)
         logits, *x_own = tie(logits, *x_own)
-        e_high, e_low, zinfo = exp_parts(where, logits, weights, dens_row, tile)
-        o1, oy, o2, theirs, e_high, *x_own = tie(o1, oy, o2, theirs, e_high, *x_own)
-        o2y, o3, o1y = hop(o2, 1), hop(o2, 2), hop(oy, 2)
-        x0, t2 = send(x_own[0]), hop(theirs, 4)
-        acc = fwd("own_early", keys[:3] + keys[4:5], [mine, oy, o1, o2], None, None, None)
-        acc, o2y, o3, theirs = tie(acc, o2y, o3, theirs)
-        o3y, ty = hop(o3, 1), hop(theirs, 1)
-        acc, o3y, o1y, theirs = tie(acc, o3y, o1y, theirs)
-        t1 = hop(theirs, 2)
-        pred_own, info = fwd("own_late", keys[3:4] + keys[5:], [o1y, o2y, o3, o3y], acc, zinfo, x_own)
+        *e_one, z_one = exp_parts(where, keys(0, 1, 2, 4), KC, logits, weights, dens_row, None, False, 2 * tile)
+        o1, oy, o2, theirs, z_one, *x_own = tie(o1, oy, o2, theirs, z_one, *x_own)
+        o2y, o3 = hop(o2, 1), hop(o2, 2)
+        x0 = send(x_own[0])
+        acc = fwd("own_early", [mine, oy, o1, o2], [(*e_one, 4 * KC, 0)], None, None, None)
+        acc, o2y, o3, oy, theirs, z_one, logits = tie(acc, o2y, o3, oy, theirs, z_one, logits)
+        o3y, o1y, ty = hop(o3, 1), hop(oy, 2), hop(theirs, 1)
+        *e_two, zinfo = exp_parts(where, keys(3, 5, 6, 7), KC, logits, weights, dens_row, z_one, True, 2 * tile)
+        acc, o3y, o1y, theirs, zinfo = tie(acc, o3y, o1y, theirs, zinfo)
+        t1, t2 = hop(theirs, 2), hop(theirs, 4)
+        pred_own, info = fwd("own_late", [o1y, o2y, o3, o3y], [(*e_two, 4 * KC, 0)], acc, zinfo, x_own)
         own = [mine, oy, o1, o1y, o2, o2y, o3, o3y]
         own_pick = lambda ix, block: [(block ^ ix[2]) == key for key in range(n_spot)]
     else:
-        x_own = turn(where, pick, spatial, tile)
+        x_own = turn(where, pick, spatial, 2 * tile)
         x_got = [swap(one, "gene", 2) for one in x_own]
-        e_high, e_low, zinfo = exp_parts(where, logits, weights, dens_row, tile)
+        *e_all, zinfo = exp_parts(where, [lambda ix: 0], cents, logits, weights, dens_row, None, True, tile)
         own = [lax.all_gather(mine, "spot", axis=1, tiled=True)]
         other = [lax.all_gather(theirs, "spot", axis=1, tiled=True)]
-        first = [lambda ix: 0]
-        pred_own, info = fwd("own_late", first, own, None, zinfo, x_own)
+        whole = [(*e_all, cents, 0)]
+        pred_own, info = fwd("own_late", own, whole, None, zinfo, x_own)
         own_pick = None
 
-    info_x = swap(info, "gene", 2)
+    infos = [swap(info, "gene", bit) for bit in (2, 1, 3)]
     if ring:
-        pred_own, t2, x0, ty, mine = tie(pred_own, t2, x0, ty, mine)
+        pred_own, t1, ty, x0, mine = tie(pred_own, t1, ty, x0, mine)
+        t1y = hop(t1, 1)
         own[0] = mine
-        t3, t2y = hop(t2, 2), hop(t2, 1)
     left_own = rows_left(where, own, rows, own_pick)
     if ring:
-        info_x, left_own, t1, held = tie(info_x, left_own, t1, x_own[1])
-        x1 = send(held)
-    half = info + info_x
-    totals, spot = pack(half, swap(half, "gene", 1), info, info_x, zinfo, genes)
+        t2, left_own, held, *infos = tie(t2, left_own, x_own[1], *infos)
+        t3, t2y, x1 = hop(t2, 2), hop(t2, 1), send(held)
+    totals, spot = pack(info, *infos, zinfo, genes)
     if ring:
-        totals, t1, t2y = tie(totals, t1, t2y)
-        t1y, t3y = hop(t1, 1), hop(t2y, 2)
         got = swap(totals, "spot", 1)
-        acc_other = fwd(
-            "other_mid", [keys[k] for k in (0, 1, 2, 4, 5)], [theirs, ty, t1, t2, t2y], None, None, None
-        )
-        acc_other, got, t1y, t3, t3y = tie(acc_other, got, t1y, t3, t3y)
+        theirs, totals = tie(theirs, totals)
+        acc_other = fwd("other_mid", [theirs, ty, t1, t2], [(*e_one, 4 * KC, 0)], None, None, None)
+        acc_other, got, t2y, t3 = tie(acc_other, got, t2y, t3)
+        t3y = hop(t2y, 2)
         totals = totals + got
         got = swap(totals, "spot", 2)
+        acc_other, totals = tie(acc_other, totals)
+        acc_other = fwd("other_more", [t2y, t3], [(*e_two, KC, 1), (*e_two, KC, 2)], acc_other, None, None)
+        t1y, t3y, acc_other = tie(t1y, t3y, acc_other)
         other = [theirs, ty, t1, t1y, t2, t2y, t3, t3y]
         left_other = rows_left(where, other, rows, own_pick)
         left_other, got = tie(left_other, got)
         totals = totals + got
         got = swap(totals, "spot", 4)
         acc_other, _ = tie(acc_other, left_other)
-        pred_other = fwd("other_late", [keys[k] for k in (3, 6, 7)], [t1y, t3, t3y], acc_other, zinfo, None)
-        pred_other, got = tie(pred_other, got)
-        more = got
+        pred_other = fwd(
+            "other_late", [t1y, t3y], [(*e_two, KC, 0), (*e_two, KC, 3)], acc_other, zinfo, None
+        )
+        pred_other, more = tie(pred_other, got)
         x_got = [x0, x1]
     else:
         totals = lax.psum(totals, "spot")
         more = jnp.zeros_like(totals)
-        pred_other = fwd("other_late", first, other, None, zinfo, None)
+        pred_other = fwd("other_late", other, whole, None, zinfo, None)
         left_other = rows_left(where, other, rows, own_pick)
 
     lefts = (left_own, left_other)
@@ -609,7 +602,7 @@
         where, (pred_own, pred_other), (*x_own, *x_got), lefts, totals, more, spot, consts, rows, tile
     )
     got = swap(sent, "gene", 1)
-    predicted = emit(where, after(pred_own, sent), pick, tile)
+    predicted = emit(where, after(pred_own, sent), pick, 2 * tile)
     predicted, got = tie(predicted, got)
     grad, loss = back_end(
         where, highs, lefts, sums, zinfo, dens_row, sent, got, logits, weights, consts, rows, tile

time: 182 us -> 174 us (0.956)
  waiting for transfers between devices: 20 us -> 5.46 us
  Pallas kernels: 118 us -> 125 us
  starting transfers between devices: 27.9 us -> 30.5 us
    ppermute x23 -> x24, waiting for transfers between devices: 20 us -> 5.46 us  [swap(): lax.ppermute(value, axis, [(i, i ^ bit) for i in range(lax.axis_size(axis...]
    pallas_call x11 -> x13, Pallas kernels: 117 us -> 123 us  [call(): pl.pallas_call(kernel, out_shape=out_shape, grid_spec=pltpu.PrefetchScala...]
    ppermute x23 -> x24, starting transfers between devices: 27.9 us -> 30.5 us  [swap(): lax.ppermute(value, axis, [(i, i ^ bit) for i in range(lax.axis_size(axis...]
  transfers between devices with their start and end apart: 23 -> 24, of which waited for: 4 -> 4; matrix products, arithmetic and copies ran while one was open for 5% -> 5% of each run, Pallas kernels for 49% -> 55%
where the time goes in v4:
time: 174 us; the launch traced here: 173 us
  Pallas kernels  125 us (72%)
  starting transfers between devices  30.5 us (18%)
  other arithmetic  7.67 us (4%)
  waiting for transfers between devices  5.46 us (3%)
  matrix products  2.55 us (1%)
    pallas_call x13, Pallas kernels, call(): pl.pallas_call(kernel, out_shape=out_shape, grid_spec=pltpu.PrefetchScala...  123 us
    ppermute x24, starting transfers between devices, swap(): lax.ppermute(value, axis, [(i, i ^ bit) for i in range(lax.axis_size(axis...  30.5 us
    ppermute x24, waiting for transfers between devices, swap(): lax.ppermute(value, axis, [(i, i ^ bit) for i in range(lax.axis_size(axis...  5.46 us
  transfers between devices with their start and end apart: 24, of which 4 were waited for; matrix products, arithmetic and copies ran while one was open for 5% of the time, Pallas kernels for 55%

profile of v4, /device:TPU:1, one launch (start us, length us, event | category | flops | bytes accessed | tf_op | source)
XLA Modules:
  0.0 172.9 jit_solution(270309163384122979)
XLA Ops:
  1.3 2.6 %fusion.1.refs_0_ = f32[512,256]{1,0:T(8,128)} fusion(f32[256,512]{1,0:T(8,128)} %param.7, s32[512]{0:T(512)S(1)} %broadcast_subtract_fusion), kind=kOutput, calls=%fused_computation.2 | convolution fusion | flops 805568512 | bytes 1050624 | tf_op jit(solution)/shard_map/dot_general | solution.py:521
  3.9 2.1 %collective-permute-start = (f32[512,256]{1,0:T(8,128)}, f32[512,256]{1,0:T(8,128)}, u32[]{:S(2)}, u32[]{:S(2)}) collective-permute-start(f32[512,256]{1,0:T(8,128)} %fusion.1.refs_0_), channel_id=1, source_target_pairs={{0,8},{4,12},{8,0},{12,4},{16,24},{20,28},{24,16},{28,20},{1,9},{5... | collective-permute-start | bytes 1572872 | tf_op jit(solution)/shard_map/ppermute | solution.py:487
  7.2 2.3 %collective-permute-start.2 = (f32[512,256]{1,0:T(8,128)}, f32[512,256]{1,0:T(8,128)}, u32[]{:S(2)}, u32[]{:S(2)}) collective-permute-start(f32[512,256]{1,0:T(8,128)} %fusion.1.refs_0_), channel_id=1, source_target_pairs={{0,16},{4,20},{8,24},{12,28},{16,0},{20,4},{24,8},{28,12},{1,17},{... | collective-permute-start | bytes 1572872 | tf_op jit(solution)/shard_map/ppermute | solution.py:487
  12.3 6.3 %turn.1 = (f32[256,2048]{1,0:T(8,128)}, f32[256,2048]{1,0:T(8,128)}) custom-call(s32[3]{0:T(128)} %pad_add_fusion.where, bf16[512,512]{1,0:T(8,128)(2,1)} %fusion.pick_ref, f32[2048,512]{1,0:T(8,128)} %x_ref.1), custom_call_target="tpu_custom_call" | custom-call | flops 1000 | bytes 1000 | tf_op jit(solution)/shard_map/turn/pallas_call | solution.py:31
  18.6 1.3 convert_reduce_fusion
  19.9 1.3 convert_divide_fusion
  21.3 1.4 copy.12.refs_4_.refs_5_.refs_6_.refs_7_.refs_12_
  22.6 8.3 %exp_parts.2 = (bf16[1024,2048]{1,0:T(8,128)(2,1)}, bf16[1024,2048]{1,0:T(8,128)(2,1)}, f32[8,2048]{1,0:T(8,128)}) custom-call(s32[3]{0:T(128)} %pad_add_fusion.where, f32[2048,2048]{1,0:T(8,128)} %refs_11_, f32[2048,2048]{1,0:T(8,128)} %refs_11_, f32[2048,2048]{1,0:T(8,128)} %refs_11_, f32[2048,2048]{1,0:T(8,128)} %refs_11_, ...), custom_call_target="tpu_custom_call" | custom-call | flops 1000 | bytes 1000 | tf_op jit(solution)/shard_map/exp_parts/pallas_call | solution.py:31
  31.6 2.3 %collective-permute-start.5 = (f32[512,256]{1,0:T(8,128)}, f32[512,256]{1,0:T(8,128)}, u32[]{:S(2)}, u32[]{:S(2)}) collective-permute-start(f32[512,256]{1,0:T(8,128)} %collective-permute-done.2.refs_3_.refs_4_), channel_id=1, source_target_pairs={{0,8},{4,12},{8,0},{12,4},{16,24},{20,28},{24,16},{28,20},{1,9},{5... | collective-permute-start | bytes 1572872 | tf_op jit(solution)/shard_map/ppermute | solution.py:487
  33.9 11.6 %own_early.1.refs_6_ = f32[512,2048]{1,0:T(8,128)} custom-call(s32[3]{0:T(128)} %pad_add_fusion.where, f32[512,256]{1,0:T(8,128)} %fusion.1.refs_0_, f32[512,256]{1,0:T(8,128)} %collective-permute-done.1.refs_1_, f32[512,256]{1,0:T(8,128)} %collective-permute-done.refs_2_, f32[512,256]{1,0:T(8,128)} %collective-permute-done.2.refs_3_.refs_4_, ...), custom_call_target="tpu_custom_call" | custom-call | flops 1000 | bytes 1000 | tf_op jit(solution)/shard_map/own_early/pallas_call | solution.py:31
  47.0 8.6 %exp_parts.3 = (bf16[1024,2048]{1,0:T(8,128)(2,1)}, bf16[1024,2048]{1,0:T(8,128)(2,1)}, f32[8,2048]{1,0:T(8,128)}) custom-call(s32[3]{0:T(128)} %pad_add_fusion.where, f32[2048,2048]{1,0:T(8,128)} %refs_11_, f32[2048,2048]{1,0:T(8,128)} %refs_11_, f32[2048,2048]{1,0:T(8,128)} %refs_11_, f32[2048,2048]{1,0:T(8,128)} %refs_11_, ...), custom_call_target="tpu_custom_call" | custom-call | flops 1000 | bytes 1000 | tf_op jit(solution)/shard_map/exp_parts/pallas_call | solution.py:31
  57.2 2.2 %collective-permute-start.8 = (f32[512,256]{1,0:T(8,128)}, f32[512,256]{1,0:T(8,128)}, u32[]{:S(2)}, u32[]{:S(2)}) collective-permute-start(f32[512,256]{1,0:T(8,128)} %collective-permute-done.3.refs_0_), channel_id=1, source_target_pairs={{0,16},{4,20},{8,24},{12,28},{16,0},{20,4},{24,8},{28,12},{1,17},{... | collective-permute-start | bytes 1572872 | tf_op jit(solution)/shard_map/ppermute | solution.py:487
  59.3 14.5 %own_late.1 = (f32[512,2048]{1,0:T(8,128)}, f32[16,2048]{1,0:T(8,128)}) custom-call(s32[3]{0:T(128)} %pad_add_fusion.where, f32[512,256]{1,0:T(8,128)} %collective-permute-done.7.refs_0_.refs_3_, f32[512,256]{1,0:T(8,128)} %collective-permute-done.4.refs_1_.refs_5_, ...), custom_call_target="tpu_custom_call", output_to_operand_aliasing={{0}: (7, {})} | custom-call | flops 1000 | bytes 1000 | tf_op jit(solution)/shard_map/own_late/pallas_call | solution.py:31
  74.2 7.0 %collective-permute-start.13 = (f32[16,2048]{1,0:T(8,128)}, f32[16,2048]{1,0:T(8,128)}, u32[]{:S(2)}, u32[]{:S(2)}) collective-permute-start(f32[16,2048]{1,0:T(8,128)} %get-tuple-element.113.mine_ref), channel_id=1, source_target_pairs={{0,1},{1,0},{2,3},{3,2},{4,5},{5,4},{6,7},{7,6},{8,9},{9,8},{10,11... | collective-permute-start | bytes 393224 | tf_op jit(solution)/shard_map/ppermute | solution.py:487
  81.2 1.7 collective-permute-start.14
  83.0 3.9 %rows_left.2 = (bf16[1024,512]{1,0:T(8,128)(2,1)}, bf16[1024,512]{1,0:T(8,128)(2,1)}) custom-call(s32[3]{0:T(128)} %pad_add_fusion.where, f32[512,256]{1,0:T(8,128)} %fusion.1.refs_0_, f32[512,256]{1,0:T(8,128)} %collective-permute-done.1.refs_1_, f32[512,256]{1,0:T(8,128)} %collective-permute-done.refs_2_, ...), custom_call_target="tpu_custom_call" | custom-call | flops 1000 | bytes 1000 | tf_op jit(solution)/shard_map/rows_left/pallas_call | solution.py:31
  86.9 1.2 collective-permute-done.14.far_ref
  89.9 1.4 collective-permute-start.18
  91.3 1.9 %pack.1 = (f32[8,1024]{1,0:T(8,128)}, f32[16,2048]{1,0:T(8,128)}) custom-call(f32[16,2048]{1,0:T(8,128)} %get-tuple-element.113.mine_ref, f32[16,2048]{1,0:T(8,128)} %collective-permute-done.12.theirs_ref, f32[16,2048]{1,0:T(8,128)} %collective-permute-done.13.core_ref, f32[16,2048]{1,0:T(8,128)} %collective-permute-done.14.far_ref, ...), custom_call_target="tpu_custom_call" | custom-call | flops 1000 | bytes 1000 | tf_op jit(solution)/shard_map/pack/pallas_call | solution.py:314
  93.4 1.2 collective-permute-start.15
  94.6 11.7 %other_mid.1.refs_6_ = f32[512,2048]{1,0:T(8,128)} custom-call(s32[3]{0:T(128)} %pad_add_fusion.where, f32[512,256]{1,0:T(8,128)} %collective-permute-done.3.refs_0_, f32[512,256]{1,0:T(8,128)} %collective-permute-done.10.refs_1_, f32[512,256]{1,0:T(8,128)} %collective-permute-done.9.refs_2_, f32[512,256]{1,0:T(8,128)} %collective-permute-done.8.refs_3_.refs_4_, ...), custom_call_target="tpu_custom_call" | custom-call | flops 1000 | bytes 1000 | tf_op jit(solution)/shard_map/other_mid/pallas_call | solution.py:31
  106.5 1.4 add.6
  107.9 1.4 collective-permute-start.20
  109.2 9.3 %other_more.1.refs_6_ = f32[512,2048]{1,0:T(8,128)} custom-call(s32[3]{0:T(128)} %pad_add_fusion.where, f32[512,256]{1,0:T(8,128)} %collective-permute-done.17.refs_0_.refs_5_, f32[512,256]{1,0:T(8,128)} %collective-permute-done.18.refs_1_.refs_6_, bf16[1024,2048]{1,0:T(8,128)(2,1)} %get-tuple-element.103.refs_4_.refs_2_.refs_3_, ...), custom_call_target="tpu_custom_call", output_to_operand_aliasing={{}: (7, {})} | custom-call | flops 1000 | bytes 1000 | tf_op jit(solution)/shard_map/other_more/pallas_call | solution.py:31
  118.5 3.9 %rows_left.3 = (bf16[1024,512]{1,0:T(8,128)(2,1)}, bf16[1024,512]{1,0:T(8,128)(2,1)}) custom-call(s32[3]{0:T(128)} %pad_add_fusion.where, f32[512,256]{1,0:T(8,128)} %collective-permute-done.3.refs_0_, f32[512,256]{1,0:T(8,128)} %collective-permute-done.10.refs_1_, f32[512,256]{1,0:T(8,128)} %collective-permute-done.9.refs_2_, ...), custom_call_target="tpu_custom_call" | custom-call | flops 1000 | bytes 1000 | tf_op jit(solution)/shard_map/rows_left/pallas_call | solution.py:31
  122.4 1.4 add.7.refs_10_
  123.8 9.2 %other_late.1.refs_1_ = f32[512,2048]{1,0:T(8,128)} custom-call(s32[3]{0:T(128)} %pad_add_fusion.where, f32[512,256]{1,0:T(8,128)} %collective-permute-done.15.refs_3_.refs_0_, f32[512,256]{1,0:T(8,128)} %collective-permute-done.19.refs_7_.refs_1_, bf16[1024,2048]{1,0:T(8,128)(2,1)} %get-tuple-element.103.refs_4_.refs_2_.refs_3_, ...), custom_call_target="tpu_custom_call", output_to_operand_aliasing={{}: (7, {})} | custom-call | flops 1000 | bytes 1000 | tf_op jit(solution)/shard_map/other_late/pallas_call | solution.py:31
  133.0 2.0 %collective-permute-done.22.refs_5_ = f32[256,2048]{1,0:T(8,128)} collective-permute-done((f32[256,2048]{1,0:T(8,128)}, f32[256,2048]{1,0:T(8,128)}, u32[]{:S(2)}, u32[]{:S(2)}) %collective-permute-start.22) | collective-permute-done | bytes 2097184 | tf_op jit(solution)/shard_map/ppermute | solution.py:487
  135.0 15.3 %back_sum.1 = (f32[520,2048]{1,0:T(8,128)}, bf16[1024,2048]{1,0:T(8,128)(2,1)}, bf16[1024,2048]{1,0:T(8,128)(2,1)}, f32[8,128]{1,0:T(8,128)}) custom-call(s32[3]{0:T(128)} %pad_add_fusion.where, f32[512,2048]{1,0:T(8,128)} %get-tuple-element.150.refs_0_.pred_ref, f32[512,2048]{1,0:T(8,128)} %other_late.1.refs_1_, ...), custom_call_target="tpu_custom_call" | custom-call | flops 1000 | bytes 1000 | tf_op jit(solution)/shard_map/back_sum/pallas_call | solution.py:31
  150.3 1.6 collective-permute-start.23
  151.9 6.3 %emit.1 = f32[2048,512]{1,0:T(8,128)} custom-call(s32[3]{0:T(128)} %pad_add_fusion.where, f32[512,2048]{1,0:T(8,128)} %get-tuple-element.150.refs_0_.pred_ref, bf16[512,512]{1,0:T(8,128)(2,1)} %fusion.pick_ref), custom_call_target="tpu_custom_call" | custom-call | flops 1000 | bytes 1000 | tf_op jit(solution)/shard_map/emit/pallas_call | solution.py:31
  159.1 13.8 %back_end.1 = (f32[512,2048]{1,0:T(8,128)}, f32[3]{0:T(128)}) custom-call(s32[3]{0:T(128)} %pad_add_fusion.where, bf16[1024,512]{1,0:T(8,128)(2,1)} %get-tuple-element.114.refs_6_.refs_0_, bf16[1024,512]{1,0:T(8,128)(2,1)} %get-tuple-element.133.refs_7_.refs_1_, bf16[1024,512]{1,0:T(8,128)(2,1)} %get-tuple-element.134.refs_8_.refs_2_, ...), custom_call_target="tpu_custom_call" | custom-call | flops 1000 | bytes 1000 | tf_op jit(solution)/shard_map/back_end/pallas_call | solution.py:31
  (39 shorter events, 11.8 us)
Async XLA Ops:
  3.9 27.1 %collective-permute-start = (f32[512,256]{1,0:T(8,128)}, f32[512,256]{1,0:T(8,128)}, u32[]{:S(2)}, u32[]{:S(2)}) collective-permute-start(f32[512,256]{1,0:T(8,128)} %fusion.1.refs_0_), channel_id=1, source_target_pairs={{0,8},{4,12},{8,0},{12,4},{16,24},{20,28},{24,16},{28,20},{1,9},{5... | collective-permute-start | bytes 1572872 | tf_op jit(solution)/shard_map/ppermute | solution.py:487
  6.0 25.0 %collective-permute-start.1 = (f32[512,256]{1,0:T(8,128)}, f32[512,256]{1,0:T(8,128)}, u32[]{:S(2)}, u32[]{:S(2)}) collective-permute-start(f32[512,256]{1,0:T(8,128)} %fusion.1.refs_0_), channel_id=1, source_target_pairs={{0,4},{4,0},{8,12},{12,8},{16,20},{20,16},{24,28},{28,24},{1,5},{5... | collective-permute-start | bytes 1572872 | tf_op jit(solution)/shard_map/ppermute | solution.py:487
  7.2 23.7 %collective-permute-start.2 = (f32[512,256]{1,0:T(8,128)}, f32[512,256]{1,0:T(8,128)}, u32[]{:S(2)}, u32[]{:S(2)}) collective-permute-start(f32[512,256]{1,0:T(8,128)} %fusion.1.refs_0_), channel_id=1, source_target_pairs={{0,16},{4,20},{8,24},{12,28},{16,0},{20,4},{24,8},{28,12},{1,17},{... | collective-permute-start | bytes 1572872 | tf_op jit(solution)/shard_map/ppermute | solution.py:487
  9.6 21.4 %collective-permute-start.3 = (f32[512,256]{1,0:T(8,128)}, f32[512,256]{1,0:T(8,128)}, u32[]{:S(2)}, u32[]{:S(2)}) collective-permute-start(f32[512,256]{1,0:T(8,128)} %fusion.1.refs_0_), channel_id=1, source_target_pairs={{0,2},{1,3},{2,0},{3,1},{4,6},{5,7},{6,4},{7,5},{8,10},{9,11},{10,... | collective-permute-start | bytes 1572872 | tf_op jit(solution)/shard_map/ppermute | solution.py:487
  31.0 52.0 %collective-permute-start.11 = (f32[256,2048]{1,0:T(8,128)}, f32[256,2048]{1,0:T(8,128)}, u32[]{:S(2)}, u32[]{:S(2)}) collective-permute-start(f32[256,2048]{1,0:T(8,128)} %get-tuple-element.107.refs_8_.refs_2_), channel_id=1, source_target_pairs={{0,2},{1,3},{2,0},{3,1},{4,6},{5,7},{6,4},{7,5},{8,10},{9,11},{10,... | collective-permute-start | bytes 6291464 | tf_op jit(solution)/shard_map/ppermute | solution.py:487
  31.3 14.2 %collective-permute-start.4 = (f32[512,256]{1,0:T(8,128)}, f32[512,256]{1,0:T(8,128)}, u32[]{:S(2)}, u32[]{:S(2)}) collective-permute-start(f32[512,256]{1,0:T(8,128)} %collective-permute-done.2.refs_3_.refs_4_), channel_id=1, source_target_pairs={{0,4},{4,0},{8,12},{12,8},{16,20},{20,16},{24,28},{28,24},{1,5},{5... | collective-permute-start | bytes 1572872 | tf_op jit(solution)/shard_map/ppermute | solution.py:487
  31.6 13.9 %collective-permute-start.5 = (f32[512,256]{1,0:T(8,128)}, f32[512,256]{1,0:T(8,128)}, u32[]{:S(2)}, u32[]{:S(2)}) collective-permute-start(f32[512,256]{1,0:T(8,128)} %collective-permute-done.2.refs_3_.refs_4_), channel_id=1, source_target_pairs={{0,8},{4,12},{8,0},{12,4},{16,24},{20,28},{24,16},{28,20},{1,9},{5... | collective-permute-start | bytes 1572872 | tf_op jit(solution)/shard_map/ppermute | solution.py:487
  45.5 11.4 %collective-permute-start.6 = (f32[512,256]{1,0:T(8,128)}, f32[512,256]{1,0:T(8,128)}, u32[]{:S(2)}, u32[]{:S(2)}) collective-permute-start(f32[512,256]{1,0:T(8,128)} %collective-permute-done.5.refs_2_.refs_6_), channel_id=1, source_target_pairs={{0,4},{4,0},{8,12},{12,8},{16,20},{20,16},{24,28},{28,24},{1,5},{5... | collective-permute-start | bytes 1572872 | tf_op jit(solution)/shard_map/ppermute | solution.py:487
  45.8 11.1 %collective-permute-start.7 = (f32[512,256]{1,0:T(8,128)}, f32[512,256]{1,0:T(8,128)}, u32[]{:S(2)}, u32[]{:S(2)}) collective-permute-start(f32[512,256]{1,0:T(8,128)} %collective-permute-done.1.refs_1_), channel_id=1, source_target_pairs={{0,8},{4,12},{8,0},{12,4},{16,24},{20,28},{24,16},{28,20},{1,9},{5... | collective-permute-start | bytes 1572872 | tf_op jit(solution)/shard_map/ppermute | solution.py:487
  46.0 28.2 %collective-permute-start.10 = (f32[512,256]{1,0:T(8,128)}, f32[512,256]{1,0:T(8,128)}, u32[]{:S(2)}, u32[]{:S(2)}) collective-permute-start(f32[512,256]{1,0:T(8,128)} %collective-permute-done.3.refs_0_), channel_id=1, source_target_pairs={{0,4},{4,0},{8,12},{12,8},{16,20},{20,16},{24,28},{28,24},{1,5},{5... | collective-permute-start | bytes 1572872 | tf_op jit(solution)/shard_map/ppermute | solution.py:487
  56.9 24.4 %collective-permute-start.9 = (f32[512,256]{1,0:T(8,128)}, f32[512,256]{1,0:T(8,128)}, u32[]{:S(2)}, u32[]{:S(2)}) collective-permute-start(f32[512,256]{1,0:T(8,128)} %collective-permute-done.3.refs_0_), channel_id=1, source_target_pairs={{0,8},{4,12},{8,0},{12,4},{16,24},{20,28},{24,16},{28,20},{1,9},{5... | collective-permute-start | bytes 1572872 | tf_op jit(solution)/shard_map/ppermute | solution.py:487
  57.2 30.9 %collective-permute-start.8 = (f32[512,256]{1,0:T(8,128)}, f32[512,256]{1,0:T(8,128)}, u32[]{:S(2)}, u32[]{:S(2)}) collective-permute-start(f32[512,256]{1,0:T(8,128)} %collective-permute-done.3.refs_0_), channel_id=1, source_target_pairs={{0,16},{4,20},{8,24},{12,28},{16,0},{20,4},{24,8},{28,12},{1,17},{... | collective-permute-start | bytes 1572872 | tf_op jit(solution)/shard_map/ppermute | solution.py:487
  73.9 13.0 %collective-permute-start.12 = (f32[16,2048]{1,0:T(8,128)}, f32[16,2048]{1,0:T(8,128)}, u32[]{:S(2)}, u32[]{:S(2)}) collective-permute-start(f32[16,2048]{1,0:T(8,128)} %get-tuple-element.113.mine_ref), channel_id=1, source_target_pairs={{0,2},{1,3},{2,0},{3,1},{4,6},{5,7},{6,4},{7,5},{8,10},{9,11},{10,... | collective-permute-start | bytes 393224 | tf_op jit(solution)/shard_map/ppermute | solution.py:487
  74.2 12.7 %collective-permute-start.13 = (f32[16,2048]{1,0:T(8,128)}, f32[16,2048]{1,0:T(8,128)}, u32[]{:S(2)}, u32[]{:S(2)}) collective-permute-start(f32[16,2048]{1,0:T(8,128)} %get-tuple-element.113.mine_ref), channel_id=1, source_target_pairs={{0,1},{1,0},{2,3},{3,2},{4,5},{5,4},{6,7},{7,6},{8,9},{9,8},{10,11... | collective-permute-start | bytes 393224 | tf_op jit(solution)/shard_map/ppermute | solution.py:487
  81.2 6.9 %collective-permute-start.14 = (f32[16,2048]{1,0:T(8,128)}, f32[16,2048]{1,0:T(8,128)}, u32[]{:S(2)}, u32[]{:S(2)}) collective-permute-start(f32[16,2048]{1,0:T(8,128)} %get-tuple-element.113.mine_ref), channel_id=1, source_target_pairs={{0,3},{1,2},{2,1},{3,0},{4,7},{5,6},{6,5},{7,4},{8,11},{9,10},{10,... | collective-permute-start | bytes 393224 | tf_op jit(solution)/shard_map/ppermute | solution.py:487
  88.1 46.8 %collective-permute-start.22 = (f32[256,2048]{1,0:T(8,128)}, f32[256,2048]{1,0:T(8,128)}, u32[]{:S(2)}, u32[]{:S(2)}) collective-permute-start(f32[256,2048]{1,0:T(8,128)} %get-tuple-element.143.refs_9_.refs_3_), channel_id=1, source_target_pairs={{0,2},{1,3},{2,0},{3,1},{4,6},{5,7},{6,4},{7,5},{8,10},{9,11},{10,... | collective-permute-start | bytes 6291464 | tf_op jit(solution)/shard_map/ppermute | solution.py:487
  88.8 17.5 %collective-permute-start.17 = (f32[512,256]{1,0:T(8,128)}, f32[512,256]{1,0:T(8,128)}, u32[]{:S(2)}, u32[]{:S(2)}) collective-permute-start(f32[512,256]{1,0:T(8,128)} %collective-permute-done.8.refs_3_.refs_4_), channel_id=1, source_target_pairs={{0,4},{4,0},{8,12},{12,8},{16,20},{20,16},{24,28},{28,24},{1,5},{5... | collective-permute-start | bytes 1572872 | tf_op jit(solution)/shard_map/ppermute | solution.py:487
  89.9 16.4 %collective-permute-start.18 = (f32[512,256]{1,0:T(8,128)}, f32[512,256]{1,0:T(8,128)}, u32[]{:S(2)}, u32[]{:S(2)}) collective-permute-start(f32[512,256]{1,0:T(8,128)} %collective-permute-done.8.refs_3_.refs_4_), channel_id=1, source_target_pairs={{0,8},{4,12},{8,0},{12,4},{16,24},{20,28},{24,16},{28,20},{1,9},{5... | collective-permute-start | bytes 1572872 | tf_op jit(solution)/shard_map/ppermute | solution.py:487
  93.1 13.2 %collective-permute-start.16 = (f32[8,1024]{1,0:T(8,128)}, f32[8,1024]{1,0:T(8,128)}, u32[]{:S(2)}, u32[]{:S(2)}) collective-permute-start(f32[8,1024]{1,0:T(8,128)} %get-tuple-element.126), channel_id=1, source_target_pairs={{0,4},{4,0},{8,12},{12,8},{16,20},{20,16},{24,28},{28,24},{1,5},{5... | collective-permute-start | bytes 98312 | tf_op jit(solution)/shard_map/ppermute | solution.py:487
  93.4 25.2 %collective-permute-start.15 = (f32[512,256]{1,0:T(8,128)}, f32[512,256]{1,0:T(8,128)}, u32[]{:S(2)}, u32[]{:S(2)}) collective-permute-start(f32[512,256]{1,0:T(8,128)} %collective-permute-done.9.refs_2_), channel_id=1, source_target_pairs={{0,4},{4,0},{8,12},{12,8},{16,20},{20,16},{24,28},{28,24},{1,5},{5... | collective-permute-start | bytes 1572872 | tf_op jit(solution)/shard_map/ppermute | solution.py:487
  106.3 12.2 %collective-permute-start.19 = (f32[512,256]{1,0:T(8,128)}, f32[512,256]{1,0:T(8,128)}, u32[]{:S(2)}, u32[]{:S(2)}) collective-permute-start(f32[512,256]{1,0:T(8,128)} %collective-permute-done.17.refs_0_.refs_5_), channel_id=1, source_target_pairs={{0,8},{4,12},{8,0},{12,4},{16,24},{20,28},{24,16},{28,20},{1,9},{5... | collective-permute-start | bytes 1572872 | tf_op jit(solution)/shard_map/ppermute | solution.py:487
  107.9 14.5 %collective-permute-start.20 = (f32[8,1024]{1,0:T(8,128)}, f32[8,1024]{1,0:T(8,128)}, u32[]{:S(2)}, u32[]{:S(2)}) collective-permute-start(f32[8,1024]{1,0:T(8,128)} %add.6), channel_id=1, source_target_pairs={{0,8},{4,12},{8,0},{12,4},{16,24},{20,28},{24,16},{28,20},{1,9},{5... | collective-permute-start | bytes 98312 | tf_op jit(solution)/shard_map/ppermute | solution.py:487
  123.8 9.2 %collective-permute-start.21 = (f32[8,1024]{1,0:T(8,128)}, f32[8,1024]{1,0:T(8,128)}, u32[]{:S(2)}, u32[]{:S(2)}) collective-permute-start(f32[8,1024]{1,0:T(8,128)} %add.7.refs_10_), channel_id=1, source_target_pairs={{0,16},{4,20},{8,24},{12,28},{16,0},{20,4},{24,8},{28,12},{1,17},{... | collective-permute-start | bytes 98312 | tf_op jit(solution)/shard_map/ppermute | solution.py:487
  150.3 8.8 %collective-permute-start.23 = (f32[520,2048]{1,0:T(8,128)}, f32[520,2048]{1,0:T(8,128)}, u32[]{:S(2)}, u32[]{:S(2)}) collective-permute-start(f32[520,2048]{1,0:T(8,128)} %get-tuple-element.149.refs_9_), channel_id=1, source_target_pairs={{0,1},{1,0},{2,3},{3,2},{4,5},{5,4},{6,7},{7,6},{8,9},{9,8},{10,11... | collective-permute-start | bytes 12779528 | tf_op jit(solution)/shard_map/ppermute | solution.py:487

commit v5 on v4

--- a/solution.py
+++ b/solution.py
@@ -7,14 +7,16 @@
 from jax.sharding import PartitionSpec as P
 
 NB = 4
-XS = 2
+XS = 3
+XCUT = (0, 2, 3, NB)
 EPS = 1e-06
 BF = jnp.bfloat16
 F32 = jnp.float32
 KC = 256
 NT = (((1,), (1,)), ((), ()))
 TN = (((0,), (0,)), ((), ()))
-VMEM_LIMIT = 67043328
+VMEM_LIMIT = 24 << 20
+LARGE_LIMIT = 60 << 20
 CHEAP = pl.CostEstimate(flops=1000, bytes_accessed=1000, transcendentals=0)
 
 
@@ -27,7 +29,7 @@
     return lax.dot_general(left, right, dims, preferred_element_type=F32)
 
 
-def call(kernel, name, where, args, specs, out_shape, out_specs, grid, scratch=(), alias=None):
+def call(kernel, name, where, args, specs, out_shape, out_specs, grid, scratch=(), alias=None, limit=VMEM_LIMIT):
     return pl.pallas_call(
         kernel,
         out_shape=out_shape,
@@ -40,11 +42,15 @@
         ),
         input_output_aliases=alias or {},
         compiler_params=pltpu.CompilerParams(
-            dimension_semantics=("arbitrary",), vmem_limit_bytes=VMEM_LIMIT
+            dimension_semantics=("arbitrary",), vmem_limit_bytes=limit
         ),
         cost_estimate=CHEAP,
         name=name,
     )(where, *args)
+
+
+def limit_of(depth):
+    return VMEM_LIMIT if depth <= 5 * KC else LARGE_LIMIT
 
 
 def fixed(shape):
@@ -124,6 +130,7 @@
         (by_tile(rows, tile), by_tile(rows, tile), by_tile(8, tile)),
         (spots // tile,),
         [pltpu.VMEM((8, tile), F32)],
+        limit=limit_of(rows),
     )
 
 
@@ -131,30 +138,34 @@
     high, low = split(x_ref[...])
     pick = pick_ref[...]
     value = dot(pick, high, NT) + dot(pick, low, NT)
-    width = out_refs[0].shape[0]
-    for batch, out_ref in enumerate(out_refs):
-        out_ref[...] = value[batch * width : (batch + 1) * width]
+    start = 0
+    for out_ref in out_refs:
+        out_ref[...] = value[start : start + out_ref.shape[0]]
+        start += out_ref.shape[0]
+
+
+def heights(genes):
+    return [(b - a) * genes // NB for a, b in zip(XCUT, XCUT[1:])]
 
 
 def turn(where, pick, x, tile):
     spots, genes = x.shape
-    width = genes // XS
     return call(
         turn_kernel,
         "turn",
         where,
         [pick, x],
         [fixed((genes, genes)), pl.BlockSpec((tile, genes), lambda i, ix: (i, 0))],
-        (jax.ShapeDtypeStruct((width, spots), F32),) * XS,
-        (by_tile(width, tile),) * XS,
+        tuple(jax.ShapeDtypeStruct((height, spots), F32) for height in heights(genes)),
+        tuple(by_tile(height, tile) for height in heights(genes)),
         (spots // tile,),
     )
 
 
 def of_batch(refs, batch, width):
-    each = NB // XS
-    start = batch % each * width
-    return refs[batch // each][start : start + width, :]
+    place = sum(batch >= cut for cut in XCUT[1:])
+    start = (batch - XCUT[place]) * width
+    return refs[place][start : start + width, :]
 
 
 def load_left(refs, high, low):
@@ -243,7 +254,7 @@
     outs = by_tile(genes, tile)
     scratch = [pltpu.VMEM((genes, deep * len(blocks)), BF)] * 2
     if stats:
-        specs += [by_tile(genes // XS, tile)] * XS
+        specs += [by_tile(height, tile) for height in heights(genes)]
         args += x
         shapes = (shapes, jax.ShapeDtypeStruct((16, spots), F32))
         outs = (outs, fixed_out((16, spots)))
@@ -259,6 +270,7 @@
         (spots // tile,),
         scratch,
         alias,
+        limit_of(deep * len(blocks)),
     )
 
 
@@ -283,6 +295,7 @@
         jax.ShapeDtypeStruct((spots, genes), F32),
         pl.BlockSpec((tile, genes), lambda i, ix: (i, 0)),
         (spots // tile,),
+        limit=VMEM_LIMIT,
     )
 
 
@@ -293,9 +306,9 @@
     return cos, inv, cos / left
 
 
-def pack_kernel(mine_ref, theirs_ref, core_ref, far_ref, z_ref, out_ref, spot_ref):
+def pack_kernel(mine_ref, theirs_ref, core_ref, z_ref, out_ref, spot_ref):
     genes = out_ref.shape[1] // 2
-    totals = (mine_ref[...] + theirs_ref[...]) + (core_ref[...] + far_ref[...])
+    totals = (mine_ref[...] + theirs_ref[...]) + core_ref[...]
     spot_ref[...] = totals
     cos, _, _ = cosine(totals[0:NB], totals[NB : 2 * NB], totals[2 * NB : 3 * NB])
     out_ref[...] = jnp.zeros_like(out_ref)
@@ -310,7 +323,7 @@
     )
 
 
-def pack(mine, theirs, core, far, zinfo, genes):
+def pack(mine, theirs, core, zinfo, genes):
     return pl.pallas_call(
         pack_kernel,
         out_shape=(
@@ -320,7 +333,7 @@
         compiler_params=pltpu.CompilerParams(vmem_limit_bytes=VMEM_LIMIT),
         cost_estimate=CHEAP,
         name="pack",
-    )(mine, theirs, core, far, zinfo)
+    )(mine, theirs, core, zinfo)
 
 
 def rows_kernel(count, chosen, where, *refs):
@@ -360,6 +373,7 @@
         (fixed_out((2 * rows, genes)), fixed_out((2 * rows, genes))),
         (1,),
         [pltpu.VMEM((slots, genes, KC), F32), pltpu.SemaphoreType.DMA((slots,))],
+        limit=VMEM_LIMIT,
     )
 
 
@@ -373,17 +387,23 @@
     return value
 
 
-def back_sum_kernel(sizes, where, *refs):
+def back_sum_kernel(blocks, count, first, sizes, where, *refs):
     batch_scale, gene_scale = sizes
-    pred_refs, x_refs, refs = refs[0:2], refs[2 : 2 + 2 * XS], refs[2 + 2 * XS :]
+    s_refs, h_refs, l_refs = refs[:blocks], refs[blocks : blocks + count], refs[blocks + count : blocks + 2 * count]
+    refs = refs[blocks + 2 * count :]
+    if not first:
+        acc_ref, refs = refs[0], refs[1:]
+    z_ref, own_ref, x_refs, refs = refs[0], refs[1], refs[2 : 2 + 2 * XS], refs[2 + 2 * XS :]
     high_refs, low_refs = refs[0:2], refs[2:4]
-    totals_ref, more_ref, spot_ref, out_ref, bhigh, blow, sum_ref, coef = refs[4:]
-    genes, tile = pred_refs[0].shape
+    totals_ref, more_ref, spot_ref, out_ref, bhigh, blow, sum_ref, coef, other_ref, high, low = refs[4:]
+    pred_refs = (own_ref, other_ref)
+    genes, tile = own_ref.shape
     rows = high_refs[0].shape[0]
     width = genes // NB
 
     @pl.when(pl.program_id(0) == 0)
     def _():
+        load_left(s_refs, high, low)
         totals = totals_ref[...] + more_ref[...]
         gene_cos, inv_gene, over_gene = cosine(totals[0:1], totals[1:2], totals[2:3])
         coef[0] = jnp.broadcast_to(-gene_scale * inv_gene, (128, 2 * genes)).T
@@ -391,6 +411,10 @@
         cos = jnp.broadcast_to(jnp.sum(gene_cos, axis=1, keepdims=True), (1, 128))
         sum_ref[...] = jnp.concatenate([totals[3:7, 0:128], cos, jnp.zeros((3, 128), F32)], axis=0)
 
+    other = product(high, low, h_refs, l_refs)
+    if not first:
+        other = other + acc_ref[...]
+    other_ref[...] = other * z_ref[0:1, :]
     spot = spot_ref[...]
     _, inv_spot, over_spot = cosine(spot[0:NB], spot[NB : 2 * NB], spot[2 * NB : 3 * NB])
     column = jnp.zeros((1, tile), F32)
@@ -414,14 +438,21 @@
     out_ref[rows + 2 : rows + 8] = jnp.zeros((6, tile), F32)
 
 
-def back_sum(where, preds, xs, lefts, totals, more, spot, consts, rows, tile):
-    genes, spots = preds[0].shape
+def back_sum(where, blocks, terms, acc, zinfo, own, xs, lefts, totals, more, spot, consts, rows, tile):
+    genes, spots = own.shape
+    deep = blocks[0].shape[1]
     left = pl.BlockSpec((rows, genes), lambda i, ix: (0, 0), pipeline_mode=pl.Buffered(1))
-    specs = [by_tile(genes, tile)] * 2 + [by_tile(genes // XS, tile)] * (2 * XS) + [left] * 4
-    specs += [fixed((8, 2 * genes))] * 2 + [by_tile(16, tile)]
-    args = [*preds, *xs, lefts[0][0], lefts[1][0], lefts[0][1], lefts[1][1], totals, more, spot]
+    specs = [fixed((genes, deep)) for _ in blocks]
+    specs += [by_tile(height, tile, place) for _, _, height, place in terms] * 2
+    args = [*blocks, *(term[0] for term in terms), *(term[1] for term in terms)]
+    if acc is not None:
+        specs.append(by_tile(genes, tile))
+        args.append(acc)
+    specs += [by_tile(8, tile), by_tile(genes, tile)] + [by_tile(height, tile) for height in heights(genes)] * 2
+    specs += [left] * 4 + [fixed((8, 2 * genes))] * 2 + [by_tile(16, tile)]
+    args += [zinfo, own, *xs, lefts[0][0], lefts[1][0], lefts[0][1], lefts[1][1], totals, more, spot]
     return call(
-        functools.partial(back_sum_kernel, consts[:2]),
+        functools.partial(back_sum_kernel, len(blocks), len(terms), acc is None, consts[:2]),
         "back_sum",
         where,
         args,
@@ -434,7 +465,13 @@
         ),
         (by_tile(rows + 8, tile), by_tile(2 * genes, tile), by_tile(2 * genes, tile), fixed_out((8, 128))),
         (spots // tile,),
-        [pltpu.VMEM((2, 2 * genes, 128), F32)],
+        [
+            pltpu.VMEM((2, 2 * genes, 128), F32),
+            pltpu.VMEM((genes, tile), F32),
+            pltpu.VMEM((genes, deep * len(blocks)), BF),
+            pltpu.VMEM((genes, deep * len(blocks)), BF),
+        ],
+        limit=limit_of(deep * len(blocks)),
     )
 
 
@@ -480,6 +517,7 @@
         (jax.ShapeDtypeStruct((rows, spots), F32), jax.ShapeDtypeStruct((3,), F32)),
         (by_tile(rows, tile), pl.BlockSpec(memory_space=pltpu.SMEM)),
         (spots // tile,),
+        limit=VMEM_LIMIT,
     )
 
 
@@ -519,7 +557,7 @@
     order = (gene_order - col * genes).reshape(genes, 1)
     pick = order == lax.broadcasted_iota(jnp.int32, (genes, genes), 1)
     mine = lax.dot_general(
-        pick.astype(F32), centroid_expr, NT, precision=lax.Precision.HIGHEST, preferred_element_type=F32
+        pick.astype(F32), centroid_expr, NT, precision=lax.Precision.HIGH, preferred_element_type=F32
     )
     pick = pick.astype(BF)
     theirs = swap(mine, "gene", 2)
@@ -534,18 +572,19 @@
         send = lambda one, *others: swap(after(one, *others), "gene", 2)
         keys = lambda *order: [functools.partial(lambda k, ix: ix[2] ^ k, k) for k in order]
         o1, o2, oy = [hop(mine, bit) for bit in (2, 4, 1)]
-        x_own = turn(where, pick, spatial, 2 * tile)
+        x_own = list(turn(where, pick, spatial, 2 * tile))
+        x_own[0], oy = tie(x_own[0], oy)
+        x0 = send(x_own[0])
         logits, *x_own = tie(logits, *x_own)
         *e_one, z_one = exp_parts(where, keys(0, 1, 2, 4), KC, logits, weights, dens_row, None, False, 2 * tile)
         o1, oy, o2, theirs, z_one, *x_own = tie(o1, oy, o2, theirs, z_one, *x_own)
         o2y, o3 = hop(o2, 1), hop(o2, 2)
-        x0 = send(x_own[0])
         acc = fwd("own_early", [mine, oy, o1, o2], [(*e_one, 4 * KC, 0)], None, None, None)
         acc, o2y, o3, oy, theirs, z_one, logits = tie(acc, o2y, o3, oy, theirs, z_one, logits)
         o3y, o1y, ty = hop(o3, 1), hop(oy, 2), hop(theirs, 1)
         *e_two, zinfo = exp_parts(where, keys(3, 5, 6, 7), KC, logits, weights, dens_row, z_one, True, 2 * tile)
-        acc, o3y, o1y, theirs, zinfo = tie(acc, o3y, o1y, theirs, zinfo)
-        t1, t2 = hop(theirs, 2), hop(theirs, 4)
+        acc, o3y, o1y, theirs, zinfo, held = tie(acc, o3y, o1y, theirs, zinfo, x_own[1])
+        t1, t2, x1 = hop(theirs, 2), hop(theirs, 4), send(held)
         pred_own, info = fwd("own_late", [o1y, o2y, o3, o3y], [(*e_two, 4 * KC, 0)], acc, zinfo, x_own)
         own = [mine, oy, o1, o1y, o2, o2y, o3, o3y]
         own_pick = lambda ix, block: [(block ^ ix[2]) == key for key in range(n_spot)]
@@ -559,47 +598,41 @@
         pred_own, info = fwd("own_late", own, whole, None, zinfo, x_own)
         own_pick = None
 
-    infos = [swap(info, "gene", bit) for bit in (2, 1, 3)]
+    info_x = swap(info, "gene", 2)
     if ring:
-        pred_own, t1, ty, x0, mine = tie(pred_own, t1, ty, x0, mine)
-        t1y = hop(t1, 1)
-        own[0] = mine
-    left_own = rows_left(where, own, rows, own_pick)
-    if ring:
-        t2, left_own, held, *infos = tie(t2, left_own, x_own[1], *infos)
-        t3, t2y, x1 = hop(t2, 2), hop(t2, 1), send(held)
-    totals, spot = pack(info, *infos, zinfo, genes)
+        pred_own, t1, ty, t2, theirs, x0 = tie(pred_own, t1, ty, t2, theirs, x0)
+        t2y, t3 = hop(t2, 1), hop(t2, 2)
+        acc_other = fwd("other_mid", [theirs, ty, t1, t2], [(*e_one, 4 * KC, 0)], None, None, None)
+        acc_other, t2y, t3, t1, x1, held, info_x = tie(acc_other, t2y, t3, t1, x1, x_own[2], info_x)
+        x2, t3y, t1y = send(held), hop(t2y, 2), hop(t1, 1)
+        x_got = [x0, x1, x2]
+    totals, spot = pack(info, info_x, swap(info + info_x, "gene", 1), zinfo, genes)
     if ring:
         got = swap(totals, "spot", 1)
-        theirs, totals = tie(theirs, totals)
-        acc_other = fwd("other_mid", [theirs, ty, t1, t2], [(*e_one, 4 * KC, 0)], None, None, None)
-        acc_other, got, t2y, t3 = tie(acc_other, got, t2y, t3)
-        t3y = hop(t2y, 2)
+        acc_other, totals = tie(acc_other, totals)
+        acc_other = fwd("other_more", [t2y, t3], [(*e_two, KC, 1), (*e_two, KC, 2)], acc_other, None, None)
+        acc_other, got, mine = tie(acc_other, got, mine)
         totals = totals + got
         got = swap(totals, "spot", 2)
-        acc_other, totals = tie(acc_other, totals)
-        acc_other = fwd("other_more", [t2y, t3], [(*e_two, KC, 1), (*e_two, KC, 2)], acc_other, None, None)
-        t1y, t3y, acc_other = tie(t1y, t3y, acc_other)
+        own[0] = mine
+        left_own = rows_left(where, own, rows, own_pick)
+        left_own, got, t1y, t3y = tie(left_own, got, t1y, t3y)
+        totals = totals + got
+        more = swap(totals, "spot", 4)
         other = [theirs, ty, t1, t1y, t2, t2y, t3, t3y]
-        left_other = rows_left(where, other, rows, own_pick)
-        left_other, got = tie(left_other, got)
-        totals = totals + got
-        got = swap(totals, "spot", 4)
-        acc_other, _ = tie(acc_other, left_other)
-        pred_other = fwd(
-            "other_late", [t1y, t3y], [(*e_two, KC, 0), (*e_two, KC, 3)], acc_other, zinfo, None
-        )
-        pred_other, more = tie(pred_other, got)
-        x_got = [x0, x1]
+        last = ([t1y, t3y], [(*e_two, KC, 0), (*e_two, KC, 3)], acc_other)
     else:
         totals = lax.psum(totals, "spot")
         more = jnp.zeros_like(totals)
-        pred_other = fwd("other_late", other, whole, None, zinfo, None)
-        left_other = rows_left(where, other, rows, own_pick)
+        left_own = rows_left(where, own, rows, own_pick)
+        last = (other, whole, None)
+    left_other = rows_left(where, other, rows, own_pick)
+    if ring:
+        left_other, more = tie(left_other, more)
 
     lefts = (left_own, left_other)
     sent, *highs, sums = back_sum(
-        where, (pred_own, pred_other), (*x_own, *x_got), lefts, totals, more, spot, consts, rows, tile
+        where, *last, zinfo, pred_own, (*x_own, *x_got), lefts, totals, more, spot, consts, rows, tile
     )
     got = swap(sent, "gene", 1)
     predicted = emit(where, after(pred_own, sent), pick, 2 * tile)

time: 174 us -> 159 us (0.914)
  Pallas kernels: 125 us -> 90.8 us
  local copies, waits for them, and re-layouts: 1.37 us -> 19.4 us
  waiting for transfers between devices: 5.46 us -> 12.2 us
  other arithmetic: 7.67 us -> 2.25 us
  matrix products: 2.55 us -> 0.48 us
    pallas_call x13 -> x12, Pallas kernels: 123 us -> 90.7 us  [call(): pl.pallas_call(kernel, out_shape=out_shape, grid_spec=pltpu.PrefetchScala...]
    unnamed x0 -> x54, local copies, waits for them, and re-layouts: none -> 19.1 us
    ppermute x24, waiting for transfers between devices: 5.46 us -> 12.2 us  [swap(): lax.ppermute(value, axis, [(i, i ^ bit) for i in range(lax.axis_size(axis...]
    add x2, other arithmetic: 2.79 us -> 0.01 us  [local(): totals = totals + got]
    dot_general x1, matrix products: 2.55 us -> 0.48 us  [local(): lax.dot_general(pick.astype(F32), centroid_expr, NT, precision=lax.Precis...]
  transfers between devices with their start and end apart: 24 -> 24, of which waited for: 4 -> 6; matrix products, arithmetic and copies ran while one was open for 5% -> 1% of each run, Pallas kernels for 55% -> 39%
where the time goes in v5:
time: 159 us
  Pallas kernels  90.8 us (57%)
  starting transfers between devices  32.2 us (20%)
  local copies, waits for them, and re-layouts  19.4 us (12%)
  waiting for transfers between devices  12.2 us (8%)
  other arithmetic  2.25 us (1%)
    pallas_call x12, Pallas kernels, call(): pl.pallas_call(kernel, out_shape=out_shape, grid_spec=pltpu.PrefetchScala...  90.7 us
    ppermute x24, starting transfers between devices, swap(): lax.ppermute(value, axis, [(i, i ^ bit) for i in range(lax.axis_size(axis...  32.2 us
    unnamed x54, local copies, waits for them, and re-layouts  19.1 us
    ppermute x24, waiting for transfers between devices, swap(): lax.ppermute(value, axis, [(i, i ^ bit) for i in range(lax.axis_size(axis...  12.2 us
  transfers between devices with their start and end apart: 24, of which 6 were waited for; matrix products, arithmetic and copies ran while one was open for 1% of the time, Pallas kernels for 39%

profile of v5, /device:TPU:1, one launch (start us, length us, event | category | flops | bytes accessed | tf_op | source)
XLA Modules:
  0.0 158.5 jit_solution(13011816676809517140)
XLA Ops:
  2.2 2.1 %collective-permute-start.1 = (f32[512,256]{1,0:T(8,128)S(1)}, f32[512,256]{1,0:T(8,128)S(1)}, u32[]{:S(2)}, u32[]{:S(2)}) collective-permute-start(f32[512,256]{1,0:T(8,128)S(1)} %fusion.1.refs_0_), channel_id=1, source_target_pairs={{0,4},{4,0},{8,12},{12,8},{16,20},{20,16},{24,28},{28,24},{1,5},{5... | collective-permute-start | bytes 1572872 | tf_op jit(solution)/shard_map/ppermute | solution.py:525
  4.3 1.2 collective-permute-start.3
  5.5 2.3 %collective-permute-start.2 = (f32[512,256]{1,0:T(8,128)S(1)}, f32[512,256]{1,0:T(8,128)}, u32[]{:S(2)}, u32[]{:S(2)}) collective-permute-start(f32[512,256]{1,0:T(8,128)S(1)} %fusion.1.refs_0_), channel_id=1, source_target_pairs={{0,16},{4,20},{8,24},{12,28},{16,0},{20,4},{24,8},{28,12},{1,17},{... | collective-permute-start | bytes 1572872 | tf_op jit(solution)/shard_map/ppermute | solution.py:525
  7.8 1.3 collective-permute-start
  9.4 2.2 %copy-done.14 = f32[2048,512]{1,0:T(8,128)S(1)} copy-done((f32[2048,512]{1,0:T(8,128)S(1)}, f32[2048,512]{1,0:T(8,128)}, u32[]{:S(2)}) %copy-start.14) | copy-done | bytes 4194328
  11.6 4.1 %turn.1 = (f32[256,2048]{1,0:T(8,128)}, f32[128,2048]{1,0:T(8,128)S(1)}, f32[128,2048]{1,0:T(8,128)S(1)}) custom-call(s32[3]{0:T(128)S(1)} %pad_add_fusion.where, bf16[512,512]{1,0:T(8,128)(2,1)S(1)} %fusion.pick_ref, f32[2048,512]{1,0:T(8,128)S(1)} %copy-done.14), custom_call_target="tpu_custom_call" | custom-call | flops 1000 | bytes 1000 | tf_op jit(solution)/shard_map/turn/pallas_call | solution.py:33
  19.6 5.8 %copy-done.2 = f32[2048,2048]{1,0:T(8,128)S(1)} copy-done((f32[2048,2048]{1,0:T(8,128)S(1)}, f32[2048,2048]{1,0:T(8,128)}, u32[]{:S(2)}) %copy-start.2) | copy-done | bytes 16777240
  25.4 4.5 %exp_parts.2 = (bf16[1024,2048]{1,0:T(8,128)(2,1)S(1)}, bf16[1024,2048]{1,0:T(8,128)(2,1)S(1)}, f32[8,2048]{1,0:T(8,128)S(1)}) custom-call(s32[3]{0:T(128)S(1)} %pad_add_fusion.where, f32[2048,2048]{1,0:T(8,128)S(1)} %copy-done.2, f32[2048,2048]{1,0:T(8,128)S(1)} %copy-done.2, f32[2048,2048]{1,0:T(8,128)S(1)} %copy-done.2, f32[2048,2048]{1,0:T(8,128)S(1)} %copy-done.2, ...), custom_call_target="tpu_custom_call" | custom-call | flops 1000 | bytes 1000 | tf_op jit(solution)/shard_map/exp_parts/pallas_call | solution.py:33
  30.6 1.3 collective-permute-start.5
  32.6 10.1 %own_early.1.refs_6_ = f32[512,2048]{1,0:T(8,128)S(1)} custom-call(s32[3]{0:T(128)S(1)} %pad_add_fusion.where, f32[512,256]{1,0:T(8,128)S(1)} %fusion.1.refs_0_, f32[512,256]{1,0:T(8,128)S(1)} %copy-done.18, f32[512,256]{1,0:T(8,128)} %collective-permute-done.refs_2_, f32[512,256]{1,0:T(8,128)} %collective-permute-done.2.refs_3_.refs_4_, ...), custom_call_target="tpu_custom_call" | custom-call | flops 1000 | bytes 1000 | tf_op jit(solution)/shard_map/own_early/pallas_call | solution.py:33
  45.5 5.8 %copy-done.3 = f32[2048,2048]{1,0:T(8,128)S(1)} copy-done((f32[2048,2048]{1,0:T(8,128)S(1)}, f32[2048,2048]{1,0:T(8,128)}, u32[]{:S(2)}) %copy-start.3) | copy-done | bytes 16777240
  51.2 4.6 %exp_parts.3 = (bf16[1024,2048]{1,0:T(8,128)(2,1)S(1)}, bf16[1024,2048]{1,0:T(8,128)(2,1)S(1)}, f32[8,2048]{1,0:T(8,128)S(1)}) custom-call(s32[3]{0:T(128)S(1)} %pad_add_fusion.where, f32[2048,2048]{1,0:T(8,128)S(1)} %copy-done.3, f32[2048,2048]{1,0:T(8,128)S(1)} %copy-done.3, f32[2048,2048]{1,0:T(8,128)S(1)} %copy-done.3, f32[2048,2048]{1,0:T(8,128)S(1)} %copy-done.3, ...), custom_call_target="tpu_custom_call" | custom-call | flops 1000 | bytes 1000 | tf_op jit(solution)/shard_map/exp_parts/pallas_call | solution.py:33
  55.9 4.5 %collective-permute-start.10 = (f32[512,256]{1,0:T(8,128)}, f32[512,256]{1,0:T(8,128)S(1)}, u32[]{:S(2)}, u32[]{:S(2)}) collective-permute-start(f32[512,256]{1,0:T(8,128)} %collective-permute-done.3.refs_0_), channel_id=1, source_target_pairs={{0,16},{4,20},{8,24},{12,28},{16,0},{20,4},{24,8},{28,12},{1,17},{... | collective-permute-start | bytes 1572872 | tf_op jit(solution)/shard_map/ppermute | solution.py:525
  60.5 1.1 collective-permute-start.8
  61.8 12.1 %own_late.1 = (f32[512,2048]{1,0:T(8,128)S(1)}, f32[16,2048]{1,0:T(8,128)S(1)}) custom-call(s32[3]{0:T(128)S(1)} %pad_add_fusion.where, f32[512,256]{1,0:T(8,128)S(1)} %collective-permute-done.7.refs_0_.refs_3_, f32[512,256]{1,0:T(8,128)S(1)} %collective-permute-done.4.refs_1_.refs_5_, ...), custom_call_target="tpu_custom_call", output_to_operand_aliasing={{0}: (7, {})} | custom-call | flops 1000 | bytes 1000 | tf_op jit(solution)/shard_map/own_late/pallas_call | solution.py:33
  74.0 9.4 %collective-permute-done.10.refs_3_.refs_4_ = f32[512,256]{1,0:T(8,128)S(1)} collective-permute-done((f32[512,256]{1,0:T(8,128)}, f32[512,256]{1,0:T(8,128)S(1)}, u32[]{:S(2)}, u32[]{:S(2)}) %collective-permute-start.10) | collective-permute-done | bytes 524320 | tf_op jit(solution)/shard_map/ppermute | solution.py:525
  83.4 1.3 collective-permute-start.13
  85.0 10.1 %other_mid.1.refs_6_ = f32[512,2048]{1,0:T(8,128)S(1)} custom-call(s32[3]{0:T(128)S(1)} %pad_add_fusion.where, f32[512,256]{1,0:T(8,128)} %collective-permute-done.3.refs_0_, f32[512,256]{1,0:T(8,128)S(1)} %collective-permute-done.9.refs_1_, f32[512,256]{1,0:T(8,128)S(1)} %collective-permute-done.8.refs_2_, ...), custom_call_target="tpu_custom_call" | custom-call | flops 1000 | bytes 1000 | tf_op jit(solution)/shard_map/other_mid/pallas_call | solution.py:33
  95.2 1.0 copy-done.23
  96.2 1.1 collective-permute-start.22
  97.4 1.4 collective-permute-start.19
  99.0 3.6 %collective-permute-start.16 = (f32[16,2048]{1,0:T(8,128)S(1)}, f32[16,2048]{1,0:T(8,128)S(1)}, u32[]{:S(2)}, u32[]{:S(2)}) collective-permute-start(f32[16,2048]{1,0:T(8,128)S(1)} %add.9), channel_id=1, source_target_pairs={{0,1},{1,0},{2,3},{3,2},{4,5},{5,4},{6,7},{7,6},{8,9},{9,8},{10,11... | collective-permute-start | bytes 393224 | tf_op jit(solution)/shard_map/ppermute | solution.py:525
  103.8 5.6 %other_more.1.refs_6_ = f32[512,2048]{1,0:T(8,128)S(1)} custom-call(s32[3]{0:T(128)S(1)} %pad_add_fusion.where, f32[512,256]{1,0:T(8,128)S(1)} %collective-permute-done.12.refs_0_.refs_5_, f32[512,256]{1,0:T(8,128)S(1)} %collective-permute-done.13.refs_1_.refs_6_, ...), custom_call_target="tpu_custom_call", output_to_operand_aliasing={{}: (7, {})} | custom-call | flops 1000 | bytes 1000 | tf_op jit(solution)/shard_map/other_more/pallas_call | solution.py:33
  109.5 1.0 collective-permute-start.18
  110.5 3.2 %rows_left.2 = (bf16[1024,512]{1,0:T(8,128)(2,1)S(1)}, bf16[1024,512]{1,0:T(8,128)(2,1)S(1)}) custom-call(s32[3]{0:T(128)S(1)} %pad_add_fusion.where, f32[512,256]{1,0:T(8,128)S(1)} %fusion.1.refs_0_, f32[512,256]{1,0:T(8,128)S(1)} %copy-done.18, f32[512,256]{1,0:T(8,128)} %collective-permute-done.refs_2_, f32[512,256]{1,0:T(8,128)S(1)} %copy-done.20, ...), custom_call_target="tpu_custom_call" | custom-call | flops 1000 | bytes 1000 | tf_op jit(solution)/shard_map/rows_left/pallas_call | solution.py:33
  113.8 2.7 %collective-permute-start.21 = (f32[8,1024]{1,0:T(8,128)S(1)}, f32[8,1024]{1,0:T(8,128)S(1)}, u32[]{:S(2)}, u32[]{:S(2)}) collective-permute-start(f32[8,1024]{1,0:T(8,128)S(1)} %add.11.refs_19_), channel_id=1, source_target_pairs={{0,16},{4,20},{8,24},{12,28},{16,0},{20,4},{24,8},{28,12},{1,17},{... | collective-permute-start | bytes 98312 | tf_op jit(solution)/shard_map/ppermute | solution.py:525
  116.5 2.4 %rows_left.3 = (bf16[1024,512]{1,0:T(8,128)(2,1)S(1)}, bf16[1024,512]{1,0:T(8,128)(2,1)S(1)}) custom-call(s32[3]{0:T(128)S(1)} %pad_add_fusion.where, f32[512,256]{1,0:T(8,128)} %collective-permute-done.3.refs_0_, f32[512,256]{1,0:T(8,128)S(1)} %collective-permute-done.9.refs_1_, f32[512,256]{1,0:T(8,128)S(1)} %collective-permute-done.8.refs_2_, ...), custom_call_target="tpu_custom_call" | custom-call | flops 1000 | bytes 1000 | tf_op jit(solution)/shard_map/rows_left/pallas_call | solution.py:33
  119.0 17.9 %back_sum.1 = (f32[520,2048]{1,0:T(8,128)}, bf16[1024,2048]{1,0:T(8,128)(2,1)S(1)}, bf16[1024,2048]{1,0:T(8,128)(2,1)S(1)}, f32[8,128]{1,0:T(8,128)S(1)}) custom-call(s32[3]{0:T(128)S(1)} %pad_add_fusion.where, f32[512,256]{1,0:T(8,128)S(1)} %collective-permute-done.19.refs_3_.refs_0_, f32[512,256]{1,0:T(8,128)S(1)} %collective-permute-done.20.refs_7_.refs_1_, ...), custom_call_target="tpu_custom_call" | custom-call | flops 1000 | bytes 1000 | tf_op jit(solution)/shard_map/back_sum/pallas_call | solution.py:33
  136.9 3.4 %collective-permute-start.23 = (f32[520,2048]{1,0:T(8,128)}, f32[520,2048]{1,0:T(8,128)S(1)}, u32[]{:S(2)}, u32[]{:S(2)}) collective-permute-start(f32[520,2048]{1,0:T(8,128)} %get-tuple-element.155.refs_9_), channel_id=1, source_target_pairs={{0,1},{1,0},{2,3},{3,2},{4,5},{5,4},{6,7},{7,6},{8,9},{9,8},{10,11... | collective-permute-start | bytes 12779528 | tf_op jit(solution)/shard_map/ppermute | solution.py:525
  140.3 2.2 %copy-done.7 = f32[512,2048]{1,0:T(8,128)S(1)} copy-done((f32[512,2048]{1,0:T(8,128)S(1)}, f32[512,2048]{1,0:T(8,128)}, u32[]{:S(2)}) %copy-start.7) | copy-done | bytes 4194328
  142.5 4.8 %emit.1 = f32[2048,512]{1,0:T(8,128)} custom-call(s32[3]{0:T(128)S(1)} %pad_add_fusion.where, f32[512,2048]{1,0:T(8,128)S(1)} %copy-done.7, bf16[512,512]{1,0:T(8,128)(2,1)S(1)} %fusion.pick_ref), custom_call_target="tpu_custom_call" | custom-call | flops 1000 | bytes 1000 | tf_op jit(solution)/shard_map/emit/pallas_call | solution.py:33
  147.4 11.1 %back_end.1 = (f32[512,2048]{1,0:T(8,128)}, f32[3]{0:T(128)}) custom-call(s32[3]{0:T(128)S(1)} %pad_add_fusion.where, bf16[1024,512]{1,0:T(8,128)(2,1)S(1)} %get-tuple-element.136.refs_15_.refs_0_, bf16[1024,512]{1,0:T(8,128)(2,1)S(1)} %get-tuple-element.142.refs_16_.refs_1_, bf16[1024,512]{1,0:T(8,128)(2,1)S(1)} %get-tuple-element.143.refs_17_.refs_2_, ...), custom_call_target="tpu_custom_call" | custom-call | flops 1000 | bytes 1000 | tf_op jit(solution)/shard_map/back_end/pallas_call | solution.py:33
  (93 shorter events, 12.0 us)
Async XLA Ops:
  0.7 19.0 %copy-start.25 = (f32[2048]{0:T(1024)S(1)}, f32[2048]{0:T(1024)}, u32[]{:S(2)}) copy-start(f32[2048]{0:T(1024)} %param.10) | copy-start | bytes 24580
  2.2 14.5 %collective-permute-start.1 = (f32[512,256]{1,0:T(8,128)S(1)}, f32[512,256]{1,0:T(8,128)S(1)}, u32[]{:S(2)}, u32[]{:S(2)}) collective-permute-start(f32[512,256]{1,0:T(8,128)S(1)} %fusion.1.refs_0_), channel_id=1, source_target_pairs={{0,4},{4,0},{8,12},{12,8},{16,20},{20,16},{24,28},{28,24},{1,5},{5... | collective-permute-start | bytes 1572872 | tf_op jit(solution)/shard_map/ppermute | solution.py:525
  4.3 25.6 %collective-permute-start.3 = (f32[512,256]{1,0:T(8,128)S(1)}, f32[512,256]{1,0:T(8,128)}, u32[]{:S(2)}, u32[]{:S(2)}) collective-permute-start(f32[512,256]{1,0:T(8,128)S(1)} %fusion.1.refs_0_), channel_id=1, source_target_pairs={{0,2},{1,3},{2,0},{3,1},{4,6},{5,7},{6,4},{7,5},{8,10},{9,11},{10,... | collective-permute-start | bytes 1572872 | tf_op jit(solution)/shard_map/ppermute | solution.py:525
  5.5 25.0 %collective-permute-start.2 = (f32[512,256]{1,0:T(8,128)S(1)}, f32[512,256]{1,0:T(8,128)}, u32[]{:S(2)}, u32[]{:S(2)}) collective-permute-start(f32[512,256]{1,0:T(8,128)S(1)} %fusion.1.refs_0_), channel_id=1, source_target_pairs={{0,16},{4,20},{8,24},{12,28},{16,0},{20,4},{24,8},{28,12},{1,17},{... | collective-permute-start | bytes 1572872 | tf_op jit(solution)/shard_map/ppermute | solution.py:525
  7.8 22.7 %collective-permute-start = (f32[512,256]{1,0:T(8,128)S(1)}, f32[512,256]{1,0:T(8,128)}, u32[]{:S(2)}, u32[]{:S(2)}) collective-permute-start(f32[512,256]{1,0:T(8,128)S(1)} %fusion.1.refs_0_), channel_id=1, source_target_pairs={{0,8},{4,12},{8,0},{12,4},{16,24},{20,28},{24,16},{28,20},{1,9},{5... | collective-permute-start | bytes 1572872 | tf_op jit(solution)/shard_map/ppermute | solution.py:525
  17.5 66.0 %collective-permute-start.11 = (f32[256,2048]{1,0:T(8,128)}, f32[256,2048]{1,0:T(8,128)}, u32[]{:S(2)}, u32[]{:S(2)}) collective-permute-start(f32[256,2048]{1,0:T(8,128)} %get-tuple-element.114.refs_8_.refs_9_), channel_id=1, source_target_pairs={{0,2},{1,3},{2,0},{3,1},{4,6},{5,7},{6,4},{7,5},{8,10},{9,11},{10,... | collective-permute-start | bytes 6291464 | tf_op jit(solution)/shard_map/ppermute | solution.py:525
  30.6 12.1 %collective-permute-start.5 = (f32[512,256]{1,0:T(8,128)}, f32[512,256]{1,0:T(8,128)S(1)}, u32[]{:S(2)}, u32[]{:S(2)}) collective-permute-start(f32[512,256]{1,0:T(8,128)} %collective-permute-done.2.refs_3_.refs_4_), channel_id=1, source_target_pairs={{0,8},{4,12},{8,0},{12,4},{16,24},{20,28},{24,16},{28,20},{1,9},{5... | collective-permute-start | bytes 1572872 | tf_op jit(solution)/shard_map/ppermute | solution.py:525
  31.9 11.8 %collective-permute-start.4 = (f32[512,256]{1,0:T(8,128)}, f32[512,256]{1,0:T(8,128)S(1)}, u32[]{:S(2)}, u32[]{:S(2)}) collective-permute-start(f32[512,256]{1,0:T(8,128)} %collective-permute-done.2.refs_3_.refs_4_), channel_id=1, source_target_pairs={{0,4},{4,0},{8,12},{12,8},{16,20},{20,16},{24,28},{28,24},{1,5},{5... | collective-permute-start | bytes 1572872 | tf_op jit(solution)/shard_map/ppermute | solution.py:525
  32.6 29.2 %copy-start.16 = (f32[128,2048]{1,0:T(8,128)S(1)}, f32[128,2048]{1,0:T(8,128)}, u32[]{:S(2)}) copy-start(f32[128,2048]{1,0:T(8,128)} %copy-done.15) | copy-start | bytes 3145732
  43.7 12.2 %collective-permute-start.7 = (f32[512,256]{1,0:T(8,128)S(1)}, f32[512,256]{1,0:T(8,128)S(1)}, u32[]{:S(2)}, u32[]{:S(2)}) collective-permute-start(f32[512,256]{1,0:T(8,128)S(1)} %copy-done.18), channel_id=1, source_target_pairs={{0,8},{4,12},{8,0},{12,4},{16,24},{20,28},{24,16},{28,20},{1,9},{5... | collective-permute-start | bytes 1572872 | tf_op jit(solution)/shard_map/ppermute | solution.py:525
  44.0 11.9 %collective-permute-start.6 = (f32[512,256]{1,0:T(8,128)S(1)}, f32[512,256]{1,0:T(8,128)S(1)}, u32[]{:S(2)}, u32[]{:S(2)}) collective-permute-start(f32[512,256]{1,0:T(8,128)S(1)} %collective-permute-done.5.refs_2_.refs_6_), channel_id=1, source_target_pairs={{0,4},{4,0},{8,12},{12,8},{16,20},{20,16},{24,28},{28,24},{1,5},{5... | collective-permute-start | bytes 1572872 | tf_op jit(solution)/shard_map/ppermute | solution.py:525
  44.8 29.2 %collective-permute-start.9 = (f32[512,256]{1,0:T(8,128)}, f32[512,256]{1,0:T(8,128)S(1)}, u32[]{:S(2)}, u32[]{:S(2)}) collective-permute-start(f32[512,256]{1,0:T(8,128)} %collective-permute-done.3.refs_0_), channel_id=1, source_target_pairs={{0,4},{4,0},{8,12},{12,8},{16,20},{20,16},{24,28},{28,24},{1,5},{5... | collective-permute-start | bytes 1572872 | tf_op jit(solution)/shard_map/ppermute | solution.py:525
  55.9 47.9 %copy-start.4 = (bf16[1024,2048]{1,0:T(8,128)(2,1)}, bf16[1024,2048]{1,0:T(8,128)(2,1)S(1)}, u32[]{:S(2)}) copy-start(bf16[1024,2048]{1,0:T(8,128)(2,1)S(1)} %get-tuple-element.111.refs_5_.refs_4_) | copy-start | bytes 12582916
  55.9 18.1 %copy-start.19 = (f32[512,256]{1,0:T(8,128)}, f32[512,256]{1,0:T(8,128)S(1)}, u32[]{:S(2)}) copy-start(f32[512,256]{1,0:T(8,128)S(1)} %collective-permute-done.7.refs_0_.refs_3_) | copy-start | bytes 1572868
  55.9 18.1 %copy-start.21 = (f32[512,256]{1,0:T(8,128)}, f32[512,256]{1,0:T(8,128)S(1)}, u32[]{:S(2)}) copy-start(f32[512,256]{1,0:T(8,128)S(1)} %collective-permute-done.6.refs_3_.refs_7_) | copy-start | bytes 1572868
  55.9 27.5 %collective-permute-start.10 = (f32[512,256]{1,0:T(8,128)}, f32[512,256]{1,0:T(8,128)S(1)}, u32[]{:S(2)}, u32[]{:S(2)}) collective-permute-start(f32[512,256]{1,0:T(8,128)} %collective-permute-done.3.refs_0_), channel_id=1, source_target_pairs={{0,16},{4,20},{8,24},{12,28},{16,0},{20,4},{24,8},{28,12},{1,17},{... | collective-permute-start | bytes 1572872 | tf_op jit(solution)/shard_map/ppermute | solution.py:525
  60.5 23.0 %collective-permute-start.8 = (f32[512,256]{1,0:T(8,128)}, f32[512,256]{1,0:T(8,128)S(1)}, u32[]{:S(2)}, u32[]{:S(2)}) collective-permute-start(f32[512,256]{1,0:T(8,128)} %collective-permute-done.3.refs_0_), channel_id=1, source_target_pairs={{0,8},{4,12},{8,0},{12,4},{16,24},{20,28},{24,16},{28,20},{1,9},{5... | collective-permute-start | bytes 1572872 | tf_op jit(solution)/shard_map/ppermute | solution.py:525
  61.6 33.6 %collective-permute-start.14 = (f32[128,2048]{1,0:T(8,128)S(1)}, f32[128,2048]{1,0:T(8,128)S(1)}, u32[]{:S(2)}, u32[]{:S(2)}) collective-permute-start(f32[128,2048]{1,0:T(8,128)S(1)} %get-tuple-element.122.refs_9_.refs_10_), channel_id=1, source_target_pairs={{0,2},{1,3},{2,0},{3,1},{4,6},{5,7},{6,4},{7,5},{8,10},{9,11},{10,... | collective-permute-start | bytes 3145736 | tf_op jit(solution)/shard_map/ppermute | solution.py:525
  61.8 23.2 %copy-start.10 = (bf16[1024,2048]{1,0:T(8,128)(2,1)S(1)}, bf16[1024,2048]{1,0:T(8,128)(2,1)}, u32[]{:S(2)}) copy-start(bf16[1024,2048]{1,0:T(8,128)(2,1)} %copy-done.9) | copy-start | bytes 12582916
  61.8 23.2 %copy-start.12 = (bf16[1024,2048]{1,0:T(8,128)(2,1)S(1)}, bf16[1024,2048]{1,0:T(8,128)(2,1)}, u32[]{:S(2)}) copy-start(bf16[1024,2048]{1,0:T(8,128)(2,1)} %copy-done.11) | copy-start | bytes 12582916
  74.0 21.1 %copy-start.6 = (f32[512,2048]{1,0:T(8,128)}, f32[512,2048]{1,0:T(8,128)S(1)}, u32[]{:S(2)}) copy-start(f32[512,2048]{1,0:T(8,128)S(1)} %get-tuple-element.156.refs_8_.pred_ref) | copy-start | bytes 12582916
  83.4 12.7 %collective-permute-start.13 = (f32[512,256]{1,0:T(8,128)S(1)}, f32[512,256]{1,0:T(8,128)S(1)}, u32[]{:S(2)}, u32[]{:S(2)}) collective-permute-start(f32[512,256]{1,0:T(8,128)S(1)} %collective-permute-done.10.refs_3_.refs_4_), channel_id=1, source_target_pairs={{0,8},{4,12},{8,0},{12,4},{16,24},{20,28},{24,16},{28,20},{1,9},{5... | collective-permute-start | bytes 1572872 | tf_op jit(solution)/shard_map/ppermute | solution.py:525
  84.7 11.5 %collective-permute-start.12 = (f32[512,256]{1,0:T(8,128)S(1)}, f32[512,256]{1,0:T(8,128)S(1)}, u32[]{:S(2)}, u32[]{:S(2)}) collective-permute-start(f32[512,256]{1,0:T(8,128)S(1)} %collective-permute-done.10.refs_3_.refs_4_), channel_id=1, source_target_pairs={{0,4},{4,0},{8,12},{12,8},{16,20},{20,16},{24,28},{28,24},{1,5},{5... | collective-permute-start | bytes 1572872 | tf_op jit(solution)/shard_map/ppermute | solution.py:525
  84.8 10.4 %collective-permute-start.15 = (f32[16,2048]{1,0:T(8,128)S(1)}, f32[16,2048]{1,0:T(8,128)S(1)}, u32[]{:S(2)}, u32[]{:S(2)}) collective-permute-start(f32[16,2048]{1,0:T(8,128)S(1)} %get-tuple-element.123.mine_ref), channel_id=1, source_target_pairs={{0,2},{1,3},{2,0},{3,1},{4,6},{5,7},{6,4},{7,5},{8,10},{9,11},{10,... | collective-permute-start | bytes 393224 | tf_op jit(solution)/shard_map/ppermute | solution.py:525
  96.2 22.7 %collective-permute-start.22 = (f32[128,2048]{1,0:T(8,128)S(1)}, f32[128,2048]{1,0:T(8,128)S(1)}, u32[]{:S(2)}, u32[]{:S(2)}) collective-permute-start(f32[128,2048]{1,0:T(8,128)S(1)} %copy-done.16), channel_id=1, source_target_pairs={{0,2},{1,3},{2,0},{3,1},{4,6},{5,7},{6,4},{7,5},{8,10},{9,11},{10,... | collective-permute-start | bytes 3145736 | tf_op jit(solution)/shard_map/ppermute | solution.py:525
  97.4 16.4 %collective-permute-start.19 = (f32[512,256]{1,0:T(8,128)S(1)}, f32[512,256]{1,0:T(8,128)S(1)}, u32[]{:S(2)}, u32[]{:S(2)}) collective-permute-start(f32[512,256]{1,0:T(8,128)S(1)} %collective-permute-done.8.refs_2_), channel_id=1, source_target_pairs={{0,4},{4,0},{8,12},{12,8},{16,20},{20,16},{24,28},{28,24},{1,5},{5... | collective-permute-start | bytes 1572872 | tf_op jit(solution)/shard_map/ppermute | solution.py:525
  98.8 15.0 %collective-permute-start.20 = (f32[512,256]{1,0:T(8,128)S(1)}, f32[512,256]{1,0:T(8,128)S(1)}, u32[]{:S(2)}, u32[]{:S(2)}) collective-permute-start(f32[512,256]{1,0:T(8,128)S(1)} %collective-permute-done.12.refs_0_.refs_5_), channel_id=1, source_target_pairs={{0,8},{4,12},{8,0},{12,4},{16,24},{20,28},{24,16},{28,20},{1,9},{5... | collective-permute-start | bytes 1572872 | tf_op jit(solution)/shard_map/ppermute | solution.py:525
  99.0 4.6 %collective-permute-start.16 = (f32[16,2048]{1,0:T(8,128)S(1)}, f32[16,2048]{1,0:T(8,128)S(1)}, u32[]{:S(2)}, u32[]{:S(2)}) collective-permute-start(f32[16,2048]{1,0:T(8,128)S(1)} %add.9), channel_id=1, source_target_pairs={{0,1},{1,0},{2,3},{3,2},{4,5},{5,4},{6,7},{7,6},{8,9},{9,8},{10,11... | collective-permute-start | bytes 393224 | tf_op jit(solution)/shard_map/ppermute | solution.py:525
  103.8 5.6 %collective-permute-start.17 = (f32[8,1024]{1,0:T(8,128)S(1)}, f32[8,1024]{1,0:T(8,128)S(1)}, u32[]{:S(2)}, u32[]{:S(2)}) collective-permute-start(f32[8,1024]{1,0:T(8,128)S(1)} %get-tuple-element.133), channel_id=1, source_target_pairs={{0,4},{4,0},{8,12},{12,8},{16,20},{20,16},{24,28},{28,24},{1,5},{5... | collective-permute-start | bytes 98312 | tf_op jit(solution)/shard_map/ppermute | solution.py:525
  109.5 4.3 %collective-permute-start.18 = (f32[8,1024]{1,0:T(8,128)S(1)}, f32[8,1024]{1,0:T(8,128)S(1)}, u32[]{:S(2)}, u32[]{:S(2)}) collective-permute-start(f32[8,1024]{1,0:T(8,128)S(1)} %add.10), channel_id=1, source_target_pairs={{0,8},{4,12},{8,0},{12,4},{16,24},{20,28},{24,16},{28,20},{1,9},{5... | collective-permute-start | bytes 98312 | tf_op jit(solution)/shard_map/ppermute | solution.py:525
  113.8 5.2 %collective-permute-start.21 = (f32[8,1024]{1,0:T(8,128)S(1)}, f32[8,1024]{1,0:T(8,128)S(1)}, u32[]{:S(2)}, u32[]{:S(2)}) collective-permute-start(f32[8,1024]{1,0:T(8,128)S(1)} %add.11.refs_19_), channel_id=1, source_target_pairs={{0,16},{4,20},{8,24},{12,28},{16,0},{20,4},{24,8},{28,12},{1,17},{... | collective-permute-start | bytes 98312 | tf_op jit(solution)/shard_map/ppermute | solution.py:525
  136.9 10.5 %collective-permute-start.23 = (f32[520,2048]{1,0:T(8,128)}, f32[520,2048]{1,0:T(8,128)S(1)}, u32[]{:S(2)}, u32[]{:S(2)}) collective-permute-start(f32[520,2048]{1,0:T(8,128)} %get-tuple-element.155.refs_9_), channel_id=1, source_target_pairs={{0,1},{1,0},{2,3},{3,2},{4,5},{5,4},{6,7},{7,6},{8,9},{9,8},{10,11... | collective-permute-start | bytes 12779528 | tf_op jit(solution)/shard_map/ppermute | solution.py:525
  (19 other events, 128.0 us)

commit v6 on v5

--- a/solution.py
+++ b/solution.py
@@ -51,6 +51,10 @@
 
 def limit_of(depth):
     return VMEM_LIMIT if depth <= 5 * KC else LARGE_LIMIT
+
+
+def off_chip(value):
+    return pltpu.with_memory_space_constraint(value, pltpu.HBM)
 
 
 def fixed(shape):
@@ -111,7 +115,7 @@
     ]
     specs += [pl.BlockSpec((deep, 1), functools.partial(lambda key, i, ix: (key(ix), 0), key)) for key in keys]
     specs.append(by_tile(1, tile))
-    args = [*([logits] * count), *([weights] * count), density]
+    args = [*([off_chip(logits)] * count), *([weights] * count), density]
     if before is not None:
         specs.append(by_tile(8, tile))
         args.append(before)
@@ -154,7 +158,7 @@
         turn_kernel,
         "turn",
         where,
-        [pick, x],
+        [pick, off_chip(x)],
         [fixed((genes, genes)), pl.BlockSpec((tile, genes), lambda i, ix: (i, 0))],
         tuple(jax.ShapeDtypeStruct((height, spots), F32) for height in heights(genes)),
         tuple(by_tile(height, tile) for height in heights(genes)),
@@ -239,18 +243,18 @@
     spots = terms[0][0].shape[1]
     genes, deep = blocks[0].shape
     first, last, stats = acc is None, zinfo is not None, x is not None
+    kept = stats or not first
     specs = [fixed((genes, deep)) for _ in blocks]
     specs += [by_tile(rows, tile, place) for _, _, rows, place in terms] * 2
     args = [*blocks, *(term[0] for term in terms), *(term[1] for term in terms)]
     alias = {}
     if not first:
-        alias = {len(args) + 1: 0}
         specs.append(by_tile(genes, tile))
         args.append(acc)
     if last:
         specs.append(by_tile(8, tile))
         args.append(zinfo)
-    shapes = jax.ShapeDtypeStruct((genes, spots), F32)
+    shapes = pltpu.HBM((genes, spots), F32) if kept else jax.ShapeDtypeStruct((genes, spots), F32)
     outs = by_tile(genes, tile)
     scratch = [pltpu.VMEM((genes, deep * len(blocks)), BF)] * 2
     if stats:
@@ -290,7 +294,7 @@
         emit_kernel,
         "emit",
         where,
-        [pred, pick],
+        [off_chip(pred), pick],
         [by_tile(genes, tile), fixed((genes, genes))],
         jax.ShapeDtypeStruct((spots, genes), F32),
         pl.BlockSpec((tile, genes), lambda i, ix: (i, 0)),
@@ -447,10 +451,10 @@
     args = [*blocks, *(term[0] for term in terms), *(term[1] for term in terms)]
     if acc is not None:
         specs.append(by_tile(genes, tile))
-        args.append(acc)
+        args.append(off_chip(acc))
     specs += [by_tile(8, tile), by_tile(genes, tile)] + [by_tile(height, tile) for height in heights(genes)] * 2
     specs += [left] * 4 + [fixed((8, 2 * genes))] * 2 + [by_tile(16, tile)]
-    args += [zinfo, own, *xs, lefts[0][0], lefts[1][0], lefts[0][1], lefts[1][1], totals, more, spot]
+    args += [zinfo, off_chip(own), *xs, lefts[0][0], lefts[1][0], lefts[0][1], lefts[1][1], totals, more, spot]
     return call(
         functools.partial(back_sum_kernel, len(blocks), len(terms), acc is None, consts[:2]),
         "back_sum",
@@ -475,18 +479,43 @@
     )
 
 
-def back_end_kernel(sizes, where, *refs):
-    scale, (gene_loss, spot_loss, cents, spots_all) = sizes
+def back_own_kernel(scale, where, *refs):
     high_refs, low_refs = refs[0:2], refs[2:4]
-    bhigh, blow, sum_ref, z_ref, dens_ref, sent_ref, got_ref, logit_ref, w_ref, out_ref, loss_ref = refs[4:]
+    bhigh, blow, sum_ref, z_ref, dens_ref, sent_ref, w_ref, out_ref = refs[4:]
     rows, genes = high_refs[0].shape
     value = back_dots(high_refs, low_refs, bhigh, blow, genes)
-    inv, raw = z_ref[0:1, :], z_ref[1:2, :]
+    raw = z_ref[1:2, :]
     dens, mass = sum_ref[0:1, 0:1], sum_ref[1:2, 0:1]
     grad_raw = scale * (1.0 / mass - dens_ref[...] / (dens * raw))
-    column = sent_ref[0:1, :] + got_ref[rows : rows + 1, :] + raw * grad_raw
-    value = value + got_ref[0:rows, :] + w_ref[...] * grad_raw
-    out_ref[...] = jnp.exp(logit_ref[...]) * inv * (value - column)
+    out_ref[...] = value + w_ref[...] * grad_raw - (sent_ref[0:1, :] + raw * grad_raw)
+
+
+def back_own(where, highs, lefts, sums, zinfo, density, sent, weights, scale, rows, tile):
+    twice, spots = highs[0].shape
+    left = pl.BlockSpec((rows, twice // 2), lambda i, ix: (1, 0), pipeline_mode=pl.Buffered(1))
+    specs = [left] * 4 + [by_tile(twice, tile)] * 2
+    specs += [fixed((8, 128)), by_tile(8, tile), by_tile(1, tile), by_tile(8, tile, rows // 8)]
+    specs.append(pl.BlockSpec((rows, 1), lambda i, ix: (ix[0], 0)))
+    args = [lefts[0][0], lefts[1][0], lefts[0][1], lefts[1][1], *highs]
+    args += [sums, zinfo, density, off_chip(sent), weights]
+    return call(
+        functools.partial(back_own_kernel, scale),
+        "back_own",
+        where,
+        args,
+        specs,
+        jax.ShapeDtypeStruct((rows, spots), F32),
+        by_tile(rows, tile),
+        (spots // tile,),
+        limit=VMEM_LIMIT,
+    )
+
+
+def back_end_kernel(loss_scale, where, mine_ref, got_ref, logit_ref, z_ref, sum_ref, out_ref, loss_ref):
+    gene_loss, spot_loss, cents, spots_all = loss_scale
+    rows = out_ref.shape[0]
+    value = mine_ref[...] + got_ref[0:rows, :] - got_ref[rows : rows + 1, :]
+    out_ref[...] = jnp.exp(logit_ref[...]) * z_ref[0:1, :] * value
 
     @pl.when(pl.program_id(0) == 0)
     def _():
@@ -497,23 +526,20 @@
             loss_ref[number] = term[0, 0]
 
 
-def back_end(where, highs, lefts, sums, zinfo, density, sent, got, logits, weights, consts, rows, tile):
-    twice, spots = highs[0].shape
-    left = pl.BlockSpec((rows, twice // 2), lambda i, ix: (1, 0), pipeline_mode=pl.Buffered(1))
-    specs = [left] * 4 + [by_tile(twice, tile)] * 2
-    specs += [fixed((8, 128)), by_tile(8, tile), by_tile(1, tile), by_tile(8, tile, rows // 8), by_tile(rows + 8, tile)]
-    specs += [
-        pl.BlockSpec((rows, tile), lambda i, ix: (ix[0], i)),
-        pl.BlockSpec((rows, 1), lambda i, ix: (ix[0], 0)),
-    ]
-    args = [lefts[0][0], lefts[1][0], lefts[0][1], lefts[1][1], *highs]
-    args += [sums, zinfo, density, sent, got, logits, weights]
-    return call(
-        functools.partial(back_end_kernel, consts[2:]),
+def back_end(where, mine, got, logits, zinfo, sums, loss_scale, rows, tile):
+    spots = mine.shape[1]
+    return call(
+        functools.partial(back_end_kernel, loss_scale),
         "back_end",
         where,
-        args,
-        specs,
+        [mine, got, off_chip(logits), zinfo, sums],
+        [
+            by_tile(rows, tile),
+            by_tile(rows + 8, tile),
+            pl.BlockSpec((rows, tile), lambda i, ix: (ix[0], i)),
+            by_tile(8, tile),
+            fixed((8, 128)),
+        ],
         (jax.ShapeDtypeStruct((rows, spots), F32), jax.ShapeDtypeStruct((3,), F32)),
         (by_tile(rows, tile), pl.BlockSpec(memory_space=pltpu.SMEM)),
         (spots // tile,),
@@ -583,8 +609,9 @@
         acc, o2y, o3, oy, theirs, z_one, logits = tie(acc, o2y, o3, oy, theirs, z_one, logits)
         o3y, o1y, ty = hop(o3, 1), hop(oy, 2), hop(theirs, 1)
         *e_two, zinfo = exp_parts(where, keys(3, 5, 6, 7), KC, logits, weights, dens_row, z_one, True, 2 * tile)
-        acc, o3y, o1y, theirs, zinfo, held = tie(acc, o3y, o1y, theirs, zinfo, x_own[1])
+        o1y, theirs, zinfo, held = tie(o1y, theirs, zinfo, x_own[1])
         t1, t2, x1 = hop(theirs, 2), hop(theirs, 4), send(held)
+        acc, o3y, zinfo = tie(acc, o3y, zinfo)
         pred_own, info = fwd("own_late", [o1y, o2y, o3, o3y], [(*e_two, 4 * KC, 0)], acc, zinfo, x_own)
         own = [mine, oy, o1, o1y, o2, o2y, o3, o3y]
         own_pick = lambda ix, block: [(block ^ ix[2]) == key for key in range(n_spot)]
@@ -599,26 +626,29 @@
         own_pick = None
 
     info_x = swap(info, "gene", 2)
+    predicted = emit(where, pred_own, pick, 2 * tile)
     if ring:
-        pred_own, t1, ty, t2, theirs, x0 = tie(pred_own, t1, ty, t2, theirs, x0)
+        predicted, t1, ty, t2, theirs, x0 = tie(predicted, t1, ty, t2, theirs, x0)
         t2y, t3 = hop(t2, 1), hop(t2, 2)
         acc_other = fwd("other_mid", [theirs, ty, t1, t2], [(*e_one, 4 * KC, 0)], None, None, None)
         acc_other, t2y, t3, t1, x1, held, info_x = tie(acc_other, t2y, t3, t1, x1, x_own[2], info_x)
-        x2, t3y, t1y = send(held), hop(t2y, 2), hop(t1, 1)
+        x2, t3y = send(held), hop(t2y, 2)
         x_got = [x0, x1, x2]
     totals, spot = pack(info, info_x, swap(info + info_x, "gene", 1), zinfo, genes)
     if ring:
         got = swap(totals, "spot", 1)
+        own[0] = after(mine, totals)
+        left_own = rows_left(where, own, rows, own_pick)
+        got, left_own, t1 = tie(got, left_own, t1)
+        t1y = hop(t1, 1)
+        totals = totals + got
+        got = swap(totals, "spot", 2)
         acc_other, totals = tie(acc_other, totals)
         acc_other = fwd("other_more", [t2y, t3], [(*e_two, KC, 1), (*e_two, KC, 2)], acc_other, None, None)
-        acc_other, got, mine = tie(acc_other, got, mine)
-        totals = totals + got
-        got = swap(totals, "spot", 2)
-        own[0] = mine
-        left_own = rows_left(where, own, rows, own_pick)
-        left_own, got, t1y, t3y = tie(left_own, got, t1y, t3y)
+        acc_other, got = tie(acc_other, got)
         totals = totals + got
         more = swap(totals, "spot", 4)
+        t1y, t3y, acc_other = tie(t1y, t3y, acc_other)
         other = [theirs, ty, t1, t1y, t2, t2y, t3, t3y]
         last = ([t1y, t3y], [(*e_two, KC, 0), (*e_two, KC, 3)], acc_other)
     else:
@@ -635,11 +665,9 @@
         where, *last, zinfo, pred_own, (*x_own, *x_got), lefts, totals, more, spot, consts, rows, tile
     )
     got = swap(sent, "gene", 1)
-    predicted = emit(where, after(pred_own, sent), pick, 2 * tile)
-    predicted, got = tie(predicted, got)
-    grad, loss = back_end(
-        where, highs, lefts, sums, zinfo, dens_row, sent, got, logits, weights, consts, rows, tile
-    )
+    rest = back_own(where, highs, lefts, sums, zinfo, dens_row, sent, weights, consts[2], rows, tile)
+    rest, got = tie(rest, got)
+    grad, loss = back_end(where, rest, got, logits, zinfo, sums, consts[3], rows, tile)
     return loss, predicted, grad
 
 

time: 159 us -> 157 us (0.987)
  local copies, waits for them, and re-layouts: 19.4 us -> 4.49 us
  Pallas kernels: 90.8 us -> 100 us
  waiting for transfers between devices: 12.2 us -> 18.3 us
  starting transfers between devices: 32.2 us -> 28.6 us
    unnamed x54 -> x32, local copies, waits for them, and re-layouts: 19.1 us -> 4.12 us
    pallas_call x12 -> x13, Pallas kernels: 90.7 us -> 100 us  [call(): pl.pallas_call(kernel, out_shape=out_shape, grid_spec=pltpu.PrefetchScala...]
    ppermute x24, waiting for transfers between devices: 12.2 us -> 18.3 us  [swap(): lax.ppermute(value, axis, [(i, i ^ bit) for i in range(lax.axis_size(axis...]
    ppermute x24, starting transfers between devices: 32.2 us -> 28.6 us  [swap(): lax.ppermute(value, axis, [(i, i ^ bit) for i in range(lax.axis_size(axis...]
  transfers between devices with their start and end apart: 24 -> 24, of which waited for: 6 -> 7; matrix products, arithmetic and copies ran while one was open for 1% -> 1% of each run, Pallas kernels for 39% -> 49%
where the time goes in v6:
time: 157 us; the launch traced here: 156 us
  Pallas kernels  100 us (64%)
  starting transfers between devices  28.6 us (18%)
  waiting for transfers between devices  18.3 us (12%)
  local copies, waits for them, and re-layouts  4.49 us (3%)
  other arithmetic  2.25 us (1%)
    pallas_call x13, Pallas kernels, call(): pl.pallas_call(kernel, out_shape=out_shape, grid_spec=pltpu.PrefetchScala...  100 us
    ppermute x24, starting transfers between devices, swap(): lax.ppermute(value, axis, [(i, i ^ bit) for i in range(lax.axis_size(axis...  28.6 us
    ppermute x24, waiting for transfers between devices, swap(): lax.ppermute(value, axis, [(i, i ^ bit) for i in range(lax.axis_size(axis...  18.3 us
    unnamed x32, local copies, waits for them, and re-layouts  4.12 us
  transfers between devices with their start and end apart: 24, of which 7 were waited for; matrix products, arithmetic and copies ran while one was open for 1% of the time, Pallas kernels for 49%

profile of v6, /device:TPU:1, one launch (start us, length us, event | category | flops | bytes accessed | tf_op | source)
XLA Modules:
  0.0 156.2 jit_solution(6383528026865093056)
XLA Ops:
  1.7 1.3 fusion.1.refs_0_
  3.0 2.1 %collective-permute-start.1 = (f32[512,256]{1,0:T(8,128)}, f32[512,256]{1,0:T(8,128)S(1)}, u32[]{:S(2)}, u32[]{:S(2)}) collective-permute-start(f32[512,256]{1,0:T(8,128)} %fusion.1.refs_0_), channel_id=1, source_target_pairs={{0,4},{4,0},{8,12},{12,8},{16,20},{20,16},{24,28},{28,24},{1,5},{5... | collective-permute-start | bytes 1572872 | tf_op jit(solution)/shard_map/ppermute | solution.py:551
  5.1 1.2 collective-permute-start.3
  6.3 2.3 %collective-permute-start.2 = (f32[512,256]{1,0:T(8,128)}, f32[512,256]{1,0:T(8,128)}, u32[]{:S(2)}, u32[]{:S(2)}) collective-permute-start(f32[512,256]{1,0:T(8,128)} %fusion.1.refs_0_), channel_id=1, source_target_pairs={{0,16},{4,20},{8,24},{12,28},{16,0},{20,4},{24,8},{28,12},{1,17},{... | collective-permute-start | bytes 1572872 | tf_op jit(solution)/shard_map/ppermute | solution.py:551
  8.6 1.3 collective-permute-start
  10.1 5.0 %turn.1 = (f32[256,2048]{1,0:T(8,128)S(1)}, f32[128,2048]{1,0:T(8,128)S(1)}, f32[128,2048]{1,0:T(8,128)S(1)}) custom-call(s32[3]{0:T(128)S(1)} %pad_add_fusion.where, bf16[512,512]{1,0:T(8,128)(2,1)S(1)} %fusion.pick_ref, f32[2048,512]{1,0:T(8,128)} %x_ref.1), custom_call_target="tpu_custom_call" | custom-call | flops 1000 | bytes 1000 | tf_op jit(solution)/shard_map/turn/pallas_call | solution.py:33
  16.1 1.0 copy-done.8
  20.6 6.2 %exp_parts.2 = (bf16[1024,2048]{1,0:T(8,128)(2,1)S(1)}, bf16[1024,2048]{1,0:T(8,128)(2,1)S(1)}, f32[8,2048]{1,0:T(8,128)S(1)}) custom-call(s32[3]{0:T(128)S(1)} %pad_add_fusion.where, f32[2048,2048]{1,0:T(8,128)} %logit_ref, f32[2048,2048]{1,0:T(8,128)} %logit_ref, f32[2048,2048]{1,0:T(8,128)} %logit_ref, f32[2048,2048]{1,0:T(8,128)} %logit_ref, ...), custom_call_target="tpu_custom_call" | custom-call | flops 1000 | bytes 1000 | tf_op jit(solution)/shard_map/exp_parts/pallas_call | solution.py:33
  26.8 4.8 %collective-permute-done.2.refs_3_.refs_4_ = f32[512,256]{1,0:T(8,128)} collective-permute-done((f32[512,256]{1,0:T(8,128)}, f32[512,256]{1,0:T(8,128)}, u32[]{:S(2)}, u32[]{:S(2)}) %collective-permute-start.2) | collective-permute-done | bytes 524320 | tf_op jit(solution)/shard_map/ppermute | solution.py:551
  31.5 1.4 collective-permute-start.5
  33.2 10.3 %own_early.1.refs_6_ = f32[512,2048]{1,0:T(8,128)S(1)} custom-call(s32[3]{0:T(128)S(1)} %pad_add_fusion.where, f32[512,256]{1,0:T(8,128)} %fusion.1.refs_0_, f32[512,256]{1,0:T(8,128)S(1)} %copy-done.11, f32[512,256]{1,0:T(8,128)} %collective-permute-done.refs_2_, f32[512,256]{1,0:T(8,128)} %collective-permute-done.2.refs_3_.refs_4_, ...), custom_call_target="tpu_custom_call" | custom-call | flops 1000 | bytes 1000 | tf_op jit(solution)/shard_map/own_early/pallas_call | solution.py:33
  43.5 1.4 collective-permute-done.4.refs_1_.refs_5_
  45.4 1.2 collective-permute-start.9
  46.6 6.4 %exp_parts.3 = (bf16[1024,2048]{1,0:T(8,128)(2,1)S(1)}, bf16[1024,2048]{1,0:T(8,128)(2,1)S(1)}, f32[8,2048]{1,0:T(8,128)S(1)}) custom-call(s32[3]{0:T(128)S(1)} %pad_add_fusion.where, f32[2048,2048]{1,0:T(8,128)} %logit_ref, f32[2048,2048]{1,0:T(8,128)} %logit_ref, f32[2048,2048]{1,0:T(8,128)} %logit_ref, f32[2048,2048]{1,0:T(8,128)} %logit_ref, ...), custom_call_target="tpu_custom_call" | custom-call | flops 1000 | bytes 1000 | tf_op jit(solution)/shard_map/exp_parts/pallas_call | solution.py:33
  53.1 2.7 %collective-permute-done.6.refs_0_.refs_3_ = f32[512,256]{1,0:T(8,128)S(1)} collective-permute-done((f32[512,256]{1,0:T(8,128)S(1)}, f32[512,256]{1,0:T(8,128)S(1)}, u32[]{:S(2)}, u32[]{:S(2)}) %collective-permute-start.6) | collective-permute-done | bytes 524320 | tf_op jit(solution)/shard_map/ppermute | solution.py:551
  55.7 5.3 %collective-permute-start.10 = (f32[512,256]{1,0:T(8,128)}, f32[512,256]{1,0:T(8,128)S(1)}, u32[]{:S(2)}, u32[]{:S(2)}) collective-permute-start(f32[512,256]{1,0:T(8,128)} %collective-permute-done.3.refs_0_), channel_id=1, source_target_pairs={{0,16},{4,20},{8,24},{12,28},{16,0},{20,4},{24,8},{28,12},{1,17},{... | collective-permute-start | bytes 1572872 | tf_op jit(solution)/shard_map/ppermute | solution.py:551
  61.9 12.0 %own_late.1 = (f32[512,2048]{1,0:T(8,128)}, f32[16,2048]{1,0:T(8,128)S(1)}) custom-call(s32[3]{0:T(128)S(1)} %pad_add_fusion.where, f32[512,256]{1,0:T(8,128)S(1)} %collective-permute-done.6.refs_0_.refs_3_, f32[512,256]{1,0:T(8,128)S(1)} %collective-permute-done.4.refs_1_.refs_5_, f32[512,256]{1,0:T(8,128)S(1)} %collective-permute-done.5.refs_2_.refs_6_, ...), custom_call_target="tpu_custom_call" | custom-call | flops 1000 | bytes 1000 | tf_op jit(solution)/shard_map/own_late/pallas_call | solution.py:33
  73.9 6.1 %emit.1 = f32[2048,512]{1,0:T(8,128)} custom-call(s32[3]{0:T(128)S(1)} %pad_add_fusion.where, f32[512,2048]{1,0:T(8,128)} %get-tuple-element.120.pred_ref.refs_8_, bf16[512,512]{1,0:T(8,128)(2,1)S(1)} %copy-done.5), custom_call_target="tpu_custom_call" | custom-call | flops 1000 | bytes 1000 | tf_op jit(solution)/shard_map/emit/pallas_call | solution.py:33
  80.0 4.4 %collective-permute-done.10.refs_3_.refs_4_ = f32[512,256]{1,0:T(8,128)S(1)} collective-permute-done((f32[512,256]{1,0:T(8,128)}, f32[512,256]{1,0:T(8,128)S(1)}, u32[]{:S(2)}, u32[]{:S(2)}) %collective-permute-start.10) | collective-permute-done | bytes 524320 | tf_op jit(solution)/shard_map/ppermute | solution.py:551
  85.0 10.1 %other_mid.1.refs_6_ = f32[512,2048]{1,0:T(8,128)S(1)} custom-call(s32[3]{0:T(128)S(1)} %pad_add_fusion.where, f32[512,256]{1,0:T(8,128)} %collective-permute-done.3.refs_0_, f32[512,256]{1,0:T(8,128)S(1)} %collective-permute-done.9.refs_1_, f32[512,256]{1,0:T(8,128)S(1)} %collective-permute-done.8.refs_2_, ...), custom_call_target="tpu_custom_call" | custom-call | flops 1000 | bytes 1000 | tf_op jit(solution)/shard_map/other_mid/pallas_call | solution.py:33
  96.2 1.2 collective-permute-start.22
  97.4 3.5 %collective-permute-start.16 = (f32[16,2048]{1,0:T(8,128)S(1)}, f32[16,2048]{1,0:T(8,128)S(1)}, u32[]{:S(2)}, u32[]{:S(2)}) collective-permute-start(f32[16,2048]{1,0:T(8,128)S(1)} %add.9), channel_id=1, source_target_pairs={{0,1},{1,0},{2,3},{3,2},{4,5},{5,4},{6,7},{7,6},{8,9},{9,8},{10,11... | collective-permute-start | bytes 393224 | tf_op jit(solution)/shard_map/ppermute | solution.py:551
  102.0 1.2 collective-permute-start.17
  104.2 2.4 %rows_left.2 = (bf16[1024,512]{1,0:T(8,128)(2,1)S(1)}, bf16[1024,512]{1,0:T(8,128)(2,1)S(1)}) custom-call(s32[3]{0:T(128)S(1)} %pad_add_fusion.where, f32[512,256]{1,0:T(8,128)} %fusion.1.refs_0_, f32[512,256]{1,0:T(8,128)S(1)} %copy-done.11, f32[512,256]{1,0:T(8,128)} %collective-permute-done.refs_2_, ...), custom_call_target="tpu_custom_call" | custom-call | flops 1000 | bytes 1000 | tf_op jit(solution)/shard_map/rows_left/pallas_call | solution.py:33
  107.4 6.3 %other_more.1.refs_6_ = f32[512,2048]{1,0:T(8,128)} custom-call(s32[3]{0:T(128)S(1)} %pad_add_fusion.where, f32[512,256]{1,0:T(8,128)S(1)} %collective-permute-done.12.refs_0_.refs_5_, f32[512,256]{1,0:T(8,128)S(1)} %collective-permute-done.13.refs_1_.refs_6_, bf16[1024,2048]{1,0:T(8,128)(2,1)S(1)} %get-tuple-element.113.refs_4_.refs_2_.refs_3_, ...), custom_call_target="tpu_custom_call" | custom-call | flops 1000 | bytes 1000 | tf_op jit(solution)/shard_map/other_more/pallas_call | solution.py:33
  113.7 3.1 %collective-permute-done.20 = f32[8,1024]{1,0:T(8,128)S(1)} collective-permute-done((f32[8,1024]{1,0:T(8,128)S(1)}, f32[8,1024]{1,0:T(8,128)S(1)}, u32[]{:S(2)}, u32[]{:S(2)}) %collective-permute-start.20) | collective-permute-done | bytes 32800 | tf_op jit(solution)/shard_map/ppermute | solution.py:551
  116.8 1.5 collective-permute-start.21
  119.3 2.4 %rows_left.3 = (bf16[1024,512]{1,0:T(8,128)(2,1)S(1)}, bf16[1024,512]{1,0:T(8,128)(2,1)S(1)}) custom-call(s32[3]{0:T(128)S(1)} %pad_add_fusion.where, f32[512,256]{1,0:T(8,128)} %collective-permute-done.3.refs_0_, f32[512,256]{1,0:T(8,128)S(1)} %collective-permute-done.9.refs_1_, f32[512,256]{1,0:T(8,128)S(1)} %collective-permute-done.8.refs_2_, ...), custom_call_target="tpu_custom_call" | custom-call | flops 1000 | bytes 1000 | tf_op jit(solution)/shard_map/rows_left/pallas_call | solution.py:33
  121.8 17.8 %back_sum.1 = (f32[520,2048]{1,0:T(8,128)}, bf16[1024,2048]{1,0:T(8,128)(2,1)S(1)}, bf16[1024,2048]{1,0:T(8,128)(2,1)S(1)}, f32[8,128]{1,0:T(8,128)S(1)}) custom-call(s32[3]{0:T(128)S(1)} %pad_add_fusion.where, f32[512,256]{1,0:T(8,128)S(1)} %collective-permute-done.18.refs_3_.refs_0_, f32[512,256]{1,0:T(8,128)S(1)} %collective-permute-done.19.refs_7_.refs_1_, ...), custom_call_target="tpu_custom_call" | custom-call | flops 1000 | bytes 1000 | tf_op jit(solution)/shard_map/back_sum/pallas_call | solution.py:33
  139.6 1.6 %collective-permute-start.23 = (f32[520,2048]{1,0:T(8,128)}, f32[520,2048]{1,0:T(8,128)S(1)}, u32[]{:S(2)}, u32[]{:S(2)}) collective-permute-start(f32[520,2048]{1,0:T(8,128)} %get-tuple-element.159.refs_9_), channel_id=1, source_target_pairs={{0,1},{1,0},{2,3},{3,2},{4,5},{5,4},{6,7},{7,6},{8,9},{9,8},{10,11... | collective-permute-start | bytes 12779528 | tf_op jit(solution)/shard_map/ppermute | solution.py:551
  141.2 9.2 %back_own.1.mine_ref = f32[512,2048]{1,0:T(8,128)S(1)} custom-call(s32[3]{0:T(128)S(1)} %pad_add_fusion.where, bf16[1024,512]{1,0:T(8,128)(2,1)S(1)} %get-tuple-element.133.refs_15_.refs_0_, bf16[1024,512]{1,0:T(8,128)(2,1)S(1)} %get-tuple-element.147.refs_16_.refs_1_, bf16[1024,512]{1,0:T(8,128)(2,1)S(1)} %get-tuple-element.148.refs_17_.refs_2_, ...), custom_call_target="tpu_custom_call" | custom-call | flops 1000 | bytes 1000 | tf_op jit(solution)/shard_map/back_own/pallas_call | solution.py:33
  150.4 5.8 %back_end.1 = (f32[512,2048]{1,0:T(8,128)}, f32[3]{0:T(128)}) custom-call(s32[3]{0:T(128)S(1)} %pad_add_fusion.where, f32[512,2048]{1,0:T(8,128)S(1)} %back_own.1.mine_ref, f32[520,2048]{1,0:T(8,128)S(1)} %collective-permute-done.23.got_ref, f32[2048,2048]{1,0:T(8,128)} %logit_ref, f32[8,2048]{1,0:T(8,128)S(1)} %get-tuple-element.116.refs_7_.z_ref, ...), custom_call_target="tpu_custom_call" | custom-call | flops 1000 | bytes 1000 | tf_op jit(solution)/shard_map/back_end/pallas_call | solution.py:33
  (72 shorter events, 12.7 us)
Async XLA Ops:
  0.6 18.3 %copy-start.15 = (s32[2048]{0:T(1024)S(1)}, s32[2048]{0:T(1024)}, u32[]{:S(2)}) copy-start(s32[2048]{0:T(1024)} %param.9) | copy-start | bytes 24580
  0.7 19.9 %copy-start.14 = (f32[2048]{0:T(1024)S(1)}, f32[2048]{0:T(1024)}, u32[]{:S(2)}) copy-start(f32[2048]{0:T(1024)} %param.10) | copy-start | bytes 24580
  3.0 14.2 %collective-permute-start.1 = (f32[512,256]{1,0:T(8,128)}, f32[512,256]{1,0:T(8,128)S(1)}, u32[]{:S(2)}, u32[]{:S(2)}) collective-permute-start(f32[512,256]{1,0:T(8,128)} %fusion.1.refs_0_), channel_id=1, source_target_pairs={{0,4},{4,0},{8,12},{12,8},{16,20},{20,16},{24,28},{28,24},{1,5},{5... | collective-permute-start | bytes 1572872 | tf_op jit(solution)/shard_map/ppermute | solution.py:551
  5.1 21.7 %collective-permute-start.3 = (f32[512,256]{1,0:T(8,128)}, f32[512,256]{1,0:T(8,128)}, u32[]{:S(2)}, u32[]{:S(2)}) collective-permute-start(f32[512,256]{1,0:T(8,128)} %fusion.1.refs_0_), channel_id=1, source_target_pairs={{0,2},{1,3},{2,0},{3,1},{4,6},{5,7},{6,4},{7,5},{8,10},{9,11},{10,... | collective-permute-start | bytes 1572872 | tf_op jit(solution)/shard_map/ppermute | solution.py:551
  6.3 25.3 %collective-permute-start.2 = (f32[512,256]{1,0:T(8,128)}, f32[512,256]{1,0:T(8,128)}, u32[]{:S(2)}, u32[]{:S(2)}) collective-permute-start(f32[512,256]{1,0:T(8,128)} %fusion.1.refs_0_), channel_id=1, source_target_pairs={{0,16},{4,20},{8,24},{12,28},{16,0},{20,4},{24,8},{28,12},{1,17},{... | collective-permute-start | bytes 1572872 | tf_op jit(solution)/shard_map/ppermute | solution.py:551
  8.6 23.0 %collective-permute-start = (f32[512,256]{1,0:T(8,128)}, f32[512,256]{1,0:T(8,128)}, u32[]{:S(2)}, u32[]{:S(2)}) collective-permute-start(f32[512,256]{1,0:T(8,128)} %fusion.1.refs_0_), channel_id=1, source_target_pairs={{0,8},{4,12},{8,0},{12,4},{16,24},{20,28},{24,16},{28,20},{1,9},{5... | collective-permute-start | bytes 1572872 | tf_op jit(solution)/shard_map/ppermute | solution.py:551
  17.9 66.5 %collective-permute-start.11 = (f32[256,2048]{1,0:T(8,128)S(1)}, f32[256,2048]{1,0:T(8,128)}, u32[]{:S(2)}, u32[]{:S(2)}) collective-permute-start(f32[256,2048]{1,0:T(8,128)S(1)} %get-tuple-element.117.refs_8_.refs_9_), channel_id=1, source_target_pairs={{0,2},{1,3},{2,0},{3,1},{4,6},{5,7},{6,4},{7,5},{8,10},{9,11},{10,... | collective-permute-start | bytes 6291464 | tf_op jit(solution)/shard_map/ppermute | solution.py:551
  20.6 12.6 %copy-start.11 = (f32[512,256]{1,0:T(8,128)S(1)}, f32[512,256]{1,0:T(8,128)}, u32[]{:S(2)}) copy-start(f32[512,256]{1,0:T(8,128)} %copy-done.10) | copy-start | bytes 1572868
  31.5 11.9 %collective-permute-start.5 = (f32[512,256]{1,0:T(8,128)}, f32[512,256]{1,0:T(8,128)S(1)}, u32[]{:S(2)}, u32[]{:S(2)}) collective-permute-start(f32[512,256]{1,0:T(8,128)} %collective-permute-done.2.refs_3_.refs_4_), channel_id=1, source_target_pairs={{0,8},{4,12},{8,0},{12,4},{16,24},{20,28},{24,16},{28,20},{1,9},{5... | collective-permute-start | bytes 1572872 | tf_op jit(solution)/shard_map/ppermute | solution.py:551
  33.0 11.9 %collective-permute-start.4 = (f32[512,256]{1,0:T(8,128)}, f32[512,256]{1,0:T(8,128)S(1)}, u32[]{:S(2)}, u32[]{:S(2)}) collective-permute-start(f32[512,256]{1,0:T(8,128)} %collective-permute-done.2.refs_3_.refs_4_), channel_id=1, source_target_pairs={{0,4},{4,0},{8,12},{12,8},{16,20},{20,16},{24,28},{28,24},{1,5},{5... | collective-permute-start | bytes 1572872 | tf_op jit(solution)/shard_map/ppermute | solution.py:551
  43.5 18.2 %copy-start.7 = (f32[128,2048]{1,0:T(8,128)S(1)}, f32[128,2048]{1,0:T(8,128)}, u32[]{:S(2)}) copy-start(f32[128,2048]{1,0:T(8,128)} %copy-done.6) | copy-start | bytes 3145732
  43.5 18.5 %copy-start.9 = (f32[128,2048]{1,0:T(8,128)S(1)}, f32[128,2048]{1,0:T(8,128)}, u32[]{:S(2)}) copy-start(f32[128,2048]{1,0:T(8,128)} %copy-done.8) | copy-start | bytes 3145732
  44.9 10.9 %collective-permute-start.6 = (f32[512,256]{1,0:T(8,128)S(1)}, f32[512,256]{1,0:T(8,128)S(1)}, u32[]{:S(2)}, u32[]{:S(2)}) collective-permute-start(f32[512,256]{1,0:T(8,128)S(1)} %copy-done.11), channel_id=1, source_target_pairs={{0,8},{4,12},{8,0},{12,4},{16,24},{20,28},{24,16},{28,20},{1,9},{5... | collective-permute-start | bytes 1572872 | tf_op jit(solution)/shard_map/ppermute | solution.py:551
  45.1 16.5 %collective-permute-start.7 = (f32[512,256]{1,0:T(8,128)S(1)}, f32[512,256]{1,0:T(8,128)S(1)}, u32[]{:S(2)}, u32[]{:S(2)}) collective-permute-start(f32[512,256]{1,0:T(8,128)S(1)} %collective-permute-done.5.refs_2_.refs_6_), channel_id=1, source_target_pairs={{0,4},{4,0},{8,12},{12,8},{16,20},{20,16},{24,28},{28,24},{1,5},{5... | collective-permute-start | bytes 1572872 | tf_op jit(solution)/shard_map/ppermute | solution.py:551
  45.4 34.7 %collective-permute-start.9 = (f32[512,256]{1,0:T(8,128)}, f32[512,256]{1,0:T(8,128)S(1)}, u32[]{:S(2)}, u32[]{:S(2)}) collective-permute-start(f32[512,256]{1,0:T(8,128)} %collective-permute-done.3.refs_0_), channel_id=1, source_target_pairs={{0,4},{4,0},{8,12},{12,8},{16,20},{20,16},{24,28},{28,24},{1,5},{5... | collective-permute-start | bytes 1572872 | tf_op jit(solution)/shard_map/ppermute | solution.py:551
  53.0 54.3 %copy-start.2 = (bf16[1024,2048]{1,0:T(8,128)(2,1)}, bf16[1024,2048]{1,0:T(8,128)(2,1)S(1)}, u32[]{:S(2)}) copy-start(bf16[1024,2048]{1,0:T(8,128)(2,1)S(1)} %get-tuple-element.114.refs_5_.refs_4_) | copy-start | bytes 12582916
  55.7 28.7 %collective-permute-start.10 = (f32[512,256]{1,0:T(8,128)}, f32[512,256]{1,0:T(8,128)S(1)}, u32[]{:S(2)}, u32[]{:S(2)}) collective-permute-start(f32[512,256]{1,0:T(8,128)} %collective-permute-done.3.refs_0_), channel_id=1, source_target_pairs={{0,16},{4,20},{8,24},{12,28},{16,0},{20,4},{24,8},{28,12},{1,17},{... | collective-permute-start | bytes 1572872 | tf_op jit(solution)/shard_map/ppermute | solution.py:551
  61.0 23.4 %collective-permute-start.8 = (f32[512,256]{1,0:T(8,128)}, f32[512,256]{1,0:T(8,128)S(1)}, u32[]{:S(2)}, u32[]{:S(2)}) collective-permute-start(f32[512,256]{1,0:T(8,128)} %collective-permute-done.3.refs_0_), channel_id=1, source_target_pairs={{0,8},{4,12},{8,0},{12,4},{16,24},{20,28},{24,16},{28,20},{1,9},{5... | collective-permute-start | bytes 1572872 | tf_op jit(solution)/shard_map/ppermute | solution.py:551
  61.7 33.5 %collective-permute-start.14 = (f32[128,2048]{1,0:T(8,128)S(1)}, f32[128,2048]{1,0:T(8,128)S(1)}, u32[]{:S(2)}, u32[]{:S(2)}) collective-permute-start(f32[128,2048]{1,0:T(8,128)S(1)} %copy-done.7), channel_id=1, source_target_pairs={{0,2},{1,3},{2,0},{3,1},{4,6},{5,7},{6,4},{7,5},{8,10},{9,11},{10,... | collective-permute-start | bytes 3145736 | tf_op jit(solution)/shard_map/ppermute | solution.py:551
  61.9 12.0 %copy-start.5 = (bf16[512,512]{1,0:T(8,128)(2,1)S(1)}, bf16[512,512]{1,0:T(8,128)(2,1)}, u32[]{:S(2)}) copy-start(bf16[512,512]{1,0:T(8,128)(2,1)} %copy-done.4) | copy-start | bytes 1572868
  84.5 11.7 %collective-permute-start.13 = (f32[512,256]{1,0:T(8,128)S(1)}, f32[512,256]{1,0:T(8,128)S(1)}, u32[]{:S(2)}, u32[]{:S(2)}) collective-permute-start(f32[512,256]{1,0:T(8,128)S(1)} %collective-permute-done.10.refs_3_.refs_4_), channel_id=1, source_target_pairs={{0,8},{4,12},{8,0},{12,4},{16,24},{20,28},{24,16},{28,20},{1,9},{5... | collective-permute-start | bytes 1572872 | tf_op jit(solution)/shard_map/ppermute | solution.py:551
  84.5 11.7 %collective-permute-start.12 = (f32[512,256]{1,0:T(8,128)S(1)}, f32[512,256]{1,0:T(8,128)S(1)}, u32[]{:S(2)}, u32[]{:S(2)}) collective-permute-start(f32[512,256]{1,0:T(8,128)S(1)} %collective-permute-done.10.refs_3_.refs_4_), channel_id=1, source_target_pairs={{0,4},{4,0},{8,12},{12,8},{16,20},{20,16},{24,28},{28,24},{1,5},{5... | collective-permute-start | bytes 1572872 | tf_op jit(solution)/shard_map/ppermute | solution.py:551
  84.8 10.4 %collective-permute-start.15 = (f32[16,2048]{1,0:T(8,128)S(1)}, f32[16,2048]{1,0:T(8,128)S(1)}, u32[]{:S(2)}, u32[]{:S(2)}) collective-permute-start(f32[16,2048]{1,0:T(8,128)S(1)} %get-tuple-element.119.mine_ref), channel_id=1, source_target_pairs={{0,2},{1,3},{2,0},{3,1},{4,6},{5,7},{6,4},{7,5},{8,10},{9,11},{10,... | collective-permute-start | bytes 393224 | tf_op jit(solution)/shard_map/ppermute | solution.py:551
  96.2 25.6 %collective-permute-start.22 = (f32[128,2048]{1,0:T(8,128)S(1)}, f32[128,2048]{1,0:T(8,128)S(1)}, u32[]{:S(2)}, u32[]{:S(2)}) collective-permute-start(f32[128,2048]{1,0:T(8,128)S(1)} %copy-done.9), channel_id=1, source_target_pairs={{0,2},{1,3},{2,0},{3,1},{4,6},{5,7},{6,4},{7,5},{8,10},{9,11},{10,... | collective-permute-start | bytes 3145736 | tf_op jit(solution)/shard_map/ppermute | solution.py:551
  97.4 4.5 %collective-permute-start.16 = (f32[16,2048]{1,0:T(8,128)S(1)}, f32[16,2048]{1,0:T(8,128)S(1)}, u32[]{:S(2)}, u32[]{:S(2)}) collective-permute-start(f32[16,2048]{1,0:T(8,128)S(1)} %add.9), channel_id=1, source_target_pairs={{0,1},{1,0},{2,3},{3,2},{4,5},{5,4},{6,7},{7,6},{8,9},{9,8},{10,11... | collective-permute-start | bytes 393224 | tf_op jit(solution)/shard_map/ppermute | solution.py:551
  102.0 4.7 %collective-permute-start.17 = (f32[8,1024]{1,0:T(8,128)S(1)}, f32[8,1024]{1,0:T(8,128)S(1)}, u32[]{:S(2)}, u32[]{:S(2)}) collective-permute-start(f32[8,1024]{1,0:T(8,128)S(1)} %get-tuple-element.128), channel_id=1, source_target_pairs={{0,4},{4,0},{8,12},{12,8},{16,20},{20,16},{24,28},{28,24},{1,5},{5... | collective-permute-start | bytes 98312 | tf_op jit(solution)/shard_map/ppermute | solution.py:551
  103.3 15.1 %collective-permute-start.19 = (f32[512,256]{1,0:T(8,128)S(1)}, f32[512,256]{1,0:T(8,128)S(1)}, u32[]{:S(2)}, u32[]{:S(2)}) collective-permute-start(f32[512,256]{1,0:T(8,128)S(1)} %collective-permute-done.12.refs_0_.refs_5_), channel_id=1, source_target_pairs={{0,8},{4,12},{8,0},{12,4},{16,24},{20,28},{24,16},{28,20},{1,9},{5... | collective-permute-start | bytes 1572872 | tf_op jit(solution)/shard_map/ppermute | solution.py:551
  106.7 12.6 %collective-permute-start.18 = (f32[512,256]{1,0:T(8,128)S(1)}, f32[512,256]{1,0:T(8,128)S(1)}, u32[]{:S(2)}, u32[]{:S(2)}) collective-permute-start(f32[512,256]{1,0:T(8,128)S(1)} %collective-permute-done.8.refs_2_), channel_id=1, source_target_pairs={{0,4},{4,0},{8,12},{12,8},{16,20},{20,16},{24,28},{28,24},{1,5},{5... | collective-permute-start | bytes 1572872 | tf_op jit(solution)/shard_map/ppermute | solution.py:551
  106.9 10.0 %collective-permute-start.20 = (f32[8,1024]{1,0:T(8,128)S(1)}, f32[8,1024]{1,0:T(8,128)S(1)}, u32[]{:S(2)}, u32[]{:S(2)}) collective-permute-start(f32[8,1024]{1,0:T(8,128)S(1)} %add.10), channel_id=1, source_target_pairs={{0,8},{4,12},{8,0},{12,4},{16,24},{20,28},{24,16},{28,20},{1,9},{5... | collective-permute-start | bytes 98312 | tf_op jit(solution)/shard_map/ppermute | solution.py:551
  107.4 14.4 %copy-start.13 = (f32[128,2048]{1,0:T(8,128)S(1)}, f32[128,2048]{1,0:T(8,128)}, u32[]{:S(2)}) copy-start(f32[128,2048]{1,0:T(8,128)} %copy-done.12) | copy-start | bytes 3145732
  116.8 4.9 %collective-permute-start.21 = (f32[8,1024]{1,0:T(8,128)S(1)}, f32[8,1024]{1,0:T(8,128)S(1)}, u32[]{:S(2)}, u32[]{:S(2)}) collective-permute-start(f32[8,1024]{1,0:T(8,128)S(1)} %add.11.refs_19_), channel_id=1, source_target_pairs={{0,16},{4,20},{8,24},{12,28},{16,0},{20,4},{24,8},{28,12},{1,17},{... | collective-permute-start | bytes 98312 | tf_op jit(solution)/shard_map/ppermute | solution.py:551
  139.6 10.8 %collective-permute-start.23 = (f32[520,2048]{1,0:T(8,128)}, f32[520,2048]{1,0:T(8,128)S(1)}, u32[]{:S(2)}, u32[]{:S(2)}) collective-permute-start(f32[520,2048]{1,0:T(8,128)} %get-tuple-element.159.refs_9_), channel_id=1, source_target_pairs={{0,1},{1,0},{2,3},{3,2},{4,5},{5,4},{6,7},{7,6},{8,9},{9,8},{10,11... | collective-permute-start | bytes 12779528 | tf_op jit(solution)/shard_map/ppermute | solution.py:551
  (8 other events, 28.9 us)

commit v7 on v6

--- a/solution.py
+++ b/solution.py
@@ -8,7 +8,7 @@
 
 NB = 4
 XS = 3
-XCUT = (0, 2, 3, NB)
+XCUT = (0, 8, 11, 16)
 EPS = 1e-06
 BF = jnp.bfloat16
 F32 = jnp.float32
@@ -149,7 +149,7 @@
 
 
 def heights(genes):
-    return [(b - a) * genes // NB for a, b in zip(XCUT, XCUT[1:])]
+    return [(b - a) * genes // XCUT[-1] for a, b in zip(XCUT, XCUT[1:])]
 
 
 def turn(where, pick, x, tile):
@@ -167,9 +167,14 @@
 
 
 def of_batch(refs, batch, width):
-    place = sum(batch >= cut for cut in XCUT[1:])
-    start = (batch - XCUT[place]) * width
-    return refs[place][start : start + width, :]
+    start, stop, at, pieces = batch * width, (batch + 1) * width, 0, []
+    for ref in refs[:XS]:
+        height = ref.shape[0]
+        low, high = max(start, at), min(stop, at + height)
+        if low < high:
+            pieces.append(ref[low - at : high - at, :])
+        at += height
+    return pieces[0] if len(pieces) == 1 else jnp.concatenate(pieces, axis=0)
 
 
 def load_left(refs, high, low):
@@ -628,27 +633,28 @@
     info_x = swap(info, "gene", 2)
     predicted = emit(where, pred_own, pick, 2 * tile)
     if ring:
-        predicted, t1, ty, t2, theirs, x0 = tie(predicted, t1, ty, t2, theirs, x0)
-        t2y, t3 = hop(t2, 1), hop(t2, 2)
-        acc_other = fwd("other_mid", [theirs, ty, t1, t2], [(*e_one, 4 * KC, 0)], None, None, None)
-        acc_other, t2y, t3, t1, x1, held, info_x = tie(acc_other, t2y, t3, t1, x1, x_own[2], info_x)
-        x2, t3y = send(held), hop(t2y, 2)
+        predicted, info_x, t1, ty, t2, theirs, x0, x1, held = tie(
+            predicted, info_x, t1, ty, t2, theirs, x0, x1, x_own[2]
+        )
+        t2y, t3, x2, t1y = hop(t2, 1), hop(t2, 2), send(held), hop(t1, 1)
         x_got = [x0, x1, x2]
     totals, spot = pack(info, info_x, swap(info + info_x, "gene", 1), zinfo, genes)
     if ring:
+        got = swap(totals, "spot", 2)
+        theirs, totals = tie(theirs, totals)
+        acc_other = fwd("other_mid", [theirs, ty, t1, t2], [(*e_one, 4 * KC, 0)], None, None, None)
+        acc_other, got, t2y, t3 = tie(acc_other, got, t2y, t3)
+        totals = totals + got
         got = swap(totals, "spot", 1)
-        own[0] = after(mine, totals)
-        left_own = rows_left(where, own, rows, own_pick)
-        got, left_own, t1 = tie(got, left_own, t1)
-        t1y = hop(t1, 1)
-        totals = totals + got
-        got = swap(totals, "spot", 2)
+        t3y = hop(t2y, 2)
         acc_other, totals = tie(acc_other, totals)
         acc_other = fwd("other_more", [t2y, t3], [(*e_two, KC, 1), (*e_two, KC, 2)], acc_other, None, None)
-        acc_other, got = tie(acc_other, got)
+        acc_other, got, mine = tie(acc_other, got, mine)
         totals = totals + got
         more = swap(totals, "spot", 4)
-        t1y, t3y, acc_other = tie(t1y, t3y, acc_other)
+        own[0] = mine
+        left_own = rows_left(where, own, rows, own_pick)
+        t1y, t3y, left_own = tie(t1y, t3y, left_own)
         other = [theirs, ty, t1, t1y, t2, t2y, t3, t3y]
         last = ([t1y, t3y], [(*e_two, KC, 0), (*e_two, KC, 3)], acc_other)
     else:

time: 157 us -> 155 us (0.987)
  waiting for transfers between devices: 18.3 us -> 15.1 us
    ppermute x24, waiting for transfers between devices: 18.3 us -> 15.1 us  [swap(): lax.ppermute(value, axis, [(i, i ^ bit) for i in range(lax.axis_size(axis...]
  transfers between devices with their start and end apart: 24 -> 24, of which waited for: 7 -> 7; matrix products, arithmetic and copies ran while one was open for 1% -> 1% of each run, Pallas kernels for 49% -> 50%
where the time goes in v7:
time: 155 us; the launch traced here: 154 us
  Pallas kernels  100 us (65%)
  starting transfers between devices  30.1 us (19%)
  waiting for transfers between devices  15.1 us (10%)
  local copies, waits for them, and re-layouts  4.34 us (3%)
  other arithmetic  2.24 us (1%)
    pallas_call x13, Pallas kernels, call(): pl.pallas_call(kernel, out_shape=out_shape, grid_spec=pltpu.PrefetchScala...  100 us
    ppermute x24, starting transfers between devices, swap(): lax.ppermute(value, axis, [(i, i ^ bit) for i in range(lax.axis_size(axis...  30.1 us
    ppermute x24, waiting for transfers between devices, swap(): lax.ppermute(value, axis, [(i, i ^ bit) for i in range(lax.axis_size(axis...  15.1 us
    unnamed x32, local copies, waits for them, and re-layouts  3.98 us
  transfers between devices with their start and end apart: 24, of which 7 were waited for; matrix products, arithmetic and copies ran while one was open for 1% of the time, Pallas kernels for 50%

profile of v7, /device:TPU:1, one launch (start us, length us, event | category | flops | bytes accessed | tf_op | source)
XLA Modules:
  0.0 154.2 jit_solution(10605272985949786941)
XLA Ops:
  1.7 1.3 fusion.1.refs_0_
  3.0 2.1 %collective-permute-start.1 = (f32[512,256]{1,0:T(8,128)}, f32[512,256]{1,0:T(8,128)S(1)}, u32[]{:S(2)}, u32[]{:S(2)}) collective-permute-start(f32[512,256]{1,0:T(8,128)} %fusion.1.refs_0_), channel_id=1, source_target_pairs={{0,4},{4,0},{8,12},{12,8},{16,20},{20,16},{24,28},{28,24},{1,5},{5... | collective-permute-start | bytes 1572872 | tf_op jit(solution)/shard_map/ppermute | solution.py:556
  5.1 1.2 collective-permute-start.3
  6.3 2.3 %collective-permute-start.2 = (f32[512,256]{1,0:T(8,128)}, f32[512,256]{1,0:T(8,128)}, u32[]{:S(2)}, u32[]{:S(2)}) collective-permute-start(f32[512,256]{1,0:T(8,128)} %fusion.1.refs_0_), channel_id=1, source_target_pairs={{0,16},{4,20},{8,24},{12,28},{16,0},{20,4},{24,8},{28,12},{1,17},{... | collective-permute-start | bytes 1572872 | tf_op jit(solution)/shard_map/ppermute | solution.py:556
  8.6 1.3 collective-permute-start
  10.1 5.0 %turn.1 = (f32[256,2048]{1,0:T(8,128)S(1)}, f32[96,2048]{1,0:T(8,128)S(1)}, f32[160,2048]{1,0:T(8,128)S(1)}) custom-call(s32[3]{0:T(128)S(1)} %pad_add_fusion.where, bf16[512,512]{1,0:T(8,128)(2,1)S(1)} %fusion.pick_ref, f32[2048,512]{1,0:T(8,128)} %x_ref.1), custom_call_target="tpu_custom_call" | custom-call | flops 1000 | bytes 1000 | tf_op jit(solution)/shard_map/turn/pallas_call | solution.py:33
  20.6 6.2 %exp_parts.2 = (bf16[1024,2048]{1,0:T(8,128)(2,1)S(1)}, bf16[1024,2048]{1,0:T(8,128)(2,1)S(1)}, f32[8,2048]{1,0:T(8,128)S(1)}) custom-call(s32[3]{0:T(128)S(1)} %pad_add_fusion.where, f32[2048,2048]{1,0:T(8,128)} %logit_ref, f32[2048,2048]{1,0:T(8,128)} %logit_ref, f32[2048,2048]{1,0:T(8,128)} %logit_ref, f32[2048,2048]{1,0:T(8,128)} %logit_ref, ...), custom_call_target="tpu_custom_call" | custom-call | flops 1000 | bytes 1000 | tf_op jit(solution)/shard_map/exp_parts/pallas_call | solution.py:33
  26.8 4.8 %collective-permute-done.2.refs_3_.refs_4_ = f32[512,256]{1,0:T(8,128)} collective-permute-done((f32[512,256]{1,0:T(8,128)}, f32[512,256]{1,0:T(8,128)}, u32[]{:S(2)}, u32[]{:S(2)}) %collective-permute-start.2) | collective-permute-done | bytes 524320 | tf_op jit(solution)/shard_map/ppermute | solution.py:556
  31.5 1.4 collective-permute-start.5
  33.2 10.3 %own_early.1.refs_6_ = f32[512,2048]{1,0:T(8,128)S(1)} custom-call(s32[3]{0:T(128)S(1)} %pad_add_fusion.where, f32[512,256]{1,0:T(8,128)} %fusion.1.refs_0_, f32[512,256]{1,0:T(8,128)S(1)} %copy-done.11, f32[512,256]{1,0:T(8,128)} %collective-permute-done.refs_2_, f32[512,256]{1,0:T(8,128)} %collective-permute-done.2.refs_3_.refs_4_, ...), custom_call_target="tpu_custom_call" | custom-call | flops 1000 | bytes 1000 | tf_op jit(solution)/shard_map/own_early/pallas_call | solution.py:33
  43.5 1.4 collective-permute-done.4.refs_1_.refs_5_
  45.4 6.4 %exp_parts.3 = (bf16[1024,2048]{1,0:T(8,128)(2,1)S(1)}, bf16[1024,2048]{1,0:T(8,128)(2,1)S(1)}, f32[8,2048]{1,0:T(8,128)S(1)}) custom-call(s32[3]{0:T(128)S(1)} %pad_add_fusion.where, f32[2048,2048]{1,0:T(8,128)} %logit_ref, f32[2048,2048]{1,0:T(8,128)} %logit_ref, f32[2048,2048]{1,0:T(8,128)} %logit_ref, f32[2048,2048]{1,0:T(8,128)} %logit_ref, ...), custom_call_target="tpu_custom_call" | custom-call | flops 1000 | bytes 1000 | tf_op jit(solution)/shard_map/exp_parts/pallas_call | solution.py:33
  51.8 3.9 %collective-permute-done.6.refs_0_.refs_3_ = f32[512,256]{1,0:T(8,128)S(1)} collective-permute-done((f32[512,256]{1,0:T(8,128)S(1)}, f32[512,256]{1,0:T(8,128)S(1)}, u32[]{:S(2)}, u32[]{:S(2)}) %collective-permute-start.6) | collective-permute-done | bytes 524320 | tf_op jit(solution)/shard_map/ppermute | solution.py:556
  56.2 5.3 %collective-permute-start.11 = (f32[512,256]{1,0:T(8,128)}, f32[512,256]{1,0:T(8,128)S(1)}, u32[]{:S(2)}, u32[]{:S(2)}) collective-permute-start(f32[512,256]{1,0:T(8,128)} %collective-permute-done.3.refs_0_), channel_id=1, source_target_pairs={{0,16},{4,20},{8,24},{12,28},{16,0},{20,4},{24,8},{28,12},{1,17},{... | collective-permute-start | bytes 1572872 | tf_op jit(solution)/shard_map/ppermute | solution.py:556
  62.2 12.0 %own_late.1 = (f32[512,2048]{1,0:T(8,128)}, f32[16,2048]{1,0:T(8,128)S(1)}) custom-call(s32[3]{0:T(128)S(1)} %pad_add_fusion.where, f32[512,256]{1,0:T(8,128)S(1)} %collective-permute-done.6.refs_0_.refs_3_, f32[512,256]{1,0:T(8,128)S(1)} %collective-permute-done.4.refs_1_.refs_5_, f32[512,256]{1,0:T(8,128)S(1)} %collective-permute-done.5.refs_2_.refs_6_, ...), custom_call_target="tpu_custom_call" | custom-call | flops 1000 | bytes 1000 | tf_op jit(solution)/shard_map/own_late/pallas_call | solution.py:33
  74.1 1.2 collective-permute-start.8
  75.4 6.1 %emit.1 = f32[2048,512]{1,0:T(8,128)} custom-call(s32[3]{0:T(128)S(1)} %pad_add_fusion.where, f32[512,2048]{1,0:T(8,128)} %get-tuple-element.118.pred_ref.refs_8_, bf16[512,512]{1,0:T(8,128)(2,1)S(1)} %copy-done.7), custom_call_target="tpu_custom_call" | custom-call | flops 1000 | bytes 1000 | tf_op jit(solution)/shard_map/emit/pallas_call | solution.py:33
  81.5 1.4 collective-permute-done.8.theirs_ref
  82.9 2.1 %collective-permute-done.11.refs_3_.refs_4_ = f32[512,256]{1,0:T(8,128)S(1)} collective-permute-done((f32[512,256]{1,0:T(8,128)}, f32[512,256]{1,0:T(8,128)S(1)}, u32[]{:S(2)}, u32[]{:S(2)}) %collective-permute-start.11) | collective-permute-done | bytes 524320 | tf_op jit(solution)/shard_map/ppermute | solution.py:556
  85.9 1.2 collective-permute-start.22
  87.1 1.2 collective-permute-start.17
  88.4 3.3 %collective-permute-start.15 = (f32[16,2048]{1,0:T(8,128)S(1)}, f32[16,2048]{1,0:T(8,128)S(1)}, u32[]{:S(2)}, u32[]{:S(2)}) collective-permute-start(f32[16,2048]{1,0:T(8,128)S(1)} %add.9), channel_id=1, source_target_pairs={{0,1},{1,0},{2,3},{3,2},{4,5},{5,4},{6,7},{7,6},{8,9},{9,8},{10,11... | collective-permute-start | bytes 393224 | tf_op jit(solution)/shard_map/ppermute | solution.py:556
  93.9 10.1 %other_mid.1.refs_6_ = f32[512,2048]{1,0:T(8,128)S(1)} custom-call(s32[3]{0:T(128)S(1)} %pad_add_fusion.where, f32[512,256]{1,0:T(8,128)} %collective-permute-done.3.refs_0_, f32[512,256]{1,0:T(8,128)S(1)} %collective-permute-done.10.refs_1_, f32[512,256]{1,0:T(8,128)S(1)} %collective-permute-done.9.refs_2_, ...), custom_call_target="tpu_custom_call" | custom-call | flops 1000 | bytes 1000 | tf_op jit(solution)/shard_map/other_mid/pallas_call | solution.py:33
  104.6 1.2 collective-permute-start.20
  105.9 6.3 %other_more.1.refs_6_ = f32[512,2048]{1,0:T(8,128)} custom-call(s32[3]{0:T(128)S(1)} %pad_add_fusion.where, f32[512,256]{1,0:T(8,128)S(1)} %collective-permute-done.17.refs_0_.refs_5_, f32[512,256]{1,0:T(8,128)S(1)} %collective-permute-done.18.refs_1_.refs_6_, bf16[1024,2048]{1,0:T(8,128)(2,1)S(1)} %get-tuple-element.112.refs_4_.refs_2_.refs_3_, ...), custom_call_target="tpu_custom_call" | custom-call | flops 1000 | bytes 1000 | tf_op jit(solution)/shard_map/other_more/pallas_call | solution.py:33
  112.2 1.8 %collective-permute-start.21 = (f32[8,1024]{1,0:T(8,128)S(1)}, f32[8,1024]{1,0:T(8,128)S(1)}, u32[]{:S(2)}, u32[]{:S(2)}) collective-permute-start(f32[8,1024]{1,0:T(8,128)S(1)} %add.11.refs_19_), channel_id=1, source_target_pairs={{0,16},{4,20},{8,24},{12,28},{16,0},{20,4},{24,8},{28,12},{1,17},{... | collective-permute-start | bytes 98312 | tf_op jit(solution)/shard_map/ppermute | solution.py:556
  114.0 2.4 %rows_left.2 = (bf16[1024,512]{1,0:T(8,128)(2,1)S(1)}, bf16[1024,512]{1,0:T(8,128)(2,1)S(1)}) custom-call(s32[3]{0:T(128)S(1)} %pad_add_fusion.where, f32[512,256]{1,0:T(8,128)} %fusion.1.refs_0_, f32[512,256]{1,0:T(8,128)S(1)} %copy-done.11, f32[512,256]{1,0:T(8,128)} %collective-permute-done.refs_2_, ...), custom_call_target="tpu_custom_call" | custom-call | flops 1000 | bytes 1000 | tf_op jit(solution)/shard_map/rows_left/pallas_call | solution.py:33
  117.0 2.4 %rows_left.3 = (bf16[1024,512]{1,0:T(8,128)(2,1)S(1)}, bf16[1024,512]{1,0:T(8,128)(2,1)S(1)}) custom-call(s32[3]{0:T(128)S(1)} %pad_add_fusion.where, f32[512,256]{1,0:T(8,128)} %collective-permute-done.3.refs_0_, f32[512,256]{1,0:T(8,128)S(1)} %collective-permute-done.10.refs_1_, f32[512,256]{1,0:T(8,128)S(1)} %collective-permute-done.9.refs_2_, ...), custom_call_target="tpu_custom_call" | custom-call | flops 1000 | bytes 1000 | tf_op jit(solution)/shard_map/rows_left/pallas_call | solution.py:33
  119.5 17.8 %back_sum.1 = (f32[520,2048]{1,0:T(8,128)}, bf16[1024,2048]{1,0:T(8,128)(2,1)S(1)}, bf16[1024,2048]{1,0:T(8,128)(2,1)S(1)}, f32[8,128]{1,0:T(8,128)S(1)}) custom-call(s32[3]{0:T(128)S(1)} %pad_add_fusion.where, f32[512,256]{1,0:T(8,128)S(1)} %collective-permute-done.14.refs_3_.refs_0_, f32[512,256]{1,0:T(8,128)S(1)} %collective-permute-done.19.refs_7_.refs_1_, ...), custom_call_target="tpu_custom_call" | custom-call | flops 1000 | bytes 1000 | tf_op jit(solution)/shard_map/back_sum/pallas_call | solution.py:33
  137.3 1.9 %collective-permute-start.23 = (f32[520,2048]{1,0:T(8,128)}, f32[520,2048]{1,0:T(8,128)S(1)}, u32[]{:S(2)}, u32[]{:S(2)}) collective-permute-start(f32[520,2048]{1,0:T(8,128)} %get-tuple-element.157.refs_9_), channel_id=1, source_target_pairs={{0,1},{1,0},{2,3},{3,2},{4,5},{5,4},{6,7},{7,6},{8,9},{9,8},{10,11... | collective-permute-start | bytes 12779528 | tf_op jit(solution)/shard_map/ppermute | solution.py:556
  139.2 9.2 %back_own.1.mine_ref = f32[512,2048]{1,0:T(8,128)S(1)} custom-call(s32[3]{0:T(128)S(1)} %pad_add_fusion.where, bf16[1024,512]{1,0:T(8,128)(2,1)S(1)} %get-tuple-element.138.refs_15_.refs_0_, bf16[1024,512]{1,0:T(8,128)(2,1)S(1)} %get-tuple-element.145.refs_16_.refs_1_, bf16[1024,512]{1,0:T(8,128)(2,1)S(1)} %get-tuple-element.146.refs_17_.refs_2_, ...), custom_call_target="tpu_custom_call" | custom-call | flops 1000 | bytes 1000 | tf_op jit(solution)/shard_map/back_own/pallas_call | solution.py:33
  148.4 5.8 %back_end.1 = (f32[512,2048]{1,0:T(8,128)}, f32[3]{0:T(128)}) custom-call(s32[3]{0:T(128)S(1)} %pad_add_fusion.where, f32[512,2048]{1,0:T(8,128)S(1)} %back_own.1.mine_ref, f32[520,2048]{1,0:T(8,128)S(1)} %collective-permute-done.23.got_ref, f32[2048,2048]{1,0:T(8,128)} %logit_ref, f32[8,2048]{1,0:T(8,128)S(1)} %get-tuple-element.115.refs_7_.z_ref, ...), custom_call_target="tpu_custom_call" | custom-call | flops 1000 | bytes 1000 | tf_op jit(solution)/shard_map/back_end/pallas_call | solution.py:33
  (72 shorter events, 12.9 us)
Async XLA Ops:
  0.6 18.3 %copy-start.15 = (s32[2048]{0:T(1024)S(1)}, s32[2048]{0:T(1024)}, u32[]{:S(2)}) copy-start(s32[2048]{0:T(1024)} %param.9) | copy-start | bytes 24580
  0.7 19.9 %copy-start.14 = (f32[2048]{0:T(1024)S(1)}, f32[2048]{0:T(1024)}, u32[]{:S(2)}) copy-start(f32[2048]{0:T(1024)} %param.10) | copy-start | bytes 24580
  3.0 14.1 %collective-permute-start.1 = (f32[512,256]{1,0:T(8,128)}, f32[512,256]{1,0:T(8,128)S(1)}, u32[]{:S(2)}, u32[]{:S(2)}) collective-permute-start(f32[512,256]{1,0:T(8,128)} %fusion.1.refs_0_), channel_id=1, source_target_pairs={{0,4},{4,0},{8,12},{12,8},{16,20},{20,16},{24,28},{28,24},{1,5},{5... | collective-permute-start | bytes 1572872 | tf_op jit(solution)/shard_map/ppermute | solution.py:556
  5.1 21.7 %collective-permute-start.3 = (f32[512,256]{1,0:T(8,128)}, f32[512,256]{1,0:T(8,128)}, u32[]{:S(2)}, u32[]{:S(2)}) collective-permute-start(f32[512,256]{1,0:T(8,128)} %fusion.1.refs_0_), channel_id=1, source_target_pairs={{0,2},{1,3},{2,0},{3,1},{4,6},{5,7},{6,4},{7,5},{8,10},{9,11},{10,... | collective-permute-start | bytes 1572872 | tf_op jit(solution)/shard_map/ppermute | solution.py:556
  6.3 25.3 %collective-permute-start.2 = (f32[512,256]{1,0:T(8,128)}, f32[512,256]{1,0:T(8,128)}, u32[]{:S(2)}, u32[]{:S(2)}) collective-permute-start(f32[512,256]{1,0:T(8,128)} %fusion.1.refs_0_), channel_id=1, source_target_pairs={{0,16},{4,20},{8,24},{12,28},{16,0},{20,4},{24,8},{28,12},{1,17},{... | collective-permute-start | bytes 1572872 | tf_op jit(solution)/shard_map/ppermute | solution.py:556
  8.6 23.0 %collective-permute-start = (f32[512,256]{1,0:T(8,128)}, f32[512,256]{1,0:T(8,128)}, u32[]{:S(2)}, u32[]{:S(2)}) collective-permute-start(f32[512,256]{1,0:T(8,128)} %fusion.1.refs_0_), channel_id=1, source_target_pairs={{0,8},{4,12},{8,0},{12,4},{16,24},{20,28},{24,16},{28,20},{1,9},{5... | collective-permute-start | bytes 1572872 | tf_op jit(solution)/shard_map/ppermute | solution.py:556
  10.1 10.1 %copy-start.6 = (bf16[512,512]{1,0:T(8,128)(2,1)}, bf16[512,512]{1,0:T(8,128)(2,1)S(1)}, u32[]{:S(2)}) copy-start(bf16[512,512]{1,0:T(8,128)(2,1)S(1)} %fusion.pick_ref) | copy-start | bytes 1572868
  17.9 68.0 %collective-permute-start.12 = (f32[256,2048]{1,0:T(8,128)S(1)}, f32[256,2048]{1,0:T(8,128)}, u32[]{:S(2)}, u32[]{:S(2)}) collective-permute-start(f32[256,2048]{1,0:T(8,128)S(1)} %get-tuple-element.116.refs_8_.refs_9_), channel_id=1, source_target_pairs={{0,2},{1,3},{2,0},{3,1},{4,6},{5,7},{6,4},{7,5},{8,10},{9,11},{10,... | collective-permute-start | bytes 6291464 | tf_op jit(solution)/shard_map/ppermute | solution.py:556
  20.6 12.6 %copy-start.11 = (f32[512,256]{1,0:T(8,128)S(1)}, f32[512,256]{1,0:T(8,128)}, u32[]{:S(2)}) copy-start(f32[512,256]{1,0:T(8,128)} %copy-done.10) | copy-start | bytes 1572868
  31.5 11.9 %collective-permute-start.5 = (f32[512,256]{1,0:T(8,128)}, f32[512,256]{1,0:T(8,128)S(1)}, u32[]{:S(2)}, u32[]{:S(2)}) collective-permute-start(f32[512,256]{1,0:T(8,128)} %collective-permute-done.2.refs_3_.refs_4_), channel_id=1, source_target_pairs={{0,8},{4,12},{8,0},{12,4},{16,24},{20,28},{24,16},{28,20},{1,9},{5... | collective-permute-start | bytes 1572872 | tf_op jit(solution)/shard_map/ppermute | solution.py:556
  33.0 11.9 %collective-permute-start.4 = (f32[512,256]{1,0:T(8,128)}, f32[512,256]{1,0:T(8,128)S(1)}, u32[]{:S(2)}, u32[]{:S(2)}) collective-permute-start(f32[512,256]{1,0:T(8,128)} %collective-permute-done.2.refs_3_.refs_4_), channel_id=1, source_target_pairs={{0,4},{4,0},{8,12},{12,8},{16,20},{20,16},{24,28},{28,24},{1,5},{5... | collective-permute-start | bytes 1572872 | tf_op jit(solution)/shard_map/ppermute | solution.py:556
  43.5 12.3 %copy-start.9 = (f32[96,2048]{1,0:T(8,128)S(1)}, f32[96,2048]{1,0:T(8,128)}, u32[]{:S(2)}) copy-start(f32[96,2048]{1,0:T(8,128)} %copy-done.8) | copy-start | bytes 2359300
  43.5 18.7 %copy-start.5 = (f32[160,2048]{1,0:T(8,128)S(1)}, f32[160,2048]{1,0:T(8,128)}, u32[]{:S(2)}) copy-start(f32[160,2048]{1,0:T(8,128)} %copy-done.4) | copy-start | bytes 3932164
  44.9 10.9 %collective-permute-start.6 = (f32[512,256]{1,0:T(8,128)S(1)}, f32[512,256]{1,0:T(8,128)S(1)}, u32[]{:S(2)}, u32[]{:S(2)}) collective-permute-start(f32[512,256]{1,0:T(8,128)S(1)} %copy-done.11), channel_id=1, source_target_pairs={{0,8},{4,12},{8,0},{12,4},{16,24},{20,28},{24,16},{28,20},{1,9},{5... | collective-permute-start | bytes 1572872 | tf_op jit(solution)/shard_map/ppermute | solution.py:556
  45.1 16.4 %collective-permute-start.7 = (f32[512,256]{1,0:T(8,128)S(1)}, f32[512,256]{1,0:T(8,128)S(1)}, u32[]{:S(2)}, u32[]{:S(2)}) collective-permute-start(f32[512,256]{1,0:T(8,128)S(1)} %collective-permute-done.5.refs_2_.refs_6_), channel_id=1, source_target_pairs={{0,4},{4,0},{8,12},{12,8},{16,20},{20,16},{24,28},{28,24},{1,5},{5... | collective-permute-start | bytes 1572872 | tf_op jit(solution)/shard_map/ppermute | solution.py:556
  51.8 54.1 %copy-start.2 = (bf16[1024,2048]{1,0:T(8,128)(2,1)}, bf16[1024,2048]{1,0:T(8,128)(2,1)S(1)}, u32[]{:S(2)}) copy-start(bf16[1024,2048]{1,0:T(8,128)(2,1)S(1)} %get-tuple-element.113.refs_5_.refs_4_) | copy-start | bytes 12582916
  55.7 29.2 %collective-permute-start.13 = (f32[96,2048]{1,0:T(8,128)S(1)}, f32[96,2048]{1,0:T(8,128)S(1)}, u32[]{:S(2)}, u32[]{:S(2)}) collective-permute-start(f32[96,2048]{1,0:T(8,128)S(1)} %copy-done.9), channel_id=1, source_target_pairs={{0,2},{1,3},{2,0},{3,1},{4,6},{5,7},{6,4},{7,5},{8,10},{9,11},{10,... | collective-permute-start | bytes 2359304 | tf_op jit(solution)/shard_map/ppermute | solution.py:556
  56.0 18.2 %collective-permute-start.10 = (f32[512,256]{1,0:T(8,128)}, f32[512,256]{1,0:T(8,128)S(1)}, u32[]{:S(2)}, u32[]{:S(2)}) collective-permute-start(f32[512,256]{1,0:T(8,128)} %collective-permute-done.3.refs_0_), channel_id=1, source_target_pairs={{0,4},{4,0},{8,12},{12,8},{16,20},{20,16},{24,28},{28,24},{1,5},{5... | collective-permute-start | bytes 1572872 | tf_op jit(solution)/shard_map/ppermute | solution.py:556
  56.2 28.8 %collective-permute-start.11 = (f32[512,256]{1,0:T(8,128)}, f32[512,256]{1,0:T(8,128)S(1)}, u32[]{:S(2)}, u32[]{:S(2)}) collective-permute-start(f32[512,256]{1,0:T(8,128)} %collective-permute-done.3.refs_0_), channel_id=1, source_target_pairs={{0,16},{4,20},{8,24},{12,28},{16,0},{20,4},{24,8},{28,12},{1,17},{... | collective-permute-start | bytes 1572872 | tf_op jit(solution)/shard_map/ppermute | solution.py:556
  61.5 23.5 %collective-permute-start.9 = (f32[512,256]{1,0:T(8,128)}, f32[512,256]{1,0:T(8,128)S(1)}, u32[]{:S(2)}, u32[]{:S(2)}) collective-permute-start(f32[512,256]{1,0:T(8,128)} %collective-permute-done.3.refs_0_), channel_id=1, source_target_pairs={{0,8},{4,12},{8,0},{12,4},{16,24},{20,28},{24,16},{28,20},{1,9},{5... | collective-permute-start | bytes 1572872 | tf_op jit(solution)/shard_map/ppermute | solution.py:556
  62.2 13.2 %copy-start.7 = (bf16[512,512]{1,0:T(8,128)(2,1)S(1)}, bf16[512,512]{1,0:T(8,128)(2,1)}, u32[]{:S(2)}) copy-start(bf16[512,512]{1,0:T(8,128)(2,1)} %copy-done.6) | copy-start | bytes 1572868
  74.1 8.8 %collective-permute-start.8 = (f32[16,2048]{1,0:T(8,128)S(1)}, f32[16,2048]{1,0:T(8,128)S(1)}, u32[]{:S(2)}, u32[]{:S(2)}) collective-permute-start(f32[16,2048]{1,0:T(8,128)S(1)} %get-tuple-element.119.mine_ref), channel_id=1, source_target_pairs={{0,2},{1,3},{2,0},{3,1},{4,6},{5,7},{6,4},{7,5},{8,10},{9,11},{10,... | collective-permute-start | bytes 393224 | tf_op jit(solution)/shard_map/ppermute | solution.py:556
  85.9 33.6 %collective-permute-start.22 = (f32[160,2048]{1,0:T(8,128)S(1)}, f32[160,2048]{1,0:T(8,128)S(1)}, u32[]{:S(2)}, u32[]{:S(2)}) collective-permute-start(f32[160,2048]{1,0:T(8,128)S(1)} %copy-done.5), channel_id=1, source_target_pairs={{0,2},{1,3},{2,0},{3,1},{4,6},{5,7},{6,4},{7,5},{8,10},{9,11},{10,... | collective-permute-start | bytes 3932168 | tf_op jit(solution)/shard_map/ppermute | solution.py:556
  87.1 17.0 %collective-permute-start.18 = (f32[512,256]{1,0:T(8,128)S(1)}, f32[512,256]{1,0:T(8,128)S(1)}, u32[]{:S(2)}, u32[]{:S(2)}) collective-permute-start(f32[512,256]{1,0:T(8,128)S(1)} %collective-permute-done.11.refs_3_.refs_4_), channel_id=1, source_target_pairs={{0,8},{4,12},{8,0},{12,4},{16,24},{20,28},{24,16},{28,20},{1,9},{5... | collective-permute-start | bytes 1572872 | tf_op jit(solution)/shard_map/ppermute | solution.py:556
  87.1 17.0 %collective-permute-start.17 = (f32[512,256]{1,0:T(8,128)S(1)}, f32[512,256]{1,0:T(8,128)S(1)}, u32[]{:S(2)}, u32[]{:S(2)}) collective-permute-start(f32[512,256]{1,0:T(8,128)S(1)} %collective-permute-done.11.refs_3_.refs_4_), channel_id=1, source_target_pairs={{0,4},{4,0},{8,12},{12,8},{16,20},{20,16},{24,28},{28,24},{1,5},{5... | collective-permute-start | bytes 1572872 | tf_op jit(solution)/shard_map/ppermute | solution.py:556
  88.4 4.2 %collective-permute-start.15 = (f32[16,2048]{1,0:T(8,128)S(1)}, f32[16,2048]{1,0:T(8,128)S(1)}, u32[]{:S(2)}, u32[]{:S(2)}) collective-permute-start(f32[16,2048]{1,0:T(8,128)S(1)} %add.9), channel_id=1, source_target_pairs={{0,1},{1,0},{2,3},{3,2},{4,5},{5,4},{6,7},{7,6},{8,9},{9,8},{10,11... | collective-permute-start | bytes 393224 | tf_op jit(solution)/shard_map/ppermute | solution.py:556
  92.7 11.3 %collective-permute-start.16 = (f32[8,1024]{1,0:T(8,128)S(1)}, f32[8,1024]{1,0:T(8,128)S(1)}, u32[]{:S(2)}, u32[]{:S(2)}) collective-permute-start(f32[8,1024]{1,0:T(8,128)S(1)} %get-tuple-element.132), channel_id=1, source_target_pairs={{0,8},{4,12},{8,0},{12,4},{16,24},{20,28},{24,16},{28,20},{1,9},{5... | collective-permute-start | bytes 98312 | tf_op jit(solution)/shard_map/ppermute | solution.py:556
  93.7 22.8 %collective-permute-start.14 = (f32[512,256]{1,0:T(8,128)S(1)}, f32[512,256]{1,0:T(8,128)S(1)}, u32[]{:S(2)}, u32[]{:S(2)}) collective-permute-start(f32[512,256]{1,0:T(8,128)S(1)} %collective-permute-done.9.refs_2_), channel_id=1, source_target_pairs={{0,4},{4,0},{8,12},{12,8},{16,20},{20,16},{24,28},{28,24},{1,5},{5... | collective-permute-start | bytes 1572872 | tf_op jit(solution)/shard_map/ppermute | solution.py:556
  104.1 12.9 %collective-permute-start.19 = (f32[512,256]{1,0:T(8,128)S(1)}, f32[512,256]{1,0:T(8,128)S(1)}, u32[]{:S(2)}, u32[]{:S(2)}) collective-permute-start(f32[512,256]{1,0:T(8,128)S(1)} %collective-permute-done.17.refs_0_.refs_5_), channel_id=1, source_target_pairs={{0,8},{4,12},{8,0},{12,4},{16,24},{20,28},{24,16},{28,20},{1,9},{5... | collective-permute-start | bytes 1572872 | tf_op jit(solution)/shard_map/ppermute | solution.py:556
  104.6 7.6 %collective-permute-start.20 = (f32[8,1024]{1,0:T(8,128)S(1)}, f32[8,1024]{1,0:T(8,128)S(1)}, u32[]{:S(2)}, u32[]{:S(2)}) collective-permute-start(f32[8,1024]{1,0:T(8,128)S(1)} %add.10), channel_id=1, source_target_pairs={{0,4},{4,0},{8,12},{12,8},{16,20},{20,16},{24,28},{28,24},{1,5},{5... | collective-permute-start | bytes 98312 | tf_op jit(solution)/shard_map/ppermute | solution.py:556
  112.2 7.2 %collective-permute-start.21 = (f32[8,1024]{1,0:T(8,128)S(1)}, f32[8,1024]{1,0:T(8,128)S(1)}, u32[]{:S(2)}, u32[]{:S(2)}) collective-permute-start(f32[8,1024]{1,0:T(8,128)S(1)} %add.11.refs_19_), channel_id=1, source_target_pairs={{0,16},{4,20},{8,24},{12,28},{16,0},{20,4},{24,8},{28,12},{1,17},{... | collective-permute-start | bytes 98312 | tf_op jit(solution)/shard_map/ppermute | solution.py:556
  137.3 11.2 %collective-permute-start.23 = (f32[520,2048]{1,0:T(8,128)}, f32[520,2048]{1,0:T(8,128)S(1)}, u32[]{:S(2)}, u32[]{:S(2)}) collective-permute-start(f32[520,2048]{1,0:T(8,128)} %get-tuple-element.157.refs_9_), channel_id=1, source_target_pairs={{0,1},{1,0},{2,3},{3,2},{4,5},{5,4},{6,7},{7,6},{8,9},{9,8},{10,11... | collective-permute-start | bytes 12779528 | tf_op jit(solution)/shard_map/ppermute | solution.py:556
  (8 other events, 25.0 us)

commit v8 on v7

--- a/solution.py
+++ b/solution.py
@@ -15,7 +15,7 @@
 KC = 256
 NT = (((1,), (1,)), ((), ()))
 TN = (((0,), (0,)), ((), ()))
-VMEM_LIMIT = 24 << 20
+VMEM_LIMIT = 22 << 20
 LARGE_LIMIT = 60 << 20
 CHEAP = pl.CostEstimate(flops=1000, bytes_accessed=1000, transcendentals=0)
 
@@ -673,7 +673,7 @@
     got = swap(sent, "gene", 1)
     rest = back_own(where, highs, lefts, sums, zinfo, dens_row, sent, weights, consts[2], rows, tile)
     rest, got = tie(rest, got)
-    grad, loss = back_end(where, rest, got, logits, zinfo, sums, consts[3], rows, tile)
+    grad, loss = back_end(where, rest, got, logits, zinfo, sums, consts[3], rows, 2 * tile)
     return loss, predicted, grad
 
 

time: 155 us -> 153 us (0.987)
    unnamed x32 -> x24, local copies, waits for them, and re-layouts: 3.98 us -> 3.07 us
where the time goes in v8:
time: 153 us
  Pallas kernels  99.6 us (65%)
  starting transfers between devices  30.2 us (20%)
  waiting for transfers between devices  15 us (10%)
  local copies, waits for them, and re-layouts  3.44 us (2%)
  other arithmetic  2.24 us (1%)
    pallas_call x13, Pallas kernels, call(): pl.pallas_call(kernel, out_shape=out_shape, grid_spec=pltpu.PrefetchScala...  99.4 us
    ppermute x24, starting transfers between devices, swap(): lax.ppermute(value, axis, [(i, i ^ bit) for i in range(lax.axis_size(axis...  30.2 us
    ppermute x24, waiting for transfers between devices, swap(): lax.ppermute(value, axis, [(i, i ^ bit) for i in range(lax.axis_size(axis...  15 us
    unnamed x24, local copies, waits for them, and re-layouts  3.07 us
  transfers between devices with their start and end apart: 24, of which 7 were waited for; matrix products, arithmetic and copies ran while one was open for 1% of the time, Pallas kernels for 50%

profile of v8, /device:TPU:1, one launch (start us, length us, event | category | flops | bytes accessed | tf_op | source)
XLA Modules:
  0.0 152.7 jit_solution(12956122513350659571)
XLA Ops:
  1.7 1.3 fusion.1.refs_0_
  3.0 2.1 %collective-permute-start.1 = (f32[512,256]{1,0:T(8,128)}, f32[512,256]{1,0:T(8,128)S(1)}, u32[]{:S(2)}, u32[]{:S(2)}) collective-permute-start(f32[512,256]{1,0:T(8,128)} %fusion.1.refs_0_), channel_id=1, source_target_pairs={{0,4},{4,0},{8,12},{12,8},{16,20},{20,16},{24,28},{28,24},{1,5},{5... | collective-permute-start | bytes 1572872 | tf_op jit(solution)/shard_map/ppermute | solution.py:556
  5.1 1.2 collective-permute-start.3
  6.3 2.3 %collective-permute-start.2 = (f32[512,256]{1,0:T(8,128)}, f32[512,256]{1,0:T(8,128)}, u32[]{:S(2)}, u32[]{:S(2)}) collective-permute-start(f32[512,256]{1,0:T(8,128)} %fusion.1.refs_0_), channel_id=1, source_target_pairs={{0,16},{4,20},{8,24},{12,28},{16,0},{20,4},{24,8},{28,12},{1,17},{... | collective-permute-start | bytes 1572872 | tf_op jit(solution)/shard_map/ppermute | solution.py:556
  8.6 1.3 collective-permute-start
  10.2 5.0 %turn.1 = (f32[256,2048]{1,0:T(8,128)S(1)}, f32[96,2048]{1,0:T(8,128)S(1)}, f32[160,2048]{1,0:T(8,128)S(1)}) custom-call(s32[3]{0:T(128)S(1)} %pad_add_fusion.where, bf16[512,512]{1,0:T(8,128)(2,1)S(1)} %fusion.pick_ref, f32[2048,512]{1,0:T(8,128)} %x_ref.1), custom_call_target="tpu_custom_call" | custom-call | flops 1000 | bytes 1000 | tf_op jit(solution)/shard_map/turn/pallas_call | solution.py:33
  20.6 6.2 %exp_parts.2 = (bf16[1024,2048]{1,0:T(8,128)(2,1)S(1)}, bf16[1024,2048]{1,0:T(8,128)(2,1)S(1)}, f32[8,2048]{1,0:T(8,128)S(1)}) custom-call(s32[3]{0:T(128)S(1)} %pad_add_fusion.where, f32[2048,2048]{1,0:T(8,128)} %logit_ref, f32[2048,2048]{1,0:T(8,128)} %logit_ref, f32[2048,2048]{1,0:T(8,128)} %logit_ref, f32[2048,2048]{1,0:T(8,128)} %logit_ref, ...), custom_call_target="tpu_custom_call" | custom-call | flops 1000 | bytes 1000 | tf_op jit(solution)/shard_map/exp_parts/pallas_call | solution.py:33
  26.8 4.8 %collective-permute-done.2.refs_3_.refs_4_ = f32[512,256]{1,0:T(8,128)} collective-permute-done((f32[512,256]{1,0:T(8,128)}, f32[512,256]{1,0:T(8,128)}, u32[]{:S(2)}, u32[]{:S(2)}) %collective-permute-start.2) | collective-permute-done | bytes 524320 | tf_op jit(solution)/shard_map/ppermute | solution.py:556
  31.6 1.4 collective-permute-start.5
  33.2 10.3 %own_early.1.refs_6_ = f32[512,2048]{1,0:T(8,128)S(1)} custom-call(s32[3]{0:T(128)S(1)} %pad_add_fusion.where, f32[512,256]{1,0:T(8,128)} %fusion.1.refs_0_, f32[512,256]{1,0:T(8,128)S(1)} %copy-done.9, f32[512,256]{1,0:T(8,128)} %collective-permute-done.refs_2_, f32[512,256]{1,0:T(8,128)} %collective-permute-done.2.refs_3_.refs_4_, ...), custom_call_target="tpu_custom_call" | custom-call | flops 1000 | bytes 1000 | tf_op jit(solution)/shard_map/own_early/pallas_call | solution.py:33
  43.5 1.4 collective-permute-done.4.refs_1_.refs_5_
  45.4 6.4 %exp_parts.3 = (bf16[1024,2048]{1,0:T(8,128)(2,1)S(1)}, bf16[1024,2048]{1,0:T(8,128)(2,1)S(1)}, f32[8,2048]{1,0:T(8,128)S(1)}) custom-call(s32[3]{0:T(128)S(1)} %pad_add_fusion.where, f32[2048,2048]{1,0:T(8,128)} %logit_ref, f32[2048,2048]{1,0:T(8,128)} %logit_ref, f32[2048,2048]{1,0:T(8,128)} %logit_ref, f32[2048,2048]{1,0:T(8,128)} %logit_ref, ...), custom_call_target="tpu_custom_call" | custom-call | flops 1000 | bytes 1000 | tf_op jit(solution)/shard_map/exp_parts/pallas_call | solution.py:33
  51.8 3.9 %collective-permute-done.6.refs_0_.refs_3_ = f32[512,256]{1,0:T(8,128)S(1)} collective-permute-done((f32[512,256]{1,0:T(8,128)S(1)}, f32[512,256]{1,0:T(8,128)S(1)}, u32[]{:S(2)}, u32[]{:S(2)}) %collective-permute-start.6) | collective-permute-done | bytes 524320 | tf_op jit(solution)/shard_map/ppermute | solution.py:556
  56.3 5.3 %collective-permute-start.11 = (f32[512,256]{1,0:T(8,128)}, f32[512,256]{1,0:T(8,128)S(1)}, u32[]{:S(2)}, u32[]{:S(2)}) collective-permute-start(f32[512,256]{1,0:T(8,128)} %collective-permute-done.3.refs_0_), channel_id=1, source_target_pairs={{0,16},{4,20},{8,24},{12,28},{16,0},{20,4},{24,8},{28,12},{1,17},{... | collective-permute-start | bytes 1572872 | tf_op jit(solution)/shard_map/ppermute | solution.py:556
  62.2 12.0 %own_late.1 = (f32[512,2048]{1,0:T(8,128)}, f32[16,2048]{1,0:T(8,128)S(1)}) custom-call(s32[3]{0:T(128)S(1)} %pad_add_fusion.where, f32[512,256]{1,0:T(8,128)S(1)} %collective-permute-done.6.refs_0_.refs_3_, f32[512,256]{1,0:T(8,128)S(1)} %collective-permute-done.4.refs_1_.refs_5_, f32[512,256]{1,0:T(8,128)S(1)} %collective-permute-done.5.refs_2_.refs_6_, ...), custom_call_target="tpu_custom_call" | custom-call | flops 1000 | bytes 1000 | tf_op jit(solution)/shard_map/own_late/pallas_call | solution.py:33
  74.2 1.2 collective-permute-start.8
  75.4 6.1 %emit.1 = f32[2048,512]{1,0:T(8,128)} custom-call(s32[3]{0:T(128)S(1)} %pad_add_fusion.where, f32[512,2048]{1,0:T(8,128)} %get-tuple-element.118.pred_ref.refs_8_, bf16[512,512]{1,0:T(8,128)(2,1)S(1)} %copy-done.5), custom_call_target="tpu_custom_call" | custom-call | flops 1000 | bytes 1000 | tf_op jit(solution)/shard_map/emit/pallas_call | solution.py:33
  81.6 1.4 collective-permute-done.8.theirs_ref
  82.9 2.1 %collective-permute-done.11.refs_3_.refs_4_ = f32[512,256]{1,0:T(8,128)S(1)} collective-permute-done((f32[512,256]{1,0:T(8,128)}, f32[512,256]{1,0:T(8,128)S(1)}, u32[]{:S(2)}, u32[]{:S(2)}) %collective-permute-start.11) | collective-permute-done | bytes 524320 | tf_op jit(solution)/shard_map/ppermute | solution.py:556
  85.0 1.3 collective-permute-start.22
  86.3 1.2 collective-permute-start.17
  87.6 3.2 %collective-permute-start.15 = (f32[16,2048]{1,0:T(8,128)S(1)}, f32[16,2048]{1,0:T(8,128)S(1)}, u32[]{:S(2)}, u32[]{:S(2)}) collective-permute-start(f32[16,2048]{1,0:T(8,128)S(1)} %add.9), channel_id=1, source_target_pairs={{0,1},{1,0},{2,3},{3,2},{4,5},{5,4},{6,7},{7,6},{8,9},{9,8},{10,11... | collective-permute-start | bytes 393224 | tf_op jit(solution)/shard_map/ppermute | solution.py:556
  93.1 10.1 %other_mid.1.refs_6_ = f32[512,2048]{1,0:T(8,128)S(1)} custom-call(s32[3]{0:T(128)S(1)} %pad_add_fusion.where, f32[512,256]{1,0:T(8,128)} %collective-permute-done.3.refs_0_, f32[512,256]{1,0:T(8,128)S(1)} %collective-permute-done.10.refs_1_, f32[512,256]{1,0:T(8,128)S(1)} %collective-permute-done.9.refs_2_, ...), custom_call_target="tpu_custom_call" | custom-call | flops 1000 | bytes 1000 | tf_op jit(solution)/shard_map/other_mid/pallas_call | solution.py:33
  103.8 1.2 collective-permute-start.20
  105.0 6.3 %other_more.1.refs_6_ = f32[512,2048]{1,0:T(8,128)} custom-call(s32[3]{0:T(128)S(1)} %pad_add_fusion.where, f32[512,256]{1,0:T(8,128)S(1)} %collective-permute-done.17.refs_0_.refs_5_, f32[512,256]{1,0:T(8,128)S(1)} %collective-permute-done.18.refs_1_.refs_6_, bf16[1024,2048]{1,0:T(8,128)(2,1)S(1)} %get-tuple-element.112.refs_4_.refs_2_.refs_3_, ...), custom_call_target="tpu_custom_call" | custom-call | flops 1000 | bytes 1000 | tf_op jit(solution)/shard_map/other_more/pallas_call | solution.py:33
  111.3 1.9 %collective-permute-start.21 = (f32[8,1024]{1,0:T(8,128)S(1)}, f32[8,1024]{1,0:T(8,128)S(1)}, u32[]{:S(2)}, u32[]{:S(2)}) collective-permute-start(f32[8,1024]{1,0:T(8,128)S(1)} %add.11.refs_19_), channel_id=1, source_target_pairs={{0,16},{4,20},{8,24},{12,28},{16,0},{20,4},{24,8},{28,12},{1,17},{... | collective-permute-start | bytes 98312 | tf_op jit(solution)/shard_map/ppermute | solution.py:556
  113.2 2.4 %rows_left.2 = (bf16[1024,512]{1,0:T(8,128)(2,1)S(1)}, bf16[1024,512]{1,0:T(8,128)(2,1)S(1)}) custom-call(s32[3]{0:T(128)S(1)} %pad_add_fusion.where, f32[512,256]{1,0:T(8,128)} %fusion.1.refs_0_, f32[512,256]{1,0:T(8,128)S(1)} %copy-done.9, f32[512,256]{1,0:T(8,128)} %collective-permute-done.refs_2_, f32[512,256]{1,0:T(8,128)S(1)} %collective-permute-done.6.refs_0_.refs_3_, ...), custom_call_target="tpu_custom_call" | custom-call | flops 1000 | bytes 1000 | tf_op jit(solution)/shard_map/rows_left/pallas_call | solution.py:33
  116.1 2.4 %rows_left.3 = (bf16[1024,512]{1,0:T(8,128)(2,1)S(1)}, bf16[1024,512]{1,0:T(8,128)(2,1)S(1)}) custom-call(s32[3]{0:T(128)S(1)} %pad_add_fusion.where, f32[512,256]{1,0:T(8,128)} %collective-permute-done.3.refs_0_, f32[512,256]{1,0:T(8,128)S(1)} %collective-permute-done.10.refs_1_, f32[512,256]{1,0:T(8,128)S(1)} %collective-permute-done.9.refs_2_, ...), custom_call_target="tpu_custom_call" | custom-call | flops 1000 | bytes 1000 | tf_op jit(solution)/shard_map/rows_left/pallas_call | solution.py:33
  118.6 18.0 %back_sum.1 = (f32[520,2048]{1,0:T(8,128)}, bf16[1024,2048]{1,0:T(8,128)(2,1)S(1)}, bf16[1024,2048]{1,0:T(8,128)(2,1)S(1)}, f32[8,128]{1,0:T(8,128)S(1)}) custom-call(s32[3]{0:T(128)S(1)} %pad_add_fusion.where, f32[512,256]{1,0:T(8,128)S(1)} %collective-permute-done.14.refs_3_.refs_0_, f32[512,256]{1,0:T(8,128)S(1)} %collective-permute-done.19.refs_7_.refs_1_, ...), custom_call_target="tpu_custom_call" | custom-call | flops 1000 | bytes 1000 | tf_op jit(solution)/shard_map/back_sum/pallas_call | solution.py:33
  136.6 1.9 %collective-permute-start.23 = (f32[520,2048]{1,0:T(8,128)}, f32[520,2048]{1,0:T(8,128)S(1)}, u32[]{:S(2)}, u32[]{:S(2)}) collective-permute-start(f32[520,2048]{1,0:T(8,128)} %get-tuple-element.157.refs_9_), channel_id=1, source_target_pairs={{0,1},{1,0},{2,3},{3,2},{4,5},{5,4},{6,7},{7,6},{8,9},{9,8},{10,11... | collective-permute-start | bytes 12779528 | tf_op jit(solution)/shard_map/ppermute | solution.py:556
  138.5 9.2 %back_own.1.mine_ref = f32[512,2048]{1,0:T(8,128)S(1)} custom-call(s32[3]{0:T(128)S(1)} %pad_add_fusion.where, bf16[1024,512]{1,0:T(8,128)(2,1)S(1)} %get-tuple-element.138.refs_15_.refs_0_, bf16[1024,512]{1,0:T(8,128)(2,1)S(1)} %get-tuple-element.145.refs_16_.refs_1_, bf16[1024,512]{1,0:T(8,128)(2,1)S(1)} %get-tuple-element.146.refs_17_.refs_2_, ...), custom_call_target="tpu_custom_call" | custom-call | flops 1000 | bytes 1000 | tf_op jit(solution)/shard_map/back_own/pallas_call | solution.py:33
  147.8 4.9 %back_end.1 = (f32[512,2048]{1,0:T(8,128)}, f32[3]{0:T(128)}) custom-call(s32[3]{0:T(128)S(1)} %pad_add_fusion.where, f32[512,2048]{1,0:T(8,128)S(1)} %back_own.1.mine_ref, f32[520,2048]{1,0:T(8,128)S(1)} %collective-permute-done.23.got_ref, f32[2048,2048]{1,0:T(8,128)} %logit_ref, f32[8,2048]{1,0:T(8,128)S(1)} %get-tuple-element.115.refs_7_.z_ref, ...), custom_call_target="tpu_custom_call" | custom-call | flops 1000 | bytes 1000 | tf_op jit(solution)/shard_map/back_end/pallas_call | solution.py:33
  (64 shorter events, 12.0 us)
Async XLA Ops:
  0.6 18.3 %copy-start.11 = (s32[2048]{0:T(1024)S(1)}, s32[2048]{0:T(1024)}, u32[]{:S(2)}) copy-start(s32[2048]{0:T(1024)} %param.9) | copy-start | bytes 24580
  0.7 20.0 %copy-start.10 = (f32[2048]{0:T(1024)S(1)}, f32[2048]{0:T(1024)}, u32[]{:S(2)}) copy-start(f32[2048]{0:T(1024)} %param.10) | copy-start | bytes 24580
  3.0 14.1 %collective-permute-start.1 = (f32[512,256]{1,0:T(8,128)}, f32[512,256]{1,0:T(8,128)S(1)}, u32[]{:S(2)}, u32[]{:S(2)}) collective-permute-start(f32[512,256]{1,0:T(8,128)} %fusion.1.refs_0_), channel_id=1, source_target_pairs={{0,4},{4,0},{8,12},{12,8},{16,20},{20,16},{24,28},{28,24},{1,5},{5... | collective-permute-start | bytes 1572872 | tf_op jit(solution)/shard_map/ppermute | solution.py:556
  5.1 21.7 %collective-permute-start.3 = (f32[512,256]{1,0:T(8,128)}, f32[512,256]{1,0:T(8,128)}, u32[]{:S(2)}, u32[]{:S(2)}) collective-permute-start(f32[512,256]{1,0:T(8,128)} %fusion.1.refs_0_), channel_id=1, source_target_pairs={{0,2},{1,3},{2,0},{3,1},{4,6},{5,7},{6,4},{7,5},{8,10},{9,11},{10,... | collective-permute-start | bytes 1572872 | tf_op jit(solution)/shard_map/ppermute | solution.py:556
  6.3 25.3 %collective-permute-start.2 = (f32[512,256]{1,0:T(8,128)}, f32[512,256]{1,0:T(8,128)}, u32[]{:S(2)}, u32[]{:S(2)}) collective-permute-start(f32[512,256]{1,0:T(8,128)} %fusion.1.refs_0_), channel_id=1, source_target_pairs={{0,16},{4,20},{8,24},{12,28},{16,0},{20,4},{24,8},{28,12},{1,17},{... | collective-permute-start | bytes 1572872 | tf_op jit(solution)/shard_map/ppermute | solution.py:556
  8.6 23.0 %collective-permute-start = (f32[512,256]{1,0:T(8,128)}, f32[512,256]{1,0:T(8,128)}, u32[]{:S(2)}, u32[]{:S(2)}) collective-permute-start(f32[512,256]{1,0:T(8,128)} %fusion.1.refs_0_), channel_id=1, source_target_pairs={{0,8},{4,12},{8,0},{12,4},{16,24},{20,28},{24,16},{28,20},{1,9},{5... | collective-permute-start | bytes 1572872 | tf_op jit(solution)/shard_map/ppermute | solution.py:556
  10.1 10.1 %copy-start.4 = (bf16[512,512]{1,0:T(8,128)(2,1)}, bf16[512,512]{1,0:T(8,128)(2,1)S(1)}, u32[]{:S(2)}) copy-start(bf16[512,512]{1,0:T(8,128)(2,1)S(1)} %fusion.pick_ref) | copy-start | bytes 1572868
  17.9 67.1 %collective-permute-start.12 = (f32[256,2048]{1,0:T(8,128)S(1)}, f32[256,2048]{1,0:T(8,128)}, u32[]{:S(2)}, u32[]{:S(2)}) collective-permute-start(f32[256,2048]{1,0:T(8,128)S(1)} %get-tuple-element.116.refs_8_.refs_9_), channel_id=1, source_target_pairs={{0,2},{1,3},{2,0},{3,1},{4,6},{5,7},{6,4},{7,5},{8,10},{9,11},{10,... | collective-permute-start | bytes 6291464 | tf_op jit(solution)/shard_map/ppermute | solution.py:556
  20.6 12.6 %copy-start.9 = (f32[512,256]{1,0:T(8,128)S(1)}, f32[512,256]{1,0:T(8,128)}, u32[]{:S(2)}) copy-start(f32[512,256]{1,0:T(8,128)} %copy-done.8) | copy-start | bytes 1572868
  31.6 11.9 %collective-permute-start.5 = (f32[512,256]{1,0:T(8,128)}, f32[512,256]{1,0:T(8,128)S(1)}, u32[]{:S(2)}, u32[]{:S(2)}) collective-permute-start(f32[512,256]{1,0:T(8,128)} %collective-permute-done.2.refs_3_.refs_4_), channel_id=1, source_target_pairs={{0,8},{4,12},{8,0},{12,4},{16,24},{20,28},{24,16},{28,20},{1,9},{5... | collective-permute-start | bytes 1572872 | tf_op jit(solution)/shard_map/ppermute | solution.py:556
  33.0 11.9 %collective-permute-start.4 = (f32[512,256]{1,0:T(8,128)}, f32[512,256]{1,0:T(8,128)S(1)}, u32[]{:S(2)}, u32[]{:S(2)}) collective-permute-start(f32[512,256]{1,0:T(8,128)} %collective-permute-done.2.refs_3_.refs_4_), channel_id=1, source_target_pairs={{0,4},{4,0},{8,12},{12,8},{16,20},{20,16},{24,28},{28,24},{1,5},{5... | collective-permute-start | bytes 1572872 | tf_op jit(solution)/shard_map/ppermute | solution.py:556
  43.5 12.3 %copy-start.7 = (f32[96,2048]{1,0:T(8,128)S(1)}, f32[96,2048]{1,0:T(8,128)}, u32[]{:S(2)}) copy-start(f32[96,2048]{1,0:T(8,128)} %copy-done.6) | copy-start | bytes 2359300
  43.5 18.7 %copy-start.3 = (f32[160,2048]{1,0:T(8,128)S(1)}, f32[160,2048]{1,0:T(8,128)}, u32[]{:S(2)}) copy-start(f32[160,2048]{1,0:T(8,128)} %copy-done.2) | copy-start | bytes 3932164
  44.9 10.9 %collective-permute-start.6 = (f32[512,256]{1,0:T(8,128)S(1)}, f32[512,256]{1,0:T(8,128)S(1)}, u32[]{:S(2)}, u32[]{:S(2)}) collective-permute-start(f32[512,256]{1,0:T(8,128)S(1)} %copy-done.9), channel_id=1, source_target_pairs={{0,8},{4,12},{8,0},{12,4},{16,24},{20,28},{24,16},{28,20},{1,9},{5... | collective-permute-start | bytes 1572872 | tf_op jit(solution)/shard_map/ppermute | solution.py:556
  45.2 16.4 %collective-permute-start.7 = (f32[512,256]{1,0:T(8,128)S(1)}, f32[512,256]{1,0:T(8,128)S(1)}, u32[]{:S(2)}, u32[]{:S(2)}) collective-permute-start(f32[512,256]{1,0:T(8,128)S(1)} %collective-permute-done.5.refs_2_.refs_6_), channel_id=1, source_target_pairs={{0,4},{4,0},{8,12},{12,8},{16,20},{20,16},{24,28},{28,24},{1,5},{5... | collective-permute-start | bytes 1572872 | tf_op jit(solution)/shard_map/ppermute | solution.py:556
  55.8 29.2 %collective-permute-start.13 = (f32[96,2048]{1,0:T(8,128)S(1)}, f32[96,2048]{1,0:T(8,128)S(1)}, u32[]{:S(2)}, u32[]{:S(2)}) collective-permute-start(f32[96,2048]{1,0:T(8,128)S(1)} %copy-done.7), channel_id=1, source_target_pairs={{0,2},{1,3},{2,0},{3,1},{4,6},{5,7},{6,4},{7,5},{8,10},{9,11},{10,... | collective-permute-start | bytes 2359304 | tf_op jit(solution)/shard_map/ppermute | solution.py:556
  56.0 18.2 %collective-permute-start.10 = (f32[512,256]{1,0:T(8,128)}, f32[512,256]{1,0:T(8,128)S(1)}, u32[]{:S(2)}, u32[]{:S(2)}) collective-permute-start(f32[512,256]{1,0:T(8,128)} %collective-permute-done.3.refs_0_), channel_id=1, source_target_pairs={{0,4},{4,0},{8,12},{12,8},{16,20},{20,16},{24,28},{28,24},{1,5},{5... | collective-permute-start | bytes 1572872 | tf_op jit(solution)/shard_map/ppermute | solution.py:556
  56.3 28.8 %collective-permute-start.11 = (f32[512,256]{1,0:T(8,128)}, f32[512,256]{1,0:T(8,128)S(1)}, u32[]{:S(2)}, u32[]{:S(2)}) collective-permute-start(f32[512,256]{1,0:T(8,128)} %collective-permute-done.3.refs_0_), channel_id=1, source_target_pairs={{0,16},{4,20},{8,24},{12,28},{16,0},{20,4},{24,8},{28,12},{1,17},{... | collective-permute-start | bytes 1572872 | tf_op jit(solution)/shard_map/ppermute | solution.py:556
  61.5 23.5 %collective-permute-start.9 = (f32[512,256]{1,0:T(8,128)}, f32[512,256]{1,0:T(8,128)S(1)}, u32[]{:S(2)}, u32[]{:S(2)}) collective-permute-start(f32[512,256]{1,0:T(8,128)} %collective-permute-done.3.refs_0_), channel_id=1, source_target_pairs={{0,8},{4,12},{8,0},{12,4},{16,24},{20,28},{24,16},{28,20},{1,9},{5... | collective-permute-start | bytes 1572872 | tf_op jit(solution)/shard_map/ppermute | solution.py:556
  62.2 13.2 %copy-start.5 = (bf16[512,512]{1,0:T(8,128)(2,1)S(1)}, bf16[512,512]{1,0:T(8,128)(2,1)}, u32[]{:S(2)}) copy-start(bf16[512,512]{1,0:T(8,128)(2,1)} %copy-done.4) | copy-start | bytes 1572868
  74.2 8.7 %collective-permute-start.8 = (f32[16,2048]{1,0:T(8,128)S(1)}, f32[16,2048]{1,0:T(8,128)S(1)}, u32[]{:S(2)}, u32[]{:S(2)}) collective-permute-start(f32[16,2048]{1,0:T(8,128)S(1)} %get-tuple-element.119.mine_ref), channel_id=1, source_target_pairs={{0,2},{1,3},{2,0},{3,1},{4,6},{5,7},{6,4},{7,5},{8,10},{9,11},{10,... | collective-permute-start | bytes 393224 | tf_op jit(solution)/shard_map/ppermute | solution.py:556
  85.0 33.6 %collective-permute-start.22 = (f32[160,2048]{1,0:T(8,128)S(1)}, f32[160,2048]{1,0:T(8,128)S(1)}, u32[]{:S(2)}, u32[]{:S(2)}) collective-permute-start(f32[160,2048]{1,0:T(8,128)S(1)} %copy-done.3), channel_id=1, source_target_pairs={{0,2},{1,3},{2,0},{3,1},{4,6},{5,7},{6,4},{7,5},{8,10},{9,11},{10,... | collective-permute-start | bytes 3932168 | tf_op jit(solution)/shard_map/ppermute | solution.py:556
  86.3 16.9 %collective-permute-start.18 = (f32[512,256]{1,0:T(8,128)S(1)}, f32[512,256]{1,0:T(8,128)S(1)}, u32[]{:S(2)}, u32[]{:S(2)}) collective-permute-start(f32[512,256]{1,0:T(8,128)S(1)} %collective-permute-done.11.refs_3_.refs_4_), channel_id=1, source_target_pairs={{0,8},{4,12},{8,0},{12,4},{16,24},{20,28},{24,16},{28,20},{1,9},{5... | collective-permute-start | bytes 1572872 | tf_op jit(solution)/shard_map/ppermute | solution.py:556
  86.3 16.9 %collective-permute-start.17 = (f32[512,256]{1,0:T(8,128)S(1)}, f32[512,256]{1,0:T(8,128)S(1)}, u32[]{:S(2)}, u32[]{:S(2)}) collective-permute-start(f32[512,256]{1,0:T(8,128)S(1)} %collective-permute-done.11.refs_3_.refs_4_), channel_id=1, source_target_pairs={{0,4},{4,0},{8,12},{12,8},{16,20},{20,16},{24,28},{28,24},{1,5},{5... | collective-permute-start | bytes 1572872 | tf_op jit(solution)/shard_map/ppermute | solution.py:556
  87.6 4.2 %collective-permute-start.15 = (f32[16,2048]{1,0:T(8,128)S(1)}, f32[16,2048]{1,0:T(8,128)S(1)}, u32[]{:S(2)}, u32[]{:S(2)}) collective-permute-start(f32[16,2048]{1,0:T(8,128)S(1)} %add.9), channel_id=1, source_target_pairs={{0,1},{1,0},{2,3},{3,2},{4,5},{5,4},{6,7},{7,6},{8,9},{9,8},{10,11... | collective-permute-start | bytes 393224 | tf_op jit(solution)/shard_map/ppermute | solution.py:556
  91.9 11.3 %collective-permute-start.16 = (f32[8,1024]{1,0:T(8,128)S(1)}, f32[8,1024]{1,0:T(8,128)S(1)}, u32[]{:S(2)}, u32[]{:S(2)}) collective-permute-start(f32[8,1024]{1,0:T(8,128)S(1)} %get-tuple-element.132), channel_id=1, source_target_pairs={{0,8},{4,12},{8,0},{12,4},{16,24},{20,28},{24,16},{28,20},{1,9},{5... | collective-permute-start | bytes 98312 | tf_op jit(solution)/shard_map/ppermute | solution.py:556
  92.8 22.8 %collective-permute-start.14 = (f32[512,256]{1,0:T(8,128)S(1)}, f32[512,256]{1,0:T(8,128)S(1)}, u32[]{:S(2)}, u32[]{:S(2)}) collective-permute-start(f32[512,256]{1,0:T(8,128)S(1)} %collective-permute-done.9.refs_2_), channel_id=1, source_target_pairs={{0,4},{4,0},{8,12},{12,8},{16,20},{20,16},{24,28},{28,24},{1,5},{5... | collective-permute-start | bytes 1572872 | tf_op jit(solution)/shard_map/ppermute | solution.py:556
  103.2 12.9 %collective-permute-start.19 = (f32[512,256]{1,0:T(8,128)S(1)}, f32[512,256]{1,0:T(8,128)S(1)}, u32[]{:S(2)}, u32[]{:S(2)}) collective-permute-start(f32[512,256]{1,0:T(8,128)S(1)} %collective-permute-done.17.refs_0_.refs_5_), channel_id=1, source_target_pairs={{0,8},{4,12},{8,0},{12,4},{16,24},{20,28},{24,16},{28,20},{1,9},{5... | collective-permute-start | bytes 1572872 | tf_op jit(solution)/shard_map/ppermute | solution.py:556
  103.8 7.5 %collective-permute-start.20 = (f32[8,1024]{1,0:T(8,128)S(1)}, f32[8,1024]{1,0:T(8,128)S(1)}, u32[]{:S(2)}, u32[]{:S(2)}) collective-permute-start(f32[8,1024]{1,0:T(8,128)S(1)} %add.10), channel_id=1, source_target_pairs={{0,4},{4,0},{8,12},{12,8},{16,20},{20,16},{24,28},{28,24},{1,5},{5... | collective-permute-start | bytes 98312 | tf_op jit(solution)/shard_map/ppermute | solution.py:556
  111.3 7.3 %collective-permute-start.21 = (f32[8,1024]{1,0:T(8,128)S(1)}, f32[8,1024]{1,0:T(8,128)S(1)}, u32[]{:S(2)}, u32[]{:S(2)}) collective-permute-start(f32[8,1024]{1,0:T(8,128)S(1)} %add.11.refs_19_), channel_id=1, source_target_pairs={{0,16},{4,20},{8,24},{12,28},{16,0},{20,4},{24,8},{28,12},{1,17},{... | collective-permute-start | bytes 98312 | tf_op jit(solution)/shard_map/ppermute | solution.py:556
  136.6 11.2 %collective-permute-start.23 = (f32[520,2048]{1,0:T(8,128)}, f32[520,2048]{1,0:T(8,128)S(1)}, u32[]{:S(2)}, u32[]{:S(2)}) collective-permute-start(f32[520,2048]{1,0:T(8,128)} %get-tuple-element.157.refs_9_), channel_id=1, source_target_pairs={{0,1},{1,0},{2,3},{3,2},{4,5},{5,4},{6,7},{7,6},{8,9},{9,8},{10,11... | collective-permute-start | bytes 12779528 | tf_op jit(solution)/shard_map/ppermute | solution.py:556
  147.8 4.9 %copy-start.1 = (f32[256,512]{1,0:T(8,128)S(1)}, f32[256,512]{1,0:T(8,128)}, u32[]{:S(2)}) copy-start(f32[256,512]{1,0:T(8,128)} %param.7) | copy-start | bytes 1572868
  (4 other events, 3.8 us)

commit v9 on v8

--- a/solution.py
+++ b/solution.py
@@ -8,7 +8,7 @@
 
 NB = 4
 XS = 3
-XCUT = (0, 8, 11, 16)
+XCUT = (0, 16, 21, 32)
 EPS = 1e-06
 BF = jnp.bfloat16
 F32 = jnp.float32
@@ -608,7 +608,7 @@
         x0 = send(x_own[0])
         logits, *x_own = tie(logits, *x_own)
         *e_one, z_one = exp_parts(where, keys(0, 1, 2, 4), KC, logits, weights, dens_row, None, False, 2 * tile)
-        o1, oy, o2, theirs, z_one, *x_own = tie(o1, oy, o2, theirs, z_one, *x_own)
+        theirs, o1, oy, o2, z_one, *x_own = tie(theirs, o1, oy, o2, z_one, *x_own)
         o2y, o3 = hop(o2, 1), hop(o2, 2)
         acc = fwd("own_early", [mine, oy, o1, o2], [(*e_one, 4 * KC, 0)], None, None, None)
         acc, o2y, o3, oy, theirs, z_one, logits = tie(acc, o2y, o3, oy, theirs, z_one, logits)
@@ -633,8 +633,8 @@
     info_x = swap(info, "gene", 2)
     predicted = emit(where, pred_own, pick, 2 * tile)
     if ring:
-        predicted, info_x, t1, ty, t2, theirs, x0, x1, held = tie(
-            predicted, info_x, t1, ty, t2, theirs, x0, x1, x_own[2]
+        predicted, info_x, x1, ty, t1, t2, theirs, x0, held = tie(
+            predicted, info_x, x1, ty, t1, t2, theirs, x0, x_own[2]
         )
         t2y, t3, x2, t1y = hop(t2, 1), hop(t2, 2), send(held), hop(t1, 1)
         x_got = [x0, x1, x2]

time: 153 us -> 152 us (level)
    unnamed x24 -> x28, local copies, waits for them, and re-layouts: 3.07 us -> 3.06 us
  transfers between devices with their start and end apart: 24 -> 24, of which waited for: 7 -> 7; matrix products, arithmetic and copies ran while one was open for 1% -> 1% of each run, Pallas kernels for 50% -> 51%
where the time goes in v9:
time: 152 us; the launch traced here: 151 us
  Pallas kernels  99.5 us (65%)
  starting transfers between devices  30.2 us (20%)
  waiting for transfers between devices  13.6 us (9%)
  local copies, waits for them, and re-layouts  3.43 us (2%)
  other arithmetic  2.24 us (1%)
    pallas_call x13, Pallas kernels, call(): pl.pallas_call(kernel, out_shape=out_shape, grid_spec=pltpu.PrefetchScala...  99.3 us
    ppermute x24, starting transfers between devices, swap(): lax.ppermute(value, axis, [(i, i ^ bit) for i in range(lax.axis_size(axis...  30.2 us
    ppermute x24, waiting for transfers between devices, swap(): lax.ppermute(value, axis, [(i, i ^ bit) for i in range(lax.axis_size(axis...  13.6 us
    unnamed x28, local copies, waits for them, and re-layouts  3.06 us
  transfers between devices with their start and end apart: 24, of which 7 were waited for; matrix products, arithmetic and copies ran while one was open for 1% of the time, Pallas kernels for 51%

profile of v9, /device:TPU:1, one launch (start us, length us, event | category | flops | bytes accessed | tf_op | source)
XLA Modules:
  0.0 151.2 jit_solution(18370834487413915886)
XLA Ops:
  1.7 1.3 fusion.1.refs_0_
  3.0 2.1 %collective-permute-start.2 = (f32[512,256]{1,0:T(8,128)}, f32[512,256]{1,0:T(8,128)S(1)}, u32[]{:S(2)}, u32[]{:S(2)}) collective-permute-start(f32[512,256]{1,0:T(8,128)} %fusion.1.refs_0_), channel_id=1, source_target_pairs={{0,4},{4,0},{8,12},{12,8},{16,20},{20,16},{24,28},{28,24},{1,5},{5... | collective-permute-start | bytes 1572872 | tf_op jit(solution)/shard_map/ppermute | solution.py:556
  5.1 2.3 %collective-permute-start.3 = (f32[512,256]{1,0:T(8,128)}, f32[512,256]{1,0:T(8,128)}, u32[]{:S(2)}, u32[]{:S(2)}) collective-permute-start(f32[512,256]{1,0:T(8,128)} %fusion.1.refs_0_), channel_id=1, source_target_pairs={{0,16},{4,20},{8,24},{12,28},{16,0},{20,4},{24,8},{28,12},{1,17},{... | collective-permute-start | bytes 1572872 | tf_op jit(solution)/shard_map/ppermute | solution.py:556
  7.4 1.3 collective-permute-start.1
  8.7 1.2 collective-permute-start
  10.1 5.0 %turn.1 = (f32[256,2048]{1,0:T(8,128)S(1)}, f32[80,2048]{1,0:T(8,128)S(1)}, f32[176,2048]{1,0:T(8,128)S(1)}) custom-call(s32[3]{0:T(128)S(1)} %pad_add_fusion.where, bf16[512,512]{1,0:T(8,128)(2,1)S(1)} %fusion.pick_ref, f32[2048,512]{1,0:T(8,128)} %x_ref.1), custom_call_target="tpu_custom_call" | custom-call | flops 1000 | bytes 1000 | tf_op jit(solution)/shard_map/turn/pallas_call | solution.py:33
  15.2 1.1 copy-done.2
  20.6 6.2 %exp_parts.2 = (bf16[1024,2048]{1,0:T(8,128)(2,1)S(1)}, bf16[1024,2048]{1,0:T(8,128)(2,1)S(1)}, f32[8,2048]{1,0:T(8,128)S(1)}) custom-call(s32[3]{0:T(128)S(1)} %pad_add_fusion.where, f32[2048,2048]{1,0:T(8,128)} %logit_ref, f32[2048,2048]{1,0:T(8,128)} %logit_ref, f32[2048,2048]{1,0:T(8,128)} %logit_ref, f32[2048,2048]{1,0:T(8,128)} %logit_ref, ...), custom_call_target="tpu_custom_call" | custom-call | flops 1000 | bytes 1000 | tf_op jit(solution)/shard_map/exp_parts/pallas_call | solution.py:33
  26.8 3.6 %collective-permute-done.3.refs_3_.refs_4_ = f32[512,256]{1,0:T(8,128)} collective-permute-done((f32[512,256]{1,0:T(8,128)}, f32[512,256]{1,0:T(8,128)}, u32[]{:S(2)}, u32[]{:S(2)}) %collective-permute-start.3) | collective-permute-done | bytes 524320 | tf_op jit(solution)/shard_map/ppermute | solution.py:556
  30.4 1.4 collective-permute-start.5
  32.0 10.3 %own_early.1.refs_6_ = f32[512,2048]{1,0:T(8,128)S(1)} custom-call(s32[3]{0:T(128)S(1)} %pad_add_fusion.where, f32[512,256]{1,0:T(8,128)} %fusion.1.refs_0_, f32[512,256]{1,0:T(8,128)S(1)} %copy-done.9, f32[512,256]{1,0:T(8,128)} %collective-permute-done.1.refs_2_, f32[512,256]{1,0:T(8,128)} %collective-permute-done.3.refs_3_.refs_4_, ...), custom_call_target="tpu_custom_call" | custom-call | flops 1000 | bytes 1000 | tf_op jit(solution)/shard_map/own_early/pallas_call | solution.py:33
  42.3 1.4 collective-permute-done.4.refs_1_.refs_5_
  44.2 1.2 collective-permute-start.10
  45.4 6.4 %exp_parts.3 = (bf16[1024,2048]{1,0:T(8,128)(2,1)S(1)}, bf16[1024,2048]{1,0:T(8,128)(2,1)S(1)}, f32[8,2048]{1,0:T(8,128)S(1)}) custom-call(s32[3]{0:T(128)S(1)} %pad_add_fusion.where, f32[2048,2048]{1,0:T(8,128)} %logit_ref, f32[2048,2048]{1,0:T(8,128)} %logit_ref, f32[2048,2048]{1,0:T(8,128)} %logit_ref, f32[2048,2048]{1,0:T(8,128)} %logit_ref, ...), custom_call_target="tpu_custom_call" | custom-call | flops 1000 | bytes 1000 | tf_op jit(solution)/shard_map/exp_parts/pallas_call | solution.py:33
  51.9 2.7 %collective-permute-done.6.refs_0_.refs_3_ = f32[512,256]{1,0:T(8,128)S(1)} collective-permute-done((f32[512,256]{1,0:T(8,128)S(1)}, f32[512,256]{1,0:T(8,128)S(1)}, u32[]{:S(2)}, u32[]{:S(2)}) %collective-permute-start.6) | collective-permute-done | bytes 524320 | tf_op jit(solution)/shard_map/ppermute | solution.py:556
  54.5 1.2 collective-permute-start.9
  55.8 5.3 %collective-permute-start.12 = (f32[512,256]{1,0:T(8,128)}, f32[512,256]{1,0:T(8,128)S(1)}, u32[]{:S(2)}, u32[]{:S(2)}) collective-permute-start(f32[512,256]{1,0:T(8,128)} %collective-permute-done.refs_0_), channel_id=1, source_target_pairs={{0,16},{4,20},{8,24},{12,28},{16,0},{20,4},{24,8},{28,12},{1,17},{... | collective-permute-start | bytes 1572872 | tf_op jit(solution)/shard_map/ppermute | solution.py:556
  61.8 12.0 %own_late.1 = (f32[512,2048]{1,0:T(8,128)}, f32[16,2048]{1,0:T(8,128)S(1)}) custom-call(s32[3]{0:T(128)S(1)} %pad_add_fusion.where, f32[512,256]{1,0:T(8,128)S(1)} %collective-permute-done.6.refs_0_.refs_3_, f32[512,256]{1,0:T(8,128)S(1)} %collective-permute-done.4.refs_1_.refs_5_, f32[512,256]{1,0:T(8,128)S(1)} %collective-permute-done.5.refs_2_.refs_6_, ...), custom_call_target="tpu_custom_call" | custom-call | flops 1000 | bytes 1000 | tf_op jit(solution)/shard_map/own_late/pallas_call | solution.py:33
  74.1 6.1 %emit.1 = f32[2048,512]{1,0:T(8,128)} custom-call(s32[3]{0:T(128)S(1)} %pad_add_fusion.where, f32[512,2048]{1,0:T(8,128)} %get-tuple-element.118.pred_ref.refs_8_, bf16[512,512]{1,0:T(8,128)(2,1)S(1)} %copy-done.5), custom_call_target="tpu_custom_call" | custom-call | flops 1000 | bytes 1000 | tf_op jit(solution)/shard_map/emit/pallas_call | solution.py:33
  80.1 2.4 %collective-permute-done.8.theirs_ref = f32[16,2048]{1,0:T(8,128)S(1)} collective-permute-done((f32[16,2048]{1,0:T(8,128)S(1)}, f32[16,2048]{1,0:T(8,128)S(1)}, u32[]{:S(2)}, u32[]{:S(2)}) %collective-permute-start.8) | collective-permute-done | bytes 131104 | tf_op jit(solution)/shard_map/ppermute | solution.py:556
  82.6 1.8 %collective-permute-done.12.refs_3_.refs_4_ = f32[512,256]{1,0:T(8,128)S(1)} collective-permute-done((f32[512,256]{1,0:T(8,128)}, f32[512,256]{1,0:T(8,128)S(1)}, u32[]{:S(2)}, u32[]{:S(2)}) %collective-permute-start.12) | collective-permute-done | bytes 524320 | tf_op jit(solution)/shard_map/ppermute | solution.py:556
  85.0 3.3 %collective-permute-start.15 = (f32[16,2048]{1,0:T(8,128)S(1)}, f32[16,2048]{1,0:T(8,128)S(1)}, u32[]{:S(2)}, u32[]{:S(2)}) collective-permute-start(f32[16,2048]{1,0:T(8,128)S(1)} %add.9), channel_id=1, source_target_pairs={{0,1},{1,0},{2,3},{3,2},{4,5},{5,4},{6,7},{7,6},{8,9},{9,8},{10,11... | collective-permute-start | bytes 393224 | tf_op jit(solution)/shard_map/ppermute | solution.py:556
  90.4 1.2 collective-permute-start.14
  91.6 10.1 %other_mid.1.refs_6_ = f32[512,2048]{1,0:T(8,128)S(1)} custom-call(s32[3]{0:T(128)S(1)} %pad_add_fusion.where, f32[512,256]{1,0:T(8,128)} %collective-permute-done.refs_0_, f32[512,256]{1,0:T(8,128)S(1)} %collective-permute-done.10.refs_1_, f32[512,256]{1,0:T(8,128)S(1)} %collective-permute-done.11.refs_2_, ...), custom_call_target="tpu_custom_call" | custom-call | flops 1000 | bytes 1000 | tf_op jit(solution)/shard_map/other_mid/pallas_call | solution.py:33
  102.6 6.3 %other_more.1.refs_6_ = f32[512,2048]{1,0:T(8,128)} custom-call(s32[3]{0:T(128)S(1)} %pad_add_fusion.where, f32[512,256]{1,0:T(8,128)S(1)} %collective-permute-done.17.refs_0_.refs_5_, f32[512,256]{1,0:T(8,128)S(1)} %collective-permute-done.18.refs_1_.refs_6_, bf16[1024,2048]{1,0:T(8,128)(2,1)S(1)} %get-tuple-element.112.refs_4_.refs_2_.refs_3_, ...), custom_call_target="tpu_custom_call" | custom-call | flops 1000 | bytes 1000 | tf_op jit(solution)/shard_map/other_more/pallas_call | solution.py:33
  109.0 2.6 %collective-permute-start.21 = (f32[8,1024]{1,0:T(8,128)S(1)}, f32[8,1024]{1,0:T(8,128)S(1)}, u32[]{:S(2)}, u32[]{:S(2)}) collective-permute-start(f32[8,1024]{1,0:T(8,128)S(1)} %add.11.refs_19_), channel_id=1, source_target_pairs={{0,16},{4,20},{8,24},{12,28},{16,0},{20,4},{24,8},{28,12},{1,17},{... | collective-permute-start | bytes 98312 | tf_op jit(solution)/shard_map/ppermute | solution.py:556
  111.6 2.4 %rows_left.2 = (bf16[1024,512]{1,0:T(8,128)(2,1)S(1)}, bf16[1024,512]{1,0:T(8,128)(2,1)S(1)}) custom-call(s32[3]{0:T(128)S(1)} %pad_add_fusion.where, f32[512,256]{1,0:T(8,128)} %fusion.1.refs_0_, f32[512,256]{1,0:T(8,128)S(1)} %copy-done.9, f32[512,256]{1,0:T(8,128)} %collective-permute-done.1.refs_2_, ...), custom_call_target="tpu_custom_call" | custom-call | flops 1000 | bytes 1000 | tf_op jit(solution)/shard_map/rows_left/pallas_call | solution.py:33
  114.7 2.4 %rows_left.3 = (bf16[1024,512]{1,0:T(8,128)(2,1)S(1)}, bf16[1024,512]{1,0:T(8,128)(2,1)S(1)}) custom-call(s32[3]{0:T(128)S(1)} %pad_add_fusion.where, f32[512,256]{1,0:T(8,128)} %collective-permute-done.refs_0_, f32[512,256]{1,0:T(8,128)S(1)} %collective-permute-done.10.refs_1_, f32[512,256]{1,0:T(8,128)S(1)} %collective-permute-done.11.refs_2_, ...), custom_call_target="tpu_custom_call" | custom-call | flops 1000 | bytes 1000 | tf_op jit(solution)/shard_map/rows_left/pallas_call | solution.py:33
  117.2 17.9 %back_sum.1 = (f32[520,2048]{1,0:T(8,128)}, bf16[1024,2048]{1,0:T(8,128)(2,1)S(1)}, bf16[1024,2048]{1,0:T(8,128)(2,1)S(1)}, f32[8,128]{1,0:T(8,128)S(1)}) custom-call(s32[3]{0:T(128)S(1)} %pad_add_fusion.where, f32[512,256]{1,0:T(8,128)S(1)} %collective-permute-done.14.refs_3_.refs_0_, f32[512,256]{1,0:T(8,128)S(1)} %collective-permute-done.19.refs_7_.refs_1_, ...), custom_call_target="tpu_custom_call" | custom-call | flops 1000 | bytes 1000 | tf_op jit(solution)/shard_map/back_sum/pallas_call | solution.py:33
  135.1 1.9 %collective-permute-start.23 = (f32[520,2048]{1,0:T(8,128)}, f32[520,2048]{1,0:T(8,128)S(1)}, u32[]{:S(2)}, u32[]{:S(2)}) collective-permute-start(f32[520,2048]{1,0:T(8,128)} %get-tuple-element.157.refs_9_), channel_id=1, source_target_pairs={{0,1},{1,0},{2,3},{3,2},{4,5},{5,4},{6,7},{7,6},{8,9},{9,8},{10,11... | collective-permute-start | bytes 12779528 | tf_op jit(solution)/shard_map/ppermute | solution.py:556
  137.0 9.2 %back_own.1.mine_ref = f32[512,2048]{1,0:T(8,128)S(1)} custom-call(s32[3]{0:T(128)S(1)} %pad_add_fusion.where, bf16[1024,512]{1,0:T(8,128)(2,1)S(1)} %get-tuple-element.138.refs_15_.refs_0_, bf16[1024,512]{1,0:T(8,128)(2,1)S(1)} %get-tuple-element.145.refs_16_.refs_1_, bf16[1024,512]{1,0:T(8,128)(2,1)S(1)} %get-tuple-element.146.refs_17_.refs_2_, ...), custom_call_target="tpu_custom_call" | custom-call | flops 1000 | bytes 1000 | tf_op jit(solution)/shard_map/back_own/pallas_call | solution.py:33
  146.3 4.9 %back_end.1 = (f32[512,2048]{1,0:T(8,128)}, f32[3]{0:T(128)}) custom-call(s32[3]{0:T(128)S(1)} %pad_add_fusion.where, f32[512,2048]{1,0:T(8,128)S(1)} %back_own.1.mine_ref, f32[520,2048]{1,0:T(8,128)S(1)} %collective-permute-done.23.got_ref, f32[2048,2048]{1,0:T(8,128)} %logit_ref, f32[8,2048]{1,0:T(8,128)S(1)} %get-tuple-element.115.refs_7_.z_ref, ...), custom_call_target="tpu_custom_call" | custom-call | flops 1000 | bytes 1000 | tf_op jit(solution)/shard_map/back_end/pallas_call | solution.py:33
  (68 shorter events, 11.5 us)
Async XLA Ops:
  0.6 18.3 %copy-start.13 = (s32[2048]{0:T(1024)S(1)}, s32[2048]{0:T(1024)}, u32[]{:S(2)}) copy-start(s32[2048]{0:T(1024)} %param.9) | copy-start | bytes 24580
  0.7 19.9 %copy-start.12 = (f32[2048]{0:T(1024)S(1)}, f32[2048]{0:T(1024)}, u32[]{:S(2)}) copy-start(f32[2048]{0:T(1024)} %param.10) | copy-start | bytes 24580
  3.0 14.1 %collective-permute-start.2 = (f32[512,256]{1,0:T(8,128)}, f32[512,256]{1,0:T(8,128)S(1)}, u32[]{:S(2)}, u32[]{:S(2)}) collective-permute-start(f32[512,256]{1,0:T(8,128)} %fusion.1.refs_0_), channel_id=1, source_target_pairs={{0,4},{4,0},{8,12},{12,8},{16,20},{20,16},{24,28},{28,24},{1,5},{5... | collective-permute-start | bytes 1572872 | tf_op jit(solution)/shard_map/ppermute | solution.py:556
  5.1 25.3 %collective-permute-start.3 = (f32[512,256]{1,0:T(8,128)}, f32[512,256]{1,0:T(8,128)}, u32[]{:S(2)}, u32[]{:S(2)}) collective-permute-start(f32[512,256]{1,0:T(8,128)} %fusion.1.refs_0_), channel_id=1, source_target_pairs={{0,16},{4,20},{8,24},{12,28},{16,0},{20,4},{24,8},{28,12},{1,17},{... | collective-permute-start | bytes 1572872 | tf_op jit(solution)/shard_map/ppermute | solution.py:556
  7.4 23.0 %collective-permute-start.1 = (f32[512,256]{1,0:T(8,128)}, f32[512,256]{1,0:T(8,128)}, u32[]{:S(2)}, u32[]{:S(2)}) collective-permute-start(f32[512,256]{1,0:T(8,128)} %fusion.1.refs_0_), channel_id=1, source_target_pairs={{0,8},{4,12},{8,0},{12,4},{16,24},{20,28},{24,16},{28,20},{1,9},{5... | collective-permute-start | bytes 1572872 | tf_op jit(solution)/shard_map/ppermute | solution.py:556
  8.7 21.7 %collective-permute-start = (f32[512,256]{1,0:T(8,128)}, f32[512,256]{1,0:T(8,128)}, u32[]{:S(2)}, u32[]{:S(2)}) collective-permute-start(f32[512,256]{1,0:T(8,128)} %fusion.1.refs_0_), channel_id=1, source_target_pairs={{0,2},{1,3},{2,0},{3,1},{4,6},{5,7},{6,4},{7,5},{8,10},{9,11},{10,... | collective-permute-start | bytes 1572872 | tf_op jit(solution)/shard_map/ppermute | solution.py:556
  10.0 10.2 %copy-start.4 = (bf16[512,512]{1,0:T(8,128)(2,1)}, bf16[512,512]{1,0:T(8,128)(2,1)S(1)}, u32[]{:S(2)}) copy-start(bf16[512,512]{1,0:T(8,128)(2,1)S(1)} %fusion.pick_ref) | copy-start | bytes 1572868
  17.9 66.5 %collective-permute-start.13 = (f32[256,2048]{1,0:T(8,128)S(1)}, f32[256,2048]{1,0:T(8,128)}, u32[]{:S(2)}, u32[]{:S(2)}) collective-permute-start(f32[256,2048]{1,0:T(8,128)S(1)} %get-tuple-element.116.refs_8_.refs_9_), channel_id=1, source_target_pairs={{0,2},{1,3},{2,0},{3,1},{4,6},{5,7},{6,4},{7,5},{8,10},{9,11},{10,... | collective-permute-start | bytes 6291464 | tf_op jit(solution)/shard_map/ppermute | solution.py:556
  20.6 11.4 %copy-start.9 = (f32[512,256]{1,0:T(8,128)S(1)}, f32[512,256]{1,0:T(8,128)}, u32[]{:S(2)}) copy-start(f32[512,256]{1,0:T(8,128)} %copy-done.8) | copy-start | bytes 1572868
  30.4 11.9 %collective-permute-start.5 = (f32[512,256]{1,0:T(8,128)}, f32[512,256]{1,0:T(8,128)S(1)}, u32[]{:S(2)}, u32[]{:S(2)}) collective-permute-start(f32[512,256]{1,0:T(8,128)} %collective-permute-done.3.refs_3_.refs_4_), channel_id=1, source_target_pairs={{0,8},{4,12},{8,0},{12,4},{16,24},{20,28},{24,16},{28,20},{1,9},{5... | collective-permute-start | bytes 1572872 | tf_op jit(solution)/shard_map/ppermute | solution.py:556
  31.8 11.9 %collective-permute-start.4 = (f32[512,256]{1,0:T(8,128)}, f32[512,256]{1,0:T(8,128)S(1)}, u32[]{:S(2)}, u32[]{:S(2)}) collective-permute-start(f32[512,256]{1,0:T(8,128)} %collective-permute-done.3.refs_3_.refs_4_), channel_id=1, source_target_pairs={{0,4},{4,0},{8,12},{12,8},{16,20},{20,16},{24,28},{28,24},{1,5},{5... | collective-permute-start | bytes 1572872 | tf_op jit(solution)/shard_map/ppermute | solution.py:556
  42.3 12.3 %copy-start.7 = (f32[80,2048]{1,0:T(8,128)S(1)}, f32[80,2048]{1,0:T(8,128)}, u32[]{:S(2)}) copy-start(f32[80,2048]{1,0:T(8,128)} %copy-done.6) | copy-start | bytes 1966084
  42.3 19.5 %copy-start.3 = (f32[176,2048]{1,0:T(8,128)S(1)}, f32[176,2048]{1,0:T(8,128)}, u32[]{:S(2)}) copy-start(f32[176,2048]{1,0:T(8,128)} %copy-done.2) | copy-start | bytes 4325380
  43.7 10.9 %collective-permute-start.6 = (f32[512,256]{1,0:T(8,128)S(1)}, f32[512,256]{1,0:T(8,128)S(1)}, u32[]{:S(2)}, u32[]{:S(2)}) collective-permute-start(f32[512,256]{1,0:T(8,128)S(1)} %copy-done.9), channel_id=1, source_target_pairs={{0,8},{4,12},{8,0},{12,4},{16,24},{20,28},{24,16},{28,20},{1,9},{5... | collective-permute-start | bytes 1572872 | tf_op jit(solution)/shard_map/ppermute | solution.py:556
  44.0 17.1 %collective-permute-start.7 = (f32[512,256]{1,0:T(8,128)S(1)}, f32[512,256]{1,0:T(8,128)S(1)}, u32[]{:S(2)}, u32[]{:S(2)}) collective-permute-start(f32[512,256]{1,0:T(8,128)S(1)} %collective-permute-done.5.refs_2_.refs_6_), channel_id=1, source_target_pairs={{0,4},{4,0},{8,12},{12,8},{16,20},{20,16},{24,28},{28,24},{1,5},{5... | collective-permute-start | bytes 1572872 | tf_op jit(solution)/shard_map/ppermute | solution.py:556
  44.2 29.6 %collective-permute-start.10 = (f32[512,256]{1,0:T(8,128)}, f32[512,256]{1,0:T(8,128)S(1)}, u32[]{:S(2)}, u32[]{:S(2)}) collective-permute-start(f32[512,256]{1,0:T(8,128)} %collective-permute-done.refs_0_), channel_id=1, source_target_pairs={{0,4},{4,0},{8,12},{12,8},{16,20},{20,16},{24,28},{28,24},{1,5},{5... | collective-permute-start | bytes 1572872 | tf_op jit(solution)/shard_map/ppermute | solution.py:556
  54.5 29.9 %collective-permute-start.9 = (f32[80,2048]{1,0:T(8,128)S(1)}, f32[80,2048]{1,0:T(8,128)S(1)}, u32[]{:S(2)}, u32[]{:S(2)}) collective-permute-start(f32[80,2048]{1,0:T(8,128)S(1)} %copy-done.7), channel_id=1, source_target_pairs={{0,2},{1,3},{2,0},{3,1},{4,6},{5,7},{6,4},{7,5},{8,10},{9,11},{10,... | collective-permute-start | bytes 1966088 | tf_op jit(solution)/shard_map/ppermute | solution.py:556
  55.8 28.7 %collective-permute-start.12 = (f32[512,256]{1,0:T(8,128)}, f32[512,256]{1,0:T(8,128)S(1)}, u32[]{:S(2)}, u32[]{:S(2)}) collective-permute-start(f32[512,256]{1,0:T(8,128)} %collective-permute-done.refs_0_), channel_id=1, source_target_pairs={{0,16},{4,20},{8,24},{12,28},{16,0},{20,4},{24,8},{28,12},{1,17},{... | collective-permute-start | bytes 1572872 | tf_op jit(solution)/shard_map/ppermute | solution.py:556
  61.0 23.4 %collective-permute-start.11 = (f32[512,256]{1,0:T(8,128)}, f32[512,256]{1,0:T(8,128)S(1)}, u32[]{:S(2)}, u32[]{:S(2)}) collective-permute-start(f32[512,256]{1,0:T(8,128)} %collective-permute-done.refs_0_), channel_id=1, source_target_pairs={{0,8},{4,12},{8,0},{12,4},{16,24},{20,28},{24,16},{28,20},{1,9},{5... | collective-permute-start | bytes 1572872 | tf_op jit(solution)/shard_map/ppermute | solution.py:556
  61.8 12.3 %copy-start.5 = (bf16[512,512]{1,0:T(8,128)(2,1)S(1)}, bf16[512,512]{1,0:T(8,128)(2,1)}, u32[]{:S(2)}) copy-start(bf16[512,512]{1,0:T(8,128)(2,1)} %copy-done.4) | copy-start | bytes 1572868
  73.8 8.8 %collective-permute-start.8 = (f32[16,2048]{1,0:T(8,128)S(1)}, f32[16,2048]{1,0:T(8,128)S(1)}, u32[]{:S(2)}, u32[]{:S(2)}) collective-permute-start(f32[16,2048]{1,0:T(8,128)S(1)} %get-tuple-element.119.mine_ref), channel_id=1, source_target_pairs={{0,2},{1,3},{2,0},{3,1},{4,6},{5,7},{6,4},{7,5},{8,10},{9,11},{10,... | collective-permute-start | bytes 393224 | tf_op jit(solution)/shard_map/ppermute | solution.py:556
  84.4 17.3 %copy-start.10 = (f32[80,2048]{1,0:T(8,128)}, f32[80,2048]{1,0:T(8,128)S(1)}, u32[]{:S(2)}) copy-start(f32[80,2048]{1,0:T(8,128)S(1)} %collective-permute-done.9.refs_13_) | copy-start | bytes 1966084
  84.4 32.7 %collective-permute-start.22 = (f32[176,2048]{1,0:T(8,128)S(1)}, f32[176,2048]{1,0:T(8,128)S(1)}, u32[]{:S(2)}, u32[]{:S(2)}) collective-permute-start(f32[176,2048]{1,0:T(8,128)S(1)} %copy-done.3), channel_id=1, source_target_pairs={{0,2},{1,3},{2,0},{3,1},{4,6},{5,7},{6,4},{7,5},{8,10},{9,11},{10,... | collective-permute-start | bytes 4325384 | tf_op jit(solution)/shard_map/ppermute | solution.py:556
  84.8 17.0 %collective-permute-start.18 = (f32[512,256]{1,0:T(8,128)S(1)}, f32[512,256]{1,0:T(8,128)S(1)}, u32[]{:S(2)}, u32[]{:S(2)}) collective-permute-start(f32[512,256]{1,0:T(8,128)S(1)} %collective-permute-done.12.refs_3_.refs_4_), channel_id=1, source_target_pairs={{0,8},{4,12},{8,0},{12,4},{16,24},{20,28},{24,16},{28,20},{1,9},{5... | collective-permute-start | bytes 1572872 | tf_op jit(solution)/shard_map/ppermute | solution.py:556
  84.9 16.9 %collective-permute-start.17 = (f32[512,256]{1,0:T(8,128)S(1)}, f32[512,256]{1,0:T(8,128)S(1)}, u32[]{:S(2)}, u32[]{:S(2)}) collective-permute-start(f32[512,256]{1,0:T(8,128)S(1)} %collective-permute-done.12.refs_3_.refs_4_), channel_id=1, source_target_pairs={{0,4},{4,0},{8,12},{12,8},{16,20},{20,16},{24,28},{28,24},{1,5},{5... | collective-permute-start | bytes 1572872 | tf_op jit(solution)/shard_map/ppermute | solution.py:556
  85.0 4.3 %collective-permute-start.15 = (f32[16,2048]{1,0:T(8,128)S(1)}, f32[16,2048]{1,0:T(8,128)S(1)}, u32[]{:S(2)}, u32[]{:S(2)}) collective-permute-start(f32[16,2048]{1,0:T(8,128)S(1)} %add.9), channel_id=1, source_target_pairs={{0,1},{1,0},{2,3},{3,2},{4,5},{5,4},{6,7},{7,6},{8,9},{9,8},{10,11... | collective-permute-start | bytes 393224 | tf_op jit(solution)/shard_map/ppermute | solution.py:556
  89.5 12.3 %collective-permute-start.16 = (f32[8,1024]{1,0:T(8,128)S(1)}, f32[8,1024]{1,0:T(8,128)S(1)}, u32[]{:S(2)}, u32[]{:S(2)}) collective-permute-start(f32[8,1024]{1,0:T(8,128)S(1)} %get-tuple-element.132), channel_id=1, source_target_pairs={{0,8},{4,12},{8,0},{12,4},{16,24},{20,28},{24,16},{28,20},{1,9},{5... | collective-permute-start | bytes 98312 | tf_op jit(solution)/shard_map/ppermute | solution.py:556
  90.4 23.7 %collective-permute-start.14 = (f32[512,256]{1,0:T(8,128)S(1)}, f32[512,256]{1,0:T(8,128)S(1)}, u32[]{:S(2)}, u32[]{:S(2)}) collective-permute-start(f32[512,256]{1,0:T(8,128)S(1)} %collective-permute-done.11.refs_2_), channel_id=1, source_target_pairs={{0,4},{4,0},{8,12},{12,8},{16,20},{20,16},{24,28},{28,24},{1,5},{5... | collective-permute-start | bytes 1572872 | tf_op jit(solution)/shard_map/ppermute | solution.py:556
  101.8 12.9 %collective-permute-start.19 = (f32[512,256]{1,0:T(8,128)S(1)}, f32[512,256]{1,0:T(8,128)S(1)}, u32[]{:S(2)}, u32[]{:S(2)}) collective-permute-start(f32[512,256]{1,0:T(8,128)S(1)} %collective-permute-done.17.refs_0_.refs_5_), channel_id=1, source_target_pairs={{0,8},{4,12},{8,0},{12,4},{16,24},{20,28},{24,16},{28,20},{1,9},{5... | collective-permute-start | bytes 1572872 | tf_op jit(solution)/shard_map/ppermute | solution.py:556
  102.4 6.5 %collective-permute-start.20 = (f32[8,1024]{1,0:T(8,128)S(1)}, f32[8,1024]{1,0:T(8,128)S(1)}, u32[]{:S(2)}, u32[]{:S(2)}) collective-permute-start(f32[8,1024]{1,0:T(8,128)S(1)} %add.10), channel_id=1, source_target_pairs={{0,4},{4,0},{8,12},{12,8},{16,20},{20,16},{24,28},{28,24},{1,5},{5... | collective-permute-start | bytes 98312 | tf_op jit(solution)/shard_map/ppermute | solution.py:556
  109.0 8.2 %collective-permute-start.21 = (f32[8,1024]{1,0:T(8,128)S(1)}, f32[8,1024]{1,0:T(8,128)S(1)}, u32[]{:S(2)}, u32[]{:S(2)}) collective-permute-start(f32[8,1024]{1,0:T(8,128)S(1)} %add.11.refs_19_), channel_id=1, source_target_pairs={{0,16},{4,20},{8,24},{12,28},{16,0},{20,4},{24,8},{28,12},{1,17},{... | collective-permute-start | bytes 98312 | tf_op jit(solution)/shard_map/ppermute | solution.py:556
  135.1 11.2 %collective-permute-start.23 = (f32[520,2048]{1,0:T(8,128)}, f32[520,2048]{1,0:T(8,128)S(1)}, u32[]{:S(2)}, u32[]{:S(2)}) collective-permute-start(f32[520,2048]{1,0:T(8,128)} %get-tuple-element.157.refs_9_), channel_id=1, source_target_pairs={{0,1},{1,0},{2,3},{3,2},{4,5},{5,4},{6,7},{7,6},{8,9},{9,8},{10,11... | collective-permute-start | bytes 12779528 | tf_op jit(solution)/shard_map/ppermute | solution.py:556
  (6 other events, 16.9 us)

commit v10 on v9

--- a/solution.py
+++ b/solution.py
@@ -15,7 +15,7 @@
 KC = 256
 NT = (((1,), (1,)), ((), ()))
 TN = (((0,), (0,)), ((), ()))
-VMEM_LIMIT = 22 << 20
+VMEM_LIMIT = 21 << 20
 LARGE_LIMIT = 60 << 20
 CHEAP = pl.CostEstimate(flops=1000, bytes_accessed=1000, transcendentals=0)
 
@@ -612,7 +612,7 @@
         o2y, o3 = hop(o2, 1), hop(o2, 2)
         acc = fwd("own_early", [mine, oy, o1, o2], [(*e_one, 4 * KC, 0)], None, None, None)
         acc, o2y, o3, oy, theirs, z_one, logits = tie(acc, o2y, o3, oy, theirs, z_one, logits)
-        o3y, o1y, ty = hop(o3, 1), hop(oy, 2), hop(theirs, 1)
+        o3y, o1y, ty = hop(o2y, 2), hop(o1, 1), hop(theirs, 1)
         *e_two, zinfo = exp_parts(where, keys(3, 5, 6, 7), KC, logits, weights, dens_row, z_one, True, 2 * tile)
         o1y, theirs, zinfo, held = tie(o1y, theirs, zinfo, x_own[1])
         t1, t2, x1 = hop(theirs, 2), hop(theirs, 4), send(held)

time: 152 us -> 151 us (level)
  starting transfers between devices: 30.2 us -> 27.8 us
  waiting for transfers between devices: 13.6 us -> 15.6 us
    ppermute x24, starting transfers between devices: 30.2 us -> 27.8 us  [swap(): lax.ppermute(value, axis, [(i, i ^ bit) for i in range(lax.axis_size(axis...]
    ppermute x24, waiting for transfers between devices: 13.6 us -> 15.6 us  [swap(): lax.ppermute(value, axis, [(i, i ^ bit) for i in range(lax.axis_size(axis...]
    unnamed x28 -> x24, local copies, waits for them, and re-layouts: 3.06 us -> 3.07 us
  transfers between devices with their start and end apart: 24 -> 24, of which waited for: 7 -> 6; matrix products, arithmetic and copies ran while one was open for 1% -> 1% of each run, Pallas kernels for 51% -> 51%
where the time goes in v10:
time: 151 us
  Pallas kernels  99.5 us (66%)
  starting transfers between devices  27.8 us (18%)
  waiting for transfers between devices  15.6 us (10%)
  local copies, waits for them, and re-layouts  3.44 us (2%)
  other arithmetic  2.24 us (1%)
    pallas_call x13, Pallas kernels, call(): pl.pallas_call(kernel, out_shape=out_shape, grid_spec=pltpu.PrefetchScala...  99.4 us
    ppermute x24, starting transfers between devices, swap(): lax.ppermute(value, axis, [(i, i ^ bit) for i in range(lax.axis_size(axis...  27.8 us
    ppermute x24, waiting for transfers between devices, swap(): lax.ppermute(value, axis, [(i, i ^ bit) for i in range(lax.axis_size(axis...  15.6 us
    unnamed x24, local copies, waits for them, and re-layouts  3.07 us
  transfers between devices with their start and end apart: 24, of which 6 were waited for; matrix products, arithmetic and copies ran while one was open for 1% of the time, Pallas kernels for 51%

profile of v10, /device:TPU:1, one launch (start us, length us, event | category | flops | bytes accessed | tf_op | source)
XLA Modules:
  0.0 150.8 jit_solution(17229027234915734214)
XLA Ops:
  1.7 1.3 fusion.1.refs_0_
  3.0 2.1 %collective-permute-start.2 = (f32[512,256]{1,0:T(8,128)}, f32[512,256]{1,0:T(8,128)S(1)}, u32[]{:S(2)}, u32[]{:S(2)}) collective-permute-start(f32[512,256]{1,0:T(8,128)} %fusion.1.refs_0_), channel_id=1, source_target_pairs={{0,4},{4,0},{8,12},{12,8},{16,20},{20,16},{24,28},{28,24},{1,5},{5... | collective-permute-start | bytes 1572872 | tf_op jit(solution)/shard_map/ppermute | solution.py:556
  5.0 2.3 %collective-permute-start.3 = (f32[512,256]{1,0:T(8,128)}, f32[512,256]{1,0:T(8,128)}, u32[]{:S(2)}, u32[]{:S(2)}) collective-permute-start(f32[512,256]{1,0:T(8,128)} %fusion.1.refs_0_), channel_id=1, source_target_pairs={{0,16},{4,20},{8,24},{12,28},{16,0},{20,4},{24,8},{28,12},{1,17},{... | collective-permute-start | bytes 1572872 | tf_op jit(solution)/shard_map/ppermute | solution.py:556
  7.3 1.3 collective-permute-start.1
  8.6 1.2 collective-permute-start
  10.1 5.0 %turn.1 = (f32[256,2048]{1,0:T(8,128)S(1)}, f32[80,2048]{1,0:T(8,128)S(1)}, f32[176,2048]{1,0:T(8,128)S(1)}) custom-call(s32[3]{0:T(128)S(1)} %pad_add_fusion.where, bf16[512,512]{1,0:T(8,128)(2,1)S(1)} %fusion.pick_ref, f32[2048,512]{1,0:T(8,128)} %x_ref.1), custom_call_target="tpu_custom_call" | custom-call | flops 1000 | bytes 1000 | tf_op jit(solution)/shard_map/turn/pallas_call | solution.py:33
  15.2 1.1 copy-done.2
  20.6 6.2 %exp_parts.2 = (bf16[1024,2048]{1,0:T(8,128)(2,1)S(1)}, bf16[1024,2048]{1,0:T(8,128)(2,1)S(1)}, f32[8,2048]{1,0:T(8,128)S(1)}) custom-call(s32[3]{0:T(128)S(1)} %pad_add_fusion.where, f32[2048,2048]{1,0:T(8,128)} %logit_ref, f32[2048,2048]{1,0:T(8,128)} %logit_ref, f32[2048,2048]{1,0:T(8,128)} %logit_ref, f32[2048,2048]{1,0:T(8,128)} %logit_ref, ...), custom_call_target="tpu_custom_call" | custom-call | flops 1000 | bytes 1000 | tf_op jit(solution)/shard_map/exp_parts/pallas_call | solution.py:33
  26.7 3.6 %collective-permute-done.3.refs_3_.refs_4_ = f32[512,256]{1,0:T(8,128)} collective-permute-done((f32[512,256]{1,0:T(8,128)}, f32[512,256]{1,0:T(8,128)}, u32[]{:S(2)}, u32[]{:S(2)}) %collective-permute-start.3) | collective-permute-done | bytes 524320 | tf_op jit(solution)/shard_map/ppermute | solution.py:556
  30.3 1.4 collective-permute-start.6
  32.0 1.2 collective-permute-start.4
  33.2 10.3 %own_early.1.refs_6_ = f32[512,2048]{1,0:T(8,128)S(1)} custom-call(s32[3]{0:T(128)S(1)} %pad_add_fusion.where, f32[512,256]{1,0:T(8,128)} %fusion.1.refs_0_, f32[512,256]{1,0:T(8,128)S(1)} %copy-done.9, f32[512,256]{1,0:T(8,128)} %collective-permute-done.1.refs_2_, f32[512,256]{1,0:T(8,128)} %collective-permute-done.3.refs_3_.refs_4_, ...), custom_call_target="tpu_custom_call" | custom-call | flops 1000 | bytes 1000 | tf_op jit(solution)/shard_map/own_early/pallas_call | solution.py:33
  44.1 6.4 %exp_parts.3 = (bf16[1024,2048]{1,0:T(8,128)(2,1)S(1)}, bf16[1024,2048]{1,0:T(8,128)(2,1)S(1)}, f32[8,2048]{1,0:T(8,128)S(1)}) custom-call(s32[3]{0:T(128)S(1)} %pad_add_fusion.where, f32[2048,2048]{1,0:T(8,128)} %logit_ref, f32[2048,2048]{1,0:T(8,128)} %logit_ref, f32[2048,2048]{1,0:T(8,128)} %logit_ref, f32[2048,2048]{1,0:T(8,128)} %logit_ref, ...), custom_call_target="tpu_custom_call" | custom-call | flops 1000 | bytes 1000 | tf_op jit(solution)/shard_map/exp_parts/pallas_call | solution.py:33
  50.6 4.3 %collective-permute-done.4.refs_0_.refs_3_ = f32[512,256]{1,0:T(8,128)S(1)} collective-permute-done((f32[512,256]{1,0:T(8,128)}, f32[512,256]{1,0:T(8,128)S(1)}, u32[]{:S(2)}, u32[]{:S(2)}) %collective-permute-start.4) | collective-permute-done | bytes 524320 | tf_op jit(solution)/shard_map/ppermute | solution.py:556
  54.9 1.2 collective-permute-start.9
  56.1 4.2 %collective-permute-start.12 = (f32[512,256]{1,0:T(8,128)}, f32[512,256]{1,0:T(8,128)S(1)}, u32[]{:S(2)}, u32[]{:S(2)}) collective-permute-start(f32[512,256]{1,0:T(8,128)} %collective-permute-done.refs_0_), channel_id=1, source_target_pairs={{0,16},{4,20},{8,24},{12,28},{16,0},{20,4},{24,8},{28,12},{1,17},{... | collective-permute-start | bytes 1572872 | tf_op jit(solution)/shard_map/ppermute | solution.py:556
  60.7 12.0 %own_late.1 = (f32[512,2048]{1,0:T(8,128)}, f32[16,2048]{1,0:T(8,128)S(1)}) custom-call(s32[3]{0:T(128)S(1)} %pad_add_fusion.where, f32[512,256]{1,0:T(8,128)S(1)} %collective-permute-done.4.refs_0_.refs_3_, f32[512,256]{1,0:T(8,128)S(1)} %collective-permute-done.5.refs_1_.refs_5_, f32[512,256]{1,0:T(8,128)S(1)} %collective-permute-done.6.refs_2_.refs_6_, ...), custom_call_target="tpu_custom_call" | custom-call | flops 1000 | bytes 1000 | tf_op jit(solution)/shard_map/own_late/pallas_call | solution.py:33
  72.9 6.1 %emit.1 = f32[2048,512]{1,0:T(8,128)} custom-call(s32[3]{0:T(128)S(1)} %pad_add_fusion.where, f32[512,2048]{1,0:T(8,128)} %get-tuple-element.117.pred_ref.refs_8_, bf16[512,512]{1,0:T(8,128)(2,1)S(1)} %copy-done.5), custom_call_target="tpu_custom_call" | custom-call | flops 1000 | bytes 1000 | tf_op jit(solution)/shard_map/emit/pallas_call | solution.py:33
  79.0 5.0 %collective-permute-done.12.refs_3_.refs_4_ = f32[512,256]{1,0:T(8,128)S(1)} collective-permute-done((f32[512,256]{1,0:T(8,128)}, f32[512,256]{1,0:T(8,128)S(1)}, u32[]{:S(2)}, u32[]{:S(2)}) %collective-permute-start.12) | collective-permute-done | bytes 524320 | tf_op jit(solution)/shard_map/ppermute | solution.py:556
  84.8 2.8 %collective-permute-start.15 = (f32[16,2048]{1,0:T(8,128)S(1)}, f32[16,2048]{1,0:T(8,128)S(1)}, u32[]{:S(2)}, u32[]{:S(2)}) collective-permute-start(f32[16,2048]{1,0:T(8,128)S(1)} %add.9), channel_id=1, source_target_pairs={{0,1},{1,0},{2,3},{3,2},{4,5},{5,4},{6,7},{7,6},{8,9},{9,8},{10,11... | collective-permute-start | bytes 393224 | tf_op jit(solution)/shard_map/ppermute | solution.py:556
  88.7 1.2 collective-permute-start.16
  90.0 1.2 collective-permute-start.14
  91.2 10.1 %other_mid.1.refs_6_ = f32[512,2048]{1,0:T(8,128)S(1)} custom-call(s32[3]{0:T(128)S(1)} %pad_add_fusion.where, f32[512,256]{1,0:T(8,128)} %collective-permute-done.refs_0_, f32[512,256]{1,0:T(8,128)S(1)} %collective-permute-done.10.refs_1_, f32[512,256]{1,0:T(8,128)S(1)} %collective-permute-done.11.refs_2_, ...), custom_call_target="tpu_custom_call" | custom-call | flops 1000 | bytes 1000 | tf_op jit(solution)/shard_map/other_mid/pallas_call | solution.py:33
  101.9 6.3 %other_more.1.refs_6_ = f32[512,2048]{1,0:T(8,128)} custom-call(s32[3]{0:T(128)S(1)} %pad_add_fusion.where, f32[512,256]{1,0:T(8,128)S(1)} %collective-permute-done.17.refs_0_.refs_5_, f32[512,256]{1,0:T(8,128)S(1)} %collective-permute-done.18.refs_1_.refs_6_, bf16[1024,2048]{1,0:T(8,128)(2,1)S(1)} %get-tuple-element.111.refs_4_.refs_2_.refs_3_, ...), custom_call_target="tpu_custom_call" | custom-call | flops 1000 | bytes 1000 | tf_op jit(solution)/shard_map/other_more/pallas_call | solution.py:33
  108.2 2.1 %collective-permute-start.21 = (f32[8,1024]{1,0:T(8,128)S(1)}, f32[8,1024]{1,0:T(8,128)S(1)}, u32[]{:S(2)}, u32[]{:S(2)}) collective-permute-start(f32[8,1024]{1,0:T(8,128)S(1)} %add.11.refs_19_), channel_id=1, source_target_pairs={{0,16},{4,20},{8,24},{12,28},{16,0},{20,4},{24,8},{28,12},{1,17},{... | collective-permute-start | bytes 98312 | tf_op jit(solution)/shard_map/ppermute | solution.py:556
  110.3 2.4 %rows_left.2 = (bf16[1024,512]{1,0:T(8,128)(2,1)S(1)}, bf16[1024,512]{1,0:T(8,128)(2,1)S(1)}) custom-call(s32[3]{0:T(128)S(1)} %pad_add_fusion.where, f32[512,256]{1,0:T(8,128)} %fusion.1.refs_0_, f32[512,256]{1,0:T(8,128)S(1)} %copy-done.9, f32[512,256]{1,0:T(8,128)} %collective-permute-done.1.refs_2_, ...), custom_call_target="tpu_custom_call" | custom-call | flops 1000 | bytes 1000 | tf_op jit(solution)/shard_map/rows_left/pallas_call | solution.py:33
  112.7 1.6 %collective-permute-done.19.refs_7_.refs_1_ = f32[512,256]{1,0:T(8,128)S(1)} collective-permute-done((f32[512,256]{1,0:T(8,128)S(1)}, f32[512,256]{1,0:T(8,128)S(1)}, u32[]{:S(2)}, u32[]{:S(2)}) %collective-permute-start.19) | collective-permute-done | bytes 524320 | tf_op jit(solution)/shard_map/ppermute | solution.py:556
  114.3 2.4 %rows_left.3 = (bf16[1024,512]{1,0:T(8,128)(2,1)S(1)}, bf16[1024,512]{1,0:T(8,128)(2,1)S(1)}) custom-call(s32[3]{0:T(128)S(1)} %pad_add_fusion.where, f32[512,256]{1,0:T(8,128)} %collective-permute-done.refs_0_, f32[512,256]{1,0:T(8,128)S(1)} %collective-permute-done.10.refs_1_, f32[512,256]{1,0:T(8,128)S(1)} %collective-permute-done.11.refs_2_, ...), custom_call_target="tpu_custom_call" | custom-call | flops 1000 | bytes 1000 | tf_op jit(solution)/shard_map/rows_left/pallas_call | solution.py:33
  116.8 18.0 %back_sum.1 = (f32[520,2048]{1,0:T(8,128)}, bf16[1024,2048]{1,0:T(8,128)(2,1)S(1)}, bf16[1024,2048]{1,0:T(8,128)(2,1)S(1)}, f32[8,128]{1,0:T(8,128)S(1)}) custom-call(s32[3]{0:T(128)S(1)} %pad_add_fusion.where, f32[512,256]{1,0:T(8,128)S(1)} %collective-permute-done.14.refs_3_.refs_0_, f32[512,256]{1,0:T(8,128)S(1)} %collective-permute-done.19.refs_7_.refs_1_, ...), custom_call_target="tpu_custom_call" | custom-call | flops 1000 | bytes 1000 | tf_op jit(solution)/shard_map/back_sum/pallas_call | solution.py:33
  134.7 1.9 %collective-permute-start.23 = (f32[520,2048]{1,0:T(8,128)}, f32[520,2048]{1,0:T(8,128)S(1)}, u32[]{:S(2)}, u32[]{:S(2)}) collective-permute-start(f32[520,2048]{1,0:T(8,128)} %get-tuple-element.157.refs_9_), channel_id=1, source_target_pairs={{0,1},{1,0},{2,3},{3,2},{4,5},{5,4},{6,7},{7,6},{8,9},{9,8},{10,11... | collective-permute-start | bytes 12779528 | tf_op jit(solution)/shard_map/ppermute | solution.py:556
  136.7 9.2 %back_own.1.mine_ref = f32[512,2048]{1,0:T(8,128)S(1)} custom-call(s32[3]{0:T(128)S(1)} %pad_add_fusion.where, bf16[1024,512]{1,0:T(8,128)(2,1)S(1)} %get-tuple-element.138.refs_15_.refs_0_, bf16[1024,512]{1,0:T(8,128)(2,1)S(1)} %get-tuple-element.145.refs_16_.refs_1_, bf16[1024,512]{1,0:T(8,128)(2,1)S(1)} %get-tuple-element.146.refs_17_.refs_2_, ...), custom_call_target="tpu_custom_call" | custom-call | flops 1000 | bytes 1000 | tf_op jit(solution)/shard_map/back_own/pallas_call | solution.py:33
  145.9 4.9 %back_end.1 = (f32[512,2048]{1,0:T(8,128)}, f32[3]{0:T(128)}) custom-call(s32[3]{0:T(128)S(1)} %pad_add_fusion.where, f32[512,2048]{1,0:T(8,128)S(1)} %back_own.1.mine_ref, f32[520,2048]{1,0:T(8,128)S(1)} %collective-permute-done.23.got_ref, f32[2048,2048]{1,0:T(8,128)} %logit_ref, f32[8,2048]{1,0:T(8,128)S(1)} %get-tuple-element.114.refs_7_.z_ref, ...), custom_call_target="tpu_custom_call" | custom-call | flops 1000 | bytes 1000 | tf_op jit(solution)/shard_map/back_end/pallas_call | solution.py:33
  (64 shorter events, 9.6 us)
Async XLA Ops:
  0.6 18.3 %copy-start.11 = (s32[2048]{0:T(1024)S(1)}, s32[2048]{0:T(1024)}, u32[]{:S(2)}) copy-start(s32[2048]{0:T(1024)} %param.9) | copy-start | bytes 24580
  0.7 19.9 %copy-start.10 = (f32[2048]{0:T(1024)S(1)}, f32[2048]{0:T(1024)}, u32[]{:S(2)}) copy-start(f32[2048]{0:T(1024)} %param.10) | copy-start | bytes 24580
  3.0 14.1 %collective-permute-start.2 = (f32[512,256]{1,0:T(8,128)}, f32[512,256]{1,0:T(8,128)S(1)}, u32[]{:S(2)}, u32[]{:S(2)}) collective-permute-start(f32[512,256]{1,0:T(8,128)} %fusion.1.refs_0_), channel_id=1, source_target_pairs={{0,4},{4,0},{8,12},{12,8},{16,20},{20,16},{24,28},{28,24},{1,5},{5... | collective-permute-start | bytes 1572872 | tf_op jit(solution)/shard_map/ppermute | solution.py:556
  5.0 25.3 %collective-permute-start.3 = (f32[512,256]{1,0:T(8,128)}, f32[512,256]{1,0:T(8,128)}, u32[]{:S(2)}, u32[]{:S(2)}) collective-permute-start(f32[512,256]{1,0:T(8,128)} %fusion.1.refs_0_), channel_id=1, source_target_pairs={{0,16},{4,20},{8,24},{12,28},{16,0},{20,4},{24,8},{28,12},{1,17},{... | collective-permute-start | bytes 1572872 | tf_op jit(solution)/shard_map/ppermute | solution.py:556
  7.3 23.0 %collective-permute-start.1 = (f32[512,256]{1,0:T(8,128)}, f32[512,256]{1,0:T(8,128)}, u32[]{:S(2)}, u32[]{:S(2)}) collective-permute-start(f32[512,256]{1,0:T(8,128)} %fusion.1.refs_0_), channel_id=1, source_target_pairs={{0,8},{4,12},{8,0},{12,4},{16,24},{20,28},{24,16},{28,20},{1,9},{5... | collective-permute-start | bytes 1572872 | tf_op jit(solution)/shard_map/ppermute | solution.py:556
  8.6 21.7 %collective-permute-start = (f32[512,256]{1,0:T(8,128)}, f32[512,256]{1,0:T(8,128)}, u32[]{:S(2)}, u32[]{:S(2)}) collective-permute-start(f32[512,256]{1,0:T(8,128)} %fusion.1.refs_0_), channel_id=1, source_target_pairs={{0,2},{1,3},{2,0},{3,1},{4,6},{5,7},{6,4},{7,5},{8,10},{9,11},{10,... | collective-permute-start | bytes 1572872 | tf_op jit(solution)/shard_map/ppermute | solution.py:556
  10.0 10.2 %copy-start.4 = (bf16[512,512]{1,0:T(8,128)(2,1)}, bf16[512,512]{1,0:T(8,128)(2,1)S(1)}, u32[]{:S(2)}) copy-start(bf16[512,512]{1,0:T(8,128)(2,1)S(1)} %fusion.pick_ref) | copy-start | bytes 1572868
  17.9 66.2 %collective-permute-start.13 = (f32[256,2048]{1,0:T(8,128)S(1)}, f32[256,2048]{1,0:T(8,128)}, u32[]{:S(2)}, u32[]{:S(2)}) collective-permute-start(f32[256,2048]{1,0:T(8,128)S(1)} %get-tuple-element.115.refs_8_.refs_9_), channel_id=1, source_target_pairs={{0,2},{1,3},{2,0},{3,1},{4,6},{5,7},{6,4},{7,5},{8,10},{9,11},{10,... | collective-permute-start | bytes 6291464 | tf_op jit(solution)/shard_map/ppermute | solution.py:556
  20.6 12.6 %copy-start.9 = (f32[512,256]{1,0:T(8,128)S(1)}, f32[512,256]{1,0:T(8,128)}, u32[]{:S(2)}) copy-start(f32[512,256]{1,0:T(8,128)} %copy-done.8) | copy-start | bytes 1572868
  30.3 13.2 %collective-permute-start.6 = (f32[512,256]{1,0:T(8,128)}, f32[512,256]{1,0:T(8,128)S(1)}, u32[]{:S(2)}, u32[]{:S(2)}) collective-permute-start(f32[512,256]{1,0:T(8,128)} %collective-permute-done.3.refs_3_.refs_4_), channel_id=1, source_target_pairs={{0,8},{4,12},{8,0},{12,4},{16,24},{20,28},{24,16},{28,20},{1,9},{5... | collective-permute-start | bytes 1572872 | tf_op jit(solution)/shard_map/ppermute | solution.py:556
  31.7 11.9 %collective-permute-start.5 = (f32[512,256]{1,0:T(8,128)}, f32[512,256]{1,0:T(8,128)S(1)}, u32[]{:S(2)}, u32[]{:S(2)}) collective-permute-start(f32[512,256]{1,0:T(8,128)} %collective-permute-done.3.refs_3_.refs_4_), channel_id=1, source_target_pairs={{0,4},{4,0},{8,12},{12,8},{16,20},{20,16},{24,28},{28,24},{1,5},{5... | collective-permute-start | bytes 1572872 | tf_op jit(solution)/shard_map/ppermute | solution.py:556
  32.0 22.9 %collective-permute-start.4 = (f32[512,256]{1,0:T(8,128)}, f32[512,256]{1,0:T(8,128)S(1)}, u32[]{:S(2)}, u32[]{:S(2)}) collective-permute-start(f32[512,256]{1,0:T(8,128)} %collective-permute-done.1.refs_2_), channel_id=1, source_target_pairs={{0,4},{4,0},{8,12},{12,8},{16,20},{20,16},{24,28},{28,24},{1,5},{5... | collective-permute-start | bytes 1572872 | tf_op jit(solution)/shard_map/ppermute | solution.py:556
  43.5 11.4 %copy-start.7 = (f32[80,2048]{1,0:T(8,128)S(1)}, f32[80,2048]{1,0:T(8,128)}, u32[]{:S(2)}) copy-start(f32[80,2048]{1,0:T(8,128)} %copy-done.6) | copy-start | bytes 1966084
  43.5 17.2 %copy-start.3 = (f32[176,2048]{1,0:T(8,128)S(1)}, f32[176,2048]{1,0:T(8,128)}, u32[]{:S(2)}) copy-start(f32[176,2048]{1,0:T(8,128)} %copy-done.2) | copy-start | bytes 4325380
  43.6 16.6 %collective-permute-start.7 = (f32[512,256]{1,0:T(8,128)S(1)}, f32[512,256]{1,0:T(8,128)S(1)}, u32[]{:S(2)}, u32[]{:S(2)}) collective-permute-start(f32[512,256]{1,0:T(8,128)S(1)} %collective-permute-done.5.refs_1_.refs_5_), channel_id=1, source_target_pairs={{0,8},{4,12},{8,0},{12,4},{16,24},{20,28},{24,16},{28,20},{1,9},{5... | collective-permute-start | bytes 1572872 | tf_op jit(solution)/shard_map/ppermute | solution.py:556
  43.9 28.8 %collective-permute-start.10 = (f32[512,256]{1,0:T(8,128)}, f32[512,256]{1,0:T(8,128)S(1)}, u32[]{:S(2)}, u32[]{:S(2)}) collective-permute-start(f32[512,256]{1,0:T(8,128)} %collective-permute-done.refs_0_), channel_id=1, source_target_pairs={{0,4},{4,0},{8,12},{12,8},{16,20},{20,16},{24,28},{28,24},{1,5},{5... | collective-permute-start | bytes 1572872 | tf_op jit(solution)/shard_map/ppermute | solution.py:556
  54.9 29.2 %collective-permute-start.9 = (f32[80,2048]{1,0:T(8,128)S(1)}, f32[80,2048]{1,0:T(8,128)S(1)}, u32[]{:S(2)}, u32[]{:S(2)}) collective-permute-start(f32[80,2048]{1,0:T(8,128)S(1)} %copy-done.7), channel_id=1, source_target_pairs={{0,2},{1,3},{2,0},{3,1},{4,6},{5,7},{6,4},{7,5},{8,10},{9,11},{10,... | collective-permute-start | bytes 1966088 | tf_op jit(solution)/shard_map/ppermute | solution.py:556
  56.1 27.9 %collective-permute-start.12 = (f32[512,256]{1,0:T(8,128)}, f32[512,256]{1,0:T(8,128)S(1)}, u32[]{:S(2)}, u32[]{:S(2)}) collective-permute-start(f32[512,256]{1,0:T(8,128)} %collective-permute-done.refs_0_), channel_id=1, source_target_pairs={{0,16},{4,20},{8,24},{12,28},{16,0},{20,4},{24,8},{28,12},{1,17},{... | collective-permute-start | bytes 1572872 | tf_op jit(solution)/shard_map/ppermute | solution.py:556
  60.3 23.8 %collective-permute-start.11 = (f32[512,256]{1,0:T(8,128)}, f32[512,256]{1,0:T(8,128)S(1)}, u32[]{:S(2)}, u32[]{:S(2)}) collective-permute-start(f32[512,256]{1,0:T(8,128)} %collective-permute-done.refs_0_), channel_id=1, source_target_pairs={{0,8},{4,12},{8,0},{12,4},{16,24},{20,28},{24,16},{28,20},{1,9},{5... | collective-permute-start | bytes 1572872 | tf_op jit(solution)/shard_map/ppermute | solution.py:556
  60.7 12.3 %copy-start.5 = (bf16[512,512]{1,0:T(8,128)(2,1)S(1)}, bf16[512,512]{1,0:T(8,128)(2,1)}, u32[]{:S(2)}) copy-start(bf16[512,512]{1,0:T(8,128)(2,1)} %copy-done.4) | copy-start | bytes 1572868
  72.7 11.4 %collective-permute-start.8 = (f32[16,2048]{1,0:T(8,128)S(1)}, f32[16,2048]{1,0:T(8,128)S(1)}, u32[]{:S(2)}, u32[]{:S(2)}) collective-permute-start(f32[16,2048]{1,0:T(8,128)S(1)} %get-tuple-element.118.mine_ref), channel_id=1, source_target_pairs={{0,2},{1,3},{2,0},{3,1},{4,6},{5,7},{6,4},{7,5},{8,10},{9,11},{10,... | collective-permute-start | bytes 393224 | tf_op jit(solution)/shard_map/ppermute | solution.py:556
  84.1 32.7 %collective-permute-start.22 = (f32[176,2048]{1,0:T(8,128)S(1)}, f32[176,2048]{1,0:T(8,128)S(1)}, u32[]{:S(2)}, u32[]{:S(2)}) collective-permute-start(f32[176,2048]{1,0:T(8,128)S(1)} %copy-done.3), channel_id=1, source_target_pairs={{0,2},{1,3},{2,0},{3,1},{4,6},{5,7},{6,4},{7,5},{8,10},{9,11},{10,... | collective-permute-start | bytes 4325384 | tf_op jit(solution)/shard_map/ppermute | solution.py:556
  84.1 17.2 %collective-permute-start.18 = (f32[512,256]{1,0:T(8,128)S(1)}, f32[512,256]{1,0:T(8,128)S(1)}, u32[]{:S(2)}, u32[]{:S(2)}) collective-permute-start(f32[512,256]{1,0:T(8,128)S(1)} %collective-permute-done.12.refs_3_.refs_4_), channel_id=1, source_target_pairs={{0,8},{4,12},{8,0},{12,4},{16,24},{20,28},{24,16},{28,20},{1,9},{5... | collective-permute-start | bytes 1572872 | tf_op jit(solution)/shard_map/ppermute | solution.py:556
  84.8 16.5 %collective-permute-start.17 = (f32[512,256]{1,0:T(8,128)S(1)}, f32[512,256]{1,0:T(8,128)S(1)}, u32[]{:S(2)}, u32[]{:S(2)}) collective-permute-start(f32[512,256]{1,0:T(8,128)S(1)} %collective-permute-done.12.refs_3_.refs_4_), channel_id=1, source_target_pairs={{0,4},{4,0},{8,12},{12,8},{16,20},{20,16},{24,28},{28,24},{1,5},{5... | collective-permute-start | bytes 1572872 | tf_op jit(solution)/shard_map/ppermute | solution.py:556
  84.8 3.8 %collective-permute-start.15 = (f32[16,2048]{1,0:T(8,128)S(1)}, f32[16,2048]{1,0:T(8,128)S(1)}, u32[]{:S(2)}, u32[]{:S(2)}) collective-permute-start(f32[16,2048]{1,0:T(8,128)S(1)} %add.9), channel_id=1, source_target_pairs={{0,1},{1,0},{2,3},{3,2},{4,5},{5,4},{6,7},{7,6},{8,9},{9,8},{10,11... | collective-permute-start | bytes 393224 | tf_op jit(solution)/shard_map/ppermute | solution.py:556
  88.7 12.6 %collective-permute-start.16 = (f32[8,1024]{1,0:T(8,128)S(1)}, f32[8,1024]{1,0:T(8,128)S(1)}, u32[]{:S(2)}, u32[]{:S(2)}) collective-permute-start(f32[8,1024]{1,0:T(8,128)S(1)} %get-tuple-element.131), channel_id=1, source_target_pairs={{0,8},{4,12},{8,0},{12,4},{16,24},{20,28},{24,16},{28,20},{1,9},{5... | collective-permute-start | bytes 98312 | tf_op jit(solution)/shard_map/ppermute | solution.py:556
  90.0 22.8 %collective-permute-start.14 = (f32[512,256]{1,0:T(8,128)S(1)}, f32[512,256]{1,0:T(8,128)S(1)}, u32[]{:S(2)}, u32[]{:S(2)}) collective-permute-start(f32[512,256]{1,0:T(8,128)S(1)} %collective-permute-done.11.refs_2_), channel_id=1, source_target_pairs={{0,4},{4,0},{8,12},{12,8},{16,20},{20,16},{24,28},{28,24},{1,5},{5... | collective-permute-start | bytes 1572872 | tf_op jit(solution)/shard_map/ppermute | solution.py:556
  101.3 12.9 %collective-permute-start.19 = (f32[512,256]{1,0:T(8,128)S(1)}, f32[512,256]{1,0:T(8,128)S(1)}, u32[]{:S(2)}, u32[]{:S(2)}) collective-permute-start(f32[512,256]{1,0:T(8,128)S(1)} %collective-permute-done.17.refs_0_.refs_5_), channel_id=1, source_target_pairs={{0,8},{4,12},{8,0},{12,4},{16,24},{20,28},{24,16},{28,20},{1,9},{5... | collective-permute-start | bytes 1572872 | tf_op jit(solution)/shard_map/ppermute | solution.py:556
  101.7 6.5 %collective-permute-start.20 = (f32[8,1024]{1,0:T(8,128)S(1)}, f32[8,1024]{1,0:T(8,128)S(1)}, u32[]{:S(2)}, u32[]{:S(2)}) collective-permute-start(f32[8,1024]{1,0:T(8,128)S(1)} %add.10), channel_id=1, source_target_pairs={{0,4},{4,0},{8,12},{12,8},{16,20},{20,16},{24,28},{28,24},{1,5},{5... | collective-permute-start | bytes 98312 | tf_op jit(solution)/shard_map/ppermute | solution.py:556
  108.2 8.6 %collective-permute-start.21 = (f32[8,1024]{1,0:T(8,128)S(1)}, f32[8,1024]{1,0:T(8,128)S(1)}, u32[]{:S(2)}, u32[]{:S(2)}) collective-permute-start(f32[8,1024]{1,0:T(8,128)S(1)} %add.11.refs_19_), channel_id=1, source_target_pairs={{0,16},{4,20},{8,24},{12,28},{16,0},{20,4},{24,8},{28,12},{1,17},{... | collective-permute-start | bytes 98312 | tf_op jit(solution)/shard_map/ppermute | solution.py:556
  134.7 11.2 %collective-permute-start.23 = (f32[520,2048]{1,0:T(8,128)}, f32[520,2048]{1,0:T(8,128)S(1)}, u32[]{:S(2)}, u32[]{:S(2)}) collective-permute-start(f32[520,2048]{1,0:T(8,128)} %get-tuple-element.157.refs_9_), channel_id=1, source_target_pairs={{0,1},{1,0},{2,3},{3,2},{4,5},{5,4},{6,7},{7,6},{8,9},{9,8},{10,11... | collective-permute-start | bytes 12779528 | tf_op jit(solution)/shard_map/ppermute | solution.py:556
  145.9 4.9 %copy-start.1 = (f32[256,512]{1,0:T(8,128)S(1)}, f32[256,512]{1,0:T(8,128)}, u32[]{:S(2)}) copy-start(f32[256,512]{1,0:T(8,128)} %param.7) | copy-start | bytes 1572868
  (4 other events, 3.8 us)

commit v11 on v10

--- a/solution.py
+++ b/solution.py
@@ -614,9 +614,9 @@
         acc, o2y, o3, oy, theirs, z_one, logits = tie(acc, o2y, o3, oy, theirs, z_one, logits)
         o3y, o1y, ty = hop(o2y, 2), hop(o1, 1), hop(theirs, 1)
         *e_two, zinfo = exp_parts(where, keys(3, 5, 6, 7), KC, logits, weights, dens_row, z_one, True, 2 * tile)
-        o1y, theirs, zinfo, held = tie(o1y, theirs, zinfo, x_own[1])
+        theirs, zinfo, held = tie(theirs, zinfo, x_own[1])
         t1, t2, x1 = hop(theirs, 2), hop(theirs, 4), send(held)
-        acc, o3y, zinfo = tie(acc, o3y, zinfo)
+        acc, o3y, o1y, zinfo = tie(acc, o3y, o1y, zinfo)
         pred_own, info = fwd("own_late", [o1y, o2y, o3, o3y], [(*e_two, 4 * KC, 0)], acc, zinfo, x_own)
         own = [mine, oy, o1, o1y, o2, o2y, o3, o3y]
         own_pick = lambda ix, block: [(block ^ ix[2]) == key for key in range(n_spot)]

time: 151 us -> 151 us (level)
  starting transfers between devices: 27.8 us -> 30.4 us
  waiting for transfers between devices: 15.6 us -> 13.1 us
    ppermute x24, starting transfers between devices: 27.8 us -> 30.4 us  [swap(): lax.ppermute(value, axis, [(i, i ^ bit) for i in range(lax.axis_size(axis...]
    ppermute x24, waiting for transfers between devices: 15.6 us -> 13.1 us  [swap(): lax.ppermute(value, axis, [(i, i ^ bit) for i in range(lax.axis_size(axis...]
  transfers between devices with their start and end apart: 24 -> 24, of which waited for: 6 -> 7; matrix products, arithmetic and copies ran while one was open for 1% -> 1% of each run, Pallas kernels for 51% -> 51%
where the time goes in v11:
time: 151 us
  Pallas kernels  99.5 us (66%)
  starting transfers between devices  30.4 us (20%)
  waiting for transfers between devices  13.1 us (9%)
  local copies, waits for them, and re-layouts  3.44 us (2%)
  other arithmetic  2.24 us (1%)
    pallas_call x13, Pallas kernels, call(): pl.pallas_call(kernel, out_shape=out_shape, grid_spec=pltpu.PrefetchScala...  99.4 us
    ppermute x24, starting transfers between devices, swap(): lax.ppermute(value, axis, [(i, i ^ bit) for i in range(lax.axis_size(axis...  30.4 us
    ppermute x24, waiting for transfers between devices, swap(): lax.ppermute(value, axis, [(i, i ^ bit) for i in range(lax.axis_size(axis...  13.1 us
    unnamed x24, local copies, waits for them, and re-layouts  3.07 us
  transfers between devices with their start and end apart: 24, of which 7 were waited for; matrix products, arithmetic and copies ran while one was open for 1% of the time, Pallas kernels for 51%

profile of v11, /device:TPU:1, one launch (start us, length us, event | category | flops | bytes accessed | tf_op | source)
XLA Modules:
  0.0 150.8 jit_solution(11480814968619633209)
XLA Ops:
  1.7 1.3 fusion.1.refs_0_
  3.0 2.1 %collective-permute-start.2 = (f32[512,256]{1,0:T(8,128)}, f32[512,256]{1,0:T(8,128)S(1)}, u32[]{:S(2)}, u32[]{:S(2)}) collective-permute-start(f32[512,256]{1,0:T(8,128)} %fusion.1.refs_0_), channel_id=1, source_target_pairs={{0,4},{4,0},{8,12},{12,8},{16,20},{20,16},{24,28},{28,24},{1,5},{5... | collective-permute-start | bytes 1572872 | tf_op jit(solution)/shard_map/ppermute | solution.py:556
  5.0 2.3 %collective-permute-start.3 = (f32[512,256]{1,0:T(8,128)}, f32[512,256]{1,0:T(8,128)}, u32[]{:S(2)}, u32[]{:S(2)}) collective-permute-start(f32[512,256]{1,0:T(8,128)} %fusion.1.refs_0_), channel_id=1, source_target_pairs={{0,16},{4,20},{8,24},{12,28},{16,0},{20,4},{24,8},{28,12},{1,17},{... | collective-permute-start | bytes 1572872 | tf_op jit(solution)/shard_map/ppermute | solution.py:556
  7.3 1.3 collective-permute-start.1
  10.1 5.0 %turn.1 = (f32[256,2048]{1,0:T(8,128)S(1)}, f32[80,2048]{1,0:T(8,128)S(1)}, f32[176,2048]{1,0:T(8,128)S(1)}) custom-call(s32[3]{0:T(128)S(1)} %pad_add_fusion.where, bf16[512,512]{1,0:T(8,128)(2,1)S(1)} %fusion.pick_ref, f32[2048,512]{1,0:T(8,128)} %x_ref.1), custom_call_target="tpu_custom_call" | custom-call | flops 1000 | bytes 1000 | tf_op jit(solution)/shard_map/turn/pallas_call | solution.py:33
  20.6 6.2 %exp_parts.2 = (bf16[1024,2048]{1,0:T(8,128)(2,1)S(1)}, bf16[1024,2048]{1,0:T(8,128)(2,1)S(1)}, f32[8,2048]{1,0:T(8,128)S(1)}) custom-call(s32[3]{0:T(128)S(1)} %pad_add_fusion.where, f32[2048,2048]{1,0:T(8,128)} %logit_ref, f32[2048,2048]{1,0:T(8,128)} %logit_ref, f32[2048,2048]{1,0:T(8,128)} %logit_ref, f32[2048,2048]{1,0:T(8,128)} %logit_ref, ...), custom_call_target="tpu_custom_call" | custom-call | flops 1000 | bytes 1000 | tf_op jit(solution)/shard_map/exp_parts/pallas_call | solution.py:33
  26.7 3.6 %collective-permute-done.3.refs_3_.refs_4_ = f32[512,256]{1,0:T(8,128)} collective-permute-done((f32[512,256]{1,0:T(8,128)}, f32[512,256]{1,0:T(8,128)}, u32[]{:S(2)}, u32[]{:S(2)}) %collective-permute-start.3) | collective-permute-done | bytes 524320 | tf_op jit(solution)/shard_map/ppermute | solution.py:556
  30.3 1.4 collective-permute-start.5
  32.0 1.2 collective-permute-start.7
  33.2 10.3 %own_early.1.refs_6_ = f32[512,2048]{1,0:T(8,128)S(1)} custom-call(s32[3]{0:T(128)S(1)} %pad_add_fusion.where, f32[512,256]{1,0:T(8,128)} %fusion.1.refs_0_, f32[512,256]{1,0:T(8,128)S(1)} %copy-done.9, f32[512,256]{1,0:T(8,128)} %collective-permute-done.1.refs_2_, f32[512,256]{1,0:T(8,128)} %collective-permute-done.3.refs_3_.refs_4_, ...), custom_call_target="tpu_custom_call" | custom-call | flops 1000 | bytes 1000 | tf_op jit(solution)/shard_map/own_early/pallas_call | solution.py:33
  44.1 6.4 %exp_parts.3 = (bf16[1024,2048]{1,0:T(8,128)(2,1)S(1)}, bf16[1024,2048]{1,0:T(8,128)(2,1)S(1)}, f32[8,2048]{1,0:T(8,128)S(1)}) custom-call(s32[3]{0:T(128)S(1)} %pad_add_fusion.where, f32[2048,2048]{1,0:T(8,128)} %logit_ref, f32[2048,2048]{1,0:T(8,128)} %logit_ref, f32[2048,2048]{1,0:T(8,128)} %logit_ref, f32[2048,2048]{1,0:T(8,128)} %logit_ref, ...), custom_call_target="tpu_custom_call" | custom-call | flops 1000 | bytes 1000 | tf_op jit(solution)/shard_map/exp_parts/pallas_call | solution.py:33
  50.6 1.3 collective-permute-start.9
  51.9 3.0 %collective-permute-done.7.refs_0_.refs_3_ = f32[512,256]{1,0:T(8,128)S(1)} collective-permute-done((f32[512,256]{1,0:T(8,128)}, f32[512,256]{1,0:T(8,128)S(1)}, u32[]{:S(2)}, u32[]{:S(2)}) %collective-permute-start.7) | collective-permute-done | bytes 524320 | tf_op jit(solution)/shard_map/ppermute | solution.py:556
  54.9 4.2 %collective-permute-start.12 = (f32[512,256]{1,0:T(8,128)}, f32[512,256]{1,0:T(8,128)S(1)}, u32[]{:S(2)}, u32[]{:S(2)}) collective-permute-start(f32[512,256]{1,0:T(8,128)} %collective-permute-done.refs_0_), channel_id=1, source_target_pairs={{0,16},{4,20},{8,24},{12,28},{16,0},{20,4},{24,8},{28,12},{1,17},{... | collective-permute-start | bytes 1572872 | tf_op jit(solution)/shard_map/ppermute | solution.py:556
  59.5 12.0 %own_late.1 = (f32[512,2048]{1,0:T(8,128)}, f32[16,2048]{1,0:T(8,128)S(1)}) custom-call(s32[3]{0:T(128)S(1)} %pad_add_fusion.where, f32[512,256]{1,0:T(8,128)S(1)} %collective-permute-done.7.refs_0_.refs_3_, f32[512,256]{1,0:T(8,128)S(1)} %collective-permute-done.4.refs_1_.refs_5_, f32[512,256]{1,0:T(8,128)S(1)} %collective-permute-done.5.refs_2_.refs_6_, ...), custom_call_target="tpu_custom_call" | custom-call | flops 1000 | bytes 1000 | tf_op jit(solution)/shard_map/own_late/pallas_call | solution.py:33
  71.5 1.2 collective-permute-start.8
  72.7 6.1 %emit.1 = f32[2048,512]{1,0:T(8,128)} custom-call(s32[3]{0:T(128)S(1)} %pad_add_fusion.where, f32[512,2048]{1,0:T(8,128)} %get-tuple-element.117.pred_ref.refs_8_, bf16[512,512]{1,0:T(8,128)(2,1)S(1)} %copy-done.5), custom_call_target="tpu_custom_call" | custom-call | flops 1000 | bytes 1000 | tf_op jit(solution)/shard_map/emit/pallas_call | solution.py:33
  78.7 3.2 %collective-permute-done.12.refs_3_.refs_4_ = f32[512,256]{1,0:T(8,128)S(1)} collective-permute-done((f32[512,256]{1,0:T(8,128)}, f32[512,256]{1,0:T(8,128)S(1)}, u32[]{:S(2)}, u32[]{:S(2)}) %collective-permute-start.12) | collective-permute-done | bytes 524320 | tf_op jit(solution)/shard_map/ppermute | solution.py:556
  82.6 1.2 collective-permute-start.22
  84.8 2.7 %collective-permute-start.15 = (f32[16,2048]{1,0:T(8,128)S(1)}, f32[16,2048]{1,0:T(8,128)S(1)}, u32[]{:S(2)}, u32[]{:S(2)}) collective-permute-start(f32[16,2048]{1,0:T(8,128)S(1)} %add.9), channel_id=1, source_target_pairs={{0,1},{1,0},{2,3},{3,2},{4,5},{5,4},{6,7},{7,6},{8,9},{9,8},{10,11... | collective-permute-start | bytes 393224 | tf_op jit(solution)/shard_map/ppermute | solution.py:556
  88.7 1.3 collective-permute-start.16
  90.0 1.2 collective-permute-start.14
  91.2 10.1 %other_mid.1.refs_6_ = f32[512,2048]{1,0:T(8,128)S(1)} custom-call(s32[3]{0:T(128)S(1)} %pad_add_fusion.where, f32[512,256]{1,0:T(8,128)} %collective-permute-done.refs_0_, f32[512,256]{1,0:T(8,128)S(1)} %collective-permute-done.10.refs_1_, f32[512,256]{1,0:T(8,128)S(1)} %collective-permute-done.11.refs_2_, ...), custom_call_target="tpu_custom_call" | custom-call | flops 1000 | bytes 1000 | tf_op jit(solution)/shard_map/other_mid/pallas_call | solution.py:33
  101.8 6.3 %other_more.1.refs_6_ = f32[512,2048]{1,0:T(8,128)} custom-call(s32[3]{0:T(128)S(1)} %pad_add_fusion.where, f32[512,256]{1,0:T(8,128)S(1)} %collective-permute-done.17.refs_0_.refs_5_, f32[512,256]{1,0:T(8,128)S(1)} %collective-permute-done.18.refs_1_.refs_6_, bf16[1024,2048]{1,0:T(8,128)(2,1)S(1)} %get-tuple-element.111.refs_4_.refs_2_.refs_3_, ...), custom_call_target="tpu_custom_call" | custom-call | flops 1000 | bytes 1000 | tf_op jit(solution)/shard_map/other_more/pallas_call | solution.py:33
  108.1 2.1 %collective-permute-start.21 = (f32[8,1024]{1,0:T(8,128)S(1)}, f32[8,1024]{1,0:T(8,128)S(1)}, u32[]{:S(2)}, u32[]{:S(2)}) collective-permute-start(f32[8,1024]{1,0:T(8,128)S(1)} %add.11.refs_19_), channel_id=1, source_target_pairs={{0,16},{4,20},{8,24},{12,28},{16,0},{20,4},{24,8},{28,12},{1,17},{... | collective-permute-start | bytes 98312 | tf_op jit(solution)/shard_map/ppermute | solution.py:556
  110.3 2.4 %rows_left.2 = (bf16[1024,512]{1,0:T(8,128)(2,1)S(1)}, bf16[1024,512]{1,0:T(8,128)(2,1)S(1)}) custom-call(s32[3]{0:T(128)S(1)} %pad_add_fusion.where, f32[512,256]{1,0:T(8,128)} %fusion.1.refs_0_, f32[512,256]{1,0:T(8,128)S(1)} %copy-done.9, f32[512,256]{1,0:T(8,128)} %collective-permute-done.1.refs_2_, ...), custom_call_target="tpu_custom_call" | custom-call | flops 1000 | bytes 1000 | tf_op jit(solution)/shard_map/rows_left/pallas_call | solution.py:33
  112.7 1.6 %collective-permute-done.19.refs_7_.refs_1_ = f32[512,256]{1,0:T(8,128)S(1)} collective-permute-done((f32[512,256]{1,0:T(8,128)S(1)}, f32[512,256]{1,0:T(8,128)S(1)}, u32[]{:S(2)}, u32[]{:S(2)}) %collective-permute-start.19) | collective-permute-done | bytes 524320 | tf_op jit(solution)/shard_map/ppermute | solution.py:556
  114.3 2.4 %rows_left.3 = (bf16[1024,512]{1,0:T(8,128)(2,1)S(1)}, bf16[1024,512]{1,0:T(8,128)(2,1)S(1)}) custom-call(s32[3]{0:T(128)S(1)} %pad_add_fusion.where, f32[512,256]{1,0:T(8,128)} %collective-permute-done.refs_0_, f32[512,256]{1,0:T(8,128)S(1)} %collective-permute-done.10.refs_1_, f32[512,256]{1,0:T(8,128)S(1)} %collective-permute-done.11.refs_2_, ...), custom_call_target="tpu_custom_call" | custom-call | flops 1000 | bytes 1000 | tf_op jit(solution)/shard_map/rows_left/pallas_call | solution.py:33
  116.8 18.0 %back_sum.1 = (f32[520,2048]{1,0:T(8,128)}, bf16[1024,2048]{1,0:T(8,128)(2,1)S(1)}, bf16[1024,2048]{1,0:T(8,128)(2,1)S(1)}, f32[8,128]{1,0:T(8,128)S(1)}) custom-call(s32[3]{0:T(128)S(1)} %pad_add_fusion.where, f32[512,256]{1,0:T(8,128)S(1)} %collective-permute-done.14.refs_3_.refs_0_, f32[512,256]{1,0:T(8,128)S(1)} %collective-permute-done.19.refs_7_.refs_1_, ...), custom_call_target="tpu_custom_call" | custom-call | flops 1000 | bytes 1000 | tf_op jit(solution)/shard_map/back_sum/pallas_call | solution.py:33
  134.7 1.9 %collective-permute-start.23 = (f32[520,2048]{1,0:T(8,128)}, f32[520,2048]{1,0:T(8,128)S(1)}, u32[]{:S(2)}, u32[]{:S(2)}) collective-permute-start(f32[520,2048]{1,0:T(8,128)} %get-tuple-element.157.refs_9_), channel_id=1, source_target_pairs={{0,1},{1,0},{2,3},{3,2},{4,5},{5,4},{6,7},{7,6},{8,9},{9,8},{10,11... | collective-permute-start | bytes 12779528 | tf_op jit(solution)/shard_map/ppermute | solution.py:556
  136.7 9.2 %back_own.1.mine_ref = f32[512,2048]{1,0:T(8,128)S(1)} custom-call(s32[3]{0:T(128)S(1)} %pad_add_fusion.where, bf16[1024,512]{1,0:T(8,128)(2,1)S(1)} %get-tuple-element.138.refs_15_.refs_0_, bf16[1024,512]{1,0:T(8,128)(2,1)S(1)} %get-tuple-element.145.refs_16_.refs_1_, bf16[1024,512]{1,0:T(8,128)(2,1)S(1)} %get-tuple-element.146.refs_17_.refs_2_, ...), custom_call_target="tpu_custom_call" | custom-call | flops 1000 | bytes 1000 | tf_op jit(solution)/shard_map/back_own/pallas_call | solution.py:33
  145.9 4.9 %back_end.1 = (f32[512,2048]{1,0:T(8,128)}, f32[3]{0:T(128)}) custom-call(s32[3]{0:T(128)S(1)} %pad_add_fusion.where, f32[512,2048]{1,0:T(8,128)S(1)} %back_own.1.mine_ref, f32[520,2048]{1,0:T(8,128)S(1)} %collective-permute-done.23.got_ref, f32[2048,2048]{1,0:T(8,128)} %logit_ref, f32[8,2048]{1,0:T(8,128)S(1)} %get-tuple-element.114.refs_7_.z_ref, ...), custom_call_target="tpu_custom_call" | custom-call | flops 1000 | bytes 1000 | tf_op jit(solution)/shard_map/back_end/pallas_call | solution.py:33
  (64 shorter events, 12.5 us)
Async XLA Ops:
  0.6 18.3 %copy-start.11 = (s32[2048]{0:T(1024)S(1)}, s32[2048]{0:T(1024)}, u32[]{:S(2)}) copy-start(s32[2048]{0:T(1024)} %param.9) | copy-start | bytes 24580
  0.7 19.9 %copy-start.10 = (f32[2048]{0:T(1024)S(1)}, f32[2048]{0:T(1024)}, u32[]{:S(2)}) copy-start(f32[2048]{0:T(1024)} %param.10) | copy-start | bytes 24580
  3.0 14.1 %collective-permute-start.2 = (f32[512,256]{1,0:T(8,128)}, f32[512,256]{1,0:T(8,128)S(1)}, u32[]{:S(2)}, u32[]{:S(2)}) collective-permute-start(f32[512,256]{1,0:T(8,128)} %fusion.1.refs_0_), channel_id=1, source_target_pairs={{0,4},{4,0},{8,12},{12,8},{16,20},{20,16},{24,28},{28,24},{1,5},{5... | collective-permute-start | bytes 1572872 | tf_op jit(solution)/shard_map/ppermute | solution.py:556
  5.0 25.3 %collective-permute-start.3 = (f32[512,256]{1,0:T(8,128)}, f32[512,256]{1,0:T(8,128)}, u32[]{:S(2)}, u32[]{:S(2)}) collective-permute-start(f32[512,256]{1,0:T(8,128)} %fusion.1.refs_0_), channel_id=1, source_target_pairs={{0,16},{4,20},{8,24},{12,28},{16,0},{20,4},{24,8},{28,12},{1,17},{... | collective-permute-start | bytes 1572872 | tf_op jit(solution)/shard_map/ppermute | solution.py:556
  7.3 23.0 %collective-permute-start.1 = (f32[512,256]{1,0:T(8,128)}, f32[512,256]{1,0:T(8,128)}, u32[]{:S(2)}, u32[]{:S(2)}) collective-permute-start(f32[512,256]{1,0:T(8,128)} %fusion.1.refs_0_), channel_id=1, source_target_pairs={{0,8},{4,12},{8,0},{12,4},{16,24},{20,28},{24,16},{28,20},{1,9},{5... | collective-permute-start | bytes 1572872 | tf_op jit(solution)/shard_map/ppermute | solution.py:556
  8.6 21.7 %collective-permute-start = (f32[512,256]{1,0:T(8,128)}, f32[512,256]{1,0:T(8,128)}, u32[]{:S(2)}, u32[]{:S(2)}) collective-permute-start(f32[512,256]{1,0:T(8,128)} %fusion.1.refs_0_), channel_id=1, source_target_pairs={{0,2},{1,3},{2,0},{3,1},{4,6},{5,7},{6,4},{7,5},{8,10},{9,11},{10,... | collective-permute-start | bytes 1572872 | tf_op jit(solution)/shard_map/ppermute | solution.py:556
  10.0 10.2 %copy-start.4 = (bf16[512,512]{1,0:T(8,128)(2,1)}, bf16[512,512]{1,0:T(8,128)(2,1)S(1)}, u32[]{:S(2)}) copy-start(bf16[512,512]{1,0:T(8,128)(2,1)S(1)} %fusion.pick_ref) | copy-start | bytes 1572868
  17.9 64.7 %collective-permute-start.13 = (f32[256,2048]{1,0:T(8,128)S(1)}, f32[256,2048]{1,0:T(8,128)}, u32[]{:S(2)}, u32[]{:S(2)}) collective-permute-start(f32[256,2048]{1,0:T(8,128)S(1)} %get-tuple-element.115.refs_8_.refs_9_), channel_id=1, source_target_pairs={{0,2},{1,3},{2,0},{3,1},{4,6},{5,7},{6,4},{7,5},{8,10},{9,11},{10,... | collective-permute-start | bytes 6291464 | tf_op jit(solution)/shard_map/ppermute | solution.py:556
  20.6 12.6 %copy-start.9 = (f32[512,256]{1,0:T(8,128)S(1)}, f32[512,256]{1,0:T(8,128)}, u32[]{:S(2)}) copy-start(f32[512,256]{1,0:T(8,128)} %copy-done.8) | copy-start | bytes 1572868
  30.3 13.2 %collective-permute-start.5 = (f32[512,256]{1,0:T(8,128)}, f32[512,256]{1,0:T(8,128)S(1)}, u32[]{:S(2)}, u32[]{:S(2)}) collective-permute-start(f32[512,256]{1,0:T(8,128)} %collective-permute-done.3.refs_3_.refs_4_), channel_id=1, source_target_pairs={{0,8},{4,12},{8,0},{12,4},{16,24},{20,28},{24,16},{28,20},{1,9},{5... | collective-permute-start | bytes 1572872 | tf_op jit(solution)/shard_map/ppermute | solution.py:556
  31.7 11.9 %collective-permute-start.4 = (f32[512,256]{1,0:T(8,128)}, f32[512,256]{1,0:T(8,128)S(1)}, u32[]{:S(2)}, u32[]{:S(2)}) collective-permute-start(f32[512,256]{1,0:T(8,128)} %collective-permute-done.3.refs_3_.refs_4_), channel_id=1, source_target_pairs={{0,4},{4,0},{8,12},{12,8},{16,20},{20,16},{24,28},{28,24},{1,5},{5... | collective-permute-start | bytes 1572872 | tf_op jit(solution)/shard_map/ppermute | solution.py:556
  32.0 22.9 %collective-permute-start.7 = (f32[512,256]{1,0:T(8,128)}, f32[512,256]{1,0:T(8,128)S(1)}, u32[]{:S(2)}, u32[]{:S(2)}) collective-permute-start(f32[512,256]{1,0:T(8,128)} %collective-permute-done.1.refs_2_), channel_id=1, source_target_pairs={{0,4},{4,0},{8,12},{12,8},{16,20},{20,16},{24,28},{28,24},{1,5},{5... | collective-permute-start | bytes 1572872 | tf_op jit(solution)/shard_map/ppermute | solution.py:556
  43.5 7.1 %copy-start.7 = (f32[80,2048]{1,0:T(8,128)S(1)}, f32[80,2048]{1,0:T(8,128)}, u32[]{:S(2)}) copy-start(f32[80,2048]{1,0:T(8,128)} %copy-done.6) | copy-start | bytes 1966084
  43.5 16.0 %copy-start.3 = (f32[176,2048]{1,0:T(8,128)S(1)}, f32[176,2048]{1,0:T(8,128)}, u32[]{:S(2)}) copy-start(f32[176,2048]{1,0:T(8,128)} %copy-done.2) | copy-start | bytes 4325380
  43.6 15.4 %collective-permute-start.6 = (f32[512,256]{1,0:T(8,128)S(1)}, f32[512,256]{1,0:T(8,128)S(1)}, u32[]{:S(2)}, u32[]{:S(2)}) collective-permute-start(f32[512,256]{1,0:T(8,128)S(1)} %collective-permute-done.4.refs_1_.refs_5_), channel_id=1, source_target_pairs={{0,8},{4,12},{8,0},{12,4},{16,24},{20,28},{24,16},{28,20},{1,9},{5... | collective-permute-start | bytes 1572872 | tf_op jit(solution)/shard_map/ppermute | solution.py:556
  43.9 27.5 %collective-permute-start.10 = (f32[512,256]{1,0:T(8,128)}, f32[512,256]{1,0:T(8,128)S(1)}, u32[]{:S(2)}, u32[]{:S(2)}) collective-permute-start(f32[512,256]{1,0:T(8,128)} %collective-permute-done.refs_0_), channel_id=1, source_target_pairs={{0,4},{4,0},{8,12},{12,8},{16,20},{20,16},{24,28},{28,24},{1,5},{5... | collective-permute-start | bytes 1572872 | tf_op jit(solution)/shard_map/ppermute | solution.py:556
  50.6 32.0 %collective-permute-start.9 = (f32[80,2048]{1,0:T(8,128)S(1)}, f32[80,2048]{1,0:T(8,128)S(1)}, u32[]{:S(2)}, u32[]{:S(2)}) collective-permute-start(f32[80,2048]{1,0:T(8,128)S(1)} %copy-done.7), channel_id=1, source_target_pairs={{0,2},{1,3},{2,0},{3,1},{4,6},{5,7},{6,4},{7,5},{8,10},{9,11},{10,... | collective-permute-start | bytes 1966088 | tf_op jit(solution)/shard_map/ppermute | solution.py:556
  54.9 27.0 %collective-permute-start.12 = (f32[512,256]{1,0:T(8,128)}, f32[512,256]{1,0:T(8,128)S(1)}, u32[]{:S(2)}, u32[]{:S(2)}) collective-permute-start(f32[512,256]{1,0:T(8,128)} %collective-permute-done.refs_0_), channel_id=1, source_target_pairs={{0,16},{4,20},{8,24},{12,28},{16,0},{20,4},{24,8},{28,12},{1,17},{... | collective-permute-start | bytes 1572872 | tf_op jit(solution)/shard_map/ppermute | solution.py:556
  59.1 22.8 %collective-permute-start.11 = (f32[512,256]{1,0:T(8,128)}, f32[512,256]{1,0:T(8,128)S(1)}, u32[]{:S(2)}, u32[]{:S(2)}) collective-permute-start(f32[512,256]{1,0:T(8,128)} %collective-permute-done.refs_0_), channel_id=1, source_target_pairs={{0,8},{4,12},{8,0},{12,4},{16,24},{20,28},{24,16},{28,20},{1,9},{5... | collective-permute-start | bytes 1572872 | tf_op jit(solution)/shard_map/ppermute | solution.py:556
  59.5 13.2 %copy-start.5 = (bf16[512,512]{1,0:T(8,128)(2,1)S(1)}, bf16[512,512]{1,0:T(8,128)(2,1)}, u32[]{:S(2)}) copy-start(bf16[512,512]{1,0:T(8,128)(2,1)} %copy-done.4) | copy-start | bytes 1572868
  71.5 11.1 %collective-permute-start.8 = (f32[16,2048]{1,0:T(8,128)S(1)}, f32[16,2048]{1,0:T(8,128)S(1)}, u32[]{:S(2)}, u32[]{:S(2)}) collective-permute-start(f32[16,2048]{1,0:T(8,128)S(1)} %get-tuple-element.118.mine_ref), channel_id=1, source_target_pairs={{0,2},{1,3},{2,0},{3,1},{4,6},{5,7},{6,4},{7,5},{8,10},{9,11},{10,... | collective-permute-start | bytes 393224 | tf_op jit(solution)/shard_map/ppermute | solution.py:556
  82.6 34.2 %collective-permute-start.22 = (f32[176,2048]{1,0:T(8,128)S(1)}, f32[176,2048]{1,0:T(8,128)S(1)}, u32[]{:S(2)}, u32[]{:S(2)}) collective-permute-start(f32[176,2048]{1,0:T(8,128)S(1)} %copy-done.3), channel_id=1, source_target_pairs={{0,2},{1,3},{2,0},{3,1},{4,6},{5,7},{6,4},{7,5},{8,10},{9,11},{10,... | collective-permute-start | bytes 4325384 | tf_op jit(solution)/shard_map/ppermute | solution.py:556
  83.8 17.6 %collective-permute-start.18 = (f32[512,256]{1,0:T(8,128)S(1)}, f32[512,256]{1,0:T(8,128)S(1)}, u32[]{:S(2)}, u32[]{:S(2)}) collective-permute-start(f32[512,256]{1,0:T(8,128)S(1)} %collective-permute-done.12.refs_3_.refs_4_), channel_id=1, source_target_pairs={{0,8},{4,12},{8,0},{12,4},{16,24},{20,28},{24,16},{28,20},{1,9},{5... | collective-permute-start | bytes 1572872 | tf_op jit(solution)/shard_map/ppermute | solution.py:556
  84.8 16.5 %collective-permute-start.17 = (f32[512,256]{1,0:T(8,128)S(1)}, f32[512,256]{1,0:T(8,128)S(1)}, u32[]{:S(2)}, u32[]{:S(2)}) collective-permute-start(f32[512,256]{1,0:T(8,128)S(1)} %collective-permute-done.12.refs_3_.refs_4_), channel_id=1, source_target_pairs={{0,4},{4,0},{8,12},{12,8},{16,20},{20,16},{24,28},{28,24},{1,5},{5... | collective-permute-start | bytes 1572872 | tf_op jit(solution)/shard_map/ppermute | solution.py:556
  84.8 3.7 %collective-permute-start.15 = (f32[16,2048]{1,0:T(8,128)S(1)}, f32[16,2048]{1,0:T(8,128)S(1)}, u32[]{:S(2)}, u32[]{:S(2)}) collective-permute-start(f32[16,2048]{1,0:T(8,128)S(1)} %add.9), channel_id=1, source_target_pairs={{0,1},{1,0},{2,3},{3,2},{4,5},{5,4},{6,7},{7,6},{8,9},{9,8},{10,11... | collective-permute-start | bytes 393224 | tf_op jit(solution)/shard_map/ppermute | solution.py:556
  88.7 12.7 %collective-permute-start.16 = (f32[8,1024]{1,0:T(8,128)S(1)}, f32[8,1024]{1,0:T(8,128)S(1)}, u32[]{:S(2)}, u32[]{:S(2)}) collective-permute-start(f32[8,1024]{1,0:T(8,128)S(1)} %get-tuple-element.131), channel_id=1, source_target_pairs={{0,8},{4,12},{8,0},{12,4},{16,24},{20,28},{24,16},{28,20},{1,9},{5... | collective-permute-start | bytes 98312 | tf_op jit(solution)/shard_map/ppermute | solution.py:556
  90.0 22.8 %collective-permute-start.14 = (f32[512,256]{1,0:T(8,128)S(1)}, f32[512,256]{1,0:T(8,128)S(1)}, u32[]{:S(2)}, u32[]{:S(2)}) collective-permute-start(f32[512,256]{1,0:T(8,128)S(1)} %collective-permute-done.11.refs_2_), channel_id=1, source_target_pairs={{0,4},{4,0},{8,12},{12,8},{16,20},{20,16},{24,28},{28,24},{1,5},{5... | collective-permute-start | bytes 1572872 | tf_op jit(solution)/shard_map/ppermute | solution.py:556
  101.3 12.9 %collective-permute-start.19 = (f32[512,256]{1,0:T(8,128)S(1)}, f32[512,256]{1,0:T(8,128)S(1)}, u32[]{:S(2)}, u32[]{:S(2)}) collective-permute-start(f32[512,256]{1,0:T(8,128)S(1)} %collective-permute-done.17.refs_0_.refs_5_), channel_id=1, source_target_pairs={{0,8},{4,12},{8,0},{12,4},{16,24},{20,28},{24,16},{28,20},{1,9},{5... | collective-permute-start | bytes 1572872 | tf_op jit(solution)/shard_map/ppermute | solution.py:556
  101.6 6.5 %collective-permute-start.20 = (f32[8,1024]{1,0:T(8,128)S(1)}, f32[8,1024]{1,0:T(8,128)S(1)}, u32[]{:S(2)}, u32[]{:S(2)}) collective-permute-start(f32[8,1024]{1,0:T(8,128)S(1)} %add.10), channel_id=1, source_target_pairs={{0,4},{4,0},{8,12},{12,8},{16,20},{20,16},{24,28},{28,24},{1,5},{5... | collective-permute-start | bytes 98312 | tf_op jit(solution)/shard_map/ppermute | solution.py:556
  108.1 8.6 %collective-permute-start.21 = (f32[8,1024]{1,0:T(8,128)S(1)}, f32[8,1024]{1,0:T(8,128)S(1)}, u32[]{:S(2)}, u32[]{:S(2)}) collective-permute-start(f32[8,1024]{1,0:T(8,128)S(1)} %add.11.refs_19_), channel_id=1, source_target_pairs={{0,16},{4,20},{8,24},{12,28},{16,0},{20,4},{24,8},{28,12},{1,17},{... | collective-permute-start | bytes 98312 | tf_op jit(solution)/shard_map/ppermute | solution.py:556
  134.7 11.2 %collective-permute-start.23 = (f32[520,2048]{1,0:T(8,128)}, f32[520,2048]{1,0:T(8,128)S(1)}, u32[]{:S(2)}, u32[]{:S(2)}) collective-permute-start(f32[520,2048]{1,0:T(8,128)} %get-tuple-element.157.refs_9_), channel_id=1, source_target_pairs={{0,1},{1,0},{2,3},{3,2},{4,5},{5,4},{6,7},{7,6},{8,9},{9,8},{10,11... | collective-permute-start | bytes 12779528 | tf_op jit(solution)/shard_map/ppermute | solution.py:556
  145.9 4.9 %copy-start.1 = (f32[256,512]{1,0:T(8,128)S(1)}, f32[256,512]{1,0:T(8,128)}, u32[]{:S(2)}) copy-start(f32[256,512]{1,0:T(8,128)} %param.7) | copy-start | bytes 1572868
  (4 other events, 3.8 us)
